TPU v7x, 32 devices: a whole 2x2x4 slice. The times are simulated.
32 devices in a mesh: dp: 8 (over y, x, core), shard: 4 (over z).
Axes of the slice: x: 2, y: 2, z: 4, core: 2. Of those that a mesh axis runs over, the one named last changes fastest.
Arguments:
- tokens: bfloat16 [8192, 1536], P(('dp', 'shard')), may hold values from -6 to 6
- cotangent: bfloat16 [8192, 1536], P(('dp', 'shard')), may hold values from -6 to 6
- seq_start: int32 [8192], P(('dp', 'shard')), may hold values from 0 to 192, as said below
- live_mask: int32 [8192], P(('dp', 'shard')), may hold values from 0 to 1, as said below
- input_proj: bfloat16 [2, 1536, 2048], P(None, None, 'shard'), may hold values from -0.15625 to 0.15625
- gate_blocks: bfloat16 [2, 16, 128, 128], P(None, 'shard'), may hold values from -0.5 to 0.5
- output_proj: bfloat16 [2048, 1536], P('shard'), may hold values from -0.375 to 0.375
- ffn_gate_up: bfloat16 [2, 1536, 4608], P(None, None, 'shard'), may hold values from -0.15625 to 0.15625
- ffn_down: bfloat16 [4608, 1536], P('shard'), may hold values from -0.1875 to 0.1875
- conv_taps: bfloat16 [5, 2048], P(None, 'shard'), may hold values from -3 to 3
- gate_bias: bfloat16 [2, 2048], P(None, 'shard'), may hold values from -3 to 3
- decay_param: bfloat16 [2048], P('shard'), may hold values from 3 to 8
- norm_gains: bfloat16 [2, 1536], P(None, 'shard'), may hold values from 0.5 to 1.5
- master_shard: float32 [4, 7803648], P('shard', 'dp'), may hold values from -0.75 to 0.75
- first_moment: float32 [4, 7803648], P('shard', 'dp'), may hold values from -6 to 6
- second_moment: float32 [4, 7803648], P('shard', 'dp'), may hold values from 0.1 to 10
Outputs:
- block_out: bfloat16 [8192, 1536], P(('dp', 'shard'))
- tokens_grad: bfloat16 [8192, 1536], P(('dp', 'shard'))
- weight_grads: float32 [4, 7803648], P('shard', 'dp')
- new_master: float32 [4, 7803648], P('shard', 'dp')
- new_first: float32 [4, 7803648], P('shard', 'dp')
- new_second: float32 [4, 7803648], P('shard', 'dp')
- new_weights: bfloat16 [4, 7803648], P(None, 'dp')
- bias_grad: float32 [2, 2048], P(None, 'shard')
Inputs may be any that keep to these rules, and one draw needn't show every extreme that they name: Within each device's block of 256 slots the live slots form a prefix of 2, 3 or 4 times 256 // 4 slots, and some device has all its slots live; every sequence begins at a multiple of 64, and every live sequence has 64 slots or more; seq_start is constant over a sequence and equals its first slot; the block holds one to four live sequences, and its padding forms one more sequence. `live_mask`: 1 exactly on the live prefix of each device's block.
All inputs are finite; a program needn't handle non-finite values.
Results may differ from a plain program's by a relative error of at most 0.017.
Values may be sent and summed in bfloat16 or wider, within the bound.
A program may use at most 384 MiB of HBM per device.

v0:
```python
import jax
import jax.numpy as jnp
from jax import lax
from jax.sharding import PartitionSpec as P

norm_eps = 1e-06
gate_scale = 8.0
beta_one = 0.9
beta_two = 0.95
learn_rate = 0.01
weight_decay = 0.1
adam_eps = 1e-08
corr_one = 1.0 - beta_one**10.0
corr_two = 1.0 - beta_two**10.0


def rms_scale(values, gain):
    return values * lax.rsqrt(jnp.mean(values * values, axis=-1, keepdims=True) + norm_eps) * gain


def conv_mix(signal, taps, position):
    result = taps[-1] + taps[0] * signal
    for shift_by in range(1, taps.shape[0] - 1):
        moved = jnp.pad(signal, ((shift_by, 0), (0, 0)))[:-shift_by]
        result = result + taps[shift_by] * jnp.where((position >= shift_by)[:, None], moved, 0.0)
    return result


def combine_steps(earlier, later):
    decay_first, value_first = earlier
    decay_second, value_second = later
    return (decay_first * decay_second, decay_second * value_first + value_second)


def recurrence(logits, signal, branch, bias_term, decay_term, position):
    row_count = signal.shape[0]
    recur_gate = jax.nn.sigmoid(logits[0].reshape(row_count, -1) + bias_term[0])
    input_gate = jax.nn.sigmoid(logits[1].reshape(row_count, -1) + bias_term[1])
    log_decay = -gate_scale * recur_gate * jax.nn.softplus(-decay_term)
    decay_rate = jnp.where((position > 0)[:, None], jnp.exp(log_decay), 0.0)
    drive_term = jnp.sqrt(-jnp.expm1(2.0 * log_decay)) * input_gate * signal
    states = lax.associative_scan(combine_steps, (decay_rate, drive_term), axis=0)[1]
    return states * jax.nn.gelu(branch)


def gated_gelu(ffn_pre):
    return jax.nn.gelu(ffn_pre[0]) * ffn_pre[1]


def mixer_forward(
    mix_in, input_proj, gate_blocks, output_proj, conv_taps, gate_bias, decay_param, position
):
    projected = jnp.einsum("sd,kdr->ksr", mix_in, input_proj, preferred_element_type=jnp.float32)
    conv_out, conv_pull = jax.vjp(
        lambda signal, taps: conv_mix(signal, taps, position), projected[0], conv_taps
    )
    row_count = conv_out.shape[0]
    conv_low = conv_out.astype(jnp.bfloat16).reshape(
        row_count, gate_blocks.shape[1], gate_blocks.shape[2]
    )
    gate_logits = jnp.einsum(
        "shb,khbc->kshc", conv_low, gate_blocks, preferred_element_type=jnp.float32
    )
    mixed, mix_pull = jax.vjp(
        lambda logits, signal, branch, bias_term, decay_term: recurrence(
            logits, signal, branch, bias_term, decay_term, position
        ),
        gate_logits,
        conv_out,
        projected[1],
        gate_bias,
        decay_param,
    )
    mixed_low = mixed.astype(jnp.bfloat16)
    partial_out = jnp.dot(mixed_low, output_proj, preferred_element_type=jnp.float32)
    return (partial_out, (conv_pull, conv_low, mix_pull, mixed_low))


def mixer_backward(grad_out_low, mix_in, saved, input_proj, gate_blocks, output_proj):
    conv_pull, conv_low, mix_pull, mixed_low = saved
    grad_output_proj = jnp.einsum(
        "sr,sd->rd", mixed_low, grad_out_low, preferred_element_type=jnp.float32
    )
    grad_mixed = jnp.einsum(
        "sd,rd->sr", grad_out_low, output_proj, preferred_element_type=jnp.float32
    )
    grad_logits, grad_conv_direct, grad_branch, grad_bias, grad_decay = mix_pull(grad_mixed)
    logits_low = grad_logits.astype(jnp.bfloat16)
    grad_blocks = jnp.einsum(
        "shb,kshc->khbc", conv_low, logits_low, preferred_element_type=jnp.float32
    )
    grad_conv_gates = jnp.einsum(
        "kshc,khbc->shb", logits_low, gate_blocks, preferred_element_type=jnp.float32
    )
    grad_signal, grad_taps = conv_pull(
        grad_conv_direct + grad_conv_gates.reshape(grad_conv_direct.shape)
    )
    proj_low = jnp.stack([grad_signal, grad_branch]).astype(jnp.bfloat16)
    grad_input_proj = jnp.einsum(
        "sd,ksr->kdr", mix_in, proj_low, preferred_element_type=jnp.float32
    )
    grad_mix_in = jnp.einsum(
        "ksr,kdr->sd", proj_low, input_proj, preferred_element_type=jnp.float32
    )
    return (
        grad_mix_in,
        (grad_input_proj, grad_blocks, grad_output_proj, grad_taps, grad_bias, grad_decay),
    )


def ffn_forward(ffn_in_low, ffn_gate_up, ffn_down):
    ffn_pre = jnp.einsum("sd,kdf->ksf", ffn_in_low, ffn_gate_up, preferred_element_type=jnp.float32)
    ffn_act, ffn_pull = jax.vjp(gated_gelu, ffn_pre)
    ffn_low = ffn_act.astype(jnp.bfloat16)
    partial_ffn = jnp.dot(ffn_low, ffn_down, preferred_element_type=jnp.float32)
    return (partial_ffn, (ffn_pull, ffn_low))


def ffn_backward(grad_low, ffn_in_low, saved, ffn_gate_up, ffn_down):
    ffn_pull, ffn_low = saved
    grad_down = jnp.einsum("sf,sd->fd", ffn_low, grad_low, preferred_element_type=jnp.float32)
    grad_act = jnp.einsum("sd,fd->sf", grad_low, ffn_down, preferred_element_type=jnp.float32)
    grad_pre = ffn_pull(grad_act)[0]
    pre_low = grad_pre.astype(jnp.bfloat16)
    grad_gate_up = jnp.einsum(
        "sd,ksf->kdf", ffn_in_low, pre_low, preferred_element_type=jnp.float32
    )
    grad_ffn_in = jnp.einsum(
        "ksf,kdf->sd", pre_low, ffn_gate_up, preferred_element_type=jnp.float32
    )
    return (grad_ffn_in, grad_gate_up, grad_down)


def body(
    tokens,
    cotangent,
    seq_start,
    live_mask,
    input_proj,
    gate_blocks,
    output_proj,
    ffn_gate_up,
    ffn_down,
    conv_taps,
    gate_bias,
    decay_param,
    norm_gains,
    master_shard,
    first_moment,
    second_moment,
):
    slot_count = tokens.shape[0]
    position = jnp.arange(slot_count, dtype=jnp.int32) - seq_start
    mask_rows = live_mask.astype(jnp.float32)[:, None]
    stream = tokens.astype(jnp.float32)
    grad_stream = cotangent.astype(jnp.float32) * mask_rows
    shards = (
        input_proj,
        gate_blocks,
        output_proj,
        ffn_gate_up,
        ffn_down,
        conv_taps,
        gate_bias,
        decay_param,
        norm_gains,
    )
    (
        full_in,
        full_blocks,
        full_out,
        full_up,
        full_down,
        full_taps,
        full_bias,
        full_decay,
        full_gains,
    ) = (
        lax.all_gather(shards[0], "shard", axis=2, tiled=True),
        lax.all_gather(shards[1], "shard", axis=1, tiled=True),
        lax.all_gather(shards[2], "shard", axis=0, tiled=True),
        lax.all_gather(shards[3], "shard", axis=2, tiled=True),
        lax.all_gather(shards[4], "shard", axis=0, tiled=True),
        lax.all_gather(shards[5], "shard", axis=1, tiled=True),
        lax.all_gather(shards[6], "shard", axis=1, tiled=True),
        lax.all_gather(shards[7], "shard", axis=0, tiled=True),
        lax.all_gather(shards[8], "shard", axis=1, tiled=True),
    )
    gains = full_gains.astype(jnp.float32)
    normed, norm_pull = jax.vjp(rms_scale, stream, gains[0])
    mix_in = normed.astype(jnp.bfloat16)
    mix_out, mix_saved = mixer_forward(
        mix_in,
        full_in,
        full_blocks,
        full_out,
        full_taps.astype(jnp.float32),
        full_bias.astype(jnp.float32),
        full_decay.astype(jnp.float32),
        position,
    )
    residual = stream + mix_out
    normed_two, second_pull = jax.vjp(rms_scale, residual, gains[1])
    ffn_in_low = normed_two.astype(jnp.bfloat16)
    ffn_result, ffn_saved = ffn_forward(ffn_in_low, full_up, full_down)
    block_out = (mask_rows * (residual + ffn_result)).astype(jnp.bfloat16)
    grad_ffn_in, grad_up, grad_down = ffn_backward(
        grad_stream.astype(jnp.bfloat16), ffn_in_low, ffn_saved, full_up, full_down
    )
    grad_norm_two, grad_gain_two = second_pull(grad_ffn_in)
    grad_residual = grad_stream + grad_norm_two
    grad_mix_in, mix_grads = mixer_backward(
        grad_residual.astype(jnp.bfloat16), mix_in, mix_saved, full_in, full_blocks, full_out
    )
    grad_norm_one, grad_gain_one = norm_pull(grad_mix_in)
    tokens_grad = (grad_residual + grad_norm_one).astype(jnp.bfloat16)
    grads = (
        mix_grads[0],
        mix_grads[1],
        mix_grads[2],
        grad_up,
        grad_down,
        mix_grads[3],
        mix_grads[4],
        mix_grads[5],
        jnp.stack([grad_gain_one, grad_gain_two]),
    )
    summed = (
        lax.psum_scatter(
            grads[0].astype(jnp.bfloat16), "shard", scatter_dimension=2, tiled=True
        ).astype(jnp.float32),
        lax.psum_scatter(
            grads[1].astype(jnp.bfloat16), "shard", scatter_dimension=1, tiled=True
        ).astype(jnp.float32),
        lax.psum_scatter(
            grads[2].astype(jnp.bfloat16), "shard", scatter_dimension=0, tiled=True
        ).astype(jnp.float32),
        lax.psum_scatter(
            grads[3].astype(jnp.bfloat16), "shard", scatter_dimension=2, tiled=True
        ).astype(jnp.float32),
        lax.psum_scatter(
            grads[4].astype(jnp.bfloat16), "shard", scatter_dimension=0, tiled=True
        ).astype(jnp.float32),
        lax.psum_scatter(
            grads[5].astype(jnp.bfloat16), "shard", scatter_dimension=1, tiled=True
        ).astype(jnp.float32),
        lax.psum_scatter(
            grads[6].astype(jnp.bfloat16), "shard", scatter_dimension=1, tiled=True
        ).astype(jnp.float32),
        lax.psum_scatter(
            grads[7].astype(jnp.bfloat16), "shard", scatter_dimension=0, tiled=True
        ).astype(jnp.float32),
        lax.psum_scatter(
            grads[8].astype(jnp.bfloat16), "shard", scatter_dimension=1, tiled=True
        ).astype(jnp.float32),
    )
    flat = jnp.concatenate([member.reshape(1, -1) for member in summed], axis=1)
    piece = lax.psum_scatter(flat, "dp", scatter_dimension=1, tiled=True)
    bias_total = lax.psum(summed[6], "dp")
    new_first = beta_one * first_moment + (1.0 - beta_one) * piece
    new_second = beta_two * second_moment + (1.0 - beta_two) * piece * piece
    new_master = master_shard - learn_rate * (
        new_first / corr_one / (jnp.sqrt(new_second / corr_two) + adam_eps)
        + weight_decay * master_shard
    )
    new_weights = lax.all_gather(new_master.astype(jnp.bfloat16), "shard", axis=0, tiled=True)
    return (
        block_out,
        tokens_grad,
        piece,
        new_master,
        new_first,
        new_second,
        new_weights,
        bias_total,
    )


def solution(mesh):
    placed = (
        P(("dp", "shard"), None),
        P(("dp", "shard"), None),
        P(("dp", "shard")),
        P(("dp", "shard")),
        P(None, None, "shard"),
        P(None, "shard", None, None),
        P("shard", None),
        P(None, None, "shard"),
        P("shard", None),
        P(None, "shard"),
        P(None, "shard"),
        P("shard"),
        P(None, "shard"),
        P("shard", "dp"),
        P("shard", "dp"),
        P("shard", "dp"),
    )
    return jax.shard_map(
        body,
        mesh=mesh,
        in_specs=placed,
        out_specs=(
            P(("dp", "shard"), None),
            P(("dp", "shard"), None),
            P("shard", "dp"),
            P("shard", "dp"),
            P("shard", "dp"),
            P("shard", "dp"),
            P(None, "dp"),
            P(None, "shard"),
        ),
        check_vma=False,
    )
```

profile of v0, /device:TPU:0, one launch (start us, length us, event | category | flops | bytes accessed | tf_op | source)
XLA Modules:
  0.0 3224.1 jit_solution(12165404766030103313)
XLA Ops:
  10.9 13.5 all_gather.31
  25.1 19.5 all-gather
  44.6 14.4 all_gather.34
  59.0 20.0 all_gather.30
  80.1 151.1 %all-gather.9.cloned.1.call-done = bf16[2,1536,2048]{2,1,0:T(8,128)(2,1)} async-done(((bf16[2,1536,512]{2,1,0:T(8,128)(2,1)}), bf16[2,1536,2048]{2,1,0:T(8,128)(2,1)}) %all-gather.9.cloned.1.call-update) | async-done | bytes 12582928 | tf_op jit(solution)/shard_map/all_gather | solution.py:179
  242.7 16.9 all-gather.11.cloned.1.call-done
  433.7 418.2 %all-gather.15.cloned.1.call-done = bf16[2,1536,4608]{2,1,0:T(8,128)(2,1)} async-done(((bf16[2,1536,1152]{2,1,0:T(8,128)(2,1)}), bf16[2,1536,4608]{2,1,0:T(8,128)(2,1)}) %all-gather.15.cloned.1.call-update) | async-done | bytes 28311568 | tf_op jit(solution)/shard_map/all_gather | solution.py:182
  851.9 19.1 convolution_bitcast_fusion
  870.9 224.5 %all-gather.17.cloned.1.call-done = bf16[4608,1536]{1,0:T(8,128)(2,1)} async-done(((bf16[1152,1536]{1,0:T(8,128)(2,1)}), bf16[4608,1536]{1,0:T(8,128)(2,1)}) %all-gather.17.cloned.1.call-update) | async-done | bytes 14155792 | tf_op jit(solution)/shard_map/all_gather | solution.py:183
  1095.4 14.4 multiply_bitcast_fusion
  1109.9 17.7 multiply_reduce_fusion.5
  1286.2 8.8 pad.386
  1335.2 9.6 fusion.30
  1367.9 9.3 convolution_convert_fusion
  1379.0 9.1 all-reduce.92
  1388.2 16.6 convert_bitcast_fusion
  1407.9 27.5 reduce-scatter.16.cloned.1.call-done
  1436.5 111.2 %reduce-scatter.18.cloned.1.call-done = bf16[512,1536]{1,0:T(8,128)(2,1)} async-done(((bf16[2048,1536]{1,0:T(8,128)(2,1)}), bf16[512,1536]{1,0:T(8,128)(2,1)}) %reduce-scatter.18.cloned.1.call-update) | async-done | bytes 1572880 | tf_op jit(solution)/shard_map/reduce_scatter | solution.py:235
  1554.4 208.2 %reduce-scatter.14.cloned.1.call-done = bf16[2,1536,512]{1,2,0:T(8,128)(2,1)} async-done(((bf16[2,1536,2048]{1,2,0:T(8,128)(2,1)}), bf16[2,1536,512]{1,2,0:T(8,128)(2,1)}) %reduce-scatter.14.cloned.1.call-update) | async-done | bytes 3145744 | tf_op jit(solution)/shard_map/reduce_scatter | solution.py:229
  1768.1 14.6 reshape.196
  1792.6 210.6 %reduce-scatter.22.cloned.1.call-done = bf16[1152,1536]{1,0:T(8,128)(2,1)} async-done(((bf16[4608,1536]{1,0:T(8,128)(2,1)}), bf16[1152,1536]{1,0:T(8,128)(2,1)}) %reduce-scatter.22.cloned.1.call-update) | async-done | bytes 3538960 | tf_op jit(solution)/shard_map/reduce_scatter | solution.py:241
  2006.2 24.6 copy.106
  2030.8 440.8 %reduce-scatter.20.cloned.1.call-done = bf16[2,1536,1152]{1,2,0:T(8,128)(2,1)} async-done(((bf16[2,1536,4608]{1,2,0:T(8,128)(2,1)}), bf16[2,1536,1152]{1,2,0:T(8,128)(2,1)}) %reduce-scatter.20.cloned.1.call-update) | async-done | bytes 7077904 | tf_op jit(solution)/shard_map/reduce_scatter | solution.py:238
  2471.6 11.1 copy.80
  2482.6 27.7 reshape.202
  2510.4 10.3 constant_dynamic-update-slice_fusion.5
  2531.2 374.5 %all-reduce.96.cloned.1.call-done = f32[1,7803648]{1,0:T(1,128)} async-done(((f32[1,7803648]{1,0:T(1,128)}), f32[1,7803648]{1,0:T(1,128)}) %all-reduce.96.cloned.1.call-update) | async-done | bytes 31214608
  2905.6 30.9 convert_bitcast_fusion.3
  2940.6 9.5 fusion.9
  2950.1 12.8 psum.7
  2962.8 241.6 %all-gather.19.cloned.1.call-done = bf16[4,1,975456]{2,1,0:T(2,128)(2,1)} async-done(((bf16[1,1,975456]{2,1,0:T(2,128)(2,1)}), bf16[4,1,975456]{2,1,0:T(2,128)(2,1)}) %all-gather.19.cloned.1.call-update) | async-done | bytes 7803664 | tf_op jit(solution)/shard_map/all_gather | solution.py:266
  3204.4 12.8 copy.115
  (569 shorter events, 455.2 us)
Async XLA Ops:
  7.2 224.1 %all-gather.9.cloned.1.call-start = ((), (), s32[]{:S(2)}) async-start(), calls=%async_computation.8 | async-start | bytes 15728640 | tf_op jit(solution)/shard_map/all_gather | solution.py:179
  7.9 251.7 %all-gather.11.cloned.1.call-start = ((), (), s32[]{:S(2)}) async-start(), calls=%async_computation.9 | async-start | bytes 1310720 | tf_op jit(solution)/shard_map/all_gather | solution.py:180
  8.9 417.5 %all-gather.13.cloned.1.call-start = ((), (), s32[]{:S(2)}) async-start(), calls=%async_computation.10 | async-start | bytes 7864320 | tf_op jit(solution)/shard_map/all_gather | solution.py:181
  9.6 842.3 %all-gather.15.cloned.1.call-start = ((), (), s32[]{:S(2)}) async-start(), calls=%async_computation.11 | async-start | bytes 35389440 | tf_op jit(solution)/shard_map/all_gather | solution.py:182
  10.2 48.8 %copy-start.125 = (bf16[5,512]{1,0:T(8,128)(2,1)S(1)}, bf16[5,512]{1,0:T(8,128)(2,1)}, u32[]{:S(2)}) copy-start(bf16[5,512]{1,0:T(8,128)(2,1)} %param.25) | copy-start | bytes 15364
  10.2 68.8 %copy-start.11 = (bf16[256,1536]{1,0:T(8,128)(2,1)S(1)}, bf16[256,1536]{1,0:T(8,128)(2,1)}, u32[]{:S(2)}) copy-start(bf16[256,1536]{1,0:T(8,128)(2,1)} %param.16) | copy-start | bytes 2359300
  10.2 69.6 %copy-start.133 = (s32[256]{0:T(256)S(1)}, s32[256]{0:T(256)}, u32[]{:S(2)}) copy-start(s32[256]{0:T(256)} %param.18) | copy-start | bytes 3076
  10.3 1085.2 %all-gather.17.cloned.1.call-start = ((), (), s32[]{:S(2)}) async-start(), calls=%async_computation.12 | async-start | bytes 17694720 | tf_op jit(solution)/shard_map/all_gather | solution.py:183
  10.8 1394.0 %reduce-scatter.28.cloned.1.call-start = ((), (), s32[]{:S(2)}) async-start(), calls=%async_computation.21 | async-start | bytes 491520
  79.1 152.2 %copy-start.83 = (f32[1536]{0:T(1024)}, f32[1536]{0:T(1024)S(1)}, u32[]{:S(2)}) copy-start(f32[1536]{0:T(1024)S(1)} %get-tuple-element.18) | copy-start | bytes 18436
  79.9 151.4 %copy-start.114 = (f32[256]{0:T(256)}, f32[256]{0:T(256)S(1)}, u32[]{:S(2)}) copy-start(f32[256]{0:T(256)S(1)} %fusion.74) | copy-start | bytes 3076
  79.9 159.9 %copy-start.119 = (pred[256]{0:T(512)(128)(4,1)}, pred[256]{0:T(512)(128)(4,1)S(1)}, u32[]{:S(2)}) copy-start(pred[256]{0:T(512)(128)(4,1)S(1)} %get-tuple-element.142) | copy-start | bytes 772
  79.9 159.9 %copy-start.121 = (pred[256]{0:T(512)(128)(4,1)}, pred[256]{0:T(512)(128)(4,1)S(1)}, u32[]{:S(2)}) copy-start(pred[256]{0:T(512)(128)(4,1)S(1)} %get-tuple-element.143) | copy-start | bytes 772
  79.9 159.9 %copy-start.123 = (pred[256]{0:T(512)(128)(4,1)}, pred[256]{0:T(512)(128)(4,1)S(1)}, u32[]{:S(2)}) copy-start(pred[256]{0:T(512)(128)(4,1)S(1)} %get-tuple-element.144) | copy-start | bytes 772
  79.9 189.0 %copy-start.126 = (pred[256]{0:T(512)(128)(4,1)}, pred[256]{0:T(512)(128)(4,1)S(1)}, u32[]{:S(2)}) copy-start(pred[256]{0:T(512)(128)(4,1)S(1)} %get-tuple-element.141) | copy-start | bytes 772
  80.0 151.3 %copy-start.97 = (f32[4,1,512]{2,1,0:T(1,128)}, f32[4,1,512]{2,1,0:T(1,128)S(1)}, u32[]{:S(2)}) copy-start(f32[4,1,512]{2,1,0:T(1,128)S(1)} %convert_negate_fusion) | copy-start | bytes 24580
  80.0 188.9 %copy-start.85 = (f32[2048]{0:T(1024)}, f32[2048]{0:T(1024)S(1)}, u32[]{:S(2)}) copy-start(f32[2048]{0:T(1024)S(1)} %broadcast_multiply_fusion) | copy-start | bytes 24580
  80.0 188.9 %copy-start.87 = (f32[1,2048]{1,0:T(1,128)}, f32[1,2048]{1,0:T(1,128)S(1)}, u32[]{:S(2)}) copy-start(f32[1,2048]{1,0:T(1,128)S(1)} %get-tuple-element.139) | copy-start | bytes 24580
  80.0 188.9 %copy-start.89 = (f32[1,2048]{1,0:T(1,128)}, f32[1,2048]{1,0:T(1,128)S(1)}, u32[]{:S(2)}) copy-start(f32[1,2048]{1,0:T(1,128)S(1)} %get-tuple-element.140) | copy-start | bytes 24580
  80.1 159.7 %copy-start.99 = (f32[1,2048]{1,0:T(1,128)}, f32[1,2048]{1,0:T(1,128)S(1)}, u32[]{:S(2)}) copy-start(f32[1,2048]{1,0:T(1,128)S(1)} %get-tuple-element.123) | copy-start | bytes 24580
  80.1 159.7 %copy-start.101 = (f32[1,2048]{1,0:T(1,128)}, f32[1,2048]{1,0:T(1,128)S(1)}, u32[]{:S(2)}) copy-start(f32[1,2048]{1,0:T(1,128)S(1)} %get-tuple-element.124) | copy-start | bytes 24580
  80.1 159.7 %copy-start.103 = (f32[1,2048]{1,0:T(1,128)}, f32[1,2048]{1,0:T(1,128)S(1)}, u32[]{:S(2)}) copy-start(f32[1,2048]{1,0:T(1,128)S(1)} %get-tuple-element.125) | copy-start | bytes 24580
  80.1 159.7 %copy-start.105 = (f32[1,2048]{1,0:T(1,128)}, f32[1,2048]{1,0:T(1,128)S(1)}, u32[]{:S(2)}) copy-start(f32[1,2048]{1,0:T(1,128)S(1)} %get-tuple-element.126) | copy-start | bytes 24580
  1345.9 60.0 %reduce-scatter.26.cloned.1.call-start = ((), (), s32[]{:S(2)}) async-start(), calls=%async_computation.20 | async-start | bytes 655360
  1347.0 60.1 %reduce-scatter.24.cloned.1.call-start = ((), (), s32[]{:S(2)}) async-start(), calls=%async_computation.18 | async-start | bytes 40960 | tf_op jit(solution)/shard_map/reduce_scatter | solution.py:244
  1347.8 87.6 %reduce-scatter.16.cloned.1.call-start = ((), (), s32[]{:S(2)}) async-start(), calls=%async_computation.14 | async-start | bytes 1310720 | tf_op jit(solution)/shard_map/reduce_scatter | solution.py:232
  1351.5 196.2 %reduce-scatter.18.cloned.1.call-start = ((), (), s32[]{:S(2)}) async-start(), calls=%async_computation.15 | async-start | bytes 7864320 | tf_op jit(solution)/shard_map/reduce_scatter | solution.py:235
  1358.7 403.9 %reduce-scatter.14.cloned.1.call-start = ((), (), s32[]{:S(2)}) async-start(), calls=%async_computation.13 | async-start | bytes 15728640 | tf_op jit(solution)/shard_map/reduce_scatter | solution.py:229
  1366.8 636.5 %reduce-scatter.22.cloned.1.call-start = ((), (), s32[]{:S(2)}) async-start(), calls=%async_computation.17 | async-start | bytes 17694720 | tf_op jit(solution)/shard_map/reduce_scatter | solution.py:241
  1377.2 1094.4 %reduce-scatter.20.cloned.1.call-start = ((), (), s32[]{:S(2)}) async-start(), calls=%async_computation.16 | async-start | bytes 35389440 | tf_op jit(solution)/shard_map/reduce_scatter | solution.py:238
  1404.8 1500.9 %all-reduce.96.cloned.1.call-start = ((), (), s32[]{:S(2)}) async-start(), calls=%async_computation.22 | async-start | bytes 62429184
  2529.3 675.1 %all-gather.19.cloned.1.call-start = ((), (), s32[]{:S(2)}) async-start(), calls=%async_computation.19 | async-start | bytes 19509760 | tf_op jit(solution)/shard_map/all_gather | solution.py:266
  (124 other events, 872.6 us)
Sparse Core Ops, SparseCore 0:
  9.6 221.6 all-gather.8
  233.4 26.1 all-gather.10
  261.2 114.8 all-gather.12
  377.5 474.3 all-gather.14
  853.3 242.1 all-gather.16
  1346.0 18.7 reduce-scatter.27
  1367.8 19.9 reduce-scatter.25
  1390.0 17.0 reduce-scatter.23
  1410.1 25.3 reduce-scatter.15
  1438.2 109.4 reduce-scatter.17
  1550.2 212.3 reduce-scatter.13
  1764.9 238.2 reduce-scatter.21
  2005.7 465.8 reduce-scatter.19
  2529.4 376.1 all-reduce.95
  2936.7 267.6 all-gather.18
where the time goes:
time: 3240 us; the launch traced here: 3220 us
  waiting for transfers between devices  2430 us (75%)
  local copies, waits for them, and re-layouts  407 us (13%)
  other arithmetic  144 us (4%)
  matrix products  138 us (4%)
  blocking collectives  89.4 us (3%)
    reduce_scatter x1, waiting for transfers between devices, body(): lax.psum_scatter(grads[3].astype(jnp.bfloat16), 'shard', scatter_dimensio...  441 us
    all_gather x1, waiting for transfers between devices, body(): lax.all_gather(shards[3], 'shard', axis=2, tiled=True)  418 us
    unnamed x18, waiting for transfers between devices  377 us
    all_gather x1, waiting for transfers between devices, body(): lax.all_gather(new_master.astype(jnp.bfloat16), 'shard', axis=0, tiled=True)  242 us
    all_gather x1, waiting for transfers between devices, body(): lax.all_gather(shards[4], 'shard', axis=0, tiled=True)  225 us
    reduce_scatter x1, waiting for transfers between devices, body(): lax.psum_scatter(grads[4].astype(jnp.bfloat16), 'shard', scatter_dimensio...  211 us
    reduce_scatter x1, waiting for transfers between devices, body(): lax.psum_scatter(grads[0].astype(jnp.bfloat16), 'shard', scatter_dimensio...  208 us
    all_gather x1, waiting for transfers between devices, body(): lax.all_gather(shards[0], 'shard', axis=2, tiled=True)  151 us
  transfers between devices with their start and end apart: 15, of which 12 were waited for; matrix products, arithmetic and copies ran while one was open for 10% of the time, Pallas kernels for 0%

commit v1 on v0

--- a/solution.py
+++ b/solution.py
@@ -1,6 +1,9 @@
+import functools
 import jax
 import jax.numpy as jnp
 from jax import lax
+from jax.experimental import pallas as pl
+from jax.experimental.pallas import tpu as pltpu
 from jax.sharding import PartitionSpec as P
 
 norm_eps = 1e-06
@@ -12,6 +15,725 @@
 adam_eps = 1e-08
 corr_one = 1.0 - beta_one**10.0
 corr_two = 1.0 - beta_two**10.0
+low_type = jnp.bfloat16
+wide = jnp.float32
+axes = ("dp", "shard")
+gelu_scale = 0.7978845608028654
+gelu_cube = 0.044715
+
+
+def device_pairs(target):
+    found = []
+    for chip in range(4):
+        for core in range(2):
+            for z in range(4):
+                to = target(chip, core, z)
+                if to is not None:
+                    source = (chip * 2 + core) * 4 + z
+                    found.append((source, (to[0] * 2 + to[1]) * 4 + to[2]))
+    return found
+
+
+def line_pairs(moves):
+    moves = dict(moves)
+
+    def target(chip, core, z):
+        end = z if core == 0 else 3 - z
+        if end not in moves:
+            return None
+        to = moves[end]
+        return (chip, core, to if core == 0 else 3 - to)
+
+    return device_pairs(target)
+
+
+def step_pairs(step):
+    return device_pairs(
+        lambda chip, core, z: (chip, core, z + step) if 0 <= z + step < 4 else None
+    )
+
+
+def plane_pairs(flip, owners_only=False):
+    return device_pairs(
+        lambda chip, core, z: None if owners_only and core != z // 2 else (chip ^ flip, core, z)
+    )
+
+
+core_pairs = device_pairs(lambda chip, core, z: (chip, 1 - core, z))
+owner_core_pairs = device_pairs(
+    lambda chip, core, z: (chip, 1 - core, z) if core == z // 2 else None
+)
+
+
+def move(value, pairs):
+    return lax.ppermute(value, axes, pairs)
+
+
+def plane_gather(value, dim=0, owners_only=False):
+    half = value.shape[dim] // 2
+    across_x = move(value, plane_pairs(1, owners_only))
+    across_y = move(value, plane_pairs(2, owners_only))
+    first = lax.slice_in_dim(across_x, 0, half, axis=dim)
+    second = lax.slice_in_dim(across_y, half, 2 * half, axis=dim)
+    first = move(first, plane_pairs(2, owners_only))
+    second = move(second, plane_pairs(1, owners_only))
+    return (value, across_x, across_y, jnp.concatenate([first, second], axis=dim))
+
+
+def plane_reduce(parts):
+    slots = parts.shape[0] // 4
+    half = slots // 2
+    mine, for_x, for_y, for_d = (
+        parts[number * slots : (number + 1) * slots] for number in range(4)
+    )
+    top = slice(0, half)
+    low = slice(half, slots)
+    from_x = move(jnp.concatenate([for_x[top], for_d[top]]), plane_pairs(1))
+    from_y = move(jnp.concatenate([for_y[low], for_d[low]]), plane_pairs(2))
+    send_y = (for_y[top].astype(wide) + from_x[half:].astype(wide)).astype(low_type)
+    send_x = (for_x[low].astype(wide) + from_y[half:].astype(wide)).astype(low_type)
+    last_top = move(send_y, plane_pairs(2))
+    last_low = move(send_x, plane_pairs(1))
+    return jnp.concatenate(
+        [
+            mine[top].astype(wide) + from_x[:half].astype(wide) + last_top.astype(wide),
+            mine[low].astype(wide) + from_y[:half].astype(wide) + last_low.astype(wide),
+        ]
+    )
+
+
+def pick(end, choices):
+    result = choices[3]
+    for number in (2, 1, 0):
+        result = jnp.where(end == number, choices[number], result)
+    return result
+
+
+def line_spread(own, end):
+    ahead = move(own, line_pairs({0: 1, 1: 2}))
+    back = move(own, line_pairs({1: 0}))
+    ahead_two = move(ahead, line_pairs({1: 2, 2: 3}))
+    ahead_three = move(ahead_two, line_pairs({2: 3}))
+    return (
+        pick(end, [own, ahead, ahead_two, ahead_three]),
+        pick(end, [back, own, ahead, ahead_two]),
+    )
+
+
+def add_low(left, right):
+    return (left.astype(wide) + right.astype(wide)).astype(low_type)
+
+
+def line_sum(outer, inner, end):
+    first = add_low(outer, move(outer, line_pairs({3: 2})))
+    inner_one = add_low(inner, move(inner, line_pairs({3: 2, 0: 1})))
+    second = add_low(outer, move(first, line_pairs({2: 1})))
+    inner_two = add_low(inner_one, move(inner_one, line_pairs({2: 1})))
+    third = add_low(outer, move(second, line_pairs({1: 0})))
+    return jnp.where(end == 0, third, inner_two)
+
+
+def dot_rows(left, right):
+    return lax.dot_general(left, right, (((1,), (1,)), ((), ())), preferred_element_type=wide)
+
+
+def dot_plain(left, right):
+    return lax.dot_general(left, right, (((1,), (0,)), ((), ())), preferred_element_type=wide)
+
+
+def dot_slots(left, right):
+    return lax.dot_general(left, right, (((0,), (0,)), ((), ())), preferred_element_type=wide)
+
+
+def gelu_parts(value):
+    square = value * value
+    bent = jnp.tanh(gelu_scale * value * (1.0 + gelu_cube * square))
+    half = 0.5 * (1.0 + bent)
+    slope = half + 0.5 * value * (1.0 - bent * bent) * gelu_scale * (
+        1.0 + 3.0 * gelu_cube * square
+    )
+    return (value * half, slope)
+
+
+def shift_down(value, step):
+    if step % 8 == 0:
+        return jnp.concatenate([value[-step:], value[:-step]], axis=0)
+    return pltpu.roll(value, step, 0)
+
+
+def shift_up(value, step):
+    if step % 8 == 0:
+        return jnp.concatenate([value[step:], value[:step]], axis=0)
+    return pltpu.roll(value, value.shape[0] - step, 0)
+
+
+def scan_slots(decay, value, shift):
+    step = 1
+    while step < value.shape[0]:
+        value = value + decay * shift(value, step)
+        if 2 * step < value.shape[0]:
+            decay = decay * shift(decay, step)
+        step *= 2
+    return value
+
+
+def one_minus_exp(value):
+    series = jnp.ones_like(value)
+    for number in range(11, 1, -1):
+        series = 1.0 - value * (1.0 / number) * series
+    return jnp.where(value < 0.8, value * series, 1.0 - jnp.exp(-value))
+
+
+def soft_plus(value):
+    return jnp.maximum(value, 0.0) + jnp.log1p(jnp.exp(-jnp.abs(value)))
+
+
+def mixer_parts(first, position, small, gates):
+    conv_out = small[4:5] + small[0:1] * first
+    shifted = []
+    for step in range(1, 4):
+        moved = jnp.where(position >= step, shift_down(first, step), 0.0)
+        shifted.append(moved)
+        conv_out = conv_out + small[step : step + 1] * moved
+    conv_low = conv_out.astype(low_type)
+    logits = dot_plain(conv_low, gates)
+    width = first.shape[1]
+    recur_gate = jax.nn.sigmoid(logits[:, :width] + small[5:6])
+    input_gate = jax.nn.sigmoid(logits[:, width:] + small[6:7])
+    rate = gate_scale * soft_plus(-small[7:8])
+    log_decay = -rate * recur_gate
+    decay = jnp.where(position > 0, jnp.exp(log_decay), 0.0)
+    gone = one_minus_exp(-2.0 * log_decay)
+    root = jnp.sqrt(gone)
+    return conv_out, shifted, conv_low, recur_gate, input_gate, rate, decay, gone, root
+
+
+def weight_views(w_ref, width):
+    model = w_ref.shape[2] - width
+    proj = w_ref[0, 0 : 2 * width, 0:model]
+    out = w_ref[0, 2 * width : 3 * width, 0:model]
+    gates = jnp.concatenate(
+        [w_ref[0, 0:width, model:], w_ref[0, width : 2 * width, model:]], axis=1
+    )
+    small = w_ref[0, 2 * width : 2 * width + 16, model:].astype(wide)
+    return proj, out, gates, small
+
+
+def mixer_forward_kernel(width, x_ref, pos_ref, w_ref, out_ref, p_ref, state_ref, low_ref, acc_ref):
+    head = pl.program_id(0)
+    block = pl.program_id(1)
+    slots = x_ref.shape[0]
+    proj, out, gates, small = weight_views(w_ref, width)
+    position = pos_ref[...]
+    projected = dot_rows(x_ref[...], proj)
+    p_ref[0] = projected
+    conv_out, _, _, _, input_gate, _, decay, _, root = mixer_parts(
+        projected[:, :width], position, small, gates
+    )
+    states = scan_slots(decay, root * input_gate * conv_out, shift_down)
+    state_ref[0] = states
+    mixed_low = (states * gelu_parts(projected[:, width:])[0]).astype(low_type)
+    low_ref[0] = mixed_low
+    part = dot_plain(mixed_low, out)
+    rows = pl.ds(pl.multiple_of(block * slots, slots), slots)
+
+    @pl.when(head == 0)
+    def _():
+        acc_ref[rows, :] = part
+
+    @pl.when(head > 0)
+    def _():
+        acc_ref[rows, :] += part
+
+    @pl.when(head == pl.num_programs(0) - 1)
+    def _():
+        out_ref[rows, :] = acc_ref[rows, :].astype(low_type)
+
+
+def mix_forward(mix_in, position, weights, slots, width):
+    rows, model = mix_in.shape
+    heads = weights.shape[0]
+    blocks = rows // slots
+    return pl.pallas_call(
+        functools.partial(mixer_forward_kernel, width),
+        grid=(heads, blocks),
+        in_specs=[
+            pl.BlockSpec((slots, model), lambda h, b: (b, 0)),
+            pl.BlockSpec((slots, 1), lambda h, b: (b, 0)),
+            pl.BlockSpec((1,) + weights.shape[1:], lambda h, b: (h, 0, 0)),
+        ],
+        out_specs=[
+            pl.BlockSpec((rows, model), lambda h, b: (0, 0)),
+            pl.BlockSpec((1, slots, 2 * width), lambda h, b: (h, b, 0)),
+            pl.BlockSpec((1, slots, width), lambda h, b: (h, b, 0)),
+            pl.BlockSpec((1, slots, width), lambda h, b: (h, b, 0)),
+        ],
+        out_shape=[
+            jax.ShapeDtypeStruct((rows, model), low_type),
+            jax.ShapeDtypeStruct((heads, rows, 2 * width), wide),
+            jax.ShapeDtypeStruct((heads, rows, width), wide),
+            jax.ShapeDtypeStruct((heads, rows, width), low_type),
+        ],
+        scratch_shapes=[pltpu.VMEM((rows, model), wide)],
+        compiler_params=pltpu.CompilerParams(vmem_limit_bytes=48 * 1024 * 1024),
+        cost_estimate=pl.CostEstimate(
+            flops=2 * rows * model * heads * width * 3,
+            bytes_accessed=heads * rows * width * 14 + weights.size * 2 + rows * model * 4,
+            transcendentals=heads * rows * width * 6,
+        ),
+        name="mixer_forward",
+    )(mix_in, position, weights)
+
+
+def mixer_backward_kernel(
+    width,
+    x_ref,
+    res_ref,
+    pos_ref,
+    w_ref,
+    p_ref,
+    state_ref,
+    low_ref,
+    grad_ref,
+    gin_ref,
+    acc_w,
+    acc_in,
+):
+    head = pl.program_id(0)
+    block = pl.program_id(1)
+    slots, model = x_ref.shape
+    proj, out, gates, small = weight_views(w_ref, width)
+    position = pos_ref[...]
+    first = p_ref[0, :, 0:width]
+    res_low = res_ref[...]
+    states = state_ref[0]
+    conv_out, shifted, conv_low, recur_gate, input_gate, rate, decay, gone, root = mixer_parts(
+        first, position, small, gates
+    )
+    grad_mixed = dot_rows(res_low, out)
+    active, slope = gelu_parts(p_ref[0, :, width:])
+    grad_second = grad_mixed * states * slope
+    adjoint = scan_slots(shift_up(decay, 1), grad_mixed * active, shift_up)
+    grad_decay = adjoint * shift_down(states, 1)
+    grad_root = adjoint * input_gate * conv_out
+    grad_input_gate = adjoint * root * conv_out
+    grad_conv = adjoint * root * input_gate
+    grad_log = grad_decay * decay - grad_root * (1.0 - gone) / root
+    grad_recur = -rate * grad_log
+    grad_logit_a = grad_recur * recur_gate * (1.0 - recur_gate)
+    grad_logit_b = grad_input_gate * input_gate * (1.0 - input_gate)
+    grad_param = jnp.sum(grad_log * recur_gate, axis=0, keepdims=True) * (
+        gate_scale * jax.nn.sigmoid(-small[7:8])
+    )
+    logits_low = jnp.concatenate([grad_logit_a, grad_logit_b], axis=1).astype(low_type)
+    grad_conv = grad_conv + dot_rows(logits_low, gates)
+    grad_gates = dot_slots(conv_low, logits_low)
+    sums = [jnp.sum(grad_conv * first, axis=0, keepdims=True)]
+    grad_first = small[0:1] * grad_conv
+    for step in range(1, 4):
+        sums.append(jnp.sum(grad_conv * shifted[step - 1], axis=0, keepdims=True))
+        kept = jnp.where(position >= step, grad_conv, 0.0)
+        grad_first = grad_first + small[step : step + 1] * shift_up(kept, step)
+    sums.append(jnp.sum(grad_conv, axis=0, keepdims=True))
+    sums.append(jnp.sum(grad_logit_a, axis=0, keepdims=True))
+    sums.append(jnp.sum(grad_logit_b, axis=0, keepdims=True))
+    sums.append(grad_param)
+    grad_small = jnp.concatenate(sums, axis=0)
+    proj_low = jnp.concatenate([grad_first, grad_second], axis=1).astype(low_type)
+    part = dot_plain(proj_low, proj)
+    rows = pl.ds(pl.multiple_of(block * slots, slots), slots)
+
+    @pl.when(block == 0)
+    def _():
+        acc_w[...] = jnp.zeros_like(acc_w)
+
+    acc_w[0 : 2 * width, 0:model] += dot_slots(proj_low, x_ref[...])
+    acc_w[2 * width : 3 * width, 0:model] += dot_slots(low_ref[0], res_low)
+    acc_w[0:width, model:] += grad_gates[:, :width]
+    acc_w[width : 2 * width, model:] += grad_gates[:, width:]
+    acc_w[2 * width : 2 * width + 8, model:] += grad_small
+
+    @pl.when(head == 0)
+    def _():
+        acc_in[rows, :] = part
+
+    @pl.when(head > 0)
+    def _():
+        acc_in[rows, :] += part
+
+    @pl.when(block == pl.num_programs(1) - 1)
+    def _():
+        grad_ref[0] = acc_w[...].astype(low_type)
+
+    @pl.when(head == pl.num_programs(0) - 1)
+    def _():
+        gin_ref[rows, :] = acc_in[rows, :].astype(low_type)
+
+
+def mix_backward(mix_in, res_low, position, weights, saved, slots, width):
+    rows, model = mix_in.shape
+    heads = weights.shape[0]
+    blocks = rows // slots
+    return pl.pallas_call(
+        functools.partial(mixer_backward_kernel, width),
+        grid=(heads, blocks),
+        in_specs=[
+            pl.BlockSpec((slots, model), lambda h, b: (b, 0)),
+            pl.BlockSpec((slots, model), lambda h, b: (b, 0)),
+            pl.BlockSpec((slots, 1), lambda h, b: (b, 0)),
+            pl.BlockSpec((1,) + weights.shape[1:], lambda h, b: (h, 0, 0)),
+            pl.BlockSpec((1, slots, 2 * width), lambda h, b: (h, b, 0)),
+            pl.BlockSpec((1, slots, width), lambda h, b: (h, b, 0)),
+            pl.BlockSpec((1, slots, width), lambda h, b: (h, b, 0)),
+        ],
+        out_specs=[
+            pl.BlockSpec((1,) + weights.shape[1:], lambda h, b: (h, 0, 0)),
+            pl.BlockSpec((rows, model), lambda h, b: (0, 0)),
+        ],
+        out_shape=[
+            jax.ShapeDtypeStruct(weights.shape, low_type),
+            jax.ShapeDtypeStruct((rows, model), low_type),
+        ],
+        scratch_shapes=[
+            pltpu.VMEM(weights.shape[1:], wide),
+            pltpu.VMEM((rows, model), wide),
+        ],
+        compiler_params=pltpu.CompilerParams(vmem_limit_bytes=48 * 1024 * 1024),
+        cost_estimate=pl.CostEstimate(
+            flops=2 * rows * model * heads * width * 6,
+            bytes_accessed=heads * rows * width * 14 + weights.size * 4 + rows * model * 6,
+            transcendentals=heads * rows * width * 6,
+        ),
+        name="mixer_backward",
+    )(mix_in, res_low, position, weights, *saved)
+
+
+def ffn_kernel(
+    x_ref, go_ref, w_ref, grad_ref, out_ref, gin_ref, acc_w, acc_out, acc_in
+):
+    tile = pl.program_id(0)
+    block = pl.program_id(1)
+    slots = x_ref.shape[0]
+    x = x_ref[...]
+    grad_out = go_ref[...]
+    pre_gate = dot_rows(x, w_ref[0])
+    pre_up = dot_rows(x, w_ref[1])
+    active, slope = gelu_parts(pre_gate)
+    ffn_low = (active * pre_up).astype(low_type)
+    grad_act = dot_rows(grad_out, w_ref[2])
+    gate_low = (grad_act * pre_up * slope).astype(low_type)
+    up_low = (grad_act * active).astype(low_type)
+    part_out = dot_plain(ffn_low, w_ref[2])
+    part_in = dot_plain(gate_low, w_ref[0]) + dot_plain(up_low, w_ref[1])
+    rows = pl.ds(pl.multiple_of(block * slots, slots), slots)
+
+    @pl.when(block == 0)
+    def _():
+        acc_w[...] = jnp.zeros_like(acc_w)
+
+    acc_w[0] += dot_slots(gate_low, x)
+    acc_w[1] += dot_slots(up_low, x)
+    acc_w[2] += dot_slots(ffn_low, grad_out)
+
+    @pl.when(tile == 0)
+    def _():
+        acc_out[rows, :] = part_out
+        acc_in[rows, :] = part_in
+
+    @pl.when(tile > 0)
+    def _():
+        acc_out[rows, :] += part_out
+        acc_in[rows, :] += part_in
+
+    @pl.when(block == pl.num_programs(1) - 1)
+    def _():
+        grad_ref[...] = acc_w[...].astype(low_type)
+
+    @pl.when(tile == pl.num_programs(0) - 1)
+    def _():
+        out_ref[rows, :] = acc_out[rows, :].astype(low_type)
+        gin_ref[rows, :] = acc_in[rows, :].astype(low_type)
+
+
+def ffn_both(x, grad_out, weights, slots, tile):
+    rows, model = x.shape
+    hidden = weights.shape[1]
+    return pl.pallas_call(
+        ffn_kernel,
+        grid=(hidden // tile, rows // slots),
+        in_specs=[
+            pl.BlockSpec((slots, model), lambda j, b: (b, 0)),
+            pl.BlockSpec((slots, model), lambda j, b: (b, 0)),
+            pl.BlockSpec((3, tile, model), lambda j, b: (0, j, 0)),
+        ],
+        out_specs=[
+            pl.BlockSpec((3, tile, model), lambda j, b: (0, j, 0)),
+            pl.BlockSpec((rows, model), lambda j, b: (0, 0)),
+            pl.BlockSpec((rows, model), lambda j, b: (0, 0)),
+        ],
+        out_shape=[
+            jax.ShapeDtypeStruct(weights.shape, low_type),
+            jax.ShapeDtypeStruct((rows, model), low_type),
+            jax.ShapeDtypeStruct((rows, model), low_type),
+        ],
+        scratch_shapes=[
+            pltpu.VMEM((3, tile, model), wide),
+            pltpu.VMEM((rows, model), wide),
+            pltpu.VMEM((rows, model), wide),
+        ],
+        compiler_params=pltpu.CompilerParams(vmem_limit_bytes=58 * 1024 * 1024),
+        cost_estimate=pl.CostEstimate(
+            flops=2 * rows * model * hidden * 9,
+            bytes_accessed=weights.size * 4 + rows * model * 16,
+            transcendentals=rows * hidden,
+        ),
+        name="ffn_both",
+    )(x, grad_out, weights)
+
+
+def piece_rows(start, length, low, high):
+    return max(low - start, 0), min(high - start, length)
+
+
+def build_piece(member, piece_length, sizes, mix, ffn):
+    model, width, ffn_width, slice_rec, slice_ffn = sizes
+    chip = member // 2
+    mix = [mix[number ^ chip] for number in range(4)]
+    ffn = [ffn[number ^ chip] for number in range(4)]
+    low = member * piece_length
+    high = low + piece_length
+    parts = []
+    start = 0
+
+    def add(length, row, rows_of):
+        nonlocal start
+        first, last = piece_rows(start, length, low, high)
+        if first < last:
+            row_low, row_high = first // row, -(-last // row)
+            block = rows_of(row_low, row_high)
+            flat = block.reshape(-1)
+            parts.append(flat[first - row_low * row : last - row_low * row])
+        start += length
+
+    def columns(source, kinds, row_low, row_high):
+        found = []
+        for kind in range(kinds):
+            a, b = max(row_low - kind * model, 0), min(row_high - kind * model, model)
+            if a < b:
+                found.append(
+                    jnp.concatenate([source(q, kind)[:, a:b] for q in range(4)], axis=0).T
+                )
+        return jnp.concatenate(found, axis=0)
+
+    def quarter_rows(source, count, row_low, row_high):
+        found = []
+        for q in range(4):
+            a, b = max(row_low - q * count, 0), min(row_high - q * count, count)
+            if a < b:
+                found.append(source(q)[a:b])
+        return jnp.concatenate(found, axis=0)
+
+    def gate_rows(row_low, row_high):
+        found = []
+        for number in range(8):
+            kind, q = number // 4, number % 4
+            a, b = max(row_low - number * width, 0), min(row_high - number * width, width)
+            if a < b:
+                found.append(mix[q][kind * width + a : kind * width + b, model:])
+        return jnp.concatenate(found, axis=0)
+
+    def small_rows(offset):
+        return lambda a, b: jnp.concatenate(
+            [mix[q][2 * width + offset + a : 2 * width + offset + b, model:] for q in range(4)],
+            axis=1,
+        )
+
+    add(
+        2 * model * slice_rec,
+        slice_rec,
+        lambda a, b: columns(lambda q, k: mix[q][k * width : (k + 1) * width, :model], 2, a, b),
+    )
+    add(2 * 4 * width * width, width, gate_rows)
+    add(
+        slice_rec * model,
+        model,
+        lambda a, b: quarter_rows(lambda q: mix[q][2 * width : 3 * width, :model], width, a, b),
+    )
+    add(2 * model * slice_ffn, slice_ffn, lambda a, b: columns(lambda q, k: ffn[q][k], 2, a, b))
+    add(
+        slice_ffn * model,
+        model,
+        lambda a, b: quarter_rows(lambda q: ffn[q][2], ffn_width, a, b),
+    )
+    add(5 * slice_rec, slice_rec, small_rows(0))
+    add(2 * slice_rec, slice_rec, small_rows(5))
+    add(slice_rec, slice_rec, small_rows(7))
+    gains = 2 * (model // 4)
+    add(gains, gains, lambda a, b: jnp.zeros((gains,), low_type))
+    bias = jnp.concatenate(
+        [mix[q][2 * width + 5 : 2 * width + 7, model:] for q in range(4)], axis=1
+    )
+    return jnp.concatenate(parts).astype(wide), bias.astype(wide)
+
+
+def group_body(
+    tokens,
+    cotangent,
+    seq_start,
+    live_mask,
+    input_proj,
+    gate_blocks,
+    output_proj,
+    ffn_gate_up,
+    ffn_down,
+    conv_taps,
+    gate_bias,
+    decay_param,
+    norm_gains,
+    master_shard,
+    first_moment,
+    second_moment,
+):
+    slots, model = tokens.shape
+    slice_rec = input_proj.shape[2]
+    slice_ffn = ffn_down.shape[0]
+    width = slice_rec // 4
+    ffn_width = slice_ffn // 4
+    piece_length = master_shard.shape[1]
+    member = lax.axis_index("dp")
+    chip = member // 2
+    core = member % 2
+    z = lax.axis_index("shard")
+    end = jnp.where(core == 0, z, 3 - z)
+
+    mask_rows = live_mask.astype(wide)[:, None]
+    stream = tokens.astype(wide)
+    grad_stream = cotangent.astype(wide) * mask_rows
+
+    def quarter(value, dim, count):
+        return lax.dynamic_slice_in_dim(value, chip * count, count, axis=dim)
+
+    own_proj = quarter(input_proj, 2, width).transpose(0, 2, 1).reshape(2 * width, model)
+    own_out = quarter(output_proj, 0, width)
+    own_gates = quarter(gate_blocks, 1, 1).reshape(2 * width, width)
+    own_small = jnp.concatenate(
+        [
+            quarter(conv_taps, 1, width),
+            quarter(gate_bias, 1, width),
+            quarter(decay_param[None], 1, width),
+            jnp.zeros((width - 8, width), low_type),
+        ]
+    )
+    own_mix = jnp.concatenate(
+        [
+            jnp.concatenate([own_proj, own_out]),
+            jnp.concatenate([own_gates, own_small]),
+        ],
+        axis=1,
+    )
+    own_ffn = jnp.concatenate(
+        [
+            quarter(ffn_gate_up, 2, ffn_width).transpose(0, 2, 1),
+            quarter(ffn_down, 0, ffn_width)[None],
+        ]
+    )
+
+    gains = lax.all_gather(norm_gains, "shard", axis=1, tiled=True).astype(wide)
+
+    start_row = jnp.zeros((16, model), low_type).at[0, :slots].set(seq_start.astype(low_type))
+    gathered = plane_gather(jnp.concatenate([tokens, start_row]))
+    starts = jnp.stack([block[slots, :slots] for block in gathered]).astype(jnp.int32)
+    position = (jnp.arange(slots, dtype=jnp.int32)[None] - starts).reshape(-1, 1)
+    all_tokens = jnp.concatenate([block[:slots] for block in gathered])
+    mix_in = rms_scale(all_tokens.astype(wide), gains[0]).astype(low_type)
+
+    mix_a, mix_b = line_spread(own_mix, end)
+    mix_pair = jnp.stack([mix_a, mix_b])
+    mix_weights = jnp.concatenate([mix_pair, move(mix_pair, core_pairs)])
+
+    ffn_a, ffn_b = line_spread(own_ffn, end)
+    ffn_pair = jnp.concatenate([ffn_a, ffn_b], axis=1)
+    ffn_weights = jnp.concatenate([ffn_pair, move(ffn_pair, core_pairs)], axis=1)
+
+    all_grad_out = jnp.concatenate(plane_gather(grad_stream.astype(low_type)))
+
+    mix_part, *saved = mix_forward(mix_in, position, mix_weights, slots, width)
+    residual = stream + plane_reduce(mix_part)
+    normed_two, second_pull = jax.vjp(rms_scale, residual, gains[1])
+    ffn_in = jnp.concatenate(plane_gather(normed_two.astype(low_type)))
+
+    grad_ffn, ffn_part, ffn_in_part = ffn_both(
+        ffn_in, all_grad_out, ffn_weights, slots, ffn_width * 4 // 3
+    )
+    grad_norm_two, grad_gain_two = second_pull(plane_reduce(ffn_in_part))
+    grad_residual = grad_stream + grad_norm_two
+    res_low = jnp.concatenate(plane_gather(grad_residual.astype(low_type)))
+    block_out = (mask_rows * (residual + plane_reduce(ffn_part))).astype(low_type)
+
+    grad_mix, mix_in_part = mix_backward(
+        mix_in, res_low, position, mix_weights, saved, slots, width
+    )
+    _, norm_pull = jax.vjp(rms_scale, stream, gains[0])
+    grad_norm_one, grad_gain_one = norm_pull(plane_reduce(mix_in_part))
+    tokens_grad = (grad_residual + grad_norm_one).astype(low_type)
+
+    both = 2 * ffn_width
+    pair_ffn = add_low(grad_ffn[:, :both], move(grad_ffn[:, both:], core_pairs))
+    sum_ffn = line_sum(pair_ffn[:, :ffn_width], pair_ffn[:, ffn_width:], end)
+    pair_mix = add_low(grad_mix[:2], move(grad_mix[2:], core_pairs))
+    sum_mix = line_sum(pair_mix[0], pair_mix[1], end)
+    owner = core == z // 2
+
+    def share(total, dim):
+        four = jnp.stack(plane_gather(total, dim, owners_only=True))
+        return jnp.where(owner, four, move(four, owner_core_pairs))
+
+    four_ffn = share(sum_ffn, 1)
+    four_mix = share(sum_mix, 0)
+    sizes = (model, width, ffn_width, slice_rec, slice_ffn)
+    piece, bias_total = lax.switch(
+        member,
+        [
+            functools.partial(build_piece, number, piece_length, sizes)
+            for number in range(8)
+        ],
+        four_mix,
+        four_ffn,
+    )
+    gain_total = lax.psum(jnp.stack([grad_gain_one, grad_gain_two]), axes)
+    gain_slice = lax.dynamic_slice_in_dim(gain_total, z * (model // 4), model // 4, axis=1)
+    gain_flat = gain_slice.reshape(-1)
+    tail = jnp.where(member == 7, gain_flat, piece[-gain_flat.shape[0] :])
+    piece = jnp.concatenate([piece[: -gain_flat.shape[0]], tail]).reshape(1, -1)
+
+    new_first = beta_one * first_moment + (1.0 - beta_one) * piece
+    new_second = beta_two * second_moment + (1.0 - beta_two) * piece * piece
+    new_master = master_shard - learn_rate * (
+        new_first / corr_one / (jnp.sqrt(new_second / corr_two) + adam_eps)
+        + weight_decay * master_shard
+    )
+    own = new_master.astype(low_type).reshape(-1)
+    right = [own]
+    left = [own]
+    for _ in range(3):
+        right.append(move(right[-1], step_pairs(1)))
+        left.append(move(left[-1], step_pairs(-1)))
+    new_weights = jnp.stack(
+        [
+            pick(z, [right[at - target] if at >= target else left[target - at] for at in range(4)])
+            for target in range(4)
+        ]
+    )
+    return (
+        block_out,
+        tokens_grad,
+        piece,
+        new_master,
+        new_first,
+        new_second,
+        new_weights,
+        bias_total,
+    )
 
 
 def rms_scale(values, gain):
@@ -277,6 +999,7 @@
 
 
 def solution(mesh):
+    fits = mesh.shape["dp"] == 8 and mesh.shape["shard"] == 4
     placed = (
         P(("dp", "shard"), None),
         P(("dp", "shard"), None),
@@ -296,7 +1019,7 @@
         P("shard", "dp"),
     )
     return jax.shard_map(
-        body,
+        group_body if fits else body,
         mesh=mesh,
         in_specs=placed,
         out_specs=(

time: 3240 us -> 1180 us (0.36)
  the two profiles are of different devices: /device:TPU:0 before, /device:TPU:2 now
where the time goes in v1:
time: 1180 us; the launch traced here: 1170 us
  waiting for transfers between devices  368 us (31%)
  local copies, waits for them, and re-layouts  209 us (18%)
  other arithmetic  182 us (15%)
  starting transfers between devices  158 us (13%)
  Pallas kernels  133 us (11%)
  blocking collectives  99.3 us (8%)
  loops' own time  20.5 us (2%)
    ppermute x70, waiting for transfers between devices, move(): return lax.ppermute(value, axes, pairs)  368 us
    ppermute x70, starting transfers between devices, move(): return lax.ppermute(value, axes, pairs)  158 us
    another operation x4, local copies, waits for them, and re-layouts, group_body(): jnp.stack([pick(z, [right[at - target] if at >= target else left[target -...  89.3 us
    pallas_call x1, Pallas kernels, ffn_both(): pl.pallas_call(ffn_kernel, grid=(hidden // tile, rows // slots), in_specs...  59.2 us
    all_gather x1, blocking collectives, group_body(): gains = lax.all_gather(norm_gains, 'shard', axis=1, tiled=True).astype(wide)  52.3 us
    convert_element_type x1, other arithmetic, group_body(): own = new_master.astype(low_type).reshape(-1)  48.8 us
    psum x1, blocking collectives, group_body(): gain_total = lax.psum(jnp.stack([grad_gain_one, grad_gain_two]), axes)  46.9 us
    pallas_call x1, Pallas kernels, mix_backward(): pl.pallas_call(functools.partial(mixer_backward_kernel, width), grid=(hea...  41.2 us
  transfers between devices with their start and end apart: 70, of which 36 were waited for; matrix products, arithmetic and copies ran while one was open for 10% of the time, Pallas kernels for 6%

profile of v1, /device:TPU:2, one launch (start us, length us, event | category | flops | bytes accessed | tf_op | source)
XLA Modules:
  0.0 1172.6 jit_solution(302807535380053186)
XLA Ops:
  44.7 21.4 %collective-permute-done.21 = bf16[3,288,1536]{2,1,0:T(8,128)(2,1)} collective-permute-done((bf16[3,288,1536]{2,1,0:T(8,128)(2,1)}, bf16[3,288,1536]{2,1,0:T(8,128)(2,1)}, u32[]{:S(2)}, u32[]{:S(2)}) %collective-permute-start.21) | collective-permute-done | bytes 2654240 | tf_op jit(solution)/shard_map/ppermute | solution.py:69
  73.8 26.3 %collective-permute-start.8 = (bf16[2,384,1664]{2,1,0:T(8,128)(2,1)}, bf16[2,384,1664]{2,1,0:T(8,128)(2,1)}, u32[]{:S(2)}, u32[]{:S(2)}) collective-permute-start(bf16[2,384,1664]{2,1,0:T(8,128)(2,1)} %pad_maximum_fusion.25), channel_id=1, source_target_pairs={{0,4},{1,5},{2,6},{3,7},{4,0},{5,1},{6,2},{7,3},{8,12},{9,13},{10,... | collective-permute-start | bytes 7667720 | tf_op jit(solution)/shard_map/ppermute | solution.py:69
  105.6 52.3 %all_gather.3 = bf16[2,1536]{1,0:T(2,128)(2,1)S(1)} all-gather(bf16[2,384]{1,0:T(2,128)(2,1)S(1)} %copy-done.57), channel_id=1, replica_groups=mesh['dp'=8,'shard'=4] {'shard'}, dimensions={1}, use_global_device_ids=true | all-gather | bytes 7680 | tf_op jit(solution)/shard_map/all_gather | solution.py:641
  173.3 32.5 %mixer_forward.1 = (bf16[1024,1536]{1,0:T(8,128)(2,1)}, f32[4,1024,256]{2,1,0:T(8,128)}, f32[4,1024,128]{2,1,0:T(8,128)S(1)}, bf16[4,1024,128]{2,1,0:T(8,128)(2,1)S(1)}) custom-call(bf16[1024,1536]{1,0:T(8,128)(2,1)} %fusion.2.x_ref, s32[1024,1]{1,0:T(8,128)S(1)} %bitcast.180, bf16[4,384,1664]{2,1,0:T(8,128)(2,1)} %pad_maximum_fusion.19.w_ref), custom_call_target="tpu_custom_call" | custom-call | flops 4831838208 | bytes 18743296 | tf_op jit(solution)/shard_map/mixer_forward/pallas_call | solution.py:257
  214.9 11.3 collective-permute-done.9
  268.4 13.0 %collective-permute-done.13 = bf16[256,1536]{1,0:T(8,128)(2,1)S(1)} collective-permute-done((bf16[256,1536]{1,0:T(8,128)(2,1)S(1)}, bf16[256,1536]{1,0:T(8,128)(2,1)S(1)}, u32[]{:S(2)}, u32[]{:S(2)}) %collective-permute-start.13) | collective-permute-done | bytes 786464 | tf_op jit(solution)/shard_map/ppermute | solution.py:69
  291.2 11.0 pad_maximum_fusion.15.w_ref
  302.1 59.2 %ffn_both.1 = (bf16[3,1152,1536]{2,1,0:T(8,128)(2,1)}, bf16[1024,1536]{1,0:T(8,128)(2,1)}, bf16[1024,1536]{1,0:T(8,128)(2,1)}) custom-call(bf16[1024,1536]{1,0:T(8,128)(2,1)} %copy-done.49, bf16[1024,1536]{1,0:T(8,128)(2,1)} %copy-done.48, bf16[3,1152,1536]{2,1,0:T(8,128)(2,1)} %pad_maximum_fusion.15.w_ref), custom_call_target="tpu_custom_call" | custom-call | flops 32614907904 | bytes 46399488 | tf_op jit(solution)/shard_map/ffn_both/pallas_call | solution.py:461
  370.1 15.3 %collective-permute-done.30 = bf16[256,1536]{1,0:T(8,128)(2,1)S(1)} collective-permute-done((bf16[256,1536]{1,0:T(8,128)(2,1)S(1)}, bf16[256,1536]{1,0:T(8,128)(2,1)S(1)}, u32[]{:S(2)}, u32[]{:S(2)}) %collective-permute-start.30) | collective-permute-done | bytes 786464 | tf_op jit(solution)/shard_map/ppermute | solution.py:69
  387.9 13.6 %collective-permute-done.26 = bf16[256,1536]{1,0:T(8,128)(2,1)S(1)} collective-permute-done((bf16[256,1536]{1,0:T(8,128)(2,1)S(1)}, bf16[256,1536]{1,0:T(8,128)(2,1)S(1)}, u32[]{:S(2)}, u32[]{:S(2)}) %collective-permute-start.26) | collective-permute-done | bytes 786464 | tf_op jit(solution)/shard_map/ppermute | solution.py:69
  427.9 9.5 collective-permute-done.29
  451.3 10.1 collective-permute-done.34
  472.1 41.2 %mixer_backward.1 = (bf16[4,384,1664]{2,1,0:T(8,128)(2,1)}, bf16[1024,1536]{1,0:T(8,128)(2,1)}) custom-call(bf16[1024,1536]{1,0:T(8,128)(2,1)} %fusion.2.x_ref, bf16[1024,1536]{1,0:T(8,128)(2,1)} %copy-done.47, s32[1024,1]{1,0:T(8,128)S(1)} %bitcast.181, bf16[4,384,1664]{2,1,0:T(8,128)(2,1)} %pad_maximum_fusion.19.w_ref, ...), custom_call_target="tpu_custom_call" | custom-call | flops 9663676416 | bytes 27000832 | tf_op jit(solution)/shard_map/mixer_backward/pallas_call | solution.py:377
  530.7 30.2 %collective-permute-done.56 = bf16[3,288,1536]{2,1,0:T(8,128)(2,1)} collective-permute-done((bf16[3,288,1536]{2,1,0:T(8,128)(2,1)}, bf16[3,288,1536]{2,1,0:T(8,128)(2,1)}, u32[]{:S(2)}, u32[]{:S(2)}) %collective-permute-start.56) | collective-permute-done | bytes 2654240 | tf_op jit(solution)/shard_map/ppermute | solution.py:69
  571.4 14.3 %collective-permute-start.46 = (bf16[384,1664]{1,0:T(8,128)(2,1)S(1)}, bf16[384,1664]{1,0:T(8,128)(2,1)S(1)}, u32[]{:S(2)}, u32[]{:S(2)}) collective-permute-start(bf16[384,1664]{1,0:T(8,128)(2,1)S(1)} %get-tuple-element.363), channel_id=1, source_target_pairs={{0,1},{3,2},{4,5},{7,6},{8,9},{11,10},{12,13},{15,14},{16,17},{19,... | collective-permute-start | bytes 3833864 | tf_op jit(solution)/shard_map/ppermute | solution.py:69
  586.8 11.9 %collective-permute-done.60 = bf16[3,288,1536]{2,1,0:T(8,128)(2,1)S(1)} collective-permute-done((bf16[3,288,1536]{2,1,0:T(8,128)(2,1)S(1)}, bf16[3,288,1536]{2,1,0:T(8,128)(2,1)S(1)}, u32[]{:S(2)}, u32[]{:S(2)}) %collective-permute-start.60) | collective-permute-done | bytes 2654240 | tf_op jit(solution)/shard_map/ppermute | solution.py:69
  647.6 22.2 %collective-permute-done.49 = bf16[384,1664]{1,0:T(8,128)(2,1)S(1)} collective-permute-done((bf16[384,1664]{1,0:T(8,128)(2,1)S(1)}, bf16[384,1664]{1,0:T(8,128)(2,1)S(1)}, u32[]{:S(2)}, u32[]{:S(2)}) %collective-permute-start.49) | collective-permute-done | bytes 1277984 | tf_op jit(solution)/shard_map/ppermute | solution.py:69
  693.5 10.8 collective-permute-done.38
  725.6 46.9 %psum.7 = f32[2,1536]{1,0:T(2,128)S(1)} all-reduce(f32[2,1536]{1,0:T(2,128)S(1)} %pad_maximum_fusion.37), channel_id=1, replica_groups=mesh['dp'=8,'shard'=4] {'dp','shard'}, use_global_device_ids=true, to_apply=%region_15.16 | all-reduce | flops 3072 | bytes 24576 | tf_op jit(solution)/shard_map/psum | solution.py:703
  777.9 82.7 %conditional.4 = (f32[974688]{0:T(1024)}, f32[768]{0:T(1024)S(1)}, f32[1,974688]{1,0:T(1,128)}, bf16[2,512]{1,0:T(2,128)(2,1)S(1)}) conditional(s32[]{:T(128)} %clamp.3, bf16[4,384,1664]{2,1,0:T(8,128)(2,1)} %broadcast_select_fusion.6, bf16[4,384,1664]{2,1,0:T(8,128)(2,1)} %broadcast_select_fusion.6, ...), branch_computations={%region_5.6_spmd, %region_6.7_spmd, %region_7.8_spmd, %region_8.9_... | conditional | flops 13841792 | bytes 145993984
  783.2 15.6 %copy.49 = bf16[4,3,288,1536]{2,3,1,0:T(8,128)(2,1)} copy(bf16[4,3,288,1536]{3,2,1,0:T(8,128)(2,1)} %get-tuple-element.227) | data formatting | bytes 21233664 | tf_op jit(solution)/shard_map
  798.8 15.6 %copy.50 = bf16[4,3,288,1536]{2,3,1,0:T(8,128)(2,1)} copy(bf16[4,3,288,1536]{3,2,1,0:T(8,128)(2,1)} %get-tuple-element.228) | data formatting | bytes 21233664 | tf_op jit(solution)/shard_map
  860.7 48.8 %convert_reduce_fusion = (bf16[975456]{0:T(1024)(128)(2,1)S(1)}, f32[1,975456]{1,0:T(1,128)}, f32[1,975456]{1,0:T(1,128)}, f32[1,975456]{1,0:T(1,128)}) fusion(f32[1,975456]{1,0:T(1,128)} %param.39, f32[1,768]{1,0:T(1,128)S(1)} %concatenate.277, f32[1,974688]{1,0:T(1,128)} %get-tuple-element.202, f32[1,975456]{1,0:T(1,128)} %param.40, f32[1,975456]{1,0:T(1,128)} %param.41), kind=kLoop, calls=%fused_computation.129 | loop fusion | flops 16582752 | bytes 29263680 | tf_op jit(solution)/shard_map/convert_element_type | solution.py:715
  913.9 38.7 %collective-permute-done.64 = bf16[975456]{0:T(1024)(128)(2,1)} collective-permute-done((bf16[975456]{0:T(1024)(128)(2,1)S(1)}, bf16[975456]{0:T(1024)(128)(2,1)}, u32[]{:S(2)}, u32[]{:S(2)}) %collective-permute-start.64) | collective-permute-done | bytes 1950944 | tf_op jit(solution)/shard_map/ppermute | solution.py:69
  964.2 36.9 %collective-permute-done.65 = bf16[975456]{0:T(1024)(128)(2,1)} collective-permute-done((bf16[975456]{0:T(1024)(128)(2,1)}, bf16[975456]{0:T(1024)(128)(2,1)}, u32[]{:S(2)}, u32[]{:S(2)}) %collective-permute-start.65) | collective-permute-done | bytes 1950944 | tf_op jit(solution)/shard_map/ppermute | solution.py:69
  1010.4 19.0 %reshape.358 = f32[1,975456]{1,0:T(1,128)} reshape(f32[975456]{0:T(1024)S(1)} %pad_maximum_fusion.21) | data formatting | bytes 7803648 | tf_op jit(solution)/shard_map/reshape | solution.py:707
  1030.0 17.7 %collective-permute-done.66 = bf16[975456]{0:T(1024)(128)(2,1)S(1)} collective-permute-done((bf16[975456]{0:T(1024)(128)(2,1)}, bf16[975456]{0:T(1024)(128)(2,1)S(1)}, u32[]{:S(2)}, u32[]{:S(2)}) %collective-permute-start.66) | collective-permute-done | bytes 1950944 | tf_op jit(solution)/shard_map/ppermute | solution.py:69
  1056.5 22.3 %stack.80 = bf16[1,975456]{1,0:T(2,128)(2,1)S(1)} reshape(bf16[975456]{0:T(1024)(128)(2,1)S(1)} %get-tuple-element.329) | data formatting | bytes 3901824 | tf_op jit(solution)/shard_map/stack | solution.py:721
  1078.7 22.3 %stack.79 = bf16[1,975456]{1,0:T(2,128)(2,1)S(1)} reshape(bf16[975456]{0:T(1024)(128)(2,1)S(1)} %get-tuple-element.328) | data formatting | bytes 3901824 | tf_op jit(solution)/shard_map/stack | solution.py:721
  1101.0 22.3 %stack.78 = bf16[1,975456]{1,0:T(2,128)(2,1)S(1)} reshape(bf16[975456]{0:T(1024)(128)(2,1)S(1)} %get-tuple-element.327) | data formatting | bytes 3901824 | tf_op jit(solution)/shard_map/stack | solution.py:721
  1123.3 22.5 %stack.77 = bf16[1,975456]{1,0:T(2,128)(2,1)S(1)} reshape(bf16[975456]{0:T(1024)(128)(2,1)S(1)} %get-tuple-element.326) | data formatting | bytes 3901824 | tf_op jit(solution)/shard_map/stack | solution.py:721
  1145.8 26.3 %pad_maximum_fusion.17 = bf16[4,975456]{1,0:T(4,128)(2,1)} fusion(bf16[1,975456]{1,0:T(2,128)(2,1)S(1)} %stack.80, bf16[1,975456]{1,0:T(2,128)(2,1)S(1)} %stack.79, bf16[1,975456]{1,0:T(2,128)(2,1)S(1)} %stack.78, bf16[1,975456]{1,0:T(2,128)(2,1)S(1)} %stack.77), kind=kLoop, calls=%fused_computation.111 | loop fusion | flops 31214592 | bytes 15607296 | tf_op jit(solution)/shard_map/stack | solution.py:721
  (372 shorter events, 388.7 us)
Async XLA Ops:
  34.0 32.2 %collective-permute-start.21 = (bf16[3,288,1536]{2,1,0:T(8,128)(2,1)}, bf16[3,288,1536]{2,1,0:T(8,128)(2,1)}, u32[]{:S(2)}, u32[]{:S(2)}) collective-permute-start(bf16[3,288,1536]{2,1,0:T(8,128)(2,1)} %pad_maximum_fusion.24), channel_id=1, source_target_pairs={{0,1},{1,2},{6,5},{7,6},{8,9},{9,10},{14,13},{15,14},{16,17},{17,1... | collective-permute-start | bytes 7962632 | tf_op jit(solution)/shard_map/ppermute | solution.py:69
  38.6 29.8 %collective-permute-start.7 = (bf16[384,1664]{1,0:T(8,128)(2,1)}, bf16[384,1664]{1,0:T(8,128)(2,1)}, u32[]{:S(2)}, u32[]{:S(2)}) collective-permute-start(bf16[384,1664]{1,0:T(8,128)(2,1)} %pad_maximum_fusion.28), channel_id=1, source_target_pairs={{1,0},{6,7},{9,8},{14,15},{17,16},{22,23},{25,24},{30,31}} | collective-permute-start | bytes 3833864 | tf_op jit(solution)/shard_map/ppermute | solution.py:69
  39.9 28.5 %collective-permute-start.6 = (bf16[384,1664]{1,0:T(8,128)(2,1)S(1)}, bf16[384,1664]{1,0:T(8,128)(2,1)}, u32[]{:S(2)}, u32[]{:S(2)}) collective-permute-start(bf16[384,1664]{1,0:T(8,128)(2,1)S(1)} %collective-permute-done.5), channel_id=1, source_target_pairs={{2,3},{5,4},{10,11},{13,12},{18,19},{21,20},{26,27},{29,28}} | collective-permute-start | bytes 3833864 | tf_op jit(solution)/shard_map/ppermute | solution.py:69
  42.6 57.4 %collective-permute-start.1 = (bf16[272,1536]{1,0:T(8,128)(2,1)}, bf16[272,1536]{1,0:T(8,128)(2,1)}, u32[]{:S(2)}, u32[]{:S(2)}) collective-permute-start(bf16[272,1536]{1,0:T(8,128)(2,1)} %fusion.24), channel_id=1, source_target_pairs={{0,16},{1,17},{2,18},{3,19},{4,20},{5,21},{6,22},{7,23},{8,24},{9,... | collective-permute-start | bytes 2506760 | tf_op jit(solution)/shard_map/ppermute | solution.py:69
  43.9 57.8 %collective-permute-start = (bf16[272,1536]{1,0:T(8,128)(2,1)}, bf16[272,1536]{1,0:T(8,128)(2,1)}, u32[]{:S(2)}, u32[]{:S(2)}) collective-permute-start(bf16[272,1536]{1,0:T(8,128)(2,1)} %fusion.24), channel_id=1, source_target_pairs={{0,8},{1,9},{2,10},{3,11},{4,12},{5,13},{6,14},{7,15},{8,0},{9,1},... | collective-permute-start | bytes 2506760 | tf_op jit(solution)/shard_map/ppermute | solution.py:69
  66.2 96.5 %collective-permute-start.22 = (bf16[3,288,1536]{2,1,0:T(8,128)(2,1)}, bf16[3,288,1536]{2,1,0:T(8,128)(2,1)}, u32[]{:S(2)}, u32[]{:S(2)}) collective-permute-start(bf16[3,288,1536]{2,1,0:T(8,128)(2,1)} %collective-permute-done.21), channel_id=1, source_target_pairs={{1,2},{2,3},{5,4},{6,5},{9,10},{10,11},{13,12},{14,13},{17,18},{18... | collective-permute-start | bytes 7962632 | tf_op jit(solution)/shard_map/ppermute | solution.py:69
  73.8 94.9 %collective-permute-start.8 = (bf16[2,384,1664]{2,1,0:T(8,128)(2,1)}, bf16[2,384,1664]{2,1,0:T(8,128)(2,1)}, u32[]{:S(2)}, u32[]{:S(2)}) collective-permute-start(bf16[2,384,1664]{2,1,0:T(8,128)(2,1)} %pad_maximum_fusion.25), channel_id=1, source_target_pairs={{0,4},{1,5},{2,6},{3,7},{4,0},{5,1},{6,2},{7,3},{8,12},{9,13},{10,... | collective-permute-start | bytes 7667720 | tf_op jit(solution)/shard_map/ppermute | solution.py:69
  101.1 60.7 %collective-permute-start.3 = (bf16[136,1536]{1,0:T(8,128)(2,1)S(1)}, bf16[136,1536]{1,0:T(8,128)(2,1)S(1)}, u32[]{:S(2)}, u32[]{:S(2)}) collective-permute-start(bf16[136,1536]{1,0:T(8,128)(2,1)S(1)} %slice.1344), channel_id=1, source_target_pairs={{0,8},{1,9},{2,10},{3,11},{4,12},{5,13},{6,14},{7,15},{8,0},{9,1},... | collective-permute-start | bytes 1253384 | tf_op jit(solution)/shard_map/ppermute | solution.py:69
  102.8 59.1 %collective-permute-start.2 = (bf16[136,1536]{1,0:T(8,128)(2,1)S(1)}, bf16[136,1536]{1,0:T(8,128)(2,1)S(1)}, u32[]{:S(2)}, u32[]{:S(2)}) collective-permute-start(bf16[136,1536]{1,0:T(8,128)(2,1)S(1)} %slice.1343), channel_id=1, source_target_pairs={{0,16},{1,17},{2,18},{3,19},{4,20},{5,21},{6,22},{7,23},{8,24},{9,... | collective-permute-start | bytes 1253384 | tf_op jit(solution)/shard_map/ppermute | solution.py:69
  104.3 105.5 %collective-permute-start.24 = (bf16[3,288,1536]{2,1,0:T(8,128)(2,1)}, bf16[3,288,1536]{2,1,0:T(8,128)(2,1)}, u32[]{:S(2)}, u32[]{:S(2)}) collective-permute-start(bf16[3,288,1536]{2,1,0:T(8,128)(2,1)} %pad_maximum_fusion.24), channel_id=1, source_target_pairs={{1,0},{6,7},{9,8},{14,15},{17,16},{22,23},{25,24},{30,31}} | collective-permute-start | bytes 7962632 | tf_op jit(solution)/shard_map/ppermute | solution.py:69
  162.7 47.2 %collective-permute-start.23 = (bf16[3,288,1536]{2,1,0:T(8,128)(2,1)}, bf16[3,288,1536]{2,1,0:T(8,128)(2,1)}, u32[]{:S(2)}, u32[]{:S(2)}) collective-permute-start(bf16[3,288,1536]{2,1,0:T(8,128)(2,1)} %collective-permute-done.22), channel_id=1, source_target_pairs={{2,3},{5,4},{10,11},{13,12},{18,19},{21,20},{26,27},{29,28}} | collective-permute-start | bytes 7962632 | tf_op jit(solution)/shard_map/ppermute | solution.py:69
  214.8 74.7 %collective-permute-start.25 = (bf16[3,576,1536]{2,1,0:T(8,128)(2,1)S(1)}, bf16[3,576,1536]{2,1,0:T(8,128)(2,1)S(1)}, u32[]{:S(2)}, u32[]{:S(2)}) collective-permute-start(bf16[3,576,1536]{2,1,0:T(8,128)(2,1)S(1)} %pad_maximum_fusion.18), channel_id=1, source_target_pairs={{0,4},{1,5},{2,6},{3,7},{4,0},{5,1},{6,2},{7,3},{8,12},{9,13},{10,... | collective-permute-start | bytes 15925256 | tf_op jit(solution)/shard_map/ppermute | solution.py:69
  364.3 51.4 %collective-permute-start.53 = (bf16[3,576,1536]{2,1,0:T(8,128)(2,1)S(1)}, bf16[3,576,1536]{2,1,0:T(8,128)(2,1)}, u32[]{:S(2)}, u32[]{:S(2)}) collective-permute-start(bf16[3,576,1536]{2,1,0:T(8,128)(2,1)S(1)} %slice.1193), channel_id=1, source_target_pairs={{0,4},{1,5},{2,6},{3,7},{4,0},{5,1},{6,2},{7,3},{8,12},{9,13},{10,... | collective-permute-start | bytes 15925256 | tf_op jit(solution)/shard_map/ppermute | solution.py:69
  366.5 35.0 %collective-permute-start.26 = (bf16[256,1536]{1,0:T(8,128)(2,1)S(1)}, bf16[256,1536]{1,0:T(8,128)(2,1)S(1)}, u32[]{:S(2)}, u32[]{:S(2)}) collective-permute-start(bf16[256,1536]{1,0:T(8,128)(2,1)S(1)} %pad_maximum_fusion.31), channel_id=1, source_target_pairs={{0,8},{1,9},{2,10},{3,11},{4,12},{5,13},{6,14},{7,15},{8,0},{9,1},... | collective-permute-start | bytes 2359304 | tf_op jit(solution)/shard_map/ppermute | solution.py:69
  367.6 37.0 %collective-permute-start.32 = (bf16[256,1536]{1,0:T(8,128)(2,1)S(1)}, bf16[256,1536]{1,0:T(8,128)(2,1)S(1)}, u32[]{:S(2)}, u32[]{:S(2)}) collective-permute-start(bf16[256,1536]{1,0:T(8,128)(2,1)S(1)} %pad_maximum_fusion.34), channel_id=1, source_target_pairs={{0,16},{1,17},{2,18},{3,19},{4,20},{5,21},{6,22},{7,23},{8,24},{9,... | collective-permute-start | bytes 2359304 | tf_op jit(solution)/shard_map/ppermute | solution.py:69
  370.0 54.2 %collective-permute-start.28 = (bf16[256,1536]{1,0:T(8,128)(2,1)S(1)}, bf16[256,1536]{1,0:T(8,128)(2,1)}, u32[]{:S(2)}, u32[]{:S(2)}) collective-permute-start(bf16[256,1536]{1,0:T(8,128)(2,1)S(1)} %pad_maximum_fusion.32), channel_id=1, source_target_pairs={{0,16},{1,17},{2,18},{3,19},{4,20},{5,21},{6,22},{7,23},{8,24},{9,... | collective-permute-start | bytes 2359304 | tf_op jit(solution)/shard_map/ppermute | solution.py:69
  385.5 28.2 %collective-permute-start.31 = (bf16[128,1536]{1,0:T(8,128)(2,1)S(1)}, bf16[128,1536]{1,0:T(8,128)(2,1)S(1)}, u32[]{:S(2)}, u32[]{:S(2)}) collective-permute-start(bf16[128,1536]{1,0:T(8,128)(2,1)S(1)} %add_convert_fusion.9), channel_id=1, source_target_pairs={{0,16},{1,17},{2,18},{3,19},{4,20},{5,21},{6,22},{7,23},{8,24},{9,... | collective-permute-start | bytes 1179656 | tf_op jit(solution)/shard_map/ppermute | solution.py:69
  443.6 75.6 %collective-permute-start.57 = (bf16[3,288,1536]{2,1,0:T(8,128)(2,1)}, bf16[3,288,1536]{2,1,0:T(8,128)(2,1)}, u32[]{:S(2)}, u32[]{:S(2)}) collective-permute-start(bf16[3,288,1536]{2,1,0:T(8,128)(2,1)} %get-tuple-element.333), channel_id=1, source_target_pairs={{0,1},{3,2},{4,5},{7,6},{8,9},{11,10},{12,13},{15,14},{16,17},{19,... | collective-permute-start | bytes 7962632 | tf_op jit(solution)/shard_map/ppermute | solution.py:69
  448.8 70.5 %collective-permute-start.55 = (bf16[3,288,1536]{2,1,0:T(8,128)(2,1)}, bf16[3,288,1536]{2,1,0:T(8,128)(2,1)}, u32[]{:S(2)}, u32[]{:S(2)}) collective-permute-start(bf16[3,288,1536]{2,1,0:T(8,128)(2,1)} %fusion.3), channel_id=1, source_target_pairs={{2,1},{5,6},{10,9},{13,14},{18,17},{21,22},{26,25},{29,30}} | collective-permute-start | bytes 7962632 | tf_op jit(solution)/shard_map/ppermute | solution.py:69
  525.6 35.3 %collective-permute-start.56 = (bf16[3,288,1536]{2,1,0:T(8,128)(2,1)}, bf16[3,288,1536]{2,1,0:T(8,128)(2,1)}, u32[]{:S(2)}, u32[]{:S(2)}) collective-permute-start(bf16[3,288,1536]{2,1,0:T(8,128)(2,1)} %get-tuple-element.330), channel_id=1, source_target_pairs={{1,0},{6,7},{9,8},{14,15},{17,16},{22,23},{25,24},{30,31}} | collective-permute-start | bytes 7962632 | tf_op jit(solution)/shard_map/ppermute | solution.py:69
  564.8 33.9 %collective-permute-start.60 = (bf16[3,288,1536]{2,1,0:T(8,128)(2,1)S(1)}, bf16[3,288,1536]{2,1,0:T(8,128)(2,1)S(1)}, u32[]{:S(2)}, u32[]{:S(2)}) collective-permute-start(bf16[3,288,1536]{2,1,0:T(8,128)(2,1)S(1)} %fusion.8), channel_id=1, source_target_pairs={{0,16},{1,17},{6,22},{7,23},{8,24},{9,25},{14,30},{15,31},{16,0},{... | collective-permute-start | bytes 7962632 | tf_op jit(solution)/shard_map/ppermute | solution.py:69
  568.3 33.9 %collective-permute-start.59 = (bf16[3,288,1536]{2,1,0:T(8,128)(2,1)S(1)}, bf16[3,288,1536]{2,1,0:T(8,128)(2,1)S(1)}, u32[]{:S(2)}, u32[]{:S(2)}) collective-permute-start(bf16[3,288,1536]{2,1,0:T(8,128)(2,1)S(1)} %fusion.8), channel_id=1, source_target_pairs={{0,8},{1,9},{6,14},{7,15},{8,0},{9,1},{14,6},{15,7},{16,24},{17,25... | collective-permute-start | bytes 7962632 | tf_op jit(solution)/shard_map/ppermute | solution.py:69
  571.4 42.8 %collective-permute-start.46 = (bf16[384,1664]{1,0:T(8,128)(2,1)S(1)}, bf16[384,1664]{1,0:T(8,128)(2,1)S(1)}, u32[]{:S(2)}, u32[]{:S(2)}) collective-permute-start(bf16[384,1664]{1,0:T(8,128)(2,1)S(1)} %get-tuple-element.363), channel_id=1, source_target_pairs={{0,1},{3,2},{4,5},{7,6},{8,9},{11,10},{12,13},{15,14},{16,17},{19,... | collective-permute-start | bytes 3833864 | tf_op jit(solution)/shard_map/ppermute | solution.py:69
  586.1 28.1 %collective-permute-start.44 = (bf16[384,1664]{1,0:T(8,128)(2,1)S(1)}, bf16[384,1664]{1,0:T(8,128)(2,1)S(1)}, u32[]{:S(2)}, u32[]{:S(2)}) collective-permute-start(bf16[384,1664]{1,0:T(8,128)(2,1)S(1)} %fusion.9), channel_id=1, source_target_pairs={{2,1},{5,6},{10,9},{13,14},{18,17},{21,22},{26,25},{29,30}} | collective-permute-start | bytes 3833864 | tf_op jit(solution)/shard_map/ppermute | solution.py:69
  627.2 150.6 %collective-permute-start.63 = (bf16[4,3,288,1536]{3,2,1,0:T(8,128)(2,1)}, bf16[4,3,288,1536]{3,2,1,0:T(8,128)(2,1)}, u32[]{:S(2)}, u32[]{:S(2)}) collective-permute-start(bf16[4,3,288,1536]{3,2,1,0:T(8,128)(2,1)} %pad_maximum_fusion.16), channel_id=1, source_target_pairs={{0,4},{1,5},{6,2},{7,3},{8,12},{9,13},{14,10},{15,11},{16,20},{17,... | collective-permute-start | bytes 31850504 | tf_op jit(solution)/shard_map/ppermute | solution.py:69
  688.5 84.6 %collective-permute-start.52 = (bf16[4,384,1664]{2,1,0:T(8,128)(2,1)}, bf16[4,384,1664]{2,1,0:T(8,128)(2,1)}, u32[]{:S(2)}, u32[]{:S(2)}) collective-permute-start(bf16[4,384,1664]{2,1,0:T(8,128)(2,1)} %pad_maximum_fusion.20), channel_id=1, source_target_pairs={{0,4},{1,5},{6,2},{7,3},{8,12},{9,13},{14,10},{15,11},{16,20},{17,... | collective-permute-start | bytes 15335432 | tf_op jit(solution)/shard_map/ppermute | solution.py:69
  909.5 43.1 %collective-permute-start.64 = (bf16[975456]{0:T(1024)(128)(2,1)S(1)}, bf16[975456]{0:T(1024)(128)(2,1)}, u32[]{:S(2)}, u32[]{:S(2)}) collective-permute-start(bf16[975456]{0:T(1024)(128)(2,1)S(1)} %get-tuple-element.252), channel_id=1, source_target_pairs={{0,1},{1,2},{2,3},{4,5},{5,6},{6,7},{8,9},{9,10},{10,11},{12,13},{... | collective-permute-start | bytes 5852744 | tf_op jit(solution)/shard_map/ppermute | solution.py:69
  912.6 46.7 %collective-permute-start.67 = (bf16[975456]{0:T(1024)(128)(2,1)S(1)}, bf16[975456]{0:T(1024)(128)(2,1)}, u32[]{:S(2)}, u32[]{:S(2)}) collective-permute-start(bf16[975456]{0:T(1024)(128)(2,1)S(1)} %get-tuple-element.252), channel_id=1, source_target_pairs={{1,0},{2,1},{3,2},{5,4},{6,5},{7,6},{9,8},{10,9},{11,10},{13,12},{... | collective-permute-start | bytes 5852744 | tf_op jit(solution)/shard_map/ppermute | solution.py:69
  952.6 48.5 %collective-permute-start.65 = (bf16[975456]{0:T(1024)(128)(2,1)}, bf16[975456]{0:T(1024)(128)(2,1)}, u32[]{:S(2)}, u32[]{:S(2)}) collective-permute-start(bf16[975456]{0:T(1024)(128)(2,1)} %collective-permute-done.64), channel_id=1, source_target_pairs={{0,1},{1,2},{2,3},{4,5},{5,6},{6,7},{8,9},{9,10},{10,11},{12,13},{... | collective-permute-start | bytes 5852744 | tf_op jit(solution)/shard_map/ppermute | solution.py:69
  959.3 47.2 %collective-permute-start.68 = (bf16[975456]{0:T(1024)(128)(2,1)}, bf16[975456]{0:T(1024)(128)(2,1)}, u32[]{:S(2)}, u32[]{:S(2)}) collective-permute-start(bf16[975456]{0:T(1024)(128)(2,1)} %collective-permute-done.67), channel_id=1, source_target_pairs={{1,0},{2,1},{3,2},{5,4},{6,5},{7,6},{9,8},{10,9},{11,10},{13,12},{... | collective-permute-start | bytes 5852744 | tf_op jit(solution)/shard_map/ppermute | solution.py:69
  1001.1 46.6 %collective-permute-start.66 = (bf16[975456]{0:T(1024)(128)(2,1)}, bf16[975456]{0:T(1024)(128)(2,1)S(1)}, u32[]{:S(2)}, u32[]{:S(2)}) collective-permute-start(bf16[975456]{0:T(1024)(128)(2,1)} %collective-permute-done.65), channel_id=1, source_target_pairs={{0,1},{1,2},{2,3},{4,5},{5,6},{6,7},{8,9},{9,10},{10,11},{12,13},{... | collective-permute-start | bytes 5852744 | tf_op jit(solution)/shard_map/ppermute | solution.py:69
  1006.5 46.3 %collective-permute-start.69 = (bf16[975456]{0:T(1024)(128)(2,1)}, bf16[975456]{0:T(1024)(128)(2,1)S(1)}, u32[]{:S(2)}, u32[]{:S(2)}) collective-permute-start(bf16[975456]{0:T(1024)(128)(2,1)} %collective-permute-done.68), channel_id=1, source_target_pairs={{1,0},{2,1},{3,2},{5,4},{6,5},{7,6},{9,8},{10,9},{11,10},{13,12},{... | collective-permute-start | bytes 5852744 | tf_op jit(solution)/shard_map/ppermute | solution.py:69
  (88 other events, 2826.6 us)

commit v2 on v1

--- a/solution.py
+++ b/solution.py
@@ -131,6 +131,30 @@
     inner_two = add_low(inner_one, move(inner_one, line_pairs({2: 1})))
     third = add_low(outer, move(second, line_pairs({1: 0})))
     return jnp.where(end == 0, third, inner_two)
+
+
+def turn_pairs(turn):
+    return device_pairs(lambda chip, core, z: (chip, core, (z + turn) % 4))
+
+
+def all_slices(own, z):
+    found = [own] + [move(own, turn_pairs(turn)) for turn in (1, 2, 3)]
+    return jnp.concatenate(
+        [
+            sum(jnp.where((z - at) % 4 == turn, found[turn], 0) for turn in range(4))
+            for at in range(4)
+        ],
+        axis=-1,
+    )
+
+
+def shard_slices(value, z):
+    size = value.shape[-1] // 4
+
+    def part(turn):
+        return lax.dynamic_slice_in_dim(value, ((z + turn) % 4) * size, size, axis=1)
+
+    return part(0) + sum(move(part(turn), turn_pairs(turn)) for turn in (1, 2, 3))
 
 
 def dot_rows(left, right):
@@ -491,89 +515,351 @@
     )(x, grad_out, weights)
 
 
-def piece_rows(start, length, low, high):
-    return max(low - start, 0), min(high - start, length)
-
-
-def build_piece(member, piece_length, sizes, mix, ffn):
-    model, width, ffn_width, slice_rec, slice_ffn = sizes
+def tail_kernel(
+    sizes,
+    mix_ref,
+    ffn_ref,
+    gain_ref,
+    master_ref,
+    first_ref,
+    second_ref,
+    piece_ref,
+    new_master_ref,
+    new_first_ref,
+    new_second_ref,
+    weights_ref,
+    bias_ref,
+    grad,
+    held,
+    spread,
+    send_sem,
+    recv_sem,
+):
+    model, width, ffn_width, piece_length, chunks, lines, margin = sizes
+    member = lax.axis_index("dp")
+    z = lax.axis_index("shard")
     chip = member // 2
-    mix = [mix[number ^ chip] for number in range(4)]
-    ffn = [ffn[number ^ chip] for number in range(4)]
-    low = member * piece_length
-    high = low + piece_length
-    parts = []
-    start = 0
-
-    def add(length, row, rows_of):
-        nonlocal start
-        first, last = piece_rows(start, length, low, high)
-        if first < last:
-            row_low, row_high = first // row, -(-last // row)
-            block = rows_of(row_low, row_high)
-            flat = block.reshape(-1)
-            parts.append(flat[first - row_low * row : last - row_low * row])
-        start += length
-
-    def columns(source, kinds, row_low, row_high):
-        found = []
-        for kind in range(kinds):
-            a, b = max(row_low - kind * model, 0), min(row_high - kind * model, model)
-            if a < b:
-                found.append(
-                    jnp.concatenate([source(q, kind)[:, a:b] for q in range(4)], axis=0).T
-                )
-        return jnp.concatenate(found, axis=0)
-
-    def quarter_rows(source, count, row_low, row_high):
-        found = []
-        for q in range(4):
-            a, b = max(row_low - q * count, 0), min(row_high - q * count, count)
-            if a < b:
-                found.append(source(q)[a:b])
-        return jnp.concatenate(found, axis=0)
-
-    def gate_rows(row_low, row_high):
-        found = []
-        for number in range(8):
-            kind, q = number // 4, number % 4
-            a, b = max(row_low - number * width, 0), min(row_high - number * width, width)
-            if a < b:
-                found.append(mix[q][kind * width + a : kind * width + b, model:])
-        return jnp.concatenate(found, axis=0)
-
-    def small_rows(offset):
-        return lambda a, b: jnp.concatenate(
-            [mix[q][2 * width + offset + a : 2 * width + offset + b, model:] for q in range(4)],
-            axis=1,
+    step = pl.program_id(0)
+    lead = 128
+    start_row = (member * piece_length) // lead
+    offset = (member * piece_length) % lead
+    used_rows = piece_length // lead + 2
+    tiles_in = 4 * width // lead
+    tiles_ffn = 4 * ffn_width // lead
+    tiles_model = model // lead
+
+    def relative(q):
+        return ((q // 2 + chip // 2) % 2) * 2 + (q % 2 + chip % 2) % 2
+
+    def copy_to(origin, chunk, side, to):
+        return pltpu.make_async_remote_copy(
+            src_ref=held.at[origin, chunk],
+            dst_ref=held.at[origin, chunk],
+            send_sem=send_sem.at[side, origin, chunk],
+            recv_sem=recv_sem.at[origin, chunk],
+            device_id=(member, to),
+            device_id_type=pl.DeviceIdType.MESH,
         )
 
-    add(
-        2 * model * slice_rec,
-        slice_rec,
-        lambda a, b: columns(lambda q, k: mix[q][k * width : (k + 1) * width, :model], 2, a, b),
-    )
-    add(2 * 4 * width * width, width, gate_rows)
-    add(
-        slice_rec * model,
-        model,
-        lambda a, b: quarter_rows(lambda q: mix[q][2 * width : 3 * width, :model], width, a, b),
-    )
-    add(2 * model * slice_ffn, slice_ffn, lambda a, b: columns(lambda q, k: ffn[q][k], 2, a, b))
-    add(
-        slice_ffn * model,
-        model,
-        lambda a, b: quarter_rows(lambda q: ffn[q][2], ffn_width, a, b),
-    )
-    add(5 * slice_rec, slice_rec, small_rows(0))
-    add(2 * slice_rec, slice_rec, small_rows(5))
-    add(slice_rec, slice_rec, small_rows(7))
-    gains = 2 * (model // 4)
-    add(gains, gains, lambda a, b: jnp.zeros((gains,), low_type))
-    bias = jnp.concatenate(
-        [mix[q][2 * width + 5 : 2 * width + 7, model:] for q in range(4)], axis=1
-    )
-    return jnp.concatenate(parts).astype(wide), bias.astype(wide)
+    @pl.when(step == 0)
+    def _():
+        barrier = pltpu.get_barrier_semaphore()
+
+        @pl.when(z > 0)
+        def _():
+            pl.semaphore_signal(
+                barrier, inc=1, device_id=(member, z - 1), device_id_type=pl.DeviceIdType.MESH
+            )
+
+        @pl.when(z < 3)
+        def _():
+            pl.semaphore_signal(
+                barrier, inc=1, device_id=(member, z + 1), device_id_type=pl.DeviceIdType.MESH
+            )
+
+        @pl.when((z == 0) | (z == 3))
+        def _():
+            pl.semaphore_wait(barrier, 1)
+
+        @pl.when((z > 0) & (z < 3))
+        def _():
+            pl.semaphore_wait(barrier, 2)
+
+        def clear(number, carry):
+            grad[pl.ds(pl.multiple_of(number * 256, 256), 256), :] = jnp.zeros((256, lead), wide)
+            return carry
+
+        lax.fori_loop(0, grad.shape[0] // 256, clear, 0)
+
+        def place(row, count, body):
+            @pl.when((row < start_row + used_rows) & (row + count > start_row))
+            def _():
+                body(row - start_row + margin)
+
+        base = 0
+
+        def in_unit(number, carry):
+            kind = number // tiles_model
+            at = number % tiles_model
+
+            def body(to):
+                for q in range(4):
+                    tile = mix_ref[
+                        relative(q),
+                        pl.ds(pl.multiple_of(kind * width, width), width),
+                        pl.ds(pl.multiple_of(at * lead, lead), lead),
+                    ].astype(wide)
+                    grad[pl.ds(to + q, lead, stride=tiles_in), :] = tile.T
+
+            place((kind * model + at * lead) * tiles_in, lead * tiles_in, body)
+            return carry
+
+        lax.fori_loop(0, 2 * tiles_model, in_unit, 0)
+        base = 2 * model * tiles_in
+
+        def gate_body(number, carry):
+            kind = number // 4
+            q = number % 4
+
+            def body(to):
+                grad[pl.ds(to, width), :] = mix_ref[
+                    relative(q), pl.ds(pl.multiple_of(kind * width, width), width), model:
+                ].astype(wide)
+
+            place(2 * model * tiles_in + number * width, width, body)
+            return carry
+
+        lax.fori_loop(0, 8, gate_body, 0)
+        base = base + 8 * width
+        out_base = base
+
+        def out_unit(q, carry):
+            def body(to):
+                for at in range(tiles_model):
+                    grad[pl.ds(to + at, width, stride=tiles_model), :] = mix_ref[
+                        relative(q), 2 * width : 3 * width, at * lead : (at + 1) * lead
+                    ].astype(wide)
+
+            place(out_base + q * width * tiles_model, width * tiles_model, body)
+            return carry
+
+        lax.fori_loop(0, 4, out_unit, 0)
+        base = base + 4 * width * tiles_model
+        up_base = base
+
+        def up_unit(number, carry):
+            kind = number // tiles_model
+            at = number % tiles_model
+            columns = pl.ds(pl.multiple_of(at * lead, lead), lead)
+
+            def body(to):
+                for tile in range(tiles_ffn):
+                    found = []
+                    row = tile * lead
+                    while row < (tile + 1) * lead:
+                        q = row // ffn_width
+                        last = min((q + 1) * ffn_width, (tile + 1) * lead)
+                        found.append(
+                            ffn_ref[
+                                relative(q),
+                                kind,
+                                row - q * ffn_width : last - q * ffn_width,
+                                columns,
+                            ].astype(wide)
+                        )
+                        row = last
+                    block = found[0] if len(found) == 1 else jnp.concatenate(found, axis=0)
+                    grad[pl.ds(to + tile, lead, stride=tiles_ffn), :] = block.T
+
+            place(up_base + (kind * model + at * lead) * tiles_ffn, lead * tiles_ffn, body)
+            return carry
+
+        lax.fori_loop(0, 2 * tiles_model, up_unit, 0)
+        base = base + 2 * model * tiles_ffn
+        down_base = base
+        third = ffn_width // 3
+
+        def down_unit(number, carry):
+            q = number // 3
+            part = number % 3
+
+            def body(to):
+                for at in range(tiles_model):
+                    grad[pl.ds(to + at, third, stride=tiles_model), :] = ffn_ref[
+                        relative(q),
+                        2,
+                        pl.ds(pl.multiple_of(part * third, 16), third),
+                        at * lead : (at + 1) * lead,
+                    ].astype(wide)
+
+            place(down_base + number * third * tiles_model, third * tiles_model, body)
+            return carry
+
+        lax.fori_loop(0, 12, down_unit, 0)
+        small_base = base + 4 * ffn_width * tiles_model
+        smalls = [
+            mix_ref[relative(q), 2 * width : 2 * width + 16, model:].astype(wide)
+            for q in range(4)
+        ]
+
+        def small_body(to):
+            for q in range(4):
+                grad[pl.ds(to + q, 8, stride=tiles_in), :] = smalls[q][:8]
+            grad[pl.ds(to + 8 * tiles_in, 6), :] = gain_ref[0:6, :]
+
+        place(small_base, 8 * tiles_in + 6, small_body)
+        bias_ref[...] = jnp.concatenate([small[5:7] for small in smalls], axis=1)
+
+    @pl.when(step < chunks)
+    def _():
+        row = margin + step * lines
+        shift = (lead - offset) % lead
+        here = pltpu.roll(grad[pl.ds(row, lines), :], shift, 1)
+        after = pltpu.roll(grad[pl.ds(row + 1, lines), :], shift, 1)
+        lane = lax.broadcasted_iota(jnp.int32, (lines, lead), 1)
+        piece = jnp.where(lane < lead - offset, here, after).reshape(1, lines * lead)
+        piece_ref[...] = piece
+        new_first = beta_one * first_ref[...] + (1.0 - beta_one) * piece
+        new_second = beta_two * second_ref[...] + (1.0 - beta_two) * piece * piece
+        master = master_ref[...]
+        new_master = master - learn_rate * (
+            new_first / corr_one / (jnp.sqrt(new_second / corr_two) + adam_eps)
+            + weight_decay * master
+        )
+        new_first_ref[...] = new_first
+        new_second_ref[...] = new_second
+        new_master_ref[...] = new_master
+        held[z, step] = new_master.reshape(lines, lead).astype(low_type)
+
+        @pl.when(z < 3)
+        def _():
+            copy_to(z, step, 0, z + 1).start()
+
+        @pl.when(z > 0)
+        def _():
+            copy_to(z, step, 1, z - 1).start()
+
+    def pass_on(origin, chunk, right):
+        copy_to(origin, chunk, 0, z).wait_recv()
+        if right:
+
+            @pl.when(z < 3)
+            def _():
+                copy_to(origin, chunk, 0, z + 1).start()
+        else:
+
+            @pl.when(z > 0)
+            def _():
+                copy_to(origin, chunk, 1, z - 1).start()
+
+    @pl.when((step >= chunks) & (step < 2 * chunks))
+    def _():
+        chunk = step - chunks
+
+        @pl.when(z > 0)
+        def _():
+            pass_on(z - 1, chunk, True)
+
+        @pl.when(z < 3)
+        def _():
+            pass_on(z + 1, chunk, False)
+
+    @pl.when(step >= 2 * chunks)
+    def _():
+        chunk = step - 2 * chunks
+
+        @pl.when(z >= 2)
+        def _():
+            pass_on(z - 2, chunk, True)
+
+        @pl.when(z <= 1)
+        def _():
+            pass_on(z + 2, chunk, False)
+
+        @pl.when(z == 3)
+        def _():
+            copy_to(0, chunk, 0, z).wait_recv()
+
+        @pl.when(z == 0)
+        def _():
+            copy_to(3, chunk, 0, z).wait_recv()
+
+        for origin in range(4):
+            spread[origin * lines : (origin + 1) * lines, :] = held[origin, chunk].astype(wide)
+
+        def line(number, carry):
+            weights_ref[:, pl.ds(pl.multiple_of(number * lead, lead), lead)] = spread[
+                pl.ds(number, 4, stride=lines), :
+            ].astype(low_type)
+            return carry
+
+        lax.fori_loop(0, lines, line, 0, unroll=8)
+
+    @pl.when(step == 3 * chunks - 1)
+    def _():
+        for origin in range(4):
+
+            def finish(chunk, carry):
+                @pl.when((origin <= z) & (z < 3))
+                def _():
+                    copy_to(origin, chunk, 0, z).wait_send()
+
+                @pl.when((origin >= z) & (z > 0))
+                def _():
+                    copy_to(origin, chunk, 1, z).wait_send()
+
+                return carry
+
+            lax.fori_loop(0, chunks, finish, 0)
+
+
+def tail(mix, ffn, gains, master, first, second, sizes):
+    model, width, ffn_width = sizes
+    piece_length = master.shape[1]
+    chunks = 8
+    lines = -(-piece_length // (chunks * 128 * 16)) * 16
+    block = lines * 128
+    margin = 1536
+    rows = -(-(2 * margin + chunks * lines + 8) // 256) * 256
+    packed = jax.ShapeDtypeStruct(master.shape, wide)
+    whole = lambda shape: pl.BlockSpec(shape, lambda s: (0,) * len(shape))
+    chunk_spec = pl.BlockSpec((1, block), lambda s: (0, jnp.minimum(s, chunks - 1)))
+    once = lambda shape: pl.BlockSpec(
+        shape, lambda s: (0,) * len(shape), pipeline_mode=pl.Buffered(1)
+    )
+    return pl.pallas_call(
+        functools.partial(
+            tail_kernel, (model, width, ffn_width, piece_length, chunks, lines, margin)
+        ),
+        grid=(3 * chunks,),
+        in_specs=[once(mix.shape), once(ffn.shape), once(gains.shape)] + [chunk_spec] * 3,
+        out_specs=[chunk_spec] * 4
+        + [
+            pl.BlockSpec((4, block), lambda s: (0, jnp.maximum(s - 2 * chunks, 0))),
+            whole((2, 4 * width)),
+        ],
+        out_shape=[packed] * 4
+        + [
+            jax.ShapeDtypeStruct((4, piece_length), low_type),
+            jax.ShapeDtypeStruct((2, 4 * width), wide),
+        ],
+        scratch_shapes=[
+            pltpu.VMEM((rows, 128), wide),
+            pltpu.VMEM((4, chunks, lines, 128), low_type),
+            pltpu.VMEM((4 * lines, 128), wide),
+            pltpu.SemaphoreType.DMA((2, 4, chunks)),
+            pltpu.SemaphoreType.DMA((4, chunks)),
+        ],
+        compiler_params=pltpu.CompilerParams(
+            collective_id=1, has_side_effects=True, vmem_limit_bytes=58 * 1024 * 1024
+        ),
+        cost_estimate=pl.CostEstimate(
+            flops=20 * piece_length,
+            bytes_accessed=40 * piece_length,
+            transcendentals=piece_length,
+        ),
+        name="tail",
+    )(mix, ffn, gains, master, first, second)
 
 
 def group_body(
@@ -638,7 +924,7 @@
         ]
     )
 
-    gains = lax.all_gather(norm_gains, "shard", axis=1, tiled=True).astype(wide)
+    gains = all_slices(norm_gains, z).astype(wide)
 
     start_row = jnp.zeros((16, model), low_type).at[0, :slots].set(seq_start.astype(low_type))
     gathered = plane_gather(jnp.concatenate([tokens, start_row]))
@@ -690,39 +976,19 @@
 
     four_ffn = share(sum_ffn, 1)
     four_mix = share(sum_mix, 0)
-    sizes = (model, width, ffn_width, slice_rec, slice_ffn)
-    piece, bias_total = lax.switch(
-        member,
-        [
-            functools.partial(build_piece, number, piece_length, sizes)
-            for number in range(8)
-        ],
+    gain_sum = jnp.stack([grad_gain_one, grad_gain_two])
+    gain_sum = gain_sum + move(gain_sum, core_pairs)
+    gain_sum = gain_sum + move(gain_sum, plane_pairs(1))
+    gain_sum = gain_sum + move(gain_sum, plane_pairs(2))
+    gain_slice = shard_slices(gain_sum, z)
+    piece, new_master, new_first, new_second, new_weights, bias_total = tail(
         four_mix,
         four_ffn,
-    )
-    gain_total = lax.psum(jnp.stack([grad_gain_one, grad_gain_two]), axes)
-    gain_slice = lax.dynamic_slice_in_dim(gain_total, z * (model // 4), model // 4, axis=1)
-    gain_flat = gain_slice.reshape(-1)
-    tail = jnp.where(member == 7, gain_flat, piece[-gain_flat.shape[0] :])
-    piece = jnp.concatenate([piece[: -gain_flat.shape[0]], tail]).reshape(1, -1)
-
-    new_first = beta_one * first_moment + (1.0 - beta_one) * piece
-    new_second = beta_two * second_moment + (1.0 - beta_two) * piece * piece
-    new_master = master_shard - learn_rate * (
-        new_first / corr_one / (jnp.sqrt(new_second / corr_two) + adam_eps)
-        + weight_decay * master_shard
-    )
-    own = new_master.astype(low_type).reshape(-1)
-    right = [own]
-    left = [own]
-    for _ in range(3):
-        right.append(move(right[-1], step_pairs(1)))
-        left.append(move(left[-1], step_pairs(-1)))
-    new_weights = jnp.stack(
-        [
-            pick(z, [right[at - target] if at >= target else left[target - at] for at in range(4)])
-            for target in range(4)
-        ]
+        jnp.concatenate([gain_slice.reshape(-1, 128), jnp.zeros((2, 128), wide)]),
+        master_shard,
+        first_moment,
+        second_moment,
+        (model, width, ffn_width),
     )
     return (
         block_out,

time: 1180 us -> 926 us (0.78)
  the two profiles are of different devices: /device:TPU:2 before, /device:TPU:0 now
where the time goes in v2:
time: 926 us; the launch traced here: 919 us
  Pallas kernels  281 us (30%)
  waiting for transfers between devices  269 us (29%)
  starting transfers between devices  198 us (21%)
  other arithmetic  98.3 us (11%)
  local copies, waits for them, and re-layouts  70.8 us (8%)
    ppermute x73, waiting for transfers between devices, move(): return lax.ppermute(value, axes, pairs)  269 us
    ppermute x73, starting transfers between devices, move(): return lax.ppermute(value, axes, pairs)  198 us
    pallas_call x1, Pallas kernels, tail(): pl.pallas_call(functools.partial(tail_kernel, (model, width, ffn_width, p...  148 us
    pallas_call x1, Pallas kernels, ffn_both(): pl.pallas_call(ffn_kernel, grid=(hidden // tile, rows // slots), in_specs...  59.1 us
    pallas_call x1, Pallas kernels, mix_backward(): pl.pallas_call(functools.partial(mixer_backward_kernel, width), grid=(hea...  41.2 us
    unnamed x120, local copies, waits for them, and re-layouts  34.6 us
    pallas_call x1, Pallas kernels, mix_forward(): pl.pallas_call(functools.partial(mixer_forward_kernel, width), grid=(head...  32.5 us
  transfers between devices with their start and end apart: 73, of which 39 were waited for; matrix products, arithmetic and copies ran while one was open for 11% of the time, Pallas kernels for 8%

profile of v2, /device:TPU:0, one launch (start us, length us, event | category | flops | bytes accessed | tf_op | source)
XLA Modules:
  0.0 919.5 jit_solution(3040362127431838873)
XLA Ops:
  47.0 20.6 %collective-permute-done.24 = bf16[3,288,1536]{2,1,0:T(8,128)(2,1)} collective-permute-done((bf16[3,288,1536]{2,1,0:T(8,128)(2,1)}, bf16[3,288,1536]{2,1,0:T(8,128)(2,1)}, u32[]{:S(2)}, u32[]{:S(2)}) %collective-permute-start.24) | collective-permute-done | bytes 2654240 | tf_op jit(solution)/shard_map/ppermute | solution.py:69
  76.0 26.4 %collective-permute-start.11 = (bf16[2,384,1664]{2,1,0:T(8,128)(2,1)}, bf16[2,384,1664]{2,1,0:T(8,128)(2,1)}, u32[]{:S(2)}, u32[]{:S(2)}) collective-permute-start(bf16[2,384,1664]{2,1,0:T(8,128)(2,1)} %pad_maximum_fusion.7), channel_id=1, source_target_pairs={{0,4},{1,5},{2,6},{3,7},{4,0},{5,1},{6,2},{7,3},{8,12},{9,13},{10,... | collective-permute-start | bytes 7667720 | tf_op jit(solution)/shard_map/ppermute | solution.py:69
  108.6 20.4 %collective-permute-start.5 = (bf16[2,384]{1,0:T(2,128)(2,1)S(1)}, bf16[2,384]{1,0:T(2,128)(2,1)S(1)}, u32[]{:S(2)}, u32[]{:S(2)}) collective-permute-start(bf16[2,384]{1,0:T(2,128)(2,1)S(1)} %copy-done.43), channel_id=1, source_target_pairs={{0,2},{1,3},{2,0},{3,1},{4,6},{5,7},{6,4},{7,5},{8,10},{9,11},{10,... | collective-permute-start | bytes 4616 | tf_op jit(solution)/shard_map/ppermute | solution.py:69
  154.4 7.1 fusion.2.x_ref
  166.0 32.5 %mixer_forward.1 = (bf16[1024,1536]{1,0:T(8,128)(2,1)}, f32[4,1024,256]{2,1,0:T(8,128)}, f32[4,1024,128]{2,1,0:T(8,128)S(1)}, bf16[4,1024,128]{2,1,0:T(8,128)(2,1)S(1)}) custom-call(bf16[1024,1536]{1,0:T(8,128)(2,1)} %fusion.2.x_ref, s32[1024,1]{1,0:T(8,128)S(1)} %bitcast.40, bf16[4,384,1664]{2,1,0:T(8,128)(2,1)} %pad_maximum_fusion.3.w_ref), custom_call_target="tpu_custom_call" | custom-call | flops 4831838208 | bytes 18743296 | tf_op jit(solution)/shard_map/mixer_forward/pallas_call | solution.py:281
  208.3 9.4 %collective-permute-done.12 = bf16[256,1536]{1,0:T(8,128)(2,1)S(1)} collective-permute-done((bf16[256,1536]{1,0:T(8,128)(2,1)}, bf16[256,1536]{1,0:T(8,128)(2,1)S(1)}, u32[]{:S(2)}, u32[]{:S(2)}) %collective-permute-start.12) | collective-permute-done | bytes 786464 | tf_op jit(solution)/shard_map/ppermute | solution.py:69
  221.2 9.7 %collective-permute-done.13 = bf16[128,1536]{1,0:T(8,128)(2,1)S(1)} collective-permute-done((bf16[128,1536]{1,0:T(8,128)(2,1)S(1)}, bf16[128,1536]{1,0:T(8,128)(2,1)S(1)}, u32[]{:S(2)}, u32[]{:S(2)}) %collective-permute-start.13) | collective-permute-done | bytes 393248 | tf_op jit(solution)/shard_map/ppermute | solution.py:69
  232.5 7.1 collective-permute-done.20
  257.6 12.6 %collective-permute-done.16 = bf16[256,1536]{1,0:T(8,128)(2,1)S(1)} collective-permute-done((bf16[256,1536]{1,0:T(8,128)(2,1)S(1)}, bf16[256,1536]{1,0:T(8,128)(2,1)S(1)}, u32[]{:S(2)}, u32[]{:S(2)}) %collective-permute-start.16) | collective-permute-done | bytes 786464 | tf_op jit(solution)/shard_map/ppermute | solution.py:69
  271.7 6.4 collective-permute-done.18
  279.9 10.9 %pad_maximum_fusion.w_ref = bf16[3,1152,1536]{2,1,0:T(8,128)(2,1)} fusion(bf16[3,576,1536]{2,1,0:T(8,128)(2,1)S(1)} %collective-permute-done.28, bf16[3,288,1536]{2,1,0:T(8,128)(2,1)S(1)} %get-tuple-element.66, bf16[3,288,1536]{2,1,0:T(8,128)(2,1)S(1)} %get-tuple-element.65), kind=kLoop, calls=%fused_computation | loop fusion | flops 31850496 | bytes 21233664 | tf_op jit(solution)/shard_map/concatenate | solution.py:942
  290.8 59.1 %ffn_both.1 = (bf16[3,1152,1536]{2,1,0:T(8,128)(2,1)}, bf16[1024,1536]{1,0:T(8,128)(2,1)}, bf16[1024,1536]{1,0:T(8,128)(2,1)}) custom-call(bf16[1024,1536]{1,0:T(8,128)(2,1)} %copy-done.42, bf16[1024,1536]{1,0:T(8,128)(2,1)} %copy-done.41, bf16[3,1152,1536]{2,1,0:T(8,128)(2,1)} %pad_maximum_fusion.w_ref), custom_call_target="tpu_custom_call" | custom-call | flops 32614907904 | bytes 46399488 | tf_op jit(solution)/shard_map/ffn_both/pallas_call | solution.py:485
  358.6 15.4 %collective-permute-done.29 = bf16[256,1536]{1,0:T(8,128)(2,1)S(1)} collective-permute-done((bf16[256,1536]{1,0:T(8,128)(2,1)S(1)}, bf16[256,1536]{1,0:T(8,128)(2,1)S(1)}, u32[]{:S(2)}, u32[]{:S(2)}) %collective-permute-start.29) | collective-permute-done | bytes 786464 | tf_op jit(solution)/shard_map/ppermute | solution.py:69
  376.2 13.9 %collective-permute-done.33 = bf16[256,1536]{1,0:T(8,128)(2,1)S(1)} collective-permute-done((bf16[256,1536]{1,0:T(8,128)(2,1)S(1)}, bf16[256,1536]{1,0:T(8,128)(2,1)S(1)}, u32[]{:S(2)}, u32[]{:S(2)}) %collective-permute-start.33) | collective-permute-done | bytes 786464 | tf_op jit(solution)/shard_map/ppermute | solution.py:69
  392.2 9.9 %collective-permute-done.30 = bf16[128,1536]{1,0:T(8,128)(2,1)S(1)} collective-permute-done((bf16[128,1536]{1,0:T(8,128)(2,1)S(1)}, bf16[128,1536]{1,0:T(8,128)(2,1)S(1)}, u32[]{:S(2)}, u32[]{:S(2)}) %collective-permute-start.30) | collective-permute-done | bytes 393248 | tf_op jit(solution)/shard_map/ppermute | solution.py:69
  416.5 9.1 collective-permute-done.36
  441.7 8.0 collective-permute-done.37
  452.7 6.3 collective-permute-done.39
  461.9 41.2 %mixer_backward.1 = (bf16[4,384,1664]{2,1,0:T(8,128)(2,1)}, bf16[1024,1536]{1,0:T(8,128)(2,1)}) custom-call(bf16[1024,1536]{1,0:T(8,128)(2,1)} %fusion.2.x_ref, bf16[1024,1536]{1,0:T(8,128)(2,1)} %copy-done.40, s32[1024,1]{1,0:T(8,128)S(1)} %bitcast.41, bf16[4,384,1664]{2,1,0:T(8,128)(2,1)} %pad_maximum_fusion.3.w_ref, ...), custom_call_target="tpu_custom_call" | custom-call | flops 9663676416 | bytes 27000832 | tf_op jit(solution)/shard_map/mixer_backward/pallas_call | solution.py:401
  521.7 28.8 %collective-permute-done.59 = bf16[3,288,1536]{2,1,0:T(8,128)(2,1)S(1)} collective-permute-done((bf16[3,288,1536]{2,1,0:T(8,128)(2,1)}, bf16[3,288,1536]{2,1,0:T(8,128)(2,1)S(1)}, u32[]{:S(2)}, u32[]{:S(2)}) %collective-permute-start.59) | collective-permute-done | bytes 2654240 | tf_op jit(solution)/shard_map/ppermute | solution.py:69
  562.8 19.0 %collective-permute-start.49 = (bf16[384,1664]{1,0:T(8,128)(2,1)S(1)}, bf16[384,1664]{1,0:T(8,128)(2,1)S(1)}, u32[]{:S(2)}, u32[]{:S(2)}) collective-permute-start(bf16[384,1664]{1,0:T(8,128)(2,1)S(1)} %get-tuple-element.100), channel_id=1, source_target_pairs={{0,1},{3,2},{4,5},{7,6},{8,9},{11,10},{12,13},{15,14},{16,17},{19,... | collective-permute-start | bytes 3833864 | tf_op jit(solution)/shard_map/ppermute | solution.py:69
  582.9 7.0 collective-permute-done.62
  596.0 14.2 %collective-permute-done.49 = bf16[384,1664]{1,0:T(8,128)(2,1)S(1)} collective-permute-done((bf16[384,1664]{1,0:T(8,128)(2,1)S(1)}, bf16[384,1664]{1,0:T(8,128)(2,1)S(1)}, u32[]{:S(2)}, u32[]{:S(2)}) %collective-permute-start.49) | collective-permute-done | bytes 1277984 | tf_op jit(solution)/shard_map/ppermute | solution.py:69
  618.9 14.2 %collective-permute-start.66 = (bf16[4,3,288,1536]{3,2,1,0:T(8,128)(2,1)}, bf16[4,3,288,1536]{3,2,1,0:T(8,128)(2,1)}, u32[]{:S(2)}, u32[]{:S(2)}) collective-permute-start(bf16[4,3,288,1536]{3,2,1,0:T(8,128)(2,1)} %pad_maximum_fusion.1), channel_id=1, source_target_pairs={{0,4},{1,5},{6,2},{7,3},{8,12},{9,13},{14,10},{15,11},{16,20},{17,... | collective-permute-start | bytes 31850504 | tf_op jit(solution)/shard_map/ppermute | solution.py:69
  642.1 15.3 %collective-permute-done.51 = bf16[384,1664]{1,0:T(8,128)(2,1)S(1)} collective-permute-done((bf16[384,1664]{1,0:T(8,128)(2,1)S(1)}, bf16[384,1664]{1,0:T(8,128)(2,1)S(1)}, u32[]{:S(2)}, u32[]{:S(2)}) %collective-permute-start.51) | collective-permute-done | bytes 1277984 | tf_op jit(solution)/shard_map/ppermute | solution.py:69
  659.3 7.5 collective-permute-done.52
  688.1 9.8 %collective-permute-done.43 = bf16[256,1536]{1,0:T(8,128)(2,1)S(1)} collective-permute-done((bf16[256,1536]{1,0:T(8,128)(2,1)S(1)}, bf16[256,1536]{1,0:T(8,128)(2,1)S(1)}, u32[]{:S(2)}, u32[]{:S(2)}) %collective-permute-start.43) | collective-permute-done | bytes 786464 | tf_op jit(solution)/shard_map/ppermute | solution.py:69
  703.3 6.8 collective-permute-done.44
  720.1 11.8 %collective-permute-start.70 = (f32[2,384]{1,0:T(2,128)S(1)}, f32[2,384]{1,0:T(2,128)S(1)}, u32[]{:S(2)}, u32[]{:S(2)}) collective-permute-start(f32[2,384]{1,0:T(2,128)S(1)} %get-tuple-element.105), channel_id=1, source_target_pairs={{0,1},{1,2},{2,3},{3,0},{4,5},{5,6},{6,7},{7,4},{8,9},{9,10},{10,1... | collective-permute-start | bytes 9224 | tf_op jit(solution)/shard_map/ppermute | solution.py:69
  738.1 6.3 broadcast_select_fusion.1.mix_ref
  749.6 148.1 %tail.1 = (f32[1,975456]{1,0:T(1,128)}, f32[1,975456]{1,0:T(1,128)}, f32[1,975456]{1,0:T(1,128)}, f32[1,975456]{1,0:T(1,128)}, bf16[4,975456]{1,0:T(4,128)(2,1)}, /*index=5*/f32[2,512]{1,0:T(2,128)}) custom-call(bf16[4,384,1664]{2,1,0:T(8,128)(2,1)} %broadcast_select_fusion.1.mix_ref, bf16[4,3,288,1536]{3,2,1,0:T(8,128)(2,1)} %broadcast_select_fusion.ffn_ref, ...), custom_call_target="tpu_custom_call" | custom-call | flops 19509120 | bytes 39018240 | tf_op jit(solution)/shard_map/tail/pallas_call | solution.py:830
  897.6 7.0 copy.51
  (354 shorter events, 295.4 us)
Async XLA Ops:
  35.3 32.3 %collective-permute-start.24 = (bf16[3,288,1536]{2,1,0:T(8,128)(2,1)}, bf16[3,288,1536]{2,1,0:T(8,128)(2,1)}, u32[]{:S(2)}, u32[]{:S(2)}) collective-permute-start(bf16[3,288,1536]{2,1,0:T(8,128)(2,1)} %pad_maximum_fusion.6), channel_id=1, source_target_pairs={{0,1},{1,2},{6,5},{7,6},{8,9},{9,10},{14,13},{15,14},{16,17},{17,1... | collective-permute-start | bytes 7962632 | tf_op jit(solution)/shard_map/ppermute | solution.py:69
  40.1 29.6 %collective-permute-start.10 = (bf16[384,1664]{1,0:T(8,128)(2,1)}, bf16[384,1664]{1,0:T(8,128)(2,1)}, u32[]{:S(2)}, u32[]{:S(2)}) collective-permute-start(bf16[384,1664]{1,0:T(8,128)(2,1)} %pad_maximum_fusion.10), channel_id=1, source_target_pairs={{1,0},{6,7},{9,8},{14,15},{17,16},{22,23},{25,24},{30,31}} | collective-permute-start | bytes 3833864 | tf_op jit(solution)/shard_map/ppermute | solution.py:69
  41.4 28.3 %collective-permute-start.9 = (bf16[384,1664]{1,0:T(8,128)(2,1)S(1)}, bf16[384,1664]{1,0:T(8,128)(2,1)}, u32[]{:S(2)}, u32[]{:S(2)}) collective-permute-start(bf16[384,1664]{1,0:T(8,128)(2,1)S(1)} %collective-permute-done.8), channel_id=1, source_target_pairs={{2,3},{5,4},{10,11},{13,12},{18,19},{21,20},{26,27},{29,28}} | collective-permute-start | bytes 3833864 | tf_op jit(solution)/shard_map/ppermute | solution.py:69
  44.2 94.0 %collective-permute-start.1 = (bf16[272,1536]{1,0:T(8,128)(2,1)}, bf16[272,1536]{1,0:T(8,128)(2,1)}, u32[]{:S(2)}, u32[]{:S(2)}) collective-permute-start(bf16[272,1536]{1,0:T(8,128)(2,1)} %fusion.23), channel_id=1, source_target_pairs={{0,16},{1,17},{2,18},{3,19},{4,20},{5,21},{6,22},{7,23},{8,24},{9,... | collective-permute-start | bytes 2506760 | tf_op jit(solution)/shard_map/ppermute | solution.py:69
  45.7 95.8 %collective-permute-start = (bf16[272,1536]{1,0:T(8,128)(2,1)}, bf16[272,1536]{1,0:T(8,128)(2,1)}, u32[]{:S(2)}, u32[]{:S(2)}) collective-permute-start(bf16[272,1536]{1,0:T(8,128)(2,1)} %fusion.23), channel_id=1, source_target_pairs={{0,8},{1,9},{2,10},{3,11},{4,12},{5,13},{6,14},{7,15},{8,0},{9,1},... | collective-permute-start | bytes 2506760 | tf_op jit(solution)/shard_map/ppermute | solution.py:69
  67.6 83.9 %collective-permute-start.25 = (bf16[3,288,1536]{2,1,0:T(8,128)(2,1)}, bf16[3,288,1536]{2,1,0:T(8,128)(2,1)}, u32[]{:S(2)}, u32[]{:S(2)}) collective-permute-start(bf16[3,288,1536]{2,1,0:T(8,128)(2,1)} %collective-permute-done.24), channel_id=1, source_target_pairs={{1,2},{2,3},{5,4},{6,5},{9,10},{10,11},{13,12},{14,13},{17,18},{18... | collective-permute-start | bytes 7962632 | tf_op jit(solution)/shard_map/ppermute | solution.py:69
  76.0 85.4 %collective-permute-start.11 = (bf16[2,384,1664]{2,1,0:T(8,128)(2,1)}, bf16[2,384,1664]{2,1,0:T(8,128)(2,1)}, u32[]{:S(2)}, u32[]{:S(2)}) collective-permute-start(bf16[2,384,1664]{2,1,0:T(8,128)(2,1)} %pad_maximum_fusion.7), channel_id=1, source_target_pairs={{0,4},{1,5},{2,6},{3,7},{4,0},{5,1},{6,2},{7,3},{8,12},{9,13},{10,... | collective-permute-start | bytes 7667720 | tf_op jit(solution)/shard_map/ppermute | solution.py:69
  136.8 66.5 %collective-permute-start.27 = (bf16[3,288,1536]{2,1,0:T(8,128)(2,1)}, bf16[3,288,1536]{2,1,0:T(8,128)(2,1)}, u32[]{:S(2)}, u32[]{:S(2)}) collective-permute-start(bf16[3,288,1536]{2,1,0:T(8,128)(2,1)} %pad_maximum_fusion.6), channel_id=1, source_target_pairs={{1,0},{6,7},{9,8},{14,15},{17,16},{22,23},{25,24},{30,31}} | collective-permute-start | bytes 7962632 | tf_op jit(solution)/shard_map/ppermute | solution.py:69
  151.5 51.8 %collective-permute-start.26 = (bf16[3,288,1536]{2,1,0:T(8,128)(2,1)}, bf16[3,288,1536]{2,1,0:T(8,128)(2,1)}, u32[]{:S(2)}, u32[]{:S(2)}) collective-permute-start(bf16[3,288,1536]{2,1,0:T(8,128)(2,1)} %collective-permute-done.25), channel_id=1, source_target_pairs={{2,3},{5,4},{10,11},{13,12},{18,19},{21,20},{26,27},{29,28}} | collective-permute-start | bytes 7962632 | tf_op jit(solution)/shard_map/ppermute | solution.py:69
  208.2 70.0 %collective-permute-start.28 = (bf16[3,576,1536]{2,1,0:T(8,128)(2,1)S(1)}, bf16[3,576,1536]{2,1,0:T(8,128)(2,1)S(1)}, u32[]{:S(2)}, u32[]{:S(2)}) collective-permute-start(bf16[3,576,1536]{2,1,0:T(8,128)(2,1)S(1)} %pad_maximum_fusion.2), channel_id=1, source_target_pairs={{0,4},{1,5},{2,6},{3,7},{4,0},{5,1},{6,2},{7,3},{8,12},{9,13},{10,... | collective-permute-start | bytes 15925256 | tf_op jit(solution)/shard_map/ppermute | solution.py:69
  219.2 26.7 %collective-permute-start.21 = (bf16[256,1536]{1,0:T(8,128)(2,1)S(1)}, bf16[256,1536]{1,0:T(8,128)(2,1)S(1)}, u32[]{:S(2)}, u32[]{:S(2)}) collective-permute-start(bf16[256,1536]{1,0:T(8,128)(2,1)S(1)} %get-tuple-element.60), channel_id=1, source_target_pairs={{0,16},{1,17},{2,18},{3,19},{4,20},{5,21},{6,22},{7,23},{8,24},{9,... | collective-permute-start | bytes 2359304 | tf_op jit(solution)/shard_map/ppermute | solution.py:69
  353.0 51.1 %collective-permute-start.56 = (bf16[3,576,1536]{2,1,0:T(8,128)(2,1)S(1)}, bf16[3,576,1536]{2,1,0:T(8,128)(2,1)}, u32[]{:S(2)}, u32[]{:S(2)}) collective-permute-start(bf16[3,576,1536]{2,1,0:T(8,128)(2,1)S(1)} %slice.368), channel_id=1, source_target_pairs={{0,4},{1,5},{2,6},{3,7},{4,0},{5,1},{6,2},{7,3},{8,12},{9,13},{10,... | collective-permute-start | bytes 15925256 | tf_op jit(solution)/shard_map/ppermute | solution.py:69
  355.1 35.0 %collective-permute-start.33 = (bf16[256,1536]{1,0:T(8,128)(2,1)S(1)}, bf16[256,1536]{1,0:T(8,128)(2,1)S(1)}, u32[]{:S(2)}, u32[]{:S(2)}) collective-permute-start(bf16[256,1536]{1,0:T(8,128)(2,1)S(1)} %pad_maximum_fusion.15), channel_id=1, source_target_pairs={{0,8},{1,9},{2,10},{3,11},{4,12},{5,13},{6,14},{7,15},{8,0},{9,1},... | collective-permute-start | bytes 2359304 | tf_op jit(solution)/shard_map/ppermute | solution.py:69
  356.4 35.9 %collective-permute-start.31 = (bf16[256,1536]{1,0:T(8,128)(2,1)S(1)}, bf16[256,1536]{1,0:T(8,128)(2,1)S(1)}, u32[]{:S(2)}, u32[]{:S(2)}) collective-permute-start(bf16[256,1536]{1,0:T(8,128)(2,1)S(1)} %pad_maximum_fusion.14), channel_id=1, source_target_pairs={{0,16},{1,17},{2,18},{3,19},{4,20},{5,21},{6,22},{7,23},{8,24},{9,... | collective-permute-start | bytes 2359304 | tf_op jit(solution)/shard_map/ppermute | solution.py:69
  358.1 54.5 %collective-permute-start.35 = (bf16[256,1536]{1,0:T(8,128)(2,1)S(1)}, bf16[256,1536]{1,0:T(8,128)(2,1)}, u32[]{:S(2)}, u32[]{:S(2)}) collective-permute-start(bf16[256,1536]{1,0:T(8,128)(2,1)S(1)} %pad_maximum_fusion.16), channel_id=1, source_target_pairs={{0,16},{1,17},{2,18},{3,19},{4,20},{5,21},{6,22},{7,23},{8,24},{9,... | collective-permute-start | bytes 2359304 | tf_op jit(solution)/shard_map/ppermute | solution.py:69
  374.1 28.1 %collective-permute-start.30 = (bf16[128,1536]{1,0:T(8,128)(2,1)S(1)}, bf16[128,1536]{1,0:T(8,128)(2,1)S(1)}, u32[]{:S(2)}, u32[]{:S(2)}) collective-permute-start(bf16[128,1536]{1,0:T(8,128)(2,1)S(1)} %add_convert_fusion.11), channel_id=1, source_target_pairs={{0,16},{1,17},{2,18},{3,19},{4,20},{5,21},{6,22},{7,23},{8,24},{9,... | collective-permute-start | bytes 1179656 | tf_op jit(solution)/shard_map/ppermute | solution.py:69
  390.2 22.4 %collective-permute-start.34 = (bf16[128,1536]{1,0:T(8,128)(2,1)S(1)}, bf16[128,1536]{1,0:T(8,128)(2,1)S(1)}, u32[]{:S(2)}, u32[]{:S(2)}) collective-permute-start(bf16[128,1536]{1,0:T(8,128)(2,1)S(1)} %add_convert_fusion.9), channel_id=1, source_target_pairs={{0,16},{1,17},{2,18},{3,19},{4,20},{5,21},{6,22},{7,23},{8,24},{9,... | collective-permute-start | bytes 1179656 | tf_op jit(solution)/shard_map/ppermute | solution.py:69
  411.6 25.5 %collective-permute-start.57 = (bf16[3,288,1536]{2,1,0:T(8,128)(2,1)S(1)}, bf16[3,288,1536]{2,1,0:T(8,128)(2,1)S(1)}, u32[]{:S(2)}, u32[]{:S(2)}) collective-permute-start(bf16[3,288,1536]{2,1,0:T(8,128)(2,1)S(1)} %get-tuple-element.69), channel_id=1, source_target_pairs={{3,2},{4,5},{11,10},{12,13},{19,18},{20,21},{27,26},{28,29}} | collective-permute-start | bytes 7962632 | tf_op jit(solution)/shard_map/ppermute | solution.py:69
  432.4 78.0 %collective-permute-start.60 = (bf16[3,288,1536]{2,1,0:T(8,128)(2,1)}, bf16[3,288,1536]{2,1,0:T(8,128)(2,1)}, u32[]{:S(2)}, u32[]{:S(2)}) collective-permute-start(bf16[3,288,1536]{2,1,0:T(8,128)(2,1)} %get-tuple-element.70), channel_id=1, source_target_pairs={{0,1},{3,2},{4,5},{7,6},{8,9},{11,10},{12,13},{15,14},{16,17},{19,... | collective-permute-start | bytes 7962632 | tf_op jit(solution)/shard_map/ppermute | solution.py:69
  439.3 71.1 %collective-permute-start.58 = (bf16[3,288,1536]{2,1,0:T(8,128)(2,1)}, bf16[3,288,1536]{2,1,0:T(8,128)(2,1)}, u32[]{:S(2)}, u32[]{:S(2)}) collective-permute-start(bf16[3,288,1536]{2,1,0:T(8,128)(2,1)} %fusion.3), channel_id=1, source_target_pairs={{2,1},{5,6},{10,9},{13,14},{18,17},{21,22},{26,25},{29,30}} | collective-permute-start | bytes 7962632 | tf_op jit(solution)/shard_map/ppermute | solution.py:69
  515.9 34.7 %collective-permute-start.59 = (bf16[3,288,1536]{2,1,0:T(8,128)(2,1)}, bf16[3,288,1536]{2,1,0:T(8,128)(2,1)S(1)}, u32[]{:S(2)}, u32[]{:S(2)}) collective-permute-start(bf16[3,288,1536]{2,1,0:T(8,128)(2,1)} %get-tuple-element.67), channel_id=1, source_target_pairs={{1,0},{6,7},{9,8},{14,15},{17,16},{22,23},{25,24},{30,31}} | collective-permute-start | bytes 7962632 | tf_op jit(solution)/shard_map/ppermute | solution.py:69
  517.2 34.9 %collective-permute-start.61 = (bf16[3,288,1536]{2,1,0:T(8,128)(2,1)S(1)}, bf16[3,288,1536]{2,1,0:T(8,128)(2,1)}, u32[]{:S(2)}, u32[]{:S(2)}) collective-permute-start(bf16[3,288,1536]{2,1,0:T(8,128)(2,1)S(1)} %get-tuple-element.68), channel_id=1, source_target_pairs={{2,1},{5,6},{10,9},{13,14},{18,17},{21,22},{26,25},{29,30}} | collective-permute-start | bytes 7962632 | tf_op jit(solution)/shard_map/ppermute | solution.py:69
  556.0 33.9 %collective-permute-start.62 = (bf16[3,288,1536]{2,1,0:T(8,128)(2,1)S(1)}, bf16[3,288,1536]{2,1,0:T(8,128)(2,1)S(1)}, u32[]{:S(2)}, u32[]{:S(2)}) collective-permute-start(bf16[3,288,1536]{2,1,0:T(8,128)(2,1)S(1)} %fusion.7), channel_id=1, source_target_pairs={{0,8},{1,9},{6,14},{7,15},{8,0},{9,1},{14,6},{15,7},{16,24},{17,25... | collective-permute-start | bytes 7962632 | tf_op jit(solution)/shard_map/ppermute | solution.py:69
  559.7 33.9 %collective-permute-start.63 = (bf16[3,288,1536]{2,1,0:T(8,128)(2,1)S(1)}, bf16[3,288,1536]{2,1,0:T(8,128)(2,1)S(1)}, u32[]{:S(2)}, u32[]{:S(2)}) collective-permute-start(bf16[3,288,1536]{2,1,0:T(8,128)(2,1)S(1)} %fusion.7), channel_id=1, source_target_pairs={{0,16},{1,17},{6,22},{7,23},{8,24},{9,25},{14,30},{15,31},{16,0},{... | collective-permute-start | bytes 7962632 | tf_op jit(solution)/shard_map/ppermute | solution.py:69
  562.8 47.4 %collective-permute-start.49 = (bf16[384,1664]{1,0:T(8,128)(2,1)S(1)}, bf16[384,1664]{1,0:T(8,128)(2,1)S(1)}, u32[]{:S(2)}, u32[]{:S(2)}) collective-permute-start(bf16[384,1664]{1,0:T(8,128)(2,1)S(1)} %get-tuple-element.100), channel_id=1, source_target_pairs={{0,1},{3,2},{4,5},{7,6},{8,9},{11,10},{12,13},{15,14},{16,17},{19,... | collective-permute-start | bytes 3833864 | tf_op jit(solution)/shard_map/ppermute | solution.py:69
  582.2 28.1 %collective-permute-start.47 = (bf16[384,1664]{1,0:T(8,128)(2,1)S(1)}, bf16[384,1664]{1,0:T(8,128)(2,1)S(1)}, u32[]{:S(2)}, u32[]{:S(2)}) collective-permute-start(bf16[384,1664]{1,0:T(8,128)(2,1)S(1)} %fusion.8), channel_id=1, source_target_pairs={{2,1},{5,6},{10,9},{13,14},{18,17},{21,22},{26,25},{29,30}} | collective-permute-start | bytes 3833864 | tf_op jit(solution)/shard_map/ppermute | solution.py:69
  590.0 22.9 %collective-permute-start.64 = (bf16[3,144,1536]{2,1,0:T(8,128)(2,1)S(1)}, bf16[3,144,1536]{2,1,0:T(8,128)(2,1)S(1)}, u32[]{:S(2)}, u32[]{:S(2)}) collective-permute-start(bf16[3,144,1536]{2,1,0:T(8,128)(2,1)S(1)} %slice.410), channel_id=1, source_target_pairs={{0,16},{1,17},{6,22},{7,23},{8,24},{9,25},{14,30},{15,31},{16,0},{... | collective-permute-start | bytes 3981320 | tf_op jit(solution)/shard_map/ppermute | solution.py:69
  610.9 25.2 %collective-permute-start.48 = (bf16[384,1664]{1,0:T(8,128)(2,1)S(1)}, bf16[384,1664]{1,0:T(8,128)(2,1)S(1)}, u32[]{:S(2)}, u32[]{:S(2)}) collective-permute-start(bf16[384,1664]{1,0:T(8,128)(2,1)S(1)} %get-tuple-element.97), channel_id=1, source_target_pairs={{1,0},{6,7},{9,8},{14,15},{17,16},{22,23},{25,24},{30,31}} | collective-permute-start | bytes 3833864 | tf_op jit(solution)/shard_map/ppermute | solution.py:69
  612.2 23.9 %collective-permute-start.50 = (bf16[384,1664]{1,0:T(8,128)(2,1)S(1)}, bf16[384,1664]{1,0:T(8,128)(2,1)S(1)}, u32[]{:S(2)}, u32[]{:S(2)}) collective-permute-start(bf16[384,1664]{1,0:T(8,128)(2,1)S(1)} %get-tuple-element.98), channel_id=1, source_target_pairs={{2,1},{5,6},{10,9},{13,14},{18,17},{21,22},{26,25},{29,30}} | collective-permute-start | bytes 3833864 | tf_op jit(solution)/shard_map/ppermute | solution.py:69
  618.9 125.5 %collective-permute-start.66 = (bf16[4,3,288,1536]{3,2,1,0:T(8,128)(2,1)}, bf16[4,3,288,1536]{3,2,1,0:T(8,128)(2,1)}, u32[]{:S(2)}, u32[]{:S(2)}) collective-permute-start(bf16[4,3,288,1536]{3,2,1,0:T(8,128)(2,1)} %pad_maximum_fusion.1), channel_id=1, source_target_pairs={{0,4},{1,5},{6,2},{7,3},{8,12},{9,13},{14,10},{15,11},{16,20},{17,... | collective-permute-start | bytes 31850504 | tf_op jit(solution)/shard_map/ppermute | solution.py:69
  640.1 26.7 %collective-permute-start.52 = (bf16[384,1664]{1,0:T(8,128)(2,1)S(1)}, bf16[384,1664]{1,0:T(8,128)(2,1)S(1)}, u32[]{:S(2)}, u32[]{:S(2)}) collective-permute-start(bf16[384,1664]{1,0:T(8,128)(2,1)S(1)} %fusion.22), channel_id=1, source_target_pairs={{0,16},{1,17},{6,22},{7,23},{8,24},{9,25},{14,30},{15,31},{16,0},{... | collective-permute-start | bytes 3833864 | tf_op jit(solution)/shard_map/ppermute | solution.py:69
  682.2 55.9 %collective-permute-start.55 = (bf16[4,384,1664]{2,1,0:T(8,128)(2,1)}, bf16[4,384,1664]{2,1,0:T(8,128)(2,1)}, u32[]{:S(2)}, u32[]{:S(2)}) collective-permute-start(bf16[4,384,1664]{2,1,0:T(8,128)(2,1)} %pad_maximum_fusion.4), channel_id=1, source_target_pairs={{0,4},{1,5},{6,2},{7,3},{8,12},{9,13},{14,10},{15,11},{16,20},{17,... | collective-permute-start | bytes 15335432 | tf_op jit(solution)/shard_map/ppermute | solution.py:69
  (92 other events, 1197.7 us)

commit v3 on v2

--- a/solution.py
+++ b/solution.py
@@ -515,6 +515,580 @@
     )(x, grad_out, weights)
 
 
+def peer_x(chip):
+    return chip + 1 - 2 * (chip % 2)
+
+
+def peer_y(chip):
+    return chip + 2 - 4 * (chip // 2)
+
+
+def line_place(end, core):
+    return end + core * (3 - 2 * end)
+
+
+def remote(source, target, send, recv, member, z):
+    return pltpu.make_async_remote_copy(
+        src_ref=source,
+        dst_ref=target,
+        send_sem=send,
+        recv_sem=recv,
+        device_id=(member, z),
+        device_id_type=pl.DeviceIdType.MESH,
+    )
+
+
+def enter(member, z):
+    barrier = pltpu.get_barrier_semaphore()
+    for other in range(8):
+
+        @pl.when(member != other)
+        def _():
+            pl.semaphore_signal(
+                barrier, inc=1, device_id=(other, z), device_id_type=pl.DeviceIdType.MESH
+            )
+
+    for other in range(4):
+
+        @pl.when(z != other)
+        def _():
+            pl.semaphore_signal(
+                barrier, inc=1, device_id=(member, other), device_id_type=pl.DeviceIdType.MESH
+            )
+
+    pl.semaphore_wait(barrier, 10)
+
+
+class Scatter:
+    def __init__(self, sizes, member, z, send_sem, recv_sem):
+        self.model, self.width, self.ffn_width, self.piece_length = sizes
+        self.member, self.z = member, z
+        self.chip, self.core = member // 2, member % 2
+        self.owner = self.core == z // 2
+        self.send_sem, self.recv_sem = send_sem, recv_sem
+        self.across = self.model // 128
+        rec, ffn, model = 4 * self.width, 4 * self.ffn_width, self.model
+        self.gate_base = 2 * model * rec
+        self.out_base = self.gate_base + 8 * self.width * self.width
+        self.up_base = self.out_base + rec * model
+        self.down_base = self.up_base + 2 * model * ffn
+        self.rec, self.ffn = rec, ffn
+        self.first_in = 0
+        self.first_gate = 2 * self.across
+        self.first_out = self.first_gate + 2
+        self.first_small = self.first_out + 4
+        self.first_up = self.first_small + 1
+        self.first_down = self.first_up + 2 * self.across
+        self.count = self.first_down + 6
+
+    def in_unit(self, number, q):
+        kind, at = number // self.across, number % self.across
+        low = (kind * self.model + at * 128) * self.rec
+        where = (
+            pl.ds(pl.multiple_of(kind * self.width, self.width), self.width),
+            pl.ds(pl.multiple_of(at * 128, 128), 128),
+        )
+        return self.first_in + number, where, low, low + 128 * self.rec
+
+    def gate_unit(self, kind, q):
+        low = self.gate_base + (kind * 4 + q) * self.width * self.width
+        where = (
+            pl.ds(pl.multiple_of(kind * self.width, self.width), self.width),
+            pl.ds(self.model, self.width),
+        )
+        return self.first_gate + kind, where, low, low + self.width * self.width
+
+    def out_unit(self, number, q):
+        rows = self.width // 4
+        low = self.out_base + (q * self.width + number * rows) * self.model
+        where = (
+            pl.ds(pl.multiple_of(2 * self.width + number * rows, rows), rows),
+            pl.ds(0, self.model),
+        )
+        return self.first_out + number, where, low, low + rows * self.model
+
+    def up_unit(self, number, q):
+        kind, at = number // self.across, number % self.across
+        low = self.up_base + (kind * self.model + at * 128) * self.ffn
+        where = (kind, pl.ds(0, self.ffn_width), pl.ds(pl.multiple_of(at * 128, 128), 128))
+        return self.first_up + number, where, low, low + 128 * self.ffn
+
+    def down_unit(self, number, q):
+        rows = self.ffn_width // 6
+        low = self.down_base + (q * self.ffn_width + number * rows) * self.model
+        where = (2, pl.ds(pl.multiple_of(number * rows, 16), rows), pl.ds(0, self.model))
+        return self.first_down + number, where, low, low + rows * self.model
+
+    def small_where(self):
+        return (pl.ds(2 * self.width, 16), pl.ds(self.model, self.width))
+
+    def copies(self, unit, source, target, q, act):
+        number, where, low, high = unit
+        first = low // self.piece_length
+        last = (high - 1) // self.piece_length
+        for which, to in ((0, first), (1, last)):
+            wanted = True if which == 0 else last != first
+
+            @pl.when((to != self.member) & wanted)
+            def _():
+                act(
+                    remote(
+                        source.at[where],
+                        target.at[(q,) + where],
+                        self.send_sem.at[which, number],
+                        self.recv_sem.at[q, number],
+                        to,
+                        self.z,
+                    ),
+                    True,
+                )
+
+            @pl.when((to == self.member) & wanted)
+            def _():
+                act(
+                    pltpu.make_async_copy(
+                        source.at[where], target.at[(q,) + where], self.recv_sem.at[q, number]
+                    ),
+                    False,
+                )
+
+    def each(self, unit_of, low, high, source, target, act):
+        def body(number, carry):
+            self.copies(unit_of(number, self.chip), source, target, self.chip, act)
+            return carry
+
+        lax.fori_loop(low, high, body, 0)
+
+    def smalls(self, source, target, act):
+        where = self.small_where()
+        for to in range(8):
+
+            @pl.when(self.member != to)
+            def _():
+                act(
+                    remote(
+                        source.at[where],
+                        target.at[(self.chip,) + where],
+                        self.send_sem.at[2, to],
+                        self.recv_sem.at[self.chip, self.first_small],
+                        to,
+                        self.z,
+                    ),
+                    True,
+                )
+
+        act(
+            pltpu.make_async_copy(
+                source.at[where],
+                target.at[(self.chip,) + where],
+                self.recv_sem.at[self.chip, self.first_small],
+            ),
+            False,
+        )
+
+    def arrivals(self, unit_of, count, source, target):
+        low = self.member * self.piece_length
+
+        def body(number, carry):
+            for q in range(4):
+                index, where, first, last = unit_of(number, q)
+                mine = (first < low + self.piece_length) & (last > low)
+                here = (self.chip == q) & self.owner
+
+                @pl.when(mine & here)
+                def _():
+                    pltpu.make_async_copy(
+                        source.at[where], target.at[(q,) + where], self.recv_sem.at[q, index]
+                    ).wait()
+
+                @pl.when(mine & jnp.logical_not(here))
+                def _():
+                    remote(
+                        source.at[where],
+                        target.at[(q,) + where],
+                        self.send_sem.at[0, index],
+                        self.recv_sem.at[q, index],
+                        self.member,
+                        self.z,
+                    ).wait_recv()
+
+            return carry
+
+        lax.fori_loop(0, count, body, 0)
+
+    def small_arrivals(self, source, target):
+        where = self.small_where()
+        for q in range(4):
+            here = (self.chip == q) & self.owner
+
+            @pl.when(here)
+            def _():
+                pltpu.make_async_copy(
+                    source.at[where],
+                    target.at[(q,) + where],
+                    self.recv_sem.at[q, self.first_small],
+                ).wait()
+
+            @pl.when(jnp.logical_not(here))
+            def _():
+                remote(
+                    source.at[where],
+                    target.at[(q,) + where],
+                    self.send_sem.at[2, 0],
+                    self.recv_sem.at[q, self.first_small],
+                    self.member,
+                    self.z,
+                ).wait_recv()
+
+
+def begin(copy, is_remote):
+    copy.start()
+
+
+def finish_send(copy, is_remote):
+    if is_remote:
+        copy.wait_send()
+
+
+def sums_kernel(
+    sizes,
+    mix_ref,
+    part_ref,
+    ffn_ref,
+    tokens_ref,
+    res_ref,
+    gain_ref,
+    mix_out,
+    ffn_out,
+    tokens_out,
+    gain_out,
+    paired,
+    arrived,
+    total,
+    from_x,
+    from_y,
+    passing,
+    last,
+    gain_part,
+    gain_plane,
+    gain_line,
+    gain_seen,
+    core_send,
+    core_recv,
+    line_send,
+    line_recv,
+    plane_send,
+    plane_recv,
+    gain_send,
+    gain_recv,
+    unit_send,
+    unit_recv,
+):
+    model, width, ffn_width, piece_length = sizes
+    member = lax.axis_index("dp")
+    z = lax.axis_index("shard")
+    chip, core = member // 2, member % 2
+    end = z + core * (3 - 2 * z)
+    slots = tokens_ref.shape[0]
+    half = slots // 2
+    to_x = peer_x(chip) * 2 + core
+    to_y = peer_y(chip) * 2 + core
+    other = chip * 2 + 1 - core
+    scatter = Scatter(sizes, member, z, unit_send, unit_recv)
+    enter(member, z)
+
+    def rows(number):
+        return pl.ds(number * width, width)
+
+    def core_copy(slot, number):
+        return remote(
+            mix_ref.at[2 + slot, rows(number)],
+            paired.at[slot, rows(number)],
+            core_send.at[slot, number],
+            core_recv.at[slot, number],
+            other,
+            z,
+        )
+
+    for slot in range(2):
+        for number in range(3):
+            core_copy(slot, number).start()
+
+    def plane_copy(number):
+        source, target, to = (
+            (part_ref.at[pl.ds(slots, half)], from_x.at[0], to_x),
+            (part_ref.at[pl.ds(3 * slots, half)], from_x.at[1], to_x),
+            (part_ref.at[pl.ds(2 * slots + half, half)], from_y.at[0], to_y),
+            (part_ref.at[pl.ds(3 * slots + half, half)], from_y.at[1], to_y),
+            (passing.at[0], last.at[0], to_y),
+            (passing.at[1], last.at[1], to_x),
+        )[number]
+        return remote(source, target, plane_send.at[number], plane_recv.at[number], to, z)
+
+    for number in (1, 3, 0, 2):
+        plane_copy(number).start()
+
+    @pl.when(scatter.owner)
+    def _():
+        scatter.each(scatter.up_unit, 0, 2 * scatter.across, ffn_ref, ffn_out, begin)
+        scatter.each(scatter.down_unit, 0, 6, ffn_ref, ffn_out, begin)
+
+    def line_copy(kind, number, source, to_end):
+        return remote(
+            source,
+            arrived.at[kind, rows(number)],
+            line_send.at[kind, number],
+            line_recv.at[kind, number],
+            member,
+            line_place(to_end, core),
+        )
+
+    for slot in range(2):
+        for number in range(3):
+            core_copy(slot, number).wait_recv()
+            both = mix_ref[slot, rows(number)].astype(wide) + paired[slot, rows(number)].astype(wide)
+            paired[slot, rows(number)] = both.astype(low_type)
+
+            @pl.when(end == 3)
+            def _():
+                line_copy(slot, number, paired.at[slot, rows(number)], 2).start()
+
+            if slot == 1:
+
+                @pl.when(end == 0)
+                def _():
+                    line_copy(2, number, paired.at[slot, rows(number)], 1).start()
+
+    plane_copy(1).wait_recv()
+    passing[0] = (
+        part_ref[2 * slots : 2 * slots + half].astype(wide) + from_x[1].astype(wide)
+    ).astype(low_type)
+    plane_copy(4).start()
+    plane_copy(3).wait_recv()
+    passing[1] = (
+        part_ref[slots + half : 2 * slots].astype(wide) + from_y[1].astype(wide)
+    ).astype(low_type)
+    plane_copy(5).start()
+
+    def summed(slot, kinds, number):
+        result = paired[slot, rows(number)].astype(wide)
+        for kind in kinds:
+            result = result + arrived[kind, rows(number)].astype(wide)
+        return result.astype(low_type)
+
+    def on_arrival(kind, number):
+        line_copy(kind, number, paired.at[0, rows(number)], 0).wait_recv()
+
+    def share(number):
+        if number < 2:
+            across = scatter.across
+            scatter.each(
+                scatter.in_unit, number * across, (number + 1) * across, total, mix_out, begin
+            )
+            scatter.each(scatter.gate_unit, number, number + 1, total, mix_out, begin)
+        else:
+            scatter.each(scatter.out_unit, 0, 4, total, mix_out, begin)
+            scatter.smalls(total, mix_out, begin)
+
+    for number in range(3):
+
+        @pl.when((end == 2) | (end == 1))
+        def _():
+            on_arrival(0, number)
+            paired[0, rows(number)] = summed(0, (0,), number)
+
+        @pl.when(end == 2)
+        def _():
+            line_copy(0, number, paired.at[0, rows(number)], 1).start()
+
+        @pl.when(end == 1)
+        def _():
+            line_copy(0, number, paired.at[0, rows(number)], 0).start()
+
+    for number in range(3):
+
+        @pl.when(end == 2)
+        def _():
+            on_arrival(1, number)
+            paired[1, rows(number)] = summed(1, (1,), number)
+            line_copy(1, number, paired.at[1, rows(number)], 1).start()
+
+        @pl.when(end == 1)
+        def _():
+            on_arrival(1, number)
+            on_arrival(2, number)
+            total[rows(number)] = summed(1, (1, 2), number)
+
+        @pl.when(end == 0)
+        def _():
+            on_arrival(0, number)
+            total[rows(number)] = summed(0, (0,), number)
+
+        @pl.when(scatter.owner)
+        def _():
+            share(number)
+
+    plane_copy(0).wait_recv()
+    plane_copy(2).wait_recv()
+    plane_copy(4).wait_recv()
+    plane_copy(5).wait_recv()
+    gain = gain_ref[0:1]
+    gain_sum = jnp.zeros((1, model), wide)
+    for number, direct in ((0, from_x), (1, from_y)):
+        at = slice(number * half, (number + 1) * half)
+        grad = part_ref[at].astype(wide) + direct[0].astype(wide) + last[number].astype(wide)
+        value = tokens_ref[at].astype(wide)
+        scale = lax.rsqrt(jnp.mean(value * value, axis=1, keepdims=True) + norm_eps)
+        scaled = grad * gain
+        gain_sum = gain_sum + jnp.sum(grad * value * scale, axis=0, keepdims=True)
+        inner = jnp.mean(scaled * value, axis=1, keepdims=True)
+        back = scale * scaled - value * (scale * scale * scale * inner)
+        tokens_out[at] = (res_ref[at] + back).astype(low_type)
+    gain_part[...] = jnp.concatenate([gain_sum, gain_ref[1:2], jnp.zeros((6, model), wide)], axis=0)
+
+    def gain_copy():
+        return remote(
+            gain_part, gain_plane.at[member], gain_send.at[0], gain_recv.at[member], 7, z
+        )
+
+    @pl.when(member != 7)
+    def _():
+        gain_copy().start()
+        gain_copy().wait_send()
+        gain_out[...] = jnp.zeros_like(gain_out)
+
+    @pl.when(member == 7)
+    def _():
+        result = gain_part[...]
+        for source in range(7):
+            remote(
+                gain_part,
+                gain_plane.at[source],
+                gain_send.at[0],
+                gain_recv.at[source],
+                7,
+                z,
+            ).wait_recv()
+            result = result + gain_plane[source]
+        quarter = model // 4
+        for place in range(4):
+            gain_line[place] = result[:, place * quarter : (place + 1) * quarter]
+
+        def line_gain(place, slot):
+            return remote(
+                gain_line.at[place],
+                gain_seen.at[slot],
+                gain_send.at[1 + place],
+                gain_recv.at[8 + slot],
+                7,
+                place,
+            )
+
+        for place in range(4):
+
+            @pl.when(place != z)
+            def _():
+                line_gain(place, z).start()
+
+        gain_out[...] = gain_line[z]
+        for place in range(4):
+
+            @pl.when(place != z)
+            def _():
+                line_gain(place, place).wait_recv()
+                gain_out[...] += gain_seen[place]
+                line_gain(place, z).wait_send()
+
+    across = scatter.across
+    scatter.arrivals(scatter.up_unit, 2 * across, ffn_ref, ffn_out)
+    scatter.arrivals(scatter.down_unit, 6, ffn_ref, ffn_out)
+    scatter.arrivals(scatter.in_unit, 2 * across, total, mix_out)
+    scatter.arrivals(scatter.gate_unit, 2, total, mix_out)
+    scatter.arrivals(scatter.out_unit, 4, total, mix_out)
+    scatter.small_arrivals(total, mix_out)
+
+    @pl.when(scatter.owner)
+    def _():
+        scatter.each(scatter.up_unit, 0, 2 * across, ffn_ref, ffn_out, finish_send)
+        scatter.each(scatter.down_unit, 0, 6, ffn_ref, ffn_out, finish_send)
+        scatter.each(scatter.in_unit, 0, 2 * across, total, mix_out, finish_send)
+        scatter.each(scatter.gate_unit, 0, 2, total, mix_out, finish_send)
+        scatter.each(scatter.out_unit, 0, 4, total, mix_out, finish_send)
+        scatter.smalls(total, mix_out, finish_send)
+
+    for number in range(6):
+        plane_copy(number).wait_send()
+    for slot in range(2):
+        for number in range(3):
+            core_copy(slot, number).wait_send()
+    for number in range(3):
+
+        @pl.when(end > 0)
+        def _():
+            line_copy(0, number, paired.at[0, rows(number)], 0).wait_send()
+
+        @pl.when(end > 1)
+        def _():
+            line_copy(1, number, paired.at[1, rows(number)], 0).wait_send()
+
+        @pl.when(end == 0)
+        def _():
+            line_copy(2, number, paired.at[1, rows(number)], 1).wait_send()
+
+
+def sums(mix, part, ffn, tokens, residual_grad, gains, piece_length, width):
+    model = tokens.shape[1]
+    ffn_width = ffn.shape[1]
+    sizes = (model, width, ffn_width, piece_length)
+    half = tokens.shape[0] // 2
+    block = mix.shape[1:]
+    count = Scatter(sizes, 0, 0, None, None).count
+    dma = pltpu.SemaphoreType.DMA
+    vmem = pl.BlockSpec(memory_space=pltpu.VMEM)
+    anywhere = pl.BlockSpec(memory_space=pl.ANY)
+    return pl.pallas_call(
+        functools.partial(sums_kernel, sizes),
+        in_specs=[vmem, vmem, anywhere, vmem, vmem, vmem],
+        out_specs=[anywhere, anywhere, vmem, vmem],
+        out_shape=[
+            jax.ShapeDtypeStruct(mix.shape, low_type),
+            jax.ShapeDtypeStruct((4,) + ffn.shape, low_type),
+            jax.ShapeDtypeStruct(tokens.shape, low_type),
+            jax.ShapeDtypeStruct((8, model // 4), wide),
+        ],
+        scratch_shapes=[
+            pltpu.VMEM((2,) + block, low_type),
+            pltpu.VMEM((3,) + block, low_type),
+            pltpu.VMEM(block, low_type),
+            pltpu.VMEM((2, half, model), low_type),
+            pltpu.VMEM((2, half, model), low_type),
+            pltpu.VMEM((2, half, model), low_type),
+            pltpu.VMEM((2, half, model), low_type),
+            pltpu.VMEM((8, model), wide),
+            pltpu.VMEM((8, 8, model), wide),
+            pltpu.VMEM((4, 8, model // 4), wide),
+            pltpu.VMEM((4, 8, model // 4), wide),
+            dma((2, 3)),
+            dma((2, 3)),
+            dma((3, 3)),
+            dma((3, 3)),
+            dma((6,)),
+            dma((6,)),
+            dma((5,)),
+            dma((12,)),
+            dma((3, count)),
+            dma((4, count)),
+        ],
+        compiler_params=pltpu.CompilerParams(
+            collective_id=2, has_side_effects=True, vmem_limit_bytes=40 * 1024 * 1024
+        ),
+        cost_estimate=pl.CostEstimate(
+            flops=mix.size * 4, bytes_accessed=mix.size * 8, transcendentals=0
+        ),
+        name="sums",
+    )(mix, part, ffn, tokens, residual_grad, gains)
+
+
 def tail_kernel(
     sizes,
     mix_ref,
@@ -538,18 +1112,13 @@
     model, width, ffn_width, piece_length, chunks, lines, margin = sizes
     member = lax.axis_index("dp")
     z = lax.axis_index("shard")
-    chip = member // 2
     step = pl.program_id(0)
     lead = 128
     start_row = (member * piece_length) // lead
     offset = (member * piece_length) % lead
-    used_rows = piece_length // lead + 2
     tiles_in = 4 * width // lead
     tiles_ffn = 4 * ffn_width // lead
     tiles_model = model // lead
-
-    def relative(q):
-        return ((q // 2 + chip // 2) % 2) * 2 + (q % 2 + chip % 2) % 2
 
     def copy_to(origin, chunk, side, to):
         return pltpu.make_async_remote_copy(
@@ -592,7 +1161,9 @@
         lax.fori_loop(0, grad.shape[0] // 256, clear, 0)
 
         def place(row, count, body):
-            @pl.when((row < start_row + used_rows) & (row + count > start_row))
+            low = member * piece_length
+
+            @pl.when((row * lead < low + piece_length) & ((row + count) * lead > low))
             def _():
                 body(row - start_row + margin)
 
@@ -605,7 +1176,7 @@
             def body(to):
                 for q in range(4):
                     tile = mix_ref[
-                        relative(q),
+                        q,
                         pl.ds(pl.multiple_of(kind * width, width), width),
                         pl.ds(pl.multiple_of(at * lead, lead), lead),
                     ].astype(wide)
@@ -623,7 +1194,7 @@
 
             def body(to):
                 grad[pl.ds(to, width), :] = mix_ref[
-                    relative(q), pl.ds(pl.multiple_of(kind * width, width), width), model:
+                    q, pl.ds(pl.multiple_of(kind * width, width), width), model:
                 ].astype(wide)
 
             place(2 * model * tiles_in + number * width, width, body)
@@ -633,17 +1204,24 @@
         base = base + 8 * width
         out_base = base
 
-        def out_unit(q, carry):
+        quarter = width // 4
+
+        def out_unit(number, carry):
+            q = number // 4
+            part = number % 4
+
             def body(to):
                 for at in range(tiles_model):
-                    grad[pl.ds(to + at, width, stride=tiles_model), :] = mix_ref[
-                        relative(q), 2 * width : 3 * width, at * lead : (at + 1) * lead
+                    grad[pl.ds(to + at, quarter, stride=tiles_model), :] = mix_ref[
+                        q,
+                        pl.ds(pl.multiple_of(2 * width + part * quarter, quarter), quarter),
+                        at * lead : (at + 1) * lead,
                     ].astype(wide)
 
-            place(out_base + q * width * tiles_model, width * tiles_model, body)
+            place(out_base + number * quarter * tiles_model, quarter * tiles_model, body)
             return carry
 
-        lax.fori_loop(0, 4, out_unit, 0)
+        lax.fori_loop(0, 16, out_unit, 0)
         base = base + 4 * width * tiles_model
         up_base = base
 
@@ -661,7 +1239,7 @@
                         last = min((q + 1) * ffn_width, (tile + 1) * lead)
                         found.append(
                             ffn_ref[
-                                relative(q),
+                                q,
                                 kind,
                                 row - q * ffn_width : last - q * ffn_width,
                                 columns,
@@ -677,35 +1255,39 @@
         lax.fori_loop(0, 2 * tiles_model, up_unit, 0)
         base = base + 2 * model * tiles_ffn
         down_base = base
-        third = ffn_width // 3
+        sixth = ffn_width // 6
 
         def down_unit(number, carry):
-            q = number // 3
-            part = number % 3
+            q = number // 6
+            part = number % 6
 
             def body(to):
                 for at in range(tiles_model):
-                    grad[pl.ds(to + at, third, stride=tiles_model), :] = ffn_ref[
-                        relative(q),
+                    grad[pl.ds(to + at, sixth, stride=tiles_model), :] = ffn_ref[
+                        q,
                         2,
-                        pl.ds(pl.multiple_of(part * third, 16), third),
+                        pl.ds(pl.multiple_of(part * sixth, 16), sixth),
                         at * lead : (at + 1) * lead,
                     ].astype(wide)
 
-            place(down_base + number * third * tiles_model, third * tiles_model, body)
+            place(down_base + number * sixth * tiles_model, sixth * tiles_model, body)
             return carry
 
-        lax.fori_loop(0, 12, down_unit, 0)
+        lax.fori_loop(0, 24, down_unit, 0)
         small_base = base + 4 * ffn_width * tiles_model
         smalls = [
-            mix_ref[relative(q), 2 * width : 2 * width + 16, model:].astype(wide)
+            mix_ref[q, 2 * width : 2 * width + 16, model:].astype(wide)
             for q in range(4)
         ]
 
         def small_body(to):
             for q in range(4):
                 grad[pl.ds(to + q, 8, stride=tiles_in), :] = smalls[q][:8]
-            grad[pl.ds(to + 8 * tiles_in, 6), :] = gain_ref[0:6, :]
+            for number in range(6):
+                kind, at = number // 3, number % 3
+                grad[pl.ds(to + 8 * tiles_in + number, 1), :] = gain_ref[
+                    kind : kind + 1, at * lead : (at + 1) * lead
+                ]
 
         place(small_base, 8 * tiles_in + 6, small_body)
         bias_ref[...] = jnp.concatenate([small[5:7] for small in smalls], axis=1)
@@ -959,32 +1541,23 @@
     grad_mix, mix_in_part = mix_backward(
         mix_in, res_low, position, mix_weights, saved, slots, width
     )
-    _, norm_pull = jax.vjp(rms_scale, stream, gains[0])
-    grad_norm_one, grad_gain_one = norm_pull(plane_reduce(mix_in_part))
-    tokens_grad = (grad_residual + grad_norm_one).astype(low_type)
-
     both = 2 * ffn_width
     pair_ffn = add_low(grad_ffn[:, :both], move(grad_ffn[:, both:], core_pairs))
     sum_ffn = line_sum(pair_ffn[:, :ffn_width], pair_ffn[:, ffn_width:], end)
-    pair_mix = add_low(grad_mix[:2], move(grad_mix[2:], core_pairs))
-    sum_mix = line_sum(pair_mix[0], pair_mix[1], end)
-    owner = core == z // 2
-
-    def share(total, dim):
-        four = jnp.stack(plane_gather(total, dim, owners_only=True))
-        return jnp.where(owner, four, move(four, owner_core_pairs))
-
-    four_ffn = share(sum_ffn, 1)
-    four_mix = share(sum_mix, 0)
-    gain_sum = jnp.stack([grad_gain_one, grad_gain_two])
-    gain_sum = gain_sum + move(gain_sum, core_pairs)
-    gain_sum = gain_sum + move(gain_sum, plane_pairs(1))
-    gain_sum = gain_sum + move(gain_sum, plane_pairs(2))
-    gain_slice = shard_slices(gain_sum, z)
+    four_mix, four_ffn, tokens_grad, gain_total = sums(
+        grad_mix,
+        mix_in_part,
+        sum_ffn,
+        tokens,
+        grad_residual,
+        jnp.concatenate([gains[0:1], grad_gain_two[None], jnp.zeros((6, model), wide)]),
+        piece_length,
+        width,
+    )
     piece, new_master, new_first, new_second, new_weights, bias_total = tail(
         four_mix,
         four_ffn,
-        jnp.concatenate([gain_slice.reshape(-1, 128), jnp.zeros((2, 128), wide)]),
+        gain_total,
         master_shard,
         first_moment,
         second_moment,

time: 926 us -> 800 us (0.86)
  waiting for transfers between devices: 269 us -> 182 us
  starting transfers between devices: 198 us -> 118 us
  Pallas kernels: 281 us -> 354 us
  other arithmetic: 98.3 us -> 68.2 us
    ppermute x73 -> x47, waiting for transfers between devices: 269 us -> 182 us  [move(): return lax.ppermute(value, axes, pairs)]
    ppermute x73 -> x47, starting transfers between devices: 198 us -> 118 us  [move(): return lax.ppermute(value, axes, pairs)]
    pallas_call x0 -> x1, Pallas kernels: none -> 65.5 us  [sums(): pl.pallas_call(functools.partial(sums_kernel, sizes), in_specs=[vmem, vme...]
    select_n x2 -> x0, other arithmetic: 11.4 us -> none  [share(): return jnp.where(owner, four, move(four, owner_core_pairs))]
    unnamed x120 -> x97, local copies, waits for them, and re-layouts: 34.6 us -> 37.8 us
  transfers between devices with their start and end apart: 73 -> 47, of which waited for: 39 -> 22; matrix products, arithmetic and copies ran while one was open for 11% -> 9% of each run, Pallas kernels for 8% -> 9%
where the time goes in v3:
time: 800 us; the launch traced here: 793 us
  Pallas kernels  354 us (44%)
  waiting for transfers between devices  182 us (23%)
  starting transfers between devices  118 us (15%)
  local copies, waits for them, and re-layouts  69.3 us (9%)
  other arithmetic  68.2 us (9%)
    ppermute x47, waiting for transfers between devices, move(): return lax.ppermute(value, axes, pairs)  182 us
    pallas_call x1, Pallas kernels, tail(): pl.pallas_call(functools.partial(tail_kernel, (model, width, ffn_width, p...  156 us
    ppermute x47, starting transfers between devices, move(): return lax.ppermute(value, axes, pairs)  118 us
    pallas_call x1, Pallas kernels, sums(): pl.pallas_call(functools.partial(sums_kernel, sizes), in_specs=[vmem, vme...  65.5 us
    pallas_call x1, Pallas kernels, ffn_both(): pl.pallas_call(ffn_kernel, grid=(hidden // tile, rows // slots), in_specs...  59.1 us
    pallas_call x1, Pallas kernels, mix_backward(): pl.pallas_call(functools.partial(mixer_backward_kernel, width), grid=(hea...  41.2 us
    unnamed x97, local copies, waits for them, and re-layouts  37.8 us
    pallas_call x1, Pallas kernels, mix_forward(): pl.pallas_call(functools.partial(mixer_forward_kernel, width), grid=(head...  32.5 us
  transfers between devices with their start and end apart: 47, of which 22 were waited for; matrix products, arithmetic and copies ran while one was open for 9% of the time, Pallas kernels for 9%

profile of v3, /device:TPU:0, one launch (start us, length us, event | category | flops | bytes accessed | tf_op | source)
XLA Modules:
  0.0 792.6 jit_solution(5980685990506825791)
XLA Ops:
  17.2 6.0 collective-permute-start.7
  23.2 4.6 constant_dynamic-slice_fusion
  46.9 20.7 %collective-permute-done.24 = bf16[3,288,1536]{2,1,0:T(8,128)(2,1)} collective-permute-done((bf16[3,288,1536]{2,1,0:T(8,128)(2,1)}, bf16[3,288,1536]{2,1,0:T(8,128)(2,1)}, u32[]{:S(2)}, u32[]{:S(2)}) %collective-permute-start.24) | collective-permute-done | bytes 2654240 | tf_op jit(solution)/shard_map/ppermute | solution.py:69
  76.1 26.3 %collective-permute-start.11 = (bf16[2,384,1664]{2,1,0:T(8,128)(2,1)}, bf16[2,384,1664]{2,1,0:T(8,128)(2,1)}, u32[]{:S(2)}, u32[]{:S(2)}) collective-permute-start(bf16[2,384,1664]{2,1,0:T(8,128)(2,1)} %pad_maximum_fusion.5), channel_id=1, source_target_pairs={{0,4},{1,5},{2,6},{3,7},{4,0},{5,1},{6,2},{7,3},{8,12},{9,13},{10,... | collective-permute-start | bytes 7667720 | tf_op jit(solution)/shard_map/ppermute | solution.py:69
  102.4 6.2 collective-permute-done.4
  108.6 20.4 %collective-permute-start.5 = (bf16[2,384]{1,0:T(2,128)(2,1)S(1)}, bf16[2,384]{1,0:T(2,128)(2,1)S(1)}, u32[]{:S(2)}, u32[]{:S(2)}) collective-permute-start(bf16[2,384]{1,0:T(2,128)(2,1)S(1)} %copy-done.33), channel_id=1, source_target_pairs={{0,2},{1,3},{2,0},{3,1},{4,6},{5,7},{6,4},{7,5},{8,10},{9,11},{10,... | collective-permute-start | bytes 4616 | tf_op jit(solution)/shard_map/ppermute | solution.py:69
  130.5 4.9 collective-permute-start.6
  154.1 7.1 fusion.2.x_ref
  161.2 4.6 pad_maximum_fusion.2.w_ref
  165.7 32.5 %mixer_forward.1 = (bf16[1024,1536]{1,0:T(8,128)(2,1)}, f32[4,1024,256]{2,1,0:T(8,128)}, f32[4,1024,128]{2,1,0:T(8,128)S(1)}, bf16[4,1024,128]{2,1,0:T(8,128)(2,1)S(1)}) custom-call(bf16[1024,1536]{1,0:T(8,128)(2,1)} %fusion.2.x_ref, s32[1024,1]{1,0:T(8,128)S(1)} %bitcast.18, bf16[4,384,1664]{2,1,0:T(8,128)(2,1)} %pad_maximum_fusion.2.w_ref), custom_call_target="tpu_custom_call" | custom-call | flops 4831838208 | bytes 18743296 | tf_op jit(solution)/shard_map/mixer_forward/pallas_call | solution.py:281
  202.2 4.6 select_select_fusion.1
  207.2 8.9 %collective-permute-done.12 = bf16[256,1536]{1,0:T(8,128)(2,1)S(1)} collective-permute-done((bf16[256,1536]{1,0:T(8,128)(2,1)S(1)}, bf16[256,1536]{1,0:T(8,128)(2,1)S(1)}, u32[]{:S(2)}, u32[]{:S(2)}) %collective-permute-start.12) | collective-permute-done | bytes 786464 | tf_op jit(solution)/shard_map/ppermute | solution.py:69
  219.7 9.7 %collective-permute-done.13 = bf16[128,1536]{1,0:T(8,128)(2,1)S(1)} collective-permute-done((bf16[128,1536]{1,0:T(8,128)(2,1)S(1)}, bf16[128,1536]{1,0:T(8,128)(2,1)S(1)}, u32[]{:S(2)}, u32[]{:S(2)}) %collective-permute-start.13) | collective-permute-done | bytes 393248 | tf_op jit(solution)/shard_map/ppermute | solution.py:69
  230.8 6.7 collective-permute-done.20
  237.6 8.4 %collective-permute-done.21 = bf16[256,1536]{1,0:T(8,128)(2,1)S(1)} collective-permute-done((bf16[256,1536]{1,0:T(8,128)(2,1)S(1)}, bf16[256,1536]{1,0:T(8,128)(2,1)S(1)}, u32[]{:S(2)}, u32[]{:S(2)}) %collective-permute-start.21) | collective-permute-done | bytes 786464 | tf_op jit(solution)/shard_map/ppermute | solution.py:69
  256.3 12.6 %collective-permute-done.16 = bf16[256,1536]{1,0:T(8,128)(2,1)S(1)} collective-permute-done((bf16[256,1536]{1,0:T(8,128)(2,1)S(1)}, bf16[256,1536]{1,0:T(8,128)(2,1)S(1)}, u32[]{:S(2)}, u32[]{:S(2)}) %collective-permute-start.16) | collective-permute-done | bytes 786464 | tf_op jit(solution)/shard_map/ppermute | solution.py:69
  270.6 6.2 collective-permute-done.18
  278.6 10.9 %pad_maximum_fusion.w_ref = bf16[3,1152,1536]{2,1,0:T(8,128)(2,1)} fusion(bf16[3,576,1536]{2,1,0:T(8,128)(2,1)S(1)} %collective-permute-done.28, bf16[3,288,1536]{2,1,0:T(8,128)(2,1)S(1)} %get-tuple-element.72, bf16[3,288,1536]{2,1,0:T(8,128)(2,1)S(1)} %get-tuple-element.71), kind=kLoop, calls=%fused_computation | loop fusion | flops 31850496 | bytes 21233664 | tf_op jit(solution)/shard_map/concatenate | solution.py:1524
  289.5 59.1 %ffn_both.1 = (bf16[3,1152,1536]{2,1,0:T(8,128)(2,1)}, bf16[1024,1536]{1,0:T(8,128)(2,1)}, bf16[1024,1536]{1,0:T(8,128)(2,1)}) custom-call(bf16[1024,1536]{1,0:T(8,128)(2,1)} %copy-done.32, bf16[1024,1536]{1,0:T(8,128)(2,1)} %copy-done.31, bf16[3,1152,1536]{2,1,0:T(8,128)(2,1)} %pad_maximum_fusion.w_ref), custom_call_target="tpu_custom_call" | custom-call | flops 32614907904 | bytes 46399488 | tf_op jit(solution)/shard_map/ffn_both/pallas_call | solution.py:485
  355.2 5.4 collective-permute-done.41
  360.6 5.6 add_convert_fusion
  376.9 11.5 %collective-permute-done.33 = bf16[256,1536]{1,0:T(8,128)(2,1)S(1)} collective-permute-done((bf16[256,1536]{1,0:T(8,128)(2,1)S(1)}, bf16[256,1536]{1,0:T(8,128)(2,1)S(1)}, u32[]{:S(2)}, u32[]{:S(2)}) %collective-permute-start.33) | collective-permute-done | bytes 786464 | tf_op jit(solution)/shard_map/ppermute | solution.py:69
  391.3 21.3 %collective-permute-done.30 = bf16[128,1536]{1,0:T(8,128)(2,1)S(1)} collective-permute-done((bf16[128,1536]{1,0:T(8,128)(2,1)S(1)}, bf16[128,1536]{1,0:T(8,128)(2,1)S(1)}, u32[]{:S(2)}, u32[]{:S(2)}) %collective-permute-start.30) | collective-permute-done | bytes 393248 | tf_op jit(solution)/shard_map/ppermute | solution.py:69
  414.0 9.7 %collective-permute-start.45 = (bf16[3,288,1536]{2,1,0:T(8,128)(2,1)S(1)}, bf16[3,288,1536]{2,1,0:T(8,128)(2,1)S(1)}, u32[]{:S(2)}, u32[]{:S(2)}) collective-permute-start(bf16[3,288,1536]{2,1,0:T(8,128)(2,1)S(1)} %get-tuple-element.76), channel_id=1, source_target_pairs={{0,1},{3,2},{4,5},{7,6},{8,9},{11,10},{12,13},{15,14},{16,17},{19,... | collective-permute-start | bytes 7962632 | tf_op jit(solution)/shard_map/ppermute | solution.py:69
  429.3 8.3 %collective-permute-done.36 = bf16[128,1536]{1,0:T(8,128)(2,1)S(1)} collective-permute-done((bf16[128,1536]{1,0:T(8,128)(2,1)S(1)}, bf16[128,1536]{1,0:T(8,128)(2,1)S(1)}, u32[]{:S(2)}, u32[]{:S(2)}) %collective-permute-start.36) | collective-permute-done | bytes 393248 | tf_op jit(solution)/shard_map/ppermute | solution.py:69
  443.9 35.9 %collective-permute-done.45 = bf16[3,288,1536]{2,1,0:T(8,128)(2,1)S(1)} collective-permute-done((bf16[3,288,1536]{2,1,0:T(8,128)(2,1)S(1)}, bf16[3,288,1536]{2,1,0:T(8,128)(2,1)S(1)}, u32[]{:S(2)}, u32[]{:S(2)}) %collective-permute-start.45) | collective-permute-done | bytes 2654240 | tf_op jit(solution)/shard_map/ppermute | solution.py:69
  479.8 4.7 fusion.4
  492.3 6.3 collective-permute-done.39
  500.6 41.2 %mixer_backward.1 = (bf16[4,384,1664]{2,1,0:T(8,128)(2,1)}, bf16[1024,1536]{1,0:T(8,128)(2,1)}) custom-call(bf16[1024,1536]{1,0:T(8,128)(2,1)} %fusion.2.x_ref, bf16[1024,1536]{1,0:T(8,128)(2,1)} %constant_dynamic-update-slice_fusion.10.res_ref, s32[1024,1]{1,0:T(8,128)S(1)} %bitcast.19, bf16[4,384,1664]{2,1,0:T(8,128)(2,1)} %pad_maximum_fusion.2.w_ref, ...), custom_call_target="tpu_custom_call" | custom-call | flops 9663676416 | bytes 27000832 | tf_op jit(solution)/shard_map/mixer_backward/pallas_call | solution.py:401
  545.9 65.5 %sums.1 = (bf16[4,384,1664]{2,1,0:T(8,128)(2,1)S(1)}, bf16[4,3,288,1536]{3,2,1,0:T(8,128)(2,1)}, bf16[256,1536]{1,0:T(8,128)(2,1)S(1)}, f32[8,384]{1,0:T(8,128)S(1)}) custom-call(bf16[4,384,1664]{2,1,0:T(8,128)(2,1)} %get-tuple-element.45.mix_ref, bf16[1024,1536]{1,0:T(8,128)(2,1)S(1)} %copy-done.4, bf16[3,288,1536]{2,1,0:T(8,128)(2,1)S(1)} %fusion.7.ffn_ref, ...), custom_call_target="tpu_custom_call" | custom-call | flops 10223616 | bytes 20447232 | tf_op jit(solution)/shard_map/sums/pallas_call | solution.py:1049
  614.3 155.8 %tail.1 = (f32[1,975456]{1,0:T(1,128)}, f32[1,975456]{1,0:T(1,128)}, f32[1,975456]{1,0:T(1,128)}, f32[1,975456]{1,0:T(1,128)}, bf16[4,975456]{1,0:T(4,128)(2,1)}, /*index=5*/f32[2,512]{1,0:T(2,128)}) custom-call(bf16[4,384,1664]{2,1,0:T(8,128)(2,1)} %copy-done.3, bf16[4,3,288,1536]{3,2,1,0:T(8,128)(2,1)} %get-tuple-element.50.ffn_ref, f32[8,384]{1,0:T(8,128)} %copy-done.5, ...), custom_call_target="tpu_custom_call" | custom-call | flops 19509120 | bytes 39018240 | tf_op jit(solution)/shard_map/tail/pallas_call | solution.py:1412
  771.0 7.0 copy.53
  (247 shorter events, 152.3 us)
Async XLA Ops:
  17.2 22.0 %collective-permute-start.7 = (bf16[384,1664]{1,0:T(8,128)(2,1)}, bf16[384,1664]{1,0:T(8,128)(2,1)}, u32[]{:S(2)}, u32[]{:S(2)}) collective-permute-start(bf16[384,1664]{1,0:T(8,128)(2,1)} %pad_maximum_fusion.7), channel_id=1, source_target_pairs={{0,1},{1,2},{6,5},{7,6},{8,9},{9,10},{14,13},{15,14},{16,17},{17,1... | collective-permute-start | bytes 3833864 | tf_op jit(solution)/shard_map/ppermute | solution.py:69
  35.3 32.3 %collective-permute-start.24 = (bf16[3,288,1536]{2,1,0:T(8,128)(2,1)}, bf16[3,288,1536]{2,1,0:T(8,128)(2,1)}, u32[]{:S(2)}, u32[]{:S(2)}) collective-permute-start(bf16[3,288,1536]{2,1,0:T(8,128)(2,1)} %pad_maximum_fusion.4), channel_id=1, source_target_pairs={{0,1},{1,2},{6,5},{7,6},{8,9},{9,10},{14,13},{15,14},{16,17},{17,1... | collective-permute-start | bytes 7962632 | tf_op jit(solution)/shard_map/ppermute | solution.py:69
  40.0 29.8 %collective-permute-start.10 = (bf16[384,1664]{1,0:T(8,128)(2,1)}, bf16[384,1664]{1,0:T(8,128)(2,1)}, u32[]{:S(2)}, u32[]{:S(2)}) collective-permute-start(bf16[384,1664]{1,0:T(8,128)(2,1)} %pad_maximum_fusion.7), channel_id=1, source_target_pairs={{1,0},{6,7},{9,8},{14,15},{17,16},{22,23},{25,24},{30,31}} | collective-permute-start | bytes 3833864 | tf_op jit(solution)/shard_map/ppermute | solution.py:69
  41.3 28.5 %collective-permute-start.9 = (bf16[384,1664]{1,0:T(8,128)(2,1)S(1)}, bf16[384,1664]{1,0:T(8,128)(2,1)}, u32[]{:S(2)}, u32[]{:S(2)}) collective-permute-start(bf16[384,1664]{1,0:T(8,128)(2,1)S(1)} %collective-permute-done.8), channel_id=1, source_target_pairs={{2,3},{5,4},{10,11},{13,12},{18,19},{21,20},{26,27},{29,28}} | collective-permute-start | bytes 3833864 | tf_op jit(solution)/shard_map/ppermute | solution.py:69
  44.1 94.0 %collective-permute-start.1 = (bf16[272,1536]{1,0:T(8,128)(2,1)}, bf16[272,1536]{1,0:T(8,128)(2,1)}, u32[]{:S(2)}, u32[]{:S(2)}) collective-permute-start(bf16[272,1536]{1,0:T(8,128)(2,1)} %fusion.13), channel_id=1, source_target_pairs={{0,16},{1,17},{2,18},{3,19},{4,20},{5,21},{6,22},{7,23},{8,24},{9,... | collective-permute-start | bytes 2506760 | tf_op jit(solution)/shard_map/ppermute | solution.py:69
  45.6 95.9 %collective-permute-start = (bf16[272,1536]{1,0:T(8,128)(2,1)}, bf16[272,1536]{1,0:T(8,128)(2,1)}, u32[]{:S(2)}, u32[]{:S(2)}) collective-permute-start(bf16[272,1536]{1,0:T(8,128)(2,1)} %fusion.13), channel_id=1, source_target_pairs={{0,8},{1,9},{2,10},{3,11},{4,12},{5,13},{6,14},{7,15},{8,0},{9,1},... | collective-permute-start | bytes 2506760 | tf_op jit(solution)/shard_map/ppermute | solution.py:69
  67.6 83.9 %collective-permute-start.25 = (bf16[3,288,1536]{2,1,0:T(8,128)(2,1)}, bf16[3,288,1536]{2,1,0:T(8,128)(2,1)}, u32[]{:S(2)}, u32[]{:S(2)}) collective-permute-start(bf16[3,288,1536]{2,1,0:T(8,128)(2,1)} %collective-permute-done.24), channel_id=1, source_target_pairs={{1,2},{2,3},{5,4},{6,5},{9,10},{10,11},{13,12},{14,13},{17,18},{18... | collective-permute-start | bytes 7962632 | tf_op jit(solution)/shard_map/ppermute | solution.py:69
  76.1 85.1 %collective-permute-start.11 = (bf16[2,384,1664]{2,1,0:T(8,128)(2,1)}, bf16[2,384,1664]{2,1,0:T(8,128)(2,1)}, u32[]{:S(2)}, u32[]{:S(2)}) collective-permute-start(bf16[2,384,1664]{2,1,0:T(8,128)(2,1)} %pad_maximum_fusion.5), channel_id=1, source_target_pairs={{0,4},{1,5},{2,6},{3,7},{4,0},{5,1},{6,2},{7,3},{8,12},{9,13},{10,... | collective-permute-start | bytes 7667720 | tf_op jit(solution)/shard_map/ppermute | solution.py:69
  108.6 21.9 %collective-permute-start.5 = (bf16[2,384]{1,0:T(2,128)(2,1)S(1)}, bf16[2,384]{1,0:T(2,128)(2,1)S(1)}, u32[]{:S(2)}, u32[]{:S(2)}) collective-permute-start(bf16[2,384]{1,0:T(2,128)(2,1)S(1)} %copy-done.33), channel_id=1, source_target_pairs={{0,2},{1,3},{2,0},{3,1},{4,6},{5,7},{6,4},{7,5},{8,10},{9,11},{10,... | collective-permute-start | bytes 4616 | tf_op jit(solution)/shard_map/ppermute | solution.py:69
  136.8 65.4 %collective-permute-start.27 = (bf16[3,288,1536]{2,1,0:T(8,128)(2,1)}, bf16[3,288,1536]{2,1,0:T(8,128)(2,1)}, u32[]{:S(2)}, u32[]{:S(2)}) collective-permute-start(bf16[3,288,1536]{2,1,0:T(8,128)(2,1)} %pad_maximum_fusion.4), channel_id=1, source_target_pairs={{1,0},{6,7},{9,8},{14,15},{17,16},{22,23},{25,24},{30,31}} | collective-permute-start | bytes 7962632 | tf_op jit(solution)/shard_map/ppermute | solution.py:69
  151.5 50.7 %collective-permute-start.26 = (bf16[3,288,1536]{2,1,0:T(8,128)(2,1)}, bf16[3,288,1536]{2,1,0:T(8,128)(2,1)}, u32[]{:S(2)}, u32[]{:S(2)}) collective-permute-start(bf16[3,288,1536]{2,1,0:T(8,128)(2,1)} %collective-permute-done.25), channel_id=1, source_target_pairs={{2,3},{5,4},{10,11},{13,12},{18,19},{21,20},{26,27},{29,28}} | collective-permute-start | bytes 7962632 | tf_op jit(solution)/shard_map/ppermute | solution.py:69
  199.9 19.8 %collective-permute-start.14 = (bf16[256,1536]{1,0:T(8,128)(2,1)S(1)}, bf16[256,1536]{1,0:T(8,128)(2,1)S(1)}, u32[]{:S(2)}, u32[]{:S(2)}) collective-permute-start(bf16[256,1536]{1,0:T(8,128)(2,1)S(1)} %pad_maximum_fusion.9), channel_id=1, source_target_pairs={{0,16},{1,17},{2,18},{3,19},{4,20},{5,21},{6,22},{7,23},{8,24},{9,... | collective-permute-start | bytes 2359304 | tf_op jit(solution)/shard_map/ppermute | solution.py:69
  207.2 69.8 %collective-permute-start.28 = (bf16[3,576,1536]{2,1,0:T(8,128)(2,1)S(1)}, bf16[3,576,1536]{2,1,0:T(8,128)(2,1)S(1)}, u32[]{:S(2)}, u32[]{:S(2)}) collective-permute-start(bf16[3,576,1536]{2,1,0:T(8,128)(2,1)S(1)} %pad_maximum_fusion.1), channel_id=1, source_target_pairs={{0,4},{1,5},{2,6},{3,7},{4,0},{5,1},{6,2},{7,3},{8,12},{9,13},{10,... | collective-permute-start | bytes 15925256 | tf_op jit(solution)/shard_map/ppermute | solution.py:69
  217.6 20.0 %collective-permute-start.20 = (bf16[256,1536]{1,0:T(8,128)(2,1)S(1)}, bf16[256,1536]{1,0:T(8,128)(2,1)S(1)}, u32[]{:S(2)}, u32[]{:S(2)}) collective-permute-start(bf16[256,1536]{1,0:T(8,128)(2,1)S(1)} %get-tuple-element.66), channel_id=1, source_target_pairs={{0,8},{1,9},{2,10},{3,11},{4,12},{5,13},{6,14},{7,15},{8,0},{9,1},... | collective-permute-start | bytes 2359304 | tf_op jit(solution)/shard_map/ppermute | solution.py:69
  217.6 28.4 %collective-permute-start.21 = (bf16[256,1536]{1,0:T(8,128)(2,1)S(1)}, bf16[256,1536]{1,0:T(8,128)(2,1)S(1)}, u32[]{:S(2)}, u32[]{:S(2)}) collective-permute-start(bf16[256,1536]{1,0:T(8,128)(2,1)S(1)} %get-tuple-element.66), channel_id=1, source_target_pairs={{0,16},{1,17},{2,18},{3,19},{4,20},{5,21},{6,22},{7,23},{8,24},{9,... | collective-permute-start | bytes 2359304 | tf_op jit(solution)/shard_map/ppermute | solution.py:69
  230.8 15.4 %collective-permute-start.15 = (bf16[128,1536]{1,0:T(8,128)(2,1)S(1)}, bf16[128,1536]{1,0:T(8,128)(2,1)S(1)}, u32[]{:S(2)}, u32[]{:S(2)}) collective-permute-start(bf16[128,1536]{1,0:T(8,128)(2,1)S(1)} %get-tuple-element.92), channel_id=1, source_target_pairs={{0,8},{1,9},{2,10},{3,11},{4,12},{5,13},{6,14},{7,15},{8,0},{9,1},... | collective-permute-start | bytes 1179656 | tf_op jit(solution)/shard_map/ppermute | solution.py:69
  237.6 16.6 %collective-permute-start.22 = (bf16[128,1536]{1,0:T(8,128)(2,1)S(1)}, bf16[128,1536]{1,0:T(8,128)(2,1)S(1)}, u32[]{:S(2)}, u32[]{:S(2)}) collective-permute-start(bf16[128,1536]{1,0:T(8,128)(2,1)S(1)} %slice.296), channel_id=1, source_target_pairs={{0,16},{1,17},{2,18},{3,19},{4,20},{5,21},{6,22},{7,23},{8,24},{9,... | collective-permute-start | bytes 1179656 | tf_op jit(solution)/shard_map/ppermute | solution.py:69
  247.9 21.0 %collective-permute-start.16 = (bf16[256,1536]{1,0:T(8,128)(2,1)S(1)}, bf16[256,1536]{1,0:T(8,128)(2,1)S(1)}, u32[]{:S(2)}, u32[]{:S(2)}) collective-permute-start(bf16[256,1536]{1,0:T(8,128)(2,1)S(1)} %get-tuple-element.68), channel_id=1, source_target_pairs={{0,8},{1,9},{2,10},{3,11},{4,12},{5,13},{6,14},{7,15},{8,0},{9,1},... | collective-permute-start | bytes 2359304 | tf_op jit(solution)/shard_map/ppermute | solution.py:69
  249.9 19.1 %collective-permute-start.17 = (bf16[256,1536]{1,0:T(8,128)(2,1)S(1)}, bf16[256,1536]{1,0:T(8,128)(2,1)S(1)}, u32[]{:S(2)}, u32[]{:S(2)}) collective-permute-start(bf16[256,1536]{1,0:T(8,128)(2,1)S(1)} %get-tuple-element.68), channel_id=1, source_target_pairs={{0,16},{1,17},{2,18},{3,19},{4,20},{5,21},{6,22},{7,23},{8,24},{9,... | collective-permute-start | bytes 2359304 | tf_op jit(solution)/shard_map/ppermute | solution.py:69
  353.9 19.9 %collective-permute-start.29 = (bf16[256,1536]{1,0:T(8,128)(2,1)}, bf16[256,1536]{1,0:T(8,128)(2,1)}, u32[]{:S(2)}, u32[]{:S(2)}) collective-permute-start(bf16[256,1536]{1,0:T(8,128)(2,1)} %pad_maximum_fusion.10), channel_id=1, source_target_pairs={{0,8},{1,9},{2,10},{3,11},{4,12},{5,13},{6,14},{7,15},{8,0},{9,1},... | collective-permute-start | bytes 2359304 | tf_op jit(solution)/shard_map/ppermute | solution.py:69
  366.6 57.2 %collective-permute-start.42 = (bf16[3,288,1536]{2,1,0:T(8,128)(2,1)S(1)}, bf16[3,288,1536]{2,1,0:T(8,128)(2,1)S(1)}, u32[]{:S(2)}, u32[]{:S(2)}) collective-permute-start(bf16[3,288,1536]{2,1,0:T(8,128)(2,1)S(1)} %get-tuple-element.75), channel_id=1, source_target_pairs={{3,2},{4,5},{11,10},{12,13},{19,18},{20,21},{27,26},{28,29}} | collective-permute-start | bytes 7962632 | tf_op jit(solution)/shard_map/ppermute | solution.py:69
  368.3 20.2 %collective-permute-start.33 = (bf16[256,1536]{1,0:T(8,128)(2,1)S(1)}, bf16[256,1536]{1,0:T(8,128)(2,1)S(1)}, u32[]{:S(2)}, u32[]{:S(2)}) collective-permute-start(bf16[256,1536]{1,0:T(8,128)(2,1)S(1)} %pad_maximum_fusion.12), channel_id=1, source_target_pairs={{0,8},{1,9},{2,10},{3,11},{4,12},{5,13},{6,14},{7,15},{8,0},{9,1},... | collective-permute-start | bytes 2359304 | tf_op jit(solution)/shard_map/ppermute | solution.py:69
  369.7 21.6 %collective-permute-start.31 = (bf16[256,1536]{1,0:T(8,128)(2,1)S(1)}, bf16[256,1536]{1,0:T(8,128)(2,1)S(1)}, u32[]{:S(2)}, u32[]{:S(2)}) collective-permute-start(bf16[256,1536]{1,0:T(8,128)(2,1)S(1)} %pad_maximum_fusion.11), channel_id=1, source_target_pairs={{0,16},{1,17},{2,18},{3,19},{4,20},{5,21},{6,22},{7,23},{8,24},{9,... | collective-permute-start | bytes 2359304 | tf_op jit(solution)/shard_map/ppermute | solution.py:69
  370.5 56.6 %collective-permute-start.35 = (bf16[256,1536]{1,0:T(8,128)(2,1)S(1)}, bf16[256,1536]{1,0:T(8,128)(2,1)S(1)}, u32[]{:S(2)}, u32[]{:S(2)}) collective-permute-start(bf16[256,1536]{1,0:T(8,128)(2,1)S(1)} %pad_maximum_fusion.13), channel_id=1, source_target_pairs={{0,16},{1,17},{2,18},{3,19},{4,20},{5,21},{6,22},{7,23},{8,24},{9,... | collective-permute-start | bytes 2359304 | tf_op jit(solution)/shard_map/ppermute | solution.py:69
  374.9 37.8 %collective-permute-start.30 = (bf16[128,1536]{1,0:T(8,128)(2,1)S(1)}, bf16[128,1536]{1,0:T(8,128)(2,1)S(1)}, u32[]{:S(2)}, u32[]{:S(2)}) collective-permute-start(bf16[128,1536]{1,0:T(8,128)(2,1)S(1)} %add_convert_fusion.6), channel_id=1, source_target_pairs={{0,16},{1,17},{2,18},{3,19},{4,20},{5,21},{6,22},{7,23},{8,24},{9,... | collective-permute-start | bytes 1179656 | tf_op jit(solution)/shard_map/ppermute | solution.py:69
  389.3 37.9 %collective-permute-start.34 = (bf16[128,1536]{1,0:T(8,128)(2,1)}, bf16[128,1536]{1,0:T(8,128)(2,1)S(1)}, u32[]{:S(2)}, u32[]{:S(2)}) collective-permute-start(bf16[128,1536]{1,0:T(8,128)(2,1)} %add_convert_fusion.4), channel_id=1, source_target_pairs={{0,16},{1,17},{2,18},{3,19},{4,20},{5,21},{6,22},{7,23},{8,24},{9,... | collective-permute-start | bytes 1179656 | tf_op jit(solution)/shard_map/ppermute | solution.py:69
  414.0 65.8 %collective-permute-start.45 = (bf16[3,288,1536]{2,1,0:T(8,128)(2,1)S(1)}, bf16[3,288,1536]{2,1,0:T(8,128)(2,1)S(1)}, u32[]{:S(2)}, u32[]{:S(2)}) collective-permute-start(bf16[3,288,1536]{2,1,0:T(8,128)(2,1)S(1)} %get-tuple-element.76), channel_id=1, source_target_pairs={{0,1},{3,2},{4,5},{7,6},{8,9},{11,10},{12,13},{15,14},{16,17},{19,... | collective-permute-start | bytes 7962632 | tf_op jit(solution)/shard_map/ppermute | solution.py:69
  424.5 55.3 %collective-permute-start.43 = (bf16[3,288,1536]{2,1,0:T(8,128)(2,1)S(1)}, bf16[3,288,1536]{2,1,0:T(8,128)(2,1)}, u32[]{:S(2)}, u32[]{:S(2)}) collective-permute-start(bf16[3,288,1536]{2,1,0:T(8,128)(2,1)S(1)} %fusion.3), channel_id=1, source_target_pairs={{2,1},{5,6},{10,9},{13,14},{18,17},{21,22},{26,25},{29,30}} | collective-permute-start | bytes 7962632 | tf_op jit(solution)/shard_map/ppermute | solution.py:69
  441.8 46.3 %collective-permute-start.37 = (bf16[256,1536]{1,0:T(8,128)(2,1)}, bf16[256,1536]{1,0:T(8,128)(2,1)S(1)}, u32[]{:S(2)}, u32[]{:S(2)}) collective-permute-start(bf16[256,1536]{1,0:T(8,128)(2,1)} %get-tuple-element.63), channel_id=1, source_target_pairs={{0,8},{1,9},{2,10},{3,11},{4,12},{5,13},{6,14},{7,15},{8,0},{9,1},... | collective-permute-start | bytes 2359304 | tf_op jit(solution)/shard_map/ppermute | solution.py:69
  442.1 47.9 %collective-permute-start.38 = (bf16[256,1536]{1,0:T(8,128)(2,1)}, bf16[256,1536]{1,0:T(8,128)(2,1)S(1)}, u32[]{:S(2)}, u32[]{:S(2)}) collective-permute-start(bf16[256,1536]{1,0:T(8,128)(2,1)} %get-tuple-element.63), channel_id=1, source_target_pairs={{0,16},{1,17},{2,18},{3,19},{4,20},{5,21},{6,22},{7,23},{8,24},{9,... | collective-permute-start | bytes 2359304 | tf_op jit(solution)/shard_map/ppermute | solution.py:69
  484.5 57.3 %collective-permute-start.44 = (bf16[3,288,1536]{2,1,0:T(8,128)(2,1)}, bf16[3,288,1536]{2,1,0:T(8,128)(2,1)}, u32[]{:S(2)}, u32[]{:S(2)}) collective-permute-start(bf16[3,288,1536]{2,1,0:T(8,128)(2,1)} %get-tuple-element.73), channel_id=1, source_target_pairs={{1,0},{6,7},{9,8},{14,15},{17,16},{22,23},{25,24},{30,31}} | collective-permute-start | bytes 7962632 | tf_op jit(solution)/shard_map/ppermute | solution.py:69
  485.8 56.0 %collective-permute-start.46 = (bf16[3,288,1536]{2,1,0:T(8,128)(2,1)S(1)}, bf16[3,288,1536]{2,1,0:T(8,128)(2,1)}, u32[]{:S(2)}, u32[]{:S(2)}) collective-permute-start(bf16[3,288,1536]{2,1,0:T(8,128)(2,1)S(1)} %get-tuple-element.74), channel_id=1, source_target_pairs={{2,1},{5,6},{10,9},{13,14},{18,17},{21,22},{26,25},{29,30}} | collective-permute-start | bytes 7962632 | tf_op jit(solution)/shard_map/ppermute | solution.py:69
  (54 other events, 579.1 us)

commit v4 on v3

--- a/solution.py
+++ b/solution.py
@@ -243,70 +243,20 @@
     return proj, out, gates, small
 
 
-def mixer_forward_kernel(width, x_ref, pos_ref, w_ref, out_ref, p_ref, state_ref, low_ref, acc_ref):
-    head = pl.program_id(0)
-    block = pl.program_id(1)
-    slots = x_ref.shape[0]
-    proj, out, gates, small = weight_views(w_ref, width)
-    position = pos_ref[...]
-    projected = dot_rows(x_ref[...], proj)
-    p_ref[0] = projected
+def slot_position(starts):
+    slot = lax.broadcasted_iota(jnp.int32, (starts.shape[0], 1), 0)
+    return slot - starts[:, 0:1].astype(wide).astype(jnp.int32)
+
+
+def mixer_step(x, position, views, width):
+    proj, out, gates, small = views
+    projected = dot_rows(x, proj)
     conv_out, _, _, _, input_gate, _, decay, _, root = mixer_parts(
         projected[:, :width], position, small, gates
     )
     states = scan_slots(decay, root * input_gate * conv_out, shift_down)
-    state_ref[0] = states
     mixed_low = (states * gelu_parts(projected[:, width:])[0]).astype(low_type)
-    low_ref[0] = mixed_low
-    part = dot_plain(mixed_low, out)
-    rows = pl.ds(pl.multiple_of(block * slots, slots), slots)
-
-    @pl.when(head == 0)
-    def _():
-        acc_ref[rows, :] = part
-
-    @pl.when(head > 0)
-    def _():
-        acc_ref[rows, :] += part
-
-    @pl.when(head == pl.num_programs(0) - 1)
-    def _():
-        out_ref[rows, :] = acc_ref[rows, :].astype(low_type)
-
-
-def mix_forward(mix_in, position, weights, slots, width):
-    rows, model = mix_in.shape
-    heads = weights.shape[0]
-    blocks = rows // slots
-    return pl.pallas_call(
-        functools.partial(mixer_forward_kernel, width),
-        grid=(heads, blocks),
-        in_specs=[
-            pl.BlockSpec((slots, model), lambda h, b: (b, 0)),
-            pl.BlockSpec((slots, 1), lambda h, b: (b, 0)),
-            pl.BlockSpec((1,) + weights.shape[1:], lambda h, b: (h, 0, 0)),
-        ],
-        out_specs=[
-            pl.BlockSpec((rows, model), lambda h, b: (0, 0)),
-            pl.BlockSpec((1, slots, 2 * width), lambda h, b: (h, b, 0)),
-            pl.BlockSpec((1, slots, width), lambda h, b: (h, b, 0)),
-            pl.BlockSpec((1, slots, width), lambda h, b: (h, b, 0)),
-        ],
-        out_shape=[
-            jax.ShapeDtypeStruct((rows, model), low_type),
-            jax.ShapeDtypeStruct((heads, rows, 2 * width), wide),
-            jax.ShapeDtypeStruct((heads, rows, width), wide),
-            jax.ShapeDtypeStruct((heads, rows, width), low_type),
-        ],
-        scratch_shapes=[pltpu.VMEM((rows, model), wide)],
-        compiler_params=pltpu.CompilerParams(vmem_limit_bytes=48 * 1024 * 1024),
-        cost_estimate=pl.CostEstimate(
-            flops=2 * rows * model * heads * width * 3,
-            bytes_accessed=heads * rows * width * 14 + weights.size * 2 + rows * model * 4,
-            transcendentals=heads * rows * width * 6,
-        ),
-        name="mixer_forward",
-    )(mix_in, position, weights)
+    return projected, states, mixed_low, dot_plain(mixed_low, out)
 
 
 def mixer_backward_kernel(
@@ -327,7 +277,7 @@
     block = pl.program_id(1)
     slots, model = x_ref.shape
     proj, out, gates, small = weight_views(w_ref, width)
-    position = pos_ref[...]
+    position = slot_position(pos_ref[...])
     first = p_ref[0, :, 0:width]
     res_low = res_ref[...]
     states = state_ref[0]
@@ -404,7 +354,7 @@
         in_specs=[
             pl.BlockSpec((slots, model), lambda h, b: (b, 0)),
             pl.BlockSpec((slots, model), lambda h, b: (b, 0)),
-            pl.BlockSpec((slots, 1), lambda h, b: (b, 0)),
+            pl.BlockSpec((slots, width), lambda h, b: (b, 0)),
             pl.BlockSpec((1,) + weights.shape[1:], lambda h, b: (h, 0, 0)),
             pl.BlockSpec((1, slots, 2 * width), lambda h, b: (h, b, 0)),
             pl.BlockSpec((1, slots, width), lambda h, b: (h, b, 0)),
@@ -557,6 +507,551 @@
             )
 
     pl.semaphore_wait(barrier, 10)
+
+
+class Gather:
+    def __init__(self, own, target, send, recv, member, z):
+        self.own, self.target = own, target
+        self.send, self.recv = send, recv
+        chip, core = member // 2, member % 2
+        self.to_x = peer_x(chip) * 2 + core
+        self.to_y = peer_y(chip) * 2 + core
+        self.z = z
+        self.half = own.shape[0] // 2
+
+    def copy(self, number):
+        low, high = pl.ds(0, self.half), pl.ds(self.half, self.half)
+        source, target, to = (
+            (self.own, self.target.at[1], self.to_x),
+            (self.own, self.target.at[2], self.to_y),
+            (self.target.at[1, low], self.target.at[3, low], self.to_y),
+            (self.target.at[2, high], self.target.at[3, high], self.to_x),
+        )[number]
+        return remote(source, target, self.send.at[number], self.recv.at[number], to, self.z)
+
+    def begin(self):
+        self.copy(0).start()
+        self.copy(1).start()
+
+    def relay(self):
+        self.copy(0).wait_recv()
+        self.copy(2).start()
+        self.copy(1).wait_recv()
+        self.copy(3).start()
+
+    def arrive(self):
+        self.copy(2).wait_recv()
+        self.copy(3).wait_recv()
+
+    def finish(self):
+        for number in range(4):
+            self.copy(number).wait_send()
+
+
+class Reduce:
+    def __init__(self, part, from_x, from_y, passing, last, send, recv, member, z):
+        self.part, self.from_x, self.from_y = part, from_x, from_y
+        self.passing, self.last = passing, last
+        self.send, self.recv = send, recv
+        chip, core = member // 2, member % 2
+        self.to_x = peer_x(chip) * 2 + core
+        self.to_y = peer_y(chip) * 2 + core
+        self.z = z
+        self.slots = part.shape[0] // 4
+        self.half = self.slots // 2
+
+    def copy(self, number):
+        slots, half = self.slots, self.half
+        source, target, to = (
+            (self.part.at[pl.ds(slots, half)], self.from_x.at[0], self.to_x),
+            (self.part.at[pl.ds(3 * slots, half)], self.from_x.at[1], self.to_x),
+            (self.part.at[pl.ds(2 * slots + half, half)], self.from_y.at[0], self.to_y),
+            (self.part.at[pl.ds(3 * slots + half, half)], self.from_y.at[1], self.to_y),
+            (self.passing.at[0], self.last.at[0], self.to_y),
+            (self.passing.at[1], self.last.at[1], self.to_x),
+        )[number]
+        return remote(source, target, self.send.at[number], self.recv.at[number], to, self.z)
+
+    def begin(self):
+        for number in (1, 3, 0, 2):
+            self.copy(number).start()
+
+    def relay(self):
+        slots, half = self.slots, self.half
+        self.copy(1).wait_recv()
+        self.passing[0] = (
+            self.part[2 * slots : 2 * slots + half].astype(wide) + self.from_x[1].astype(wide)
+        ).astype(low_type)
+        self.copy(4).start()
+        self.copy(3).wait_recv()
+        self.passing[1] = (
+            self.part[slots + half : 2 * slots].astype(wide) + self.from_y[1].astype(wide)
+        ).astype(low_type)
+        self.copy(5).start()
+
+    def arrive(self):
+        for number in (0, 2, 4, 5):
+            self.copy(number).wait_recv()
+
+    def result(self, number):
+        direct = self.from_x if number == 0 else self.from_y
+        return (
+            self.part[number * self.half : (number + 1) * self.half].astype(wide)
+            + direct[0].astype(wide)
+            + self.last[number].astype(wide)
+        )
+
+    def finish(self):
+        for number in range(6):
+            self.copy(number).wait_send()
+
+    @staticmethod
+    def scratch(slots, model):
+        return [pltpu.VMEM((2, slots // 2, model), low_type)] * 4
+
+
+def norm_rows(value, gain):
+    scale = lax.rsqrt(jnp.mean(value * value, axis=1, keepdims=True) + norm_eps)
+    return value * scale * gain
+
+
+def front_kernel(
+    sizes,
+    tokens_ref,
+    cot_ref,
+    gain_ref,
+    small_ref,
+    in_ref,
+    gate_ref,
+    out_ref,
+    up_ref,
+    down_ref,
+    mix_in,
+    weights,
+    ffn_weights,
+    saved_p,
+    saved_state,
+    saved_low,
+    starts_out,
+    residual_out,
+    ffn_in,
+    cot_out,
+    gains_out,
+    tokens_all,
+    raw_in,
+    raw_up,
+    turned,
+    gain_seen,
+    acc,
+    part,
+    from_x,
+    from_y,
+    passing,
+    last,
+    load_sem,
+    gain_send,
+    gain_recv,
+    m_send,
+    m_recv,
+    m_core_send,
+    m_core_recv,
+    f_send,
+    f_recv,
+    f_core_send,
+    f_core_recv,
+    g_send,
+    g_recv,
+    r_send,
+    r_recv,
+):
+    model, width, ffn_width = sizes
+    member = lax.axis_index("dp")
+    z = lax.axis_index("shard")
+    chip, core = member // 2, member % 2
+    end = z + core * (3 - 2 * z)
+    other = chip * 2 + 1 - core
+    slots = cot_ref.shape[0]
+    half_ffn = ffn_width // 2
+    owner = core == z // 2
+
+    window = 128 * ((chip * ffn_width) // 128)
+    skew = chip * ffn_width - window
+    quarter = pl.ds(pl.multiple_of(chip * width, width), width)
+    wide_window = pl.ds(pl.multiple_of(window, 128), raw_up.shape[2])
+
+    def loads():
+        found = []
+        for kind in range(2):
+            found.append((in_ref.at[kind, :, quarter], raw_in.at[kind]))
+            found.append(
+                (
+                    gate_ref.at[kind, chip],
+                    weights.at[end, pl.ds(kind * width, width), pl.ds(model, width)],
+                )
+            )
+        found.append((out_ref.at[quarter], weights.at[end, pl.ds(2 * width, width), pl.ds(0, model)]))
+        found.append(
+            (
+                small_ref.at[:, quarter],
+                weights.at[end, pl.ds(2 * width, 16), pl.ds(model, width)],
+            )
+        )
+        for kind in range(2):
+            found.append((up_ref.at[kind, :, wide_window], raw_up.at[kind]))
+        found.append(
+            (
+                down_ref.at[pl.ds(pl.multiple_of(chip * ffn_width, 32), ffn_width)],
+                ffn_weights.at[2, pl.ds(pl.multiple_of(end * ffn_width, 32), ffn_width)],
+            )
+        )
+        return [
+            pltpu.make_async_copy(source, target, load_sem.at[number])
+            for number, (source, target) in enumerate(found)
+        ]
+
+    def turned_copy(kind):
+        return pltpu.make_async_copy(
+            turned.at[kind, pl.ds(pl.multiple_of(skew, 32), ffn_width)],
+            ffn_weights.at[kind, pl.ds(pl.multiple_of(end * ffn_width, 32), ffn_width)],
+            load_sem.at[9 + kind],
+        )
+
+    @pl.when(owner)
+    def _():
+        for copy in loads():
+            copy.start()
+
+    enter(member, z)
+
+    gather_tokens = Gather(tokens_ref, tokens_all, g_send.at[0], g_recv.at[0], member, z)
+    gather_cot = Gather(cot_ref, cot_out, g_send.at[1], g_recv.at[1], member, z)
+    gather_ffn = Gather(ffn_in.at[0], ffn_in, g_send.at[2], g_recv.at[2], member, z)
+    reduce = Reduce(part, from_x, from_y, passing, last, r_send, r_recv, member, z)
+    own_cot = pltpu.make_async_copy(cot_ref, cot_out.at[0], load_sem.at[11])
+
+    gather_tokens.begin()
+    own_cot.start()
+
+    def gain_copy(to, slot):
+        return remote(
+            gain_ref, gain_seen.at[slot], gain_send.at[to], gain_recv.at[slot], member, to
+        )
+
+    for to in range(4):
+
+        @pl.when(to != z)
+        def _():
+            gain_copy(to, z).start()
+
+    gain_seen[z] = gain_ref[...]
+
+    def m_rows(number):
+        return pl.ds(number * width, width)
+
+    def m_copy(slot, number, way, to_end):
+        place = weights.at[slot, m_rows(number)]
+        return remote(
+            place,
+            place,
+            m_send.at[way, slot, number],
+            m_recv.at[slot, number],
+            member,
+            line_place(to_end, core),
+        )
+
+    def m_core(slot, number):
+        return remote(
+            weights.at[slot, m_rows(number)],
+            weights.at[2 + slot, m_rows(number)],
+            m_core_send.at[slot, number],
+            m_core_recv.at[slot, number],
+            other,
+            z,
+        )
+
+    def f_place(slot, number):
+        row = slot * ffn_width + (number % 2) * half_ffn
+        return ffn_weights.at[number // 2, pl.ds(row, half_ffn)]
+
+    def f_copy(slot, number, way, to_end):
+        place = f_place(slot, number)
+        return remote(
+            place,
+            place,
+            f_send.at[way, slot, number],
+            f_recv.at[slot, number],
+            member,
+            line_place(to_end, core),
+        )
+
+    def f_core(slot, number):
+        return remote(
+            f_place(slot, number),
+            f_place(2 + slot, number),
+            f_core_send.at[slot, number],
+            f_core_recv.at[slot, number],
+            other,
+            z,
+        )
+
+    def pass_on(copy, core_copy, slot, number):
+        if slot == 0:
+
+            @pl.when(end < 3)
+            def _():
+                copy(slot, number, 0, end + 1).start()
+        else:
+
+            @pl.when((end == 1) | (end == 2))
+            def _():
+                copy(slot, number, 0, end + 1).start()
+
+            @pl.when(end == 1)
+            def _():
+                copy(slot, number, 1, 0).start()
+
+        core_copy(slot, number).start()
+
+    @pl.when(owner)
+    def _():
+        for copy in loads()[:6]:
+            copy.wait()
+        for kind in range(2):
+            for at in range(model // 128):
+                weights[end, kind * width : (kind + 1) * width, at * 128 : (at + 1) * 128] = (
+                    raw_in[kind, at * 128 : (at + 1) * 128, :].astype(wide).T.astype(low_type)
+                )
+        for row in range(2 * width + 16, 3 * width, 16):
+            weights[end, row : row + 16, model:] = jnp.zeros((16, width), low_type)
+
+    for slot in range(2):
+
+        @pl.when(end == slot)
+        def _():
+            for number in range(3):
+                pass_on(m_copy, m_core, slot, number)
+
+    @pl.when(owner)
+    def _():
+        for copy in loads()[6:]:
+            copy.wait()
+        for kind in range(2):
+
+            def turn(at, carry):
+                columns = pl.ds(pl.multiple_of(at * 128, 128), 128)
+                for tile in range(raw_up.shape[2] // 128):
+                    turned[kind, tile * 128 : (tile + 1) * 128, columns] = (
+                        raw_up[kind, columns, tile * 128 : (tile + 1) * 128]
+                        .astype(wide)
+                        .T.astype(low_type)
+                    )
+                return carry
+
+            lax.fori_loop(0, model // 128, turn, 0)
+            turned_copy(kind).start()
+
+    gather_tokens.relay()
+
+    for number in range(3):
+        for slot in range(2):
+
+            @pl.when(end != slot)
+            def _():
+                m_copy(slot, number, 0, 0).wait_recv()
+                pass_on(m_copy, m_core, slot, number)
+
+    @pl.when(owner)
+    def _():
+        turned_copy(0).wait()
+        turned_copy(1).wait()
+
+    for slot in range(2):
+
+        @pl.when(end == slot)
+        def _():
+            for number in range(6):
+                pass_on(f_copy, f_core, slot, number)
+
+    def f_step(step):
+        slot, number = 1 - step % 2, step // 2
+
+        @pl.when((end != slot) & (end < 3))
+        def _():
+            f_copy(slot, number, 0, 0).wait_recv()
+            pass_on(f_copy, f_core, slot, number)
+
+    for to in range(4):
+
+        @pl.when(to != z)
+        def _():
+            gain_copy(to, to).wait_recv()
+
+    gains = jnp.concatenate([gain_seen[at].astype(wide) for at in range(4)], axis=1)
+    gains_out[...] = gains[0:8]
+    gather_tokens.arrive()
+
+    def norm_block(block):
+        if block == 0:
+            source, starts = tokens_ref[:, :model], tokens_ref[:, model:]
+        else:
+            source, starts = tokens_all[block, :, :model], tokens_all[block, :, model:]
+        at = slice(block * slots, (block + 1) * slots)
+        mix_in[at, :] = norm_rows(source.astype(wide), gains_out[0:1]).astype(low_type)
+        starts_out[at, :] = starts
+
+    for block in range(4):
+        norm_block(block)
+    gather_cot.begin()
+    for step in range(3):
+        f_step(step)
+
+    for head in range(4):
+        if head >= 2:
+            for number in range(3):
+                m_core(head - 2, number).wait_recv()
+        views = weight_views(weights.at[pl.ds(head, 1)], width)
+
+        def step_block(block, carry):
+            rows = pl.ds(pl.multiple_of(block * slots, slots), slots)
+            position = slot_position(starts_out[rows, :])
+            projected, states, mixed_low, product = mixer_step(
+                mix_in[rows, :], position, views, width
+            )
+            saved_p[head, rows, :] = projected
+            saved_state[head, rows, :] = states
+            saved_low[head, rows, :] = mixed_low
+            if head == 0:
+                acc[rows, :] = product
+            elif head < 3:
+                acc[rows, :] += product
+            else:
+                part[rows, :] = (acc[rows, :] + product).astype(low_type)
+            return carry
+
+        lax.fori_loop(0, 4, step_block, 0)
+        f_step(2 * head + 3)
+        if head < 3:
+            f_step(2 * head + 4)
+        if head == 0:
+            gather_cot.relay()
+        if head == 3:
+            reduce.begin()
+
+    f_step(10)
+    f_step(11)
+    reduce.relay()
+    reduce.arrive()
+    half = slots // 2
+    for number in range(2):
+        at = slice(number * half, (number + 1) * half)
+        residual = tokens_ref[at, :model].astype(wide) + reduce.result(number)
+        residual_out[at, :] = residual
+        ffn_in[0, at, :] = norm_rows(residual, gains_out[1:2]).astype(low_type)
+    gather_ffn.begin()
+    gather_ffn.relay()
+
+    @pl.when(end == 3)
+    def _():
+        for number in range(6):
+            for slot in (1, 0):
+                f_copy(slot, number, 0, 0).wait_recv()
+                f_core(slot, number).start()
+
+    gather_ffn.arrive()
+    gather_cot.arrive()
+    own_cot.wait()
+    for slot in range(2):
+        for number in range(6):
+            f_core(slot, number).wait_recv()
+
+    for gather in (gather_tokens, gather_cot, gather_ffn, reduce):
+        gather.finish()
+    for to in range(4):
+
+        @pl.when(to != z)
+        def _():
+            gain_copy(to, z).wait_send()
+
+    for copy, core_copy, count in ((m_copy, m_core, 3), (f_copy, f_core, 6)):
+        for number in range(count):
+            for slot in range(2):
+                core_copy(slot, number).wait_send()
+
+            @pl.when(end < 3)
+            def _():
+                copy(0, number, 0, 0).wait_send()
+
+            @pl.when((end == 1) | (end == 2))
+            def _():
+                copy(1, number, 0, 0).wait_send()
+
+            @pl.when(end == 1)
+            def _():
+                copy(1, number, 1, 0).wait_send()
+
+
+def front(tokens, cot, gains, small, in_proj, gates, out_proj, gate_up, down, sizes):
+    model, width, ffn_width = sizes
+    slots = cot.shape[0]
+    rows = 4 * slots
+    dma = pltpu.SemaphoreType.DMA
+    vmem = pl.BlockSpec(memory_space=pltpu.VMEM)
+    anywhere = pl.BlockSpec(memory_space=pl.ANY)
+    window = -(-ffn_width // 128) * 128
+    return pl.pallas_call(
+        functools.partial(front_kernel, sizes),
+        in_specs=[vmem] * 3 + [anywhere] * 6,
+        out_specs=[vmem, vmem, anywhere, vmem, vmem, vmem, vmem, vmem, vmem, anywhere, vmem],
+        out_shape=[
+            jax.ShapeDtypeStruct((rows, model), low_type),
+            jax.ShapeDtypeStruct((4, 3 * width, model + width), low_type),
+            jax.ShapeDtypeStruct((3, 4 * ffn_width, model), low_type),
+            jax.ShapeDtypeStruct((4, rows, 2 * width), wide),
+            jax.ShapeDtypeStruct((4, rows, width), wide),
+            jax.ShapeDtypeStruct((4, rows, width), low_type),
+            jax.ShapeDtypeStruct((rows, width), low_type),
+            jax.ShapeDtypeStruct((slots, model), wide),
+            jax.ShapeDtypeStruct((4, slots, model), low_type),
+            jax.ShapeDtypeStruct((4, slots, model), low_type),
+            jax.ShapeDtypeStruct((8, model), wide),
+        ],
+        scratch_shapes=[
+            pltpu.VMEM((4, slots, model + width), low_type),
+            pltpu.VMEM((2, model, width), low_type),
+            pltpu.VMEM((2, model, window), low_type),
+            pltpu.VMEM((2, window, model), low_type),
+            pltpu.VMEM((4, 16, model // 4), low_type),
+            pltpu.VMEM((rows, model), wide),
+            pltpu.VMEM((rows, model), low_type),
+        ]
+        + Reduce.scratch(slots, model)
+        + [
+            dma((12,)),
+            dma((4,)),
+            dma((4,)),
+            dma((2, 2, 3)),
+            dma((2, 3)),
+            dma((2, 3)),
+            dma((2, 3)),
+            dma((2, 2, 6)),
+            dma((2, 6)),
+            dma((2, 6)),
+            dma((2, 6)),
+            dma((3, 4)),
+            dma((3, 4)),
+            dma((6,)),
+            dma((6,)),
+        ],
+        compiler_params=pltpu.CompilerParams(
+            collective_id=3, has_side_effects=True, vmem_limit_bytes=60 * 1024 * 1024
+        ),
+        cost_estimate=pl.CostEstimate(
+            flops=2 * rows * model * 4 * width * 3,
+            bytes_accessed=6 * ffn_width * 4 * model,
+            transcendentals=rows * 4 * width * 6,
+        ),
+        name="front",
+    )(tokens, cot, gains, small, in_proj, gates, out_proj, gate_up, down)
 
 
 class Scatter:
@@ -1478,57 +1973,37 @@
     stream = tokens.astype(wide)
     grad_stream = cotangent.astype(wide) * mask_rows
 
-    def quarter(value, dim, count):
-        return lax.dynamic_slice_in_dim(value, chip * count, count, axis=dim)
-
-    own_proj = quarter(input_proj, 2, width).transpose(0, 2, 1).reshape(2 * width, model)
-    own_out = quarter(output_proj, 0, width)
-    own_gates = quarter(gate_blocks, 1, 1).reshape(2 * width, width)
-    own_small = jnp.concatenate(
-        [
-            quarter(conv_taps, 1, width),
-            quarter(gate_bias, 1, width),
-            quarter(decay_param[None], 1, width),
-            jnp.zeros((width - 8, width), low_type),
-        ]
-    )
-    own_mix = jnp.concatenate(
-        [
-            jnp.concatenate([own_proj, own_out]),
-            jnp.concatenate([own_gates, own_small]),
-        ],
-        axis=1,
-    )
-    own_ffn = jnp.concatenate(
-        [
-            quarter(ffn_gate_up, 2, ffn_width).transpose(0, 2, 1),
-            quarter(ffn_down, 0, ffn_width)[None],
-        ]
-    )
-
-    gains = all_slices(norm_gains, z).astype(wide)
-
-    start_row = jnp.zeros((16, model), low_type).at[0, :slots].set(seq_start.astype(low_type))
-    gathered = plane_gather(jnp.concatenate([tokens, start_row]))
-    starts = jnp.stack([block[slots, :slots] for block in gathered]).astype(jnp.int32)
-    position = (jnp.arange(slots, dtype=jnp.int32)[None] - starts).reshape(-1, 1)
-    all_tokens = jnp.concatenate([block[:slots] for block in gathered])
-    mix_in = rms_scale(all_tokens.astype(wide), gains[0]).astype(low_type)
-
-    mix_a, mix_b = line_spread(own_mix, end)
-    mix_pair = jnp.stack([mix_a, mix_b])
-    mix_weights = jnp.concatenate([mix_pair, move(mix_pair, core_pairs)])
-
-    ffn_a, ffn_b = line_spread(own_ffn, end)
-    ffn_pair = jnp.concatenate([ffn_a, ffn_b], axis=1)
-    ffn_weights = jnp.concatenate([ffn_pair, move(ffn_pair, core_pairs)], axis=1)
-
-    all_grad_out = jnp.concatenate(plane_gather(grad_stream.astype(low_type)))
-
-    mix_part, *saved = mix_forward(mix_in, position, mix_weights, slots, width)
-    residual = stream + plane_reduce(mix_part)
-    normed_two, second_pull = jax.vjp(rms_scale, residual, gains[1])
-    ffn_in = jnp.concatenate(plane_gather(normed_two.astype(low_type)))
+    starts = jnp.broadcast_to(seq_start.astype(low_type)[:, None], (slots, width))
+    (
+        mix_in,
+        mix_weights,
+        ffn_weights,
+        saved_p,
+        saved_state,
+        saved_low,
+        all_starts,
+        residual,
+        ffn_in,
+        all_grad_out,
+        gains,
+    ) = front(
+        jnp.concatenate([tokens, starts], axis=1),
+        grad_stream.astype(low_type),
+        jnp.concatenate([norm_gains, jnp.zeros((14, norm_gains.shape[1]), low_type)]),
+        jnp.concatenate(
+            [conv_taps, gate_bias, decay_param[None], jnp.zeros((8, slice_rec), low_type)]
+        ),
+        input_proj,
+        gate_blocks,
+        output_proj,
+        ffn_gate_up,
+        ffn_down,
+        (model, width, ffn_width),
+    )
+    saved = (saved_p, saved_state, saved_low)
+    ffn_in = ffn_in.reshape(4 * slots, model)
+    all_grad_out = all_grad_out.reshape(4 * slots, model)
+    _, second_pull = jax.vjp(rms_scale, residual, gains[1])
 
     grad_ffn, ffn_part, ffn_in_part = ffn_both(
         ffn_in, all_grad_out, ffn_weights, slots, ffn_width * 4 // 3
@@ -1539,7 +2014,7 @@
     block_out = (mask_rows * (residual + plane_reduce(ffn_part))).astype(low_type)
 
     grad_mix, mix_in_part = mix_backward(
-        mix_in, res_low, position, mix_weights, saved, slots, width
+        mix_in, res_low, all_starts, mix_weights, saved, slots, width
     )
     both = 2 * ffn_width
     pair_ffn = add_low(grad_ffn[:, :both], move(grad_ffn[:, both:], core_pairs))

time: 800 us -> 679 us (0.85)
  Pallas kernels: 354 us -> 501 us
  waiting for transfers between devices: 182 us -> 80.3 us
  starting transfers between devices: 118 us -> 21.9 us
  other arithmetic: 68.2 us -> 29.9 us
  local copies, waits for them, and re-layouts: 69.3 us -> 36.7 us
    pallas_call x1, Pallas kernels: 32.5 us -> 178 us  [front(): pl.pallas_call(functools.partial(front_kernel, sizes), in_specs=[vmem] *...]
    ppermute x47 -> x18, waiting for transfers between devices: 182 us -> 80.3 us  [move(): return lax.ppermute(value, axes, pairs)]
    ppermute x47 -> x18, starting transfers between devices: 118 us -> 21.9 us  [move(): return lax.ppermute(value, axes, pairs)]
    concatenate x6 -> x2, other arithmetic: 21 us -> 2.78 us  [the longest x1 2.1 us: group_body(): jnp.concatenate([tokens, starts], axis=1)]
    dynamic_slice x6 -> x0, local copies, waits for them, and re-layouts: 10.3 us -> none  [quarter(): return lax.dynamic_slice_in_dim(value, chip * count, count, axis=dim)]
    unnamed x97 -> x56, local copies, waits for them, and re-layouts: 37.8 us -> 29.9 us
  transfers between devices with their start and end apart: 47 -> 18, of which waited for: 22 -> 9; matrix products, arithmetic and copies ran while one was open for 9% -> 4% of each run, Pallas kernels for 9% -> 6%
where the time goes in v4:
time: 679 us; the launch traced here: 671 us
  Pallas kernels  501 us (74%)
  waiting for transfers between devices  80.3 us (12%)
  local copies, waits for them, and re-layouts  36.7 us (5%)
  other arithmetic  29.9 us (4%)
  starting transfers between devices  21.9 us (3%)
    pallas_call x1, Pallas kernels, front(): pl.pallas_call(functools.partial(front_kernel, sizes), in_specs=[vmem] *...  178 us
    pallas_call x1, Pallas kernels, tail(): pl.pallas_call(functools.partial(tail_kernel, (model, width, ffn_width, p...  154 us
    ppermute x18, waiting for transfers between devices, move(): return lax.ppermute(value, axes, pairs)  80.3 us
    pallas_call x1, Pallas kernels, sums(): pl.pallas_call(functools.partial(sums_kernel, sizes), in_specs=[vmem, vme...  68.4 us
    pallas_call x1, Pallas kernels, ffn_both(): pl.pallas_call(ffn_kernel, grid=(hidden // tile, rows // slots), in_specs...  58.9 us
    pallas_call x1, Pallas kernels, mix_backward(): pl.pallas_call(functools.partial(mixer_backward_kernel, width), grid=(hea...  41.8 us
    unnamed x56, local copies, waits for them, and re-layouts  29.9 us
    ppermute x18, starting transfers between devices, move(): return lax.ppermute(value, axes, pairs)  21.9 us
  transfers between devices with their start and end apart: 18, of which 9 were waited for; matrix products, arithmetic and copies ran while one was open for 4% of the time, Pallas kernels for 6%

profile of v4, /device:TPU:0, one launch (start us, length us, event | category | flops | bytes accessed | tf_op | source)
XLA Modules:
  0.0 670.8 jit_solution(16183697600211260337)
XLA Ops:
  2.7 2.2 fusion.7.cot_ref
  5.0 2.1 pad_maximum_fusion.1.tokens_ref
  8.5 177.5 %front.1 = (bf16[1024,1536]{1,0:T(8,128)(2,1)}, bf16[4,384,1664]{2,1,0:T(8,128)(2,1)}, bf16[3,1152,1536]{2,1,0:T(8,128)(2,1)}, f32[4,1024,256]{2,1,0:T(8,128)}, ...) custom-call(bf16[256,1664]{1,0:T(8,128)(2,1)} %pad_maximum_fusion.1., ...), custom_call_target="tpu_custom_call" | custom-call | flops 4831838208 | bytes 10616832 | tf_op jit(solution)/shard_map/front/pallas_call | solution.py:1001
  186.1 58.9 %ffn_both.1 = (bf16[3,1152,1536]{2,1,0:T(8,128)(2,1)}, bf16[1024,1536]{1,0:T(8,128)(2,1)}, bf16[1024,1536]{1,0:T(8,128)(2,1)}) custom-call(bf16[1024,1536]{1,0:T(8,128)(2,1)} %bitcast.6, bf16[1024,1536]{1,0:T(8,128)(2,1)} %bitcast.7, bf16[3,1152,1536]{2,1,0:T(8,128)(2,1)} %get-tuple-element.37.w_ref), custom_call_target="tpu_custom_call" | custom-call | flops 32614907904 | bytes 46399488 | tf_op jit(solution)/shard_map/ffn_both/pallas_call | solution.py:435
  245.0 3.0 slice.148
  249.5 2.2 collective-permute-start
  252.7 4.1 collective-permute-done.12
  256.8 4.0 add_convert_fusion
  262.1 2.5 copy-done.13
  264.8 2.3 collective-permute-start.4
  268.3 1.9 collective-permute-done
  270.4 2.1 collective-permute-start.1
  272.5 14.1 %collective-permute-done.4 = bf16[256,1536]{1,0:T(8,128)(2,1)S(1)} collective-permute-done((bf16[256,1536]{1,0:T(8,128)(2,1)S(1)}, bf16[256,1536]{1,0:T(8,128)(2,1)S(1)}, u32[]{:S(2)}, u32[]{:S(2)}) %collective-permute-start.4) | collective-permute-done | bytes 786464 | tf_op jit(solution)/shard_map/ppermute | solution.py:69
  286.8 1.8 collective-permute-start.5
  288.6 10.0 %collective-permute-done.1 = bf16[128,1536]{1,0:T(8,128)(2,1)S(1)} collective-permute-done((bf16[128,1536]{1,0:T(8,128)(2,1)S(1)}, bf16[128,1536]{1,0:T(8,128)(2,1)S(1)}, u32[]{:S(2)}, u32[]{:S(2)}) %collective-permute-start.1) | collective-permute-done | bytes 393248 | tf_op jit(solution)/shard_map/ppermute | solution.py:69
  302.1 2.4 collective-permute-start.14
  306.9 2.8 collective-permute-done.3
  310.8 6.4 collective-permute-done.7
  322.5 34.1 %collective-permute-done.16 = bf16[3,288,1536]{2,1,0:T(8,128)(2,1)S(1)} collective-permute-done((bf16[3,288,1536]{2,1,0:T(8,128)(2,1)S(1)}, bf16[3,288,1536]{2,1,0:T(8,128)(2,1)S(1)}, u32[]{:S(2)}, u32[]{:S(2)}) %collective-permute-start.16) | collective-permute-done | bytes 2654240 | tf_op jit(solution)/shard_map/ppermute | solution.py:69
  356.6 5.6 fusion.1
  363.5 2.2 collective-permute-start.17
  370.0 5.4 collective-permute-done.10
  376.9 41.8 %mixer_backward.1 = (bf16[4,384,1664]{2,1,0:T(8,128)(2,1)}, bf16[1024,1536]{1,0:T(8,128)(2,1)}) custom-call(bf16[1024,1536]{1,0:T(8,128)(2,1)} %get-tuple-element.39.x_ref, bf16[1024,1536]{1,0:T(8,128)(2,1)} %constant_dynamic-update-slice_fusion.res_ref, bf16[1024,128]{1,0:T(8,128)(2,1)S(1)} %copy-done.6, bf16[4,384,1664]{2,1,0:T(8,128)(2,1)} %get-tuple-element.43.w_ref, ...), custom_call_target="tpu_custom_call" | custom-call | flops 9663676416 | bytes 27000832 | tf_op jit(solution)/shard_map/mixer_backward/pallas_call | solution.py:351
  418.7 4.9 fusion.3.ffn_ref
  423.7 68.4 %sums.1 = (bf16[4,384,1664]{2,1,0:T(8,128)(2,1)S(1)}, bf16[4,3,288,1536]{3,2,1,0:T(8,128)(2,1)}, bf16[256,1536]{1,0:T(8,128)(2,1)S(1)}, f32[8,384]{1,0:T(8,128)S(1)}) custom-call(bf16[4,384,1664]{2,1,0:T(8,128)(2,1)} %get-tuple-element.47.mix_ref, bf16[1024,1536]{1,0:T(8,128)(2,1)S(1)} %copy-done.2, bf16[3,288,1536]{2,1,0:T(8,128)(2,1)S(1)} %fusion.3.ffn_ref, ...), custom_call_target="tpu_custom_call" | custom-call | flops 10223616 | bytes 20447232 | tf_op jit(solution)/shard_map/sums/pallas_call | solution.py:1544
  492.0 2.3 copy-done
  495.0 153.9 %tail.1 = (f32[1,975456]{1,0:T(1,128)}, f32[1,975456]{1,0:T(1,128)}, f32[1,975456]{1,0:T(1,128)}, f32[1,975456]{1,0:T(1,128)}, bf16[4,975456]{1,0:T(4,128)(2,1)}, /*index=5*/f32[2,512]{1,0:T(2,128)}) custom-call(bf16[4,384,1664]{2,1,0:T(8,128)(2,1)} %copy-done, bf16[4,3,288,1536]{3,2,1,0:T(8,128)(2,1)} %get-tuple-element.52.ffn_ref, f32[8,384]{1,0:T(8,128)} %copy-done.3, ...), custom_call_target="tpu_custom_call" | custom-call | flops 19509120 | bytes 39018240 | tf_op jit(solution)/shard_map/tail/pallas_call | solution.py:1907
  649.7 7.0 %copy.36 = f32[1,975456]{1,0:T(1,128)} copy(f32[1,975456]{1,0:T(1,128)} %get-tuple-element.94) | data formatting | bytes 7803648
  656.8 2.0 copy.37
  660.3 2.0 copy.38
  662.3 2.0 copy.39
  666.5 3.2 copy.40
  (108 shorter events, 34.1 us)
Async XLA Ops:
  0.6 6.5 copy-start.18
  0.6 7.2 %copy-start.15 = (bf16[5,512]{1,0:T(8,128)(2,1)S(1)}, bf16[5,512]{1,0:T(8,128)(2,1)}, u32[]{:S(2)}) copy-start(bf16[5,512]{1,0:T(8,128)(2,1)} %param.25) | copy-start | bytes 15364
  0.7 7.2 %copy-start.17 = (bf16[2,512]{1,0:T(2,128)(2,1)S(1)}, bf16[2,512]{1,0:T(2,128)(2,1)}, u32[]{:S(2)}) copy-start(bf16[2,512]{1,0:T(2,128)(2,1)} %param.26) | copy-start | bytes 6148
  248.0 8.8 %collective-permute-start.12 = (bf16[3,576,1536]{2,1,0:T(8,128)(2,1)S(1)}, bf16[3,576,1536]{2,1,0:T(8,128)(2,1)S(1)}, u32[]{:S(2)}, u32[]{:S(2)}) collective-permute-start(bf16[3,576,1536]{2,1,0:T(8,128)(2,1)S(1)} %slice.148), channel_id=1, source_target_pairs={{0,4},{1,5},{2,6},{3,7},{4,0},{5,1},{6,2},{7,3},{8,12},{9,13},{10,... | collective-permute-start | bytes 15925256 | tf_op jit(solution)/shard_map/ppermute | solution.py:69
  249.5 20.8 %collective-permute-start = (bf16[256,1536]{1,0:T(8,128)(2,1)}, bf16[256,1536]{1,0:T(8,128)(2,1)S(1)}, u32[]{:S(2)}, u32[]{:S(2)}) collective-permute-start(bf16[256,1536]{1,0:T(8,128)(2,1)} %pad_maximum_fusion.2), channel_id=1, source_target_pairs={{0,8},{1,9},{2,10},{3,11},{4,12},{5,13},{6,14},{7,15},{8,0},{9,1},... | collective-permute-start | bytes 2359304 | tf_op jit(solution)/shard_map/ppermute | solution.py:69
  252.7 35.9 %collective-permute-start.2 = (bf16[256,1536]{1,0:T(8,128)(2,1)}, bf16[256,1536]{1,0:T(8,128)(2,1)}, u32[]{:S(2)}, u32[]{:S(2)}) collective-permute-start(bf16[256,1536]{1,0:T(8,128)(2,1)} %pad_maximum_fusion.3), channel_id=1, source_target_pairs={{0,16},{1,17},{2,18},{3,19},{4,20},{5,21},{6,22},{7,23},{8,24},{9,... | collective-permute-start | bytes 2359304 | tf_op jit(solution)/shard_map/ppermute | solution.py:69
  260.8 95.8 %copy-start.7 = (bf16[3,576,1536]{2,1,0:T(8,128)(2,1)}, bf16[3,576,1536]{2,1,0:T(8,128)(2,1)S(1)}, u32[]{:S(2)}) copy-start(bf16[3,576,1536]{2,1,0:T(8,128)(2,1)S(1)} %add_convert_fusion) | copy-start | bytes 15925252
  261.2 40.2 %collective-permute-start.13 = (bf16[3,288,1536]{2,1,0:T(8,128)(2,1)S(1)}, bf16[3,288,1536]{2,1,0:T(8,128)(2,1)S(1)}, u32[]{:S(2)}, u32[]{:S(2)}) collective-permute-start(bf16[3,288,1536]{2,1,0:T(8,128)(2,1)S(1)} %get-tuple-element.67), channel_id=1, source_target_pairs={{3,2},{4,5},{11,10},{12,13},{19,18},{20,21},{27,26},{28,29}} | collective-permute-start | bytes 7962632 | tf_op jit(solution)/shard_map/ppermute | solution.py:69
  264.8 21.9 %collective-permute-start.4 = (bf16[256,1536]{1,0:T(8,128)(2,1)S(1)}, bf16[256,1536]{1,0:T(8,128)(2,1)S(1)}, u32[]{:S(2)}, u32[]{:S(2)}) collective-permute-start(bf16[256,1536]{1,0:T(8,128)(2,1)S(1)} %pad_maximum_fusion.4), channel_id=1, source_target_pairs={{0,8},{1,9},{2,10},{3,11},{4,12},{5,13},{6,14},{7,15},{8,0},{9,1},... | collective-permute-start | bytes 2359304 | tf_op jit(solution)/shard_map/ppermute | solution.py:69
  267.1 37.4 %collective-permute-start.6 = (bf16[256,1536]{1,0:T(8,128)(2,1)S(1)}, bf16[256,1536]{1,0:T(8,128)(2,1)S(1)}, u32[]{:S(2)}, u32[]{:S(2)}) collective-permute-start(bf16[256,1536]{1,0:T(8,128)(2,1)S(1)} %pad_maximum_fusion.5), channel_id=1, source_target_pairs={{0,16},{1,17},{2,18},{3,19},{4,20},{5,21},{6,22},{7,23},{8,24},{9,... | collective-permute-start | bytes 2359304 | tf_op jit(solution)/shard_map/ppermute | solution.py:69
  270.4 28.2 %collective-permute-start.1 = (bf16[128,1536]{1,0:T(8,128)(2,1)S(1)}, bf16[128,1536]{1,0:T(8,128)(2,1)S(1)}, u32[]{:S(2)}, u32[]{:S(2)}) collective-permute-start(bf16[128,1536]{1,0:T(8,128)(2,1)S(1)} %add_convert_fusion.6), channel_id=1, source_target_pairs={{0,16},{1,17},{2,18},{3,19},{4,20},{5,21},{6,22},{7,23},{8,24},{9,... | collective-permute-start | bytes 1179656 | tf_op jit(solution)/shard_map/ppermute | solution.py:69
  286.8 19.1 %collective-permute-start.5 = (bf16[128,1536]{1,0:T(8,128)(2,1)S(1)}, bf16[128,1536]{1,0:T(8,128)(2,1)S(1)}, u32[]{:S(2)}, u32[]{:S(2)}) collective-permute-start(bf16[128,1536]{1,0:T(8,128)(2,1)S(1)} %add_convert_fusion.4), channel_id=1, source_target_pairs={{0,16},{1,17},{2,18},{3,19},{4,20},{5,21},{6,22},{7,23},{8,24},{9,... | collective-permute-start | bytes 1179656 | tf_op jit(solution)/shard_map/ppermute | solution.py:69
  299.9 9.8 %collective-permute-start.3 = (bf16[128,1536]{1,0:T(8,128)(2,1)S(1)}, bf16[128,1536]{1,0:T(8,128)(2,1)S(1)}, u32[]{:S(2)}, u32[]{:S(2)}) collective-permute-start(bf16[128,1536]{1,0:T(8,128)(2,1)S(1)} %get-tuple-element.76), channel_id=1, source_target_pairs={{0,8},{1,9},{2,10},{3,11},{4,12},{5,13},{6,14},{7,15},{8,0},{9,1},... | collective-permute-start | bytes 1179656 | tf_op jit(solution)/shard_map/ppermute | solution.py:69
  299.9 56.7 %collective-permute-start.16 = (bf16[3,288,1536]{2,1,0:T(8,128)(2,1)S(1)}, bf16[3,288,1536]{2,1,0:T(8,128)(2,1)S(1)}, u32[]{:S(2)}, u32[]{:S(2)}) collective-permute-start(bf16[3,288,1536]{2,1,0:T(8,128)(2,1)S(1)} %get-tuple-element.68), channel_id=1, source_target_pairs={{0,1},{3,2},{4,5},{7,6},{8,9},{11,10},{12,13},{15,14},{16,17},{19,... | collective-permute-start | bytes 7962632 | tf_op jit(solution)/shard_map/ppermute | solution.py:69
  302.1 54.5 %collective-permute-start.14 = (bf16[3,288,1536]{2,1,0:T(8,128)(2,1)S(1)}, bf16[3,288,1536]{2,1,0:T(8,128)(2,1)}, u32[]{:S(2)}, u32[]{:S(2)}) collective-permute-start(bf16[3,288,1536]{2,1,0:T(8,128)(2,1)S(1)} %fusion), channel_id=1, source_target_pairs={{2,1},{5,6},{10,9},{13,14},{18,17},{21,22},{26,25},{29,30}} | collective-permute-start | bytes 7962632 | tf_op jit(solution)/shard_map/ppermute | solution.py:69
  306.2 11.0 %collective-permute-start.7 = (bf16[128,1536]{1,0:T(8,128)(2,1)S(1)}, bf16[128,1536]{1,0:T(8,128)(2,1)S(1)}, u32[]{:S(2)}, u32[]{:S(2)}) collective-permute-start(bf16[128,1536]{1,0:T(8,128)(2,1)S(1)} %get-tuple-element.70), channel_id=1, source_target_pairs={{0,8},{1,9},{2,10},{3,11},{4,12},{5,13},{6,14},{7,15},{8,0},{9,1},... | collective-permute-start | bytes 1179656 | tf_op jit(solution)/shard_map/ppermute | solution.py:69
  320.5 45.4 %collective-permute-start.8 = (bf16[256,1536]{1,0:T(8,128)(2,1)}, bf16[256,1536]{1,0:T(8,128)(2,1)S(1)}, u32[]{:S(2)}, u32[]{:S(2)}) collective-permute-start(bf16[256,1536]{1,0:T(8,128)(2,1)} %get-tuple-element.63), channel_id=1, source_target_pairs={{0,8},{1,9},{2,10},{3,11},{4,12},{5,13},{6,14},{7,15},{8,0},{9,1},... | collective-permute-start | bytes 2359304 | tf_op jit(solution)/shard_map/ppermute | solution.py:69
  321.1 46.3 %collective-permute-start.9 = (bf16[256,1536]{1,0:T(8,128)(2,1)}, bf16[256,1536]{1,0:T(8,128)(2,1)S(1)}, u32[]{:S(2)}, u32[]{:S(2)}) collective-permute-start(bf16[256,1536]{1,0:T(8,128)(2,1)} %get-tuple-element.63), channel_id=1, source_target_pairs={{0,16},{1,17},{2,18},{3,19},{4,20},{5,21},{6,22},{7,23},{8,24},{9,... | collective-permute-start | bytes 2359304 | tf_op jit(solution)/shard_map/ppermute | solution.py:69
  362.2 56.5 %collective-permute-start.15 = (bf16[3,288,1536]{2,1,0:T(8,128)(2,1)}, bf16[3,288,1536]{2,1,0:T(8,128)(2,1)}, u32[]{:S(2)}, u32[]{:S(2)}) collective-permute-start(bf16[3,288,1536]{2,1,0:T(8,128)(2,1)} %get-tuple-element.65), channel_id=1, source_target_pairs={{1,0},{6,7},{9,8},{14,15},{17,16},{22,23},{25,24},{30,31}} | collective-permute-start | bytes 7962632 | tf_op jit(solution)/shard_map/ppermute | solution.py:69
  363.5 55.2 %collective-permute-start.17 = (bf16[3,288,1536]{2,1,0:T(8,128)(2,1)}, bf16[3,288,1536]{2,1,0:T(8,128)(2,1)}, u32[]{:S(2)}, u32[]{:S(2)}) collective-permute-start(bf16[3,288,1536]{2,1,0:T(8,128)(2,1)} %get-tuple-element.66), channel_id=1, source_target_pairs={{2,1},{5,6},{10,9},{13,14},{18,17},{21,22},{26,25},{29,30}} | collective-permute-start | bytes 7962632 | tf_op jit(solution)/shard_map/ppermute | solution.py:69
  365.9 11.0 %copy-start.4 = (f32[4,1024,128]{2,1,0:T(8,128)S(1)}, f32[4,1024,128]{2,1,0:T(8,128)}, u32[]{:S(2)}) copy-start(f32[4,1024,128]{2,1,0:T(8,128)} %get-tuple-element.45.state_ref) | copy-start | bytes 6291460
  365.9 11.0 %copy-start.5 = (bf16[4,1024,128]{2,1,0:T(8,128)(2,1)S(1)}, bf16[4,1024,128]{2,1,0:T(8,128)(2,1)}, u32[]{:S(2)}) copy-start(bf16[4,1024,128]{2,1,0:T(8,128)(2,1)} %get-tuple-element.46.low_ref) | copy-start | bytes 3145732
  365.9 11.0 %copy-start.6 = (bf16[1024,128]{1,0:T(8,128)(2,1)S(1)}, bf16[1024,128]{1,0:T(8,128)(2,1)}, u32[]{:S(2)}) copy-start(bf16[1024,128]{1,0:T(8,128)(2,1)} %get-tuple-element.42.pos_ref) | copy-start | bytes 786436
  365.9 9.4 %collective-permute-start.10 = (bf16[128,1536]{1,0:T(8,128)(2,1)S(1)}, bf16[128,1536]{1,0:T(8,128)(2,1)S(1)}, u32[]{:S(2)}, u32[]{:S(2)}) collective-permute-start(bf16[128,1536]{1,0:T(8,128)(2,1)S(1)} %slice.160), channel_id=1, source_target_pairs={{0,16},{1,17},{2,18},{3,19},{4,20},{5,21},{6,22},{7,23},{8,24},{9,... | collective-permute-start | bytes 1179656 | tf_op jit(solution)/shard_map/ppermute | solution.py:69
  367.4 8.7 %collective-permute-start.11 = (bf16[128,1536]{1,0:T(8,128)(2,1)S(1)}, bf16[128,1536]{1,0:T(8,128)(2,1)S(1)}, u32[]{:S(2)}, u32[]{:S(2)}) collective-permute-start(bf16[128,1536]{1,0:T(8,128)(2,1)S(1)} %slice.161), channel_id=1, source_target_pairs={{0,8},{1,9},{2,10},{3,11},{4,12},{5,13},{6,14},{7,15},{8,0},{9,1},... | collective-permute-start | bytes 1179656 | tf_op jit(solution)/shard_map/ppermute | solution.py:69
  376.1 42.6 %slice-start = ((s8[5308416]{0:T(1024)(128)(4,1)}), s8[4194304]{0:T(1024)(128)(4,1)S(1)}, s32[]{:S(2)}) async-start(s8[5308416]{0:T(1024)(128)(4,1)} %bitcast.2), calls=%async_computation | async-start | bytes 8388608
  376.9 41.8 %slice-start.1 = ((s8[5308416]{0:T(1024)(128)(4,1)}), s8[1114112]{0:T(1024)(128)(4,1)S(1)}, s32[]{:S(2)}) async-start(s8[5308416]{0:T(1024)(128)(4,1)} %bitcast.2), calls=%async_computation.1 | async-start | bytes 2228224
  418.7 4.9 copy-start.1
  418.7 5.0 copy-start.2
  649.7 7.0 %copy-start.11 = (f32[1,975456]{1,0:T(1,128)S(1)}, f32[1,975456]{1,0:T(1,128)}, u32[]{:S(2)}) copy-start(f32[1,975456]{1,0:T(1,128)} %get-tuple-element.95) | copy-start | bytes 11705476
  656.7 5.5 copy-start.9
  660.3 5.4 slice-start.2
  (9 other events, 25.2 us)

commit v5 on v4

--- a/solution.py
+++ b/solution.py
@@ -380,89 +380,6 @@
         ),
         name="mixer_backward",
     )(mix_in, res_low, position, weights, *saved)
-
-
-def ffn_kernel(
-    x_ref, go_ref, w_ref, grad_ref, out_ref, gin_ref, acc_w, acc_out, acc_in
-):
-    tile = pl.program_id(0)
-    block = pl.program_id(1)
-    slots = x_ref.shape[0]
-    x = x_ref[...]
-    grad_out = go_ref[...]
-    pre_gate = dot_rows(x, w_ref[0])
-    pre_up = dot_rows(x, w_ref[1])
-    active, slope = gelu_parts(pre_gate)
-    ffn_low = (active * pre_up).astype(low_type)
-    grad_act = dot_rows(grad_out, w_ref[2])
-    gate_low = (grad_act * pre_up * slope).astype(low_type)
-    up_low = (grad_act * active).astype(low_type)
-    part_out = dot_plain(ffn_low, w_ref[2])
-    part_in = dot_plain(gate_low, w_ref[0]) + dot_plain(up_low, w_ref[1])
-    rows = pl.ds(pl.multiple_of(block * slots, slots), slots)
-
-    @pl.when(block == 0)
-    def _():
-        acc_w[...] = jnp.zeros_like(acc_w)
-
-    acc_w[0] += dot_slots(gate_low, x)
-    acc_w[1] += dot_slots(up_low, x)
-    acc_w[2] += dot_slots(ffn_low, grad_out)
-
-    @pl.when(tile == 0)
-    def _():
-        acc_out[rows, :] = part_out
-        acc_in[rows, :] = part_in
-
-    @pl.when(tile > 0)
-    def _():
-        acc_out[rows, :] += part_out
-        acc_in[rows, :] += part_in
-
-    @pl.when(block == pl.num_programs(1) - 1)
-    def _():
-        grad_ref[...] = acc_w[...].astype(low_type)
-
-    @pl.when(tile == pl.num_programs(0) - 1)
-    def _():
-        out_ref[rows, :] = acc_out[rows, :].astype(low_type)
-        gin_ref[rows, :] = acc_in[rows, :].astype(low_type)
-
-
-def ffn_both(x, grad_out, weights, slots, tile):
-    rows, model = x.shape
-    hidden = weights.shape[1]
-    return pl.pallas_call(
-        ffn_kernel,
-        grid=(hidden // tile, rows // slots),
-        in_specs=[
-            pl.BlockSpec((slots, model), lambda j, b: (b, 0)),
-            pl.BlockSpec((slots, model), lambda j, b: (b, 0)),
-            pl.BlockSpec((3, tile, model), lambda j, b: (0, j, 0)),
-        ],
-        out_specs=[
-            pl.BlockSpec((3, tile, model), lambda j, b: (0, j, 0)),
-            pl.BlockSpec((rows, model), lambda j, b: (0, 0)),
-            pl.BlockSpec((rows, model), lambda j, b: (0, 0)),
-        ],
-        out_shape=[
-            jax.ShapeDtypeStruct(weights.shape, low_type),
-            jax.ShapeDtypeStruct((rows, model), low_type),
-            jax.ShapeDtypeStruct((rows, model), low_type),
-        ],
-        scratch_shapes=[
-            pltpu.VMEM((3, tile, model), wide),
-            pltpu.VMEM((rows, model), wide),
-            pltpu.VMEM((rows, model), wide),
-        ],
-        compiler_params=pltpu.CompilerParams(vmem_limit_bytes=58 * 1024 * 1024),
-        cost_estimate=pl.CostEstimate(
-            flops=2 * rows * model * hidden * 9,
-            bytes_accessed=weights.size * 4 + rows * model * 16,
-            transcendentals=rows * hidden,
-        ),
-        name="ffn_both",
-    )(x, grad_out, weights)
 
 
 def peer_x(chip):
@@ -1054,6 +971,337 @@
     )(tokens, cot, gains, small, in_proj, gates, out_proj, gate_up, down)
 
 
+def middle_kernel(
+    sizes,
+    x_ref,
+    go_ref,
+    weights_ref,
+    residual_ref,
+    gain_ref,
+    mask_ref,
+    total,
+    res_low,
+    res_out,
+    gain_out,
+    block_out,
+    held,
+    lows,
+    paired,
+    arrived,
+    part_in,
+    part_out,
+    in_x,
+    in_y,
+    in_pass,
+    in_last,
+    load_sem,
+    core_send,
+    core_recv,
+    line_send,
+    line_recv,
+    i_send,
+    i_recv,
+    o_send,
+    o_recv,
+    g_send,
+    g_recv,
+):
+    model, ffn_width = sizes
+    member = lax.axis_index("dp")
+    z = lax.axis_index("shard")
+    chip, core = member // 2, member % 2
+    end = z + core * (3 - 2 * z)
+    other = chip * 2 + 1 - core
+    slots = residual_ref.shape[0]
+    half = slots // 2
+    hidden = 4 * ffn_width
+    half_ffn = ffn_width // 2
+
+    loads = [
+        pltpu.make_async_copy(weights_ref.at[kind], held.at[kind], load_sem.at[kind])
+        for kind in range(3)
+    ]
+    for load in loads:
+        load.start()
+    enter(member, z)
+    for load in loads:
+        load.wait()
+
+    cuts = []
+    low = 0
+    while low < hidden:
+        cuts.append((low, min(low + 512, hidden)))
+        low += 512
+
+    def block_step(block, carry):
+        rows = pl.ds(pl.multiple_of(block * slots, slots), slots)
+        x = x_ref[rows, :]
+        grad_out = go_ref[rows, :]
+        sum_out = jnp.zeros((slots, model), wide)
+        sum_in = jnp.zeros((slots, model), wide)
+        for low, high in cuts:
+            pre_gate = dot_rows(x, held[0, low:high])
+            pre_up = dot_rows(x, held[1, low:high])
+            active, slope = gelu_parts(pre_gate)
+            ffn_low = (active * pre_up).astype(low_type)
+            grad_act = dot_rows(grad_out, held[2, low:high])
+            gate_low = (grad_act * pre_up * slope).astype(low_type)
+            up_low = (grad_act * active).astype(low_type)
+            sum_out = sum_out + dot_plain(ffn_low, held[2, low:high])
+            sum_in = (
+                sum_in + dot_plain(gate_low, held[0, low:high]) + dot_plain(up_low, held[1, low:high])
+            )
+            lows[0, rows, low:high] = gate_low
+            lows[1, rows, low:high] = up_low
+            lows[2, rows, low:high] = ffn_low
+        part_in[rows, :] = sum_in.astype(low_type)
+        part_out[rows, :] = sum_out.astype(low_type)
+        return carry
+
+    lax.fori_loop(0, 4, block_step, 0)
+
+    reduce_in = Reduce(part_in, in_x, in_y, in_pass, in_last, i_send, i_recv, member, z)
+    reduce_out = Reduce(
+        part_out,
+        in_x.at[pl.ds(2, 2)],
+        in_y.at[pl.ds(2, 2)],
+        in_pass.at[pl.ds(2, 2)],
+        in_last.at[pl.ds(2, 2)],
+        o_send,
+        o_recv,
+        member,
+        z,
+    )
+    gather = Gather(res_low.at[0], res_low, g_send, g_recv, member, z)
+    reduce_in.begin()
+
+    split = (2 * ffn_width // 128) * 128
+    middle = model // 2
+
+    def weight_grads(kind, low, high):
+        factor = go_ref if kind == 2 else x_ref
+        for at in range(2):
+            columns = slice(at * middle, (at + 1) * middle)
+            held[kind, low:high, columns] = dot_slots(
+                lows[kind, :, low:high], factor[:, columns]
+            ).astype(low_type)
+
+    def core_copy(slot, kind):
+        return remote(
+            held.at[kind, pl.ds((2 + slot) * ffn_width, ffn_width)],
+            paired.at[slot, kind],
+            core_send.at[slot, kind],
+            core_recv.at[slot, kind],
+            other,
+            z,
+        )
+
+    for kind in range(3):
+        weight_grads(kind, split, hidden)
+        core_copy(0, kind).start()
+        core_copy(1, kind).start()
+
+    def chunk(number):
+        return number // 2, pl.ds((number % 2) * half_ffn, half_ffn)
+
+    def line_copy(kind, number, to_end):
+        at, rows = chunk(number)
+        return remote(
+            paired.at[min(kind, 1), at, rows],
+            arrived.at[kind, at, rows],
+            line_send.at[kind, number],
+            line_recv.at[kind, number],
+            member,
+            line_place(to_end, core),
+        )
+
+    def pair_up(slot, number):
+        at, rows = chunk(number)
+        own = held[at, pl.ds(slot * ffn_width + (number % 2) * half_ffn, half_ffn)]
+        paired[slot, at, rows] = add_low(own, paired[slot, at, rows])
+
+    for kind in range(3):
+        weight_grads(kind, 0, split)
+        for slot in range(2):
+            core_copy(slot, kind).wait_recv()
+            for number in (2 * kind, 2 * kind + 1):
+                pair_up(slot, number)
+
+                @pl.when(end == 3)
+                def _():
+                    line_copy(slot, number, 2).start()
+
+                if slot == 1:
+
+                    @pl.when(end == 0)
+                    def _():
+                        line_copy(2, number, 1).start()
+
+        if kind == 0:
+            reduce_in.relay()
+
+    def summed(slot, kinds, number):
+        at, rows = chunk(number)
+        result = paired[slot, at, rows].astype(wide)
+        for kind in kinds:
+            result = result + arrived[kind, at, rows].astype(wide)
+        return result.astype(low_type)
+
+    def line_step(number):
+        at, rows = chunk(number)
+
+        @pl.when((end == 2) | (end == 1))
+        def _():
+            line_copy(0, number, 0).wait_recv()
+            paired[0, at, rows] = summed(0, (0,), number)
+
+        @pl.when(end == 2)
+        def _():
+            line_copy(0, number, 1).start()
+            line_copy(1, number, 0).wait_recv()
+            paired[1, at, rows] = summed(1, (1,), number)
+            line_copy(1, number, 1).start()
+
+        @pl.when(end == 1)
+        def _():
+            line_copy(0, number, 0).start()
+
+    def out_copy(slot, number):
+        at, rows = chunk(number)
+        return pltpu.make_async_copy(
+            paired.at[slot, at, rows], total.at[at, rows], load_sem.at[number]
+        )
+
+    def last_step(number):
+        at, rows = chunk(number)
+
+        @pl.when(end == 1)
+        def _():
+            line_copy(1, number, 0).wait_recv()
+            line_copy(2, number, 0).wait_recv()
+            paired[1, at, rows] = summed(1, (1, 2), number)
+            out_copy(1, number).start()
+
+        @pl.when(end == 0)
+        def _():
+            line_copy(0, number, 0).wait_recv()
+            paired[0, at, rows] = summed(0, (0,), number)
+            out_copy(0, number).start()
+
+    line_step(0)
+
+    reduce_in.arrive()
+    gain = gain_ref[1:2]
+    gain_sum = jnp.zeros((1, model), wide)
+    for number in range(2):
+        at = slice(number * half, (number + 1) * half)
+        grad = reduce_in.result(number)
+        value = residual_ref[at]
+        scale = lax.rsqrt(jnp.mean(value * value, axis=1, keepdims=True) + norm_eps)
+        scaled = grad * gain
+        gain_sum = gain_sum + jnp.sum(grad * value * scale, axis=0, keepdims=True)
+        inner = jnp.mean(scaled * value, axis=1, keepdims=True)
+        back = scale * scaled - value * (scale * scale * scale * inner)
+        result = go_ref[at].astype(wide) + back
+        res_out[at] = result
+        res_low[0, at] = result.astype(low_type)
+    gain_out[...] = jnp.concatenate([gain_ref[0:1], gain_sum, jnp.zeros((6, model), wide)], axis=0)
+    gather.begin()
+    line_step(1)
+    line_step(2)
+    gather.relay()
+    line_step(3)
+    gather.arrive()
+    reduce_out.begin()
+    line_step(4)
+    line_step(5)
+    reduce_out.relay()
+    for number in range(6):
+        last_step(number)
+    reduce_out.arrive()
+    live = mask_ref[:, 0:1].astype(wide)
+    for number in range(2):
+        at = slice(number * half, (number + 1) * half)
+        block_out[at] = (live[at] * (residual_ref[at] + reduce_out.result(number))).astype(low_type)
+
+    for sent in (reduce_in, reduce_out, gather):
+        sent.finish()
+    for slot in range(2):
+        for kind in range(3):
+            core_copy(slot, kind).wait_send()
+    for number in range(6):
+
+        @pl.when(end > 0)
+        def _():
+            line_copy(0, number, 0).wait_send()
+
+        @pl.when(end > 1)
+        def _():
+            line_copy(1, number, 0).wait_send()
+
+        @pl.when(end == 0)
+        def _():
+            line_copy(2, number, 1).wait_send()
+
+        @pl.when(end < 2)
+        def _():
+            out_copy(0, number).wait()
+
+
+def middle(x, grad_out, weights, residual, gains, mask):
+    rows, model = x.shape
+    hidden = weights.shape[1]
+    ffn_width = hidden // 4
+    slots = rows // 4
+    dma = pltpu.SemaphoreType.DMA
+    vmem = pl.BlockSpec(memory_space=pltpu.VMEM)
+    anywhere = pl.BlockSpec(memory_space=pl.ANY)
+    quarter = (3, ffn_width, model)
+    return pl.pallas_call(
+        functools.partial(middle_kernel, (model, ffn_width)),
+        in_specs=[vmem, vmem, anywhere, vmem, vmem, vmem],
+        out_specs=[anywhere] + [vmem] * 4,
+        out_shape=[
+            jax.ShapeDtypeStruct(quarter, low_type),
+            jax.ShapeDtypeStruct((4, slots, model), low_type),
+            jax.ShapeDtypeStruct((slots, model), wide),
+            jax.ShapeDtypeStruct((8, model), wide),
+            jax.ShapeDtypeStruct((slots, model), low_type),
+        ],
+        scratch_shapes=[
+            pltpu.VMEM(weights.shape, low_type),
+            pltpu.VMEM((3, rows, hidden), low_type),
+            pltpu.VMEM((2,) + quarter, low_type),
+            pltpu.VMEM((3,) + quarter, low_type),
+            pltpu.VMEM((rows, model), low_type),
+            pltpu.VMEM((rows, model), low_type),
+        ]
+        + [pltpu.VMEM((4, slots // 2, model), low_type)] * 4
+        + [
+            dma((6,)),
+            dma((2, 3)),
+            dma((2, 3)),
+            dma((3, 6)),
+            dma((3, 6)),
+            dma((6,)),
+            dma((6,)),
+            dma((6,)),
+            dma((6,)),
+            dma((4,)),
+            dma((4,)),
+        ],
+        compiler_params=pltpu.CompilerParams(
+            collective_id=4, has_side_effects=True, vmem_limit_bytes=63 * 1024 * 1024
+        ),
+        cost_estimate=pl.CostEstimate(
+            flops=2 * rows * model * hidden * 9,
+            bytes_accessed=weights.size * 4 + rows * model * 16,
+            transcendentals=rows * hidden,
+        ),
+        name="middle",
+    )(x, grad_out, weights, residual, gains, mask)
+
+
 class Scatter:
     def __init__(self, sizes, member, z, send_sem, recv_sem):
         self.model, self.width, self.ffn_width, self.piece_length = sizes
@@ -2003,29 +2251,25 @@
     saved = (saved_p, saved_state, saved_low)
     ffn_in = ffn_in.reshape(4 * slots, model)
     all_grad_out = all_grad_out.reshape(4 * slots, model)
-    _, second_pull = jax.vjp(rms_scale, residual, gains[1])
-
-    grad_ffn, ffn_part, ffn_in_part = ffn_both(
-        ffn_in, all_grad_out, ffn_weights, slots, ffn_width * 4 // 3
-    )
-    grad_norm_two, grad_gain_two = second_pull(plane_reduce(ffn_in_part))
-    grad_residual = grad_stream + grad_norm_two
-    res_low = jnp.concatenate(plane_gather(grad_residual.astype(low_type)))
-    block_out = (mask_rows * (residual + plane_reduce(ffn_part))).astype(low_type)
-
+    sum_ffn, res_low, grad_residual, gain_sums, block_out = middle(
+        ffn_in,
+        all_grad_out,
+        ffn_weights,
+        residual,
+        gains,
+        jnp.broadcast_to(mask_rows.astype(low_type), (slots, width)),
+    )
+    res_low = res_low.reshape(4 * slots, model)
     grad_mix, mix_in_part = mix_backward(
         mix_in, res_low, all_starts, mix_weights, saved, slots, width
     )
-    both = 2 * ffn_width
-    pair_ffn = add_low(grad_ffn[:, :both], move(grad_ffn[:, both:], core_pairs))
-    sum_ffn = line_sum(pair_ffn[:, :ffn_width], pair_ffn[:, ffn_width:], end)
     four_mix, four_ffn, tokens_grad, gain_total = sums(
         grad_mix,
         mix_in_part,
         sum_ffn,
         tokens,
         grad_residual,
-        jnp.concatenate([gains[0:1], grad_gain_two[None], jnp.zeros((6, model), wide)]),
+        gain_sums,
         piece_length,
         width,
     )

time: 679 us -> 643 us (0.947)
  Pallas kernels: 501 us -> 590 us
  waiting for transfers between devices: 80.3 us -> 0 us
  other arithmetic: 29.9 us -> 7.06 us
  starting transfers between devices: 21.9 us -> 0 us
    pallas_call x1, Pallas kernels: 58.9 us -> 153 us  [middle(): pl.pallas_call(functools.partial(middle_kernel, (model, ffn_width)), in_s...]
    ppermute x18 -> x0, waiting for transfers between devices: 80.3 us -> none  [move(): return lax.ppermute(value, axes, pairs)]
    ppermute x18 -> x0, starting transfers between devices: 21.9 us -> none  [move(): return lax.ppermute(value, axes, pairs)]
    convert_element_type x6 -> x1, other arithmetic: 11.2 us -> 0.68 us  [group_body(): mask_rows.astype(low_type)]
    pallas_call x1, Pallas kernels: 68.4 us -> 61.3 us  [sums(): pl.pallas_call(functools.partial(sums_kernel, sizes), in_specs=[vmem, vme...]
    unnamed x56 -> x42, local copies, waits for them, and re-layouts: 29.9 us -> 30 us
  transfers between devices with their start and end apart: 18 -> 0, of which waited for: 9 -> 0; matrix products, arithmetic and copies ran while one was open for 4% -> 0% of each run, Pallas kernels for 6% -> 0%
where the time goes in v5:
time: 643 us; the launch traced here: 631 us
  Pallas kernels  590 us (92%)
  local copies, waits for them, and re-layouts  32.8 us (5%)
  other arithmetic  7.06 us (1%)
    pallas_call x1, Pallas kernels, front(): pl.pallas_call(functools.partial(front_kernel, sizes), in_specs=[vmem] *...  178 us
    pallas_call x1, Pallas kernels, tail(): pl.pallas_call(functools.partial(tail_kernel, (model, width, ffn_width, p...  157 us
    pallas_call x1, Pallas kernels, middle(): pl.pallas_call(functools.partial(middle_kernel, (model, ffn_width)), in_s...  153 us
    pallas_call x1, Pallas kernels, sums(): pl.pallas_call(functools.partial(sums_kernel, sizes), in_specs=[vmem, vme...  61.3 us
    pallas_call x1, Pallas kernels, mix_backward(): pl.pallas_call(functools.partial(mixer_backward_kernel, width), grid=(hea...  41.4 us
    unnamed x42, local copies, waits for them, and re-layouts  30 us

profile of v5, /device:TPU:0, one launch (start us, length us, event | category | flops | bytes accessed | tf_op | source)
XLA Modules:
  0.0 631.1 jit_solution(15857619349813024024)
XLA Ops:
  0.6 0.7 convert_element_type.16
  1.3 0.1 pad.4.clone
  1.4 0.7 convert_convert_fusion
  2.1 0.7 broadcast_in_dim.9
  2.8 1.3 concatenate.10.gain_ref
  4.0 1.4 maximum_maximum_fusion.small_ref
  5.4 0.7 broadcast_in_dim.22.mask_ref
  6.2 0.1 broadcast_in_dim.8
  6.3 2.1 pad_maximum_fusion.tokens_ref
  8.4 2.2 multiply_convert_fusion.cot_ref
  10.6 177.6 %front.1 = (bf16[1024,1536]{1,0:T(8,128)(2,1)}, bf16[4,384,1664]{2,1,0:T(8,128)(2,1)}, bf16[3,1152,1536]{2,1,0:T(8,128)(2,1)}, f32[4,1024,256]{2,1,0:T(8,128)}, ...) custom-call(bf16[256,1664]{1,0:T(8,128)(2,1)} %pad_maximum_fusion.to, ...), custom_call_target="tpu_custom_call" | custom-call | flops 4831838208 | bytes 10616832 | tf_op jit(solution)/shard_map/front/pallas_call | solution.py:918
  188.1 152.7 %middle.1 = (bf16[3,288,1536]{2,1,0:T(8,128)(2,1)}, bf16[4,256,1536]{2,1,0:T(8,128)(2,1)}, f32[256,1536]{1,0:T(8,128)}, f32[8,1536]{1,0:T(8,128)}, bf16[256,1536]{1,0:T(8,128)(2,1)}) custom-call(bf16[1024,1536]{1,0:T(8,128)(2,1)} %bitcast.5, bf16[1024,1536]{1,0:T(8,128)(2,1)} %bitcast.6, bf16[3,1152,1536]{2,1,0:T(8,128)(2,1)} %get-tuple-element.38.weights_ref, ...), custom_call_target="tpu_custom_call" | custom-call | flops 32614907904 | bytes 46399488 | tf_op jit(solution)/shard_map/middle/pallas_call | solution.py:1260
  340.8 1.6 copy-done.7
  342.4 1.2 copy-done.8
  343.7 41.4 %mixer_backward.1 = (bf16[4,384,1664]{2,1,0:T(8,128)(2,1)}, bf16[1024,1536]{1,0:T(8,128)(2,1)}) custom-call(bf16[1024,1536]{1,0:T(8,128)(2,1)} %get-tuple-element.42.x_ref, bf16[1024,1536]{1,0:T(8,128)(2,1)} %bitcast.7, bf16[1024,128]{1,0:T(8,128)(2,1)S(1)} %copy-done.9, bf16[4,384,1664]{2,1,0:T(8,128)(2,1)} %get-tuple-element.45.w_ref, ...), custom_call_target="tpu_custom_call" | custom-call | flops 9663676416 | bytes 27000832 | tf_op jit(solution)/shard_map/mixer_backward/pallas_call | solution.py:351
  385.1 0.0 copy-start.2
  385.1 1.9 copy-done.2
  387.0 61.3 %sums.1 = (bf16[4,384,1664]{2,1,0:T(8,128)(2,1)S(1)}, bf16[4,3,288,1536]{3,2,1,0:T(8,128)(2,1)}, bf16[256,1536]{1,0:T(8,128)(2,1)S(1)}, f32[8,384]{1,0:T(8,128)S(1)}) custom-call(bf16[4,384,1664]{2,1,0:T(8,128)(2,1)} %get-tuple-element.49.mix_ref, bf16[1024,1536]{1,0:T(8,128)(2,1)S(1)} %copy-done.2, bf16[3,288,1536]{2,1,0:T(8,128)(2,1)S(1)} %copy-done.3, ...), custom_call_target="tpu_custom_call" | custom-call | flops 10223616 | bytes 20447232 | tf_op jit(solution)/shard_map/sums/pallas_call | solution.py:1792
  448.3 2.3 copy-done
  450.6 0.6 copy-done.6
  451.2 157.2 %tail.1 = (f32[1,975456]{1,0:T(1,128)}, f32[1,975456]{1,0:T(1,128)}, f32[1,975456]{1,0:T(1,128)}, f32[1,975456]{1,0:T(1,128)}, bf16[4,975456]{1,0:T(4,128)(2,1)}, /*index=5*/f32[2,512]{1,0:T(2,128)}) custom-call(bf16[4,384,1664]{2,1,0:T(8,128)(2,1)} %copy-done, bf16[4,3,288,1536]{3,2,1,0:T(8,128)(2,1)} %get-tuple-element.56.ffn_ref, f32[8,384]{1,0:T(8,128)} %copy-done.6, ...), custom_call_target="tpu_custom_call" | custom-call | flops 19509120 | bytes 39018240 | tf_op jit(solution)/shard_map/tail/pallas_call | solution.py:2155
  608.5 0.9 copy.32
  609.4 0.9 copy.33
  610.3 7.0 %copy.34 = f32[1,975456]{1,0:T(1,128)} copy(f32[1,975456]{1,0:T(1,128)} %get-tuple-element.76) | data formatting | bytes 7803648
  617.3 2.0 copy.35
  619.3 1.5 copy-done.11
  620.8 2.0 copy.36
  622.8 2.0 copy.37
  624.8 1.4 slice-done
  626.2 0.8 slice-done.1
  627.0 3.2 copy.38
  630.2 0.6 copy.39
  (27 shorter events, 0.1 us)
Async XLA Ops:
  188.1 152.7 %copy-start.9 = (bf16[1024,128]{1,0:T(8,128)(2,1)S(1)}, bf16[1024,128]{1,0:T(8,128)(2,1)}, u32[]{:S(2)}) copy-start(bf16[1024,128]{1,0:T(8,128)(2,1)} %get-tuple-element.44.pos_ref) | copy-start | bytes 786436
  340.8 1.6 copy-start.7
  342.4 1.2 copy-start.8
  343.7 41.4 %copy-start.1 = (bf16[256,1536]{1,0:T(8,128)(2,1)S(1)}, bf16[256,1536]{1,0:T(8,128)(2,1)}, u32[]{:S(2)}) copy-start(bf16[256,1536]{1,0:T(8,128)(2,1)} %tokens_ref.1) | copy-start | bytes 2359300
  343.7 41.4 %copy-start.3 = (bf16[3,288,1536]{2,1,0:T(8,128)(2,1)S(1)}, bf16[3,288,1536]{2,1,0:T(8,128)(2,1)}, u32[]{:S(2)}) copy-start(bf16[3,288,1536]{2,1,0:T(8,128)(2,1)} %get-tuple-element.51.ffn_ref) | copy-start | bytes 7962628
  343.7 41.4 %copy-start.4 = (f32[256,1536]{1,0:T(8,128)S(1)}, f32[256,1536]{1,0:T(8,128)}, u32[]{:S(2)}) copy-start(f32[256,1536]{1,0:T(8,128)} %get-tuple-element.52.res_ref) | copy-start | bytes 4718596
  343.7 41.4 %copy-start.5 = (f32[8,1536]{1,0:T(8,128)S(1)}, f32[8,1536]{1,0:T(8,128)}, u32[]{:S(2)}) copy-start(f32[8,1536]{1,0:T(8,128)} %get-tuple-element.53.gain_ref) | copy-start | bytes 147460
  385.1 1.9 copy-start.2
  448.3 2.3 copy-start
  450.6 0.6 copy-start.6
  451.2 157.3 %copy-start.13 = (bf16[256,1536]{1,0:T(8,128)(2,1)S(1)}, bf16[256,1536]{1,0:T(8,128)(2,1)}, u32[]{:S(2)}) copy-start(bf16[256,1536]{1,0:T(8,128)(2,1)} %get-tuple-element.74) | copy-start | bytes 2359300
  610.3 7.0 %copy-start.12 = (f32[1,975456]{1,0:T(1,128)S(1)}, f32[1,975456]{1,0:T(1,128)}, u32[]{:S(2)}) copy-start(f32[1,975456]{1,0:T(1,128)} %get-tuple-element.77) | copy-start | bytes 11705476
  617.3 3.5 copy-start.11
  617.3 5.5 copy-start.10
  620.8 5.4 slice-start
  622.8 4.3 slice-start.1
  627.0 3.2 copy-start.14

commit v6 on v5

--- a/solution.py
+++ b/solution.py
@@ -557,6 +557,7 @@
     tokens_all,
     raw_in,
     raw_up,
+    raw_down,
     turned,
     gain_seen,
     acc,
@@ -597,7 +598,13 @@
     wide_window = pl.ds(pl.multiple_of(window, 128), raw_up.shape[2])
 
     def loads():
-        found = []
+        found = [
+            (out_ref.at[quarter], weights.at[end, pl.ds(2 * width, width), pl.ds(0, model)]),
+            (
+                small_ref.at[:, quarter],
+                weights.at[end, pl.ds(2 * width, 16), pl.ds(model, width)],
+            ),
+        ]
         for kind in range(2):
             found.append((in_ref.at[kind, :, quarter], raw_in.at[kind]))
             found.append(
@@ -606,21 +613,11 @@
                     weights.at[end, pl.ds(kind * width, width), pl.ds(model, width)],
                 )
             )
-        found.append((out_ref.at[quarter], weights.at[end, pl.ds(2 * width, width), pl.ds(0, model)]))
         found.append(
-            (
-                small_ref.at[:, quarter],
-                weights.at[end, pl.ds(2 * width, 16), pl.ds(model, width)],
-            )
+            (down_ref.at[pl.ds(pl.multiple_of(chip * ffn_width, 32), ffn_width)], raw_down)
         )
         for kind in range(2):
             found.append((up_ref.at[kind, :, wide_window], raw_up.at[kind]))
-        found.append(
-            (
-                down_ref.at[pl.ds(pl.multiple_of(chip * ffn_width, 32), ffn_width)],
-                ffn_weights.at[2, pl.ds(pl.multiple_of(end * ffn_width, 32), ffn_width)],
-            )
-        )
         return [
             pltpu.make_async_copy(source, target, load_sem.at[number])
             for number, (source, target) in enumerate(found)
@@ -628,8 +625,10 @@
 
     def turned_copy(kind):
         return pltpu.make_async_copy(
-            turned.at[kind, pl.ds(pl.multiple_of(skew, 32), ffn_width)],
-            ffn_weights.at[kind, pl.ds(pl.multiple_of(end * ffn_width, 32), ffn_width)],
+            raw_down
+            if kind == 2
+            else turned.at[kind, pl.ds(pl.multiple_of(skew, 32), ffn_width)],
+            ffn_weights.at[kind, pl.ds(pl.multiple_of(2 * end * ffn_width, 32), ffn_width)],
             load_sem.at[9 + kind],
         )
 
@@ -644,7 +643,7 @@
     gather_cot = Gather(cot_ref, cot_out, g_send.at[1], g_recv.at[1], member, z)
     gather_ffn = Gather(ffn_in.at[0], ffn_in, g_send.at[2], g_recv.at[2], member, z)
     reduce = Reduce(part, from_x, from_y, passing, last, r_send, r_recv, member, z)
-    own_cot = pltpu.make_async_copy(cot_ref, cot_out.at[0], load_sem.at[11])
+    own_cot = pltpu.make_async_copy(cot_ref, cot_out.at[0], load_sem.at[12])
 
     gather_tokens.begin()
     own_cot.start()
@@ -687,7 +686,7 @@
         )
 
     def f_place(slot, number):
-        row = slot * ffn_width + (number % 2) * half_ffn
+        row = ((slot % 2) * 2 + slot // 2) * ffn_width + (number % 2) * half_ffn
         return ffn_weights.at[number // 2, pl.ds(row, half_ffn)]
 
     def f_copy(slot, number, way, to_end):
@@ -723,79 +722,114 @@
             def _():
                 copy(slot, number, 0, end + 1).start()
 
-            @pl.when(end == 1)
+        core_copy(slot, number).start()
+
+    def pass_back(copy, numbers):
+        @pl.when(end == 1)
+        def _():
+            for number in numbers:
+                copy(1, number, 1, 0).start()
+
+    def start_own(copy, core_copy, numbers):
+        for slot in range(2):
+
+            @pl.when(end == slot)
             def _():
-                copy(slot, number, 1, 0).start()
-
-        core_copy(slot, number).start()
+                for number in numbers:
+                    pass_on(copy, core_copy, slot, number)
+
+    def turn_in(kind):
+        @pl.when(owner)
+        def _():
+            for copy in loads()[2 + 2 * kind : 4 + 2 * kind]:
+                copy.wait()
+
+            def turn(at, carry):
+                columns = pl.ds(pl.multiple_of(at * 256, 256), 256)
+                weights[end, kind * width : (kind + 1) * width, columns] = raw_in[
+                    kind, columns, :
+                ].T
+                return carry
+
+            lax.fori_loop(0, model // 256, turn, 0)
+
+        start_own(m_copy, m_core, (kind,))
+        pass_back(m_copy, (kind,))
+
+    def turn_up(kind):
+        @pl.when(owner)
+        def _():
+            loads()[7 + kind].wait()
+
+            def turn(at, carry):
+                columns = pl.ds(pl.multiple_of(at * 256, 256), 256)
+                turned[kind, :, columns] = raw_up[kind, columns, :].T
+                return carry
+
+            lax.fori_loop(0, model // 256, turn, 0)
+            turned_copy(kind).start()
 
     @pl.when(owner)
     def _():
-        for copy in loads()[:6]:
+        for copy in loads()[:2]:
             copy.wait()
-        for kind in range(2):
-            for at in range(model // 128):
-                weights[end, kind * width : (kind + 1) * width, at * 128 : (at + 1) * 128] = (
-                    raw_in[kind, at * 128 : (at + 1) * 128, :].astype(wide).T.astype(low_type)
-                )
         for row in range(2 * width + 16, 3 * width, 16):
             weights[end, row : row + 16, model:] = jnp.zeros((16, width), low_type)
 
-    for slot in range(2):
-
-        @pl.when(end == slot)
-        def _():
-            for number in range(3):
-                pass_on(m_copy, m_core, slot, number)
+    start_own(m_copy, m_core, (2,))
+    pass_back(m_copy, (2,))
+    turn_in(0)
+    turn_in(1)
 
     @pl.when(owner)
     def _():
-        for copy in loads()[6:]:
-            copy.wait()
-        for kind in range(2):
-
-            def turn(at, carry):
-                columns = pl.ds(pl.multiple_of(at * 128, 128), 128)
-                for tile in range(raw_up.shape[2] // 128):
-                    turned[kind, tile * 128 : (tile + 1) * 128, columns] = (
-                        raw_up[kind, columns, tile * 128 : (tile + 1) * 128]
-                        .astype(wide)
-                        .T.astype(low_type)
-                    )
-                return carry
-
-            lax.fori_loop(0, model // 128, turn, 0)
-            turned_copy(kind).start()
-
+        loads()[6].wait()
+        turned_copy(2).start()
+
+    turn_up(0)
+    turn_up(1)
     gather_tokens.relay()
-
-    for number in range(3):
-        for slot in range(2):
-
-            @pl.when(end != slot)
-            def _():
-                m_copy(slot, number, 0, 0).wait_recv()
-                pass_on(m_copy, m_core, slot, number)
+    m_order = (2, 0, 1)
+
+    @pl.when(end < 3)
+    def _():
+        for number in m_order:
+            for slot in (1, 0):
+
+                @pl.when(end != slot)
+                def _():
+                    m_copy(slot, number, 0, 0).wait_recv()
+                    pass_on(m_copy, m_core, slot, number)
 
     @pl.when(owner)
     def _():
-        turned_copy(0).wait()
-        turned_copy(1).wait()
-
-    for slot in range(2):
-
-        @pl.when(end == slot)
-        def _():
-            for number in range(6):
-                pass_on(f_copy, f_core, slot, number)
-
-    def f_step(step):
-        slot, number = 1 - step % 2, step // 2
-
-        @pl.when((end != slot) & (end < 3))
-        def _():
+        for kind in range(3):
+            turned_copy(kind).wait()
+
+    f_order = (4, 5, 0, 1, 2, 3)
+    start_own(f_copy, f_core, f_order)
+
+    def f_pass(slot, numbers):
+        for number in numbers:
             f_copy(slot, number, 0, 0).wait_recv()
             pass_on(f_copy, f_core, slot, number)
+
+    def f_step(step):
+        @pl.when(end == 1)
+        def _():
+            f_pass(0, ((), (4, 5), (0, 1), (2, 3), (), ())[step])
+
+        @pl.when(end == 2)
+        def _():
+            f_pass(1, ((4,), (5, 0), (1, 2), (3,), (), ())[step])
+            f_pass(0, ((), (), (), (4,), (5, 0), (1, 2, 3))[step])
+
+        if step == 0:
+            pass_back(f_copy, f_order)
+
+        @pl.when(end == 0)
+        def _():
+            f_pass(1, ((), (), (), (), (), f_order)[step])
 
     for to in range(4):
 
@@ -819,13 +853,25 @@
     for block in range(4):
         norm_block(block)
     gather_cot.begin()
-    for step in range(3):
-        f_step(step)
-
-    for head in range(4):
-        if head >= 2:
-            for number in range(3):
+    f_step(0)
+
+    late = end >= 2
+    for turn in range(4):
+        head = (turn + 2 * late) % 4
+        if turn == 2:
+
+            @pl.when(end == 3)
+            def _():
+                for number in m_order:
+                    for slot in (1, 0):
+                        m_copy(slot, number, 0, 0).wait_recv()
+                        m_core(slot, number).start()
+
+        @pl.when(head >= 2)
+        def _():
+            for number in m_order:
                 m_core(head - 2, number).wait_recv()
+
         views = weight_views(weights.at[pl.ds(head, 1)], width)
 
         def step_block(block, carry):
@@ -837,26 +883,23 @@
             saved_p[head, rows, :] = projected
             saved_state[head, rows, :] = states
             saved_low[head, rows, :] = mixed_low
-            if head == 0:
+            if turn == 0:
                 acc[rows, :] = product
-            elif head < 3:
+            elif turn < 3:
                 acc[rows, :] += product
             else:
                 part[rows, :] = (acc[rows, :] + product).astype(low_type)
             return carry
 
         lax.fori_loop(0, 4, step_block, 0)
-        f_step(2 * head + 3)
-        if head < 3:
-            f_step(2 * head + 4)
-        if head == 0:
+        if turn == 3:
+            reduce.begin()
+        f_step(turn + 1)
+        if turn == 0:
             gather_cot.relay()
-        if head == 3:
-            reduce.begin()
-
-    f_step(10)
-    f_step(11)
+
     reduce.relay()
+    f_step(5)
     reduce.arrive()
     half = slots // 2
     for number in range(2):
@@ -869,8 +912,8 @@
 
     @pl.when(end == 3)
     def _():
-        for number in range(6):
-            for slot in (1, 0):
+        for slot in (1, 0):
+            for number in f_order:
                 f_copy(slot, number, 0, 0).wait_recv()
                 f_core(slot, number).start()
 
@@ -936,6 +979,7 @@
             pltpu.VMEM((4, slots, model + width), low_type),
             pltpu.VMEM((2, model, width), low_type),
             pltpu.VMEM((2, model, window), low_type),
+            pltpu.VMEM((ffn_width, model), low_type),
             pltpu.VMEM((2, window, model), low_type),
             pltpu.VMEM((4, 16, model // 4), low_type),
             pltpu.VMEM((rows, model), wide),
@@ -943,7 +987,7 @@
         ]
         + Reduce.scratch(slots, model)
         + [
-            dma((12,)),
+            dma((13,)),
             dma((4,)),
             dma((4,)),
             dma((2, 2, 3)),
@@ -1027,38 +1071,30 @@
     for load in loads:
         load.wait()
 
-    cuts = []
-    low = 0
-    while low < hidden:
-        cuts.append((low, min(low + 512, hidden)))
-        low += 512
-
-    def block_step(block, carry):
+    split = -(-2 * ffn_width // 128) * 128
+
+    def block_step(low, high, block, carry):
         rows = pl.ds(pl.multiple_of(block * slots, slots), slots)
         x = x_ref[rows, :]
         grad_out = go_ref[rows, :]
-        sum_out = jnp.zeros((slots, model), wide)
-        sum_in = jnp.zeros((slots, model), wide)
-        for low, high in cuts:
-            pre_gate = dot_rows(x, held[0, low:high])
-            pre_up = dot_rows(x, held[1, low:high])
-            active, slope = gelu_parts(pre_gate)
-            ffn_low = (active * pre_up).astype(low_type)
-            grad_act = dot_rows(grad_out, held[2, low:high])
-            gate_low = (grad_act * pre_up * slope).astype(low_type)
-            up_low = (grad_act * active).astype(low_type)
-            sum_out = sum_out + dot_plain(ffn_low, held[2, low:high])
-            sum_in = (
-                sum_in + dot_plain(gate_low, held[0, low:high]) + dot_plain(up_low, held[1, low:high])
-            )
-            lows[0, rows, low:high] = gate_low
-            lows[1, rows, low:high] = up_low
-            lows[2, rows, low:high] = ffn_low
+        pre_gate = dot_rows(x, held[0, low:high])
+        pre_up = dot_rows(x, held[1, low:high])
+        active, slope = gelu_parts(pre_gate)
+        ffn_low = (active * pre_up).astype(low_type)
+        grad_act = dot_rows(grad_out, held[2, low:high])
+        gate_low = (grad_act * pre_up * slope).astype(low_type)
+        up_low = (grad_act * active).astype(low_type)
+        sum_out = dot_plain(ffn_low, held[2, low:high])
+        sum_in = dot_plain(gate_low, held[0, low:high]) + dot_plain(up_low, held[1, low:high])
+        lows[0, rows, low:high] = gate_low
+        lows[1, rows, low:high] = up_low
+        lows[2, rows, low:high] = ffn_low
+        if low > 0:
+            sum_in = sum_in + part_in[rows, :].astype(wide)
+            sum_out = sum_out + part_out[rows, :].astype(wide)
         part_in[rows, :] = sum_in.astype(low_type)
         part_out[rows, :] = sum_out.astype(low_type)
         return carry
-
-    lax.fori_loop(0, 4, block_step, 0)
 
     reduce_in = Reduce(part_in, in_x, in_y, in_pass, in_last, i_send, i_recv, member, z)
     reduce_out = Reduce(
@@ -1073,9 +1109,6 @@
         z,
     )
     gather = Gather(res_low.at[0], res_low, g_send, g_recv, member, z)
-    reduce_in.begin()
-
-    split = (2 * ffn_width // 128) * 128
     middle = model // 2
 
     def weight_grads(kind, low, high):
@@ -1088,18 +1121,13 @@
 
     def core_copy(slot, kind):
         return remote(
-            held.at[kind, pl.ds((2 + slot) * ffn_width, ffn_width)],
+            held.at[kind, pl.ds((2 * slot + 1) * ffn_width, ffn_width)],
             paired.at[slot, kind],
             core_send.at[slot, kind],
             core_recv.at[slot, kind],
             other,
             z,
         )
-
-    for kind in range(3):
-        weight_grads(kind, split, hidden)
-        core_copy(0, kind).start()
-        core_copy(1, kind).start()
 
     def chunk(number):
         return number // 2, pl.ds((number % 2) * half_ffn, half_ffn)
@@ -1115,30 +1143,30 @@
             line_place(to_end, core),
         )
 
-    def pair_up(slot, number):
-        at, rows = chunk(number)
-        own = held[at, pl.ds(slot * ffn_width + (number % 2) * half_ffn, half_ffn)]
-        paired[slot, at, rows] = add_low(own, paired[slot, at, rows])
-
-    for kind in range(3):
-        weight_grads(kind, 0, split)
-        for slot in range(2):
-            core_copy(slot, kind).wait_recv()
-            for number in (2 * kind, 2 * kind + 1):
-                pair_up(slot, number)
-
-                @pl.when(end == 3)
+    def pair_up(slot, kind):
+        core_copy(slot, kind).wait_recv()
+        for number in (2 * kind, 2 * kind + 1):
+            at, rows = chunk(number)
+            own = held[at, pl.ds(2 * slot * ffn_width + (number % 2) * half_ffn, half_ffn)]
+            paired[slot, at, rows] = add_low(own, paired[slot, at, rows])
+
+            @pl.when(end == 3)
+            def _():
+                line_copy(slot, number, 2).start()
+
+            if slot == 1:
+
+                @pl.when(end == 0)
                 def _():
-                    line_copy(slot, number, 2).start()
-
-                if slot == 1:
-
-                    @pl.when(end == 0)
-                    def _():
-                        line_copy(2, number, 1).start()
-
-        if kind == 0:
-            reduce_in.relay()
+                    line_copy(2, number, 1).start()
+
+    def part_grads(slot, low, high):
+        for kind in range(3):
+            weight_grads(kind, low, high)
+            core_copy(slot, kind).start()
+            if kind > 0:
+                pair_up(slot, kind - 1)
+        pair_up(slot, 2)
 
     def summed(slot, kinds, number):
         at, rows = chunk(number)
@@ -1147,24 +1175,23 @@
             result = result + arrived[kind, at, rows].astype(wide)
         return result.astype(low_type)
 
-    def line_step(number):
+    def outer_step(number):
         at, rows = chunk(number)
 
         @pl.when((end == 2) | (end == 1))
         def _():
             line_copy(0, number, 0).wait_recv()
             paired[0, at, rows] = summed(0, (0,), number)
+            line_copy(0, number, end - 1).start()
+
+    def inner_step(number):
+        at, rows = chunk(number)
 
         @pl.when(end == 2)
         def _():
-            line_copy(0, number, 1).start()
             line_copy(1, number, 0).wait_recv()
             paired[1, at, rows] = summed(1, (1,), number)
             line_copy(1, number, 1).start()
-
-        @pl.when(end == 1)
-        def _():
-            line_copy(0, number, 0).start()
 
     def out_copy(slot, number):
         at, rows = chunk(number)
@@ -1188,7 +1215,16 @@
             paired[0, at, rows] = summed(0, (0,), number)
             out_copy(0, number).start()
 
-    line_step(0)
+    lax.fori_loop(0, 4, functools.partial(block_step, 0, split), 0)
+    part_grads(0, 0, split)
+    lax.fori_loop(0, 4, functools.partial(block_step, split, hidden), 0)
+    reduce_in.begin()
+    part_grads(1, split, hidden)
+    for number in range(3):
+        outer_step(number)
+    reduce_in.relay()
+    for number in range(3, 6):
+        outer_step(number)
 
     reduce_in.arrive()
     gain = gain_ref[1:2]
@@ -1207,15 +1243,16 @@
         res_low[0, at] = result.astype(low_type)
     gain_out[...] = jnp.concatenate([gain_ref[0:1], gain_sum, jnp.zeros((6, model), wide)], axis=0)
     gather.begin()
-    line_step(1)
-    line_step(2)
+    inner_step(0)
     gather.relay()
-    line_step(3)
+    inner_step(1)
+    inner_step(2)
     gather.arrive()
     reduce_out.begin()
-    line_step(4)
-    line_step(5)
+    inner_step(3)
+    inner_step(4)
     reduce_out.relay()
+    inner_step(5)
     for number in range(6):
         last_step(number)
     reduce_out.arrive()

time: 643 us -> 598 us (0.930)
  Pallas kernels: 590 us -> 548 us
    pallas_call x1, Pallas kernels: 178 us -> 152 us  [front(): pl.pallas_call(functools.partial(front_kernel, sizes), in_specs=[vmem] *...]
    pallas_call x1, Pallas kernels: 153 us -> 134 us  [middle(): pl.pallas_call(functools.partial(middle_kernel, (model, ffn_width)), in_s...]
where the time goes in v6:
time: 598 us; the launch traced here: 589 us
  Pallas kernels  548 us (92%)
  local copies, waits for them, and re-layouts  32.8 us (5%)
  other arithmetic  7.06 us (1%)
    pallas_call x1, Pallas kernels, tail(): pl.pallas_call(functools.partial(tail_kernel, (model, width, ffn_width, p...  156 us
    pallas_call x1, Pallas kernels, front(): pl.pallas_call(functools.partial(front_kernel, sizes), in_specs=[vmem] *...  152 us
    pallas_call x1, Pallas kernels, middle(): pl.pallas_call(functools.partial(middle_kernel, (model, ffn_width)), in_s...  134 us
    pallas_call x1, Pallas kernels, sums(): pl.pallas_call(functools.partial(sums_kernel, sizes), in_specs=[vmem, vme...  64.4 us
    pallas_call x1, Pallas kernels, mix_backward(): pl.pallas_call(functools.partial(mixer_backward_kernel, width), grid=(hea...  41.6 us
    unnamed x42, local copies, waits for them, and re-layouts  30 us

profile of v6, /device:TPU:0, one launch (start us, length us, event | category | flops | bytes accessed | tf_op | source)
XLA Modules:
  0.0 589.5 jit_solution(17008471584193745816)
XLA Ops:
  0.6 0.7 convert_element_type.16
  1.3 0.1 pad.4.clone
  1.4 0.7 convert_convert_fusion
  2.1 0.7 broadcast_in_dim.9
  2.8 1.3 concatenate.10.gain_ref
  4.0 1.4 maximum_maximum_fusion.small_ref
  5.4 0.7 broadcast_in_dim.22.mask_ref
  6.2 0.1 broadcast_in_dim.8
  6.3 2.1 pad_maximum_fusion.tokens_ref
  8.4 2.2 multiply_convert_fusion.cot_ref
  10.6 152.4 %front.1 = (bf16[1024,1536]{1,0:T(8,128)(2,1)}, bf16[4,384,1664]{2,1,0:T(8,128)(2,1)}, bf16[3,1152,1536]{2,1,0:T(8,128)(2,1)}, f32[4,1024,256]{2,1,0:T(8,128)}, ...) custom-call(bf16[256,1664]{1,0:T(8,128)(2,1)} %pad_maximum_fusion.to, ...), custom_call_target="tpu_custom_call" | custom-call | flops 4831838208 | bytes 10616832 | tf_op jit(solution)/shard_map/front/pallas_call | solution.py:961
  163.0 133.8 %middle.1 = (bf16[3,288,1536]{2,1,0:T(8,128)(2,1)}, bf16[4,256,1536]{2,1,0:T(8,128)(2,1)}, f32[256,1536]{1,0:T(8,128)}, f32[8,1536]{1,0:T(8,128)}, bf16[256,1536]{1,0:T(8,128)(2,1)}) custom-call(bf16[1024,1536]{1,0:T(8,128)(2,1)} %bitcast.5, bf16[1024,1536]{1,0:T(8,128)(2,1)} %bitcast.6, bf16[3,1152,1536]{2,1,0:T(8,128)(2,1)} %get-tuple-element.38.weights_ref, ...), custom_call_target="tpu_custom_call" | custom-call | flops 32614907904 | bytes 46399488 | tf_op jit(solution)/shard_map/middle/pallas_call | solution.py:1297
  296.8 1.6 copy-done.7
  298.4 1.2 copy-done.8
  299.6 41.6 %mixer_backward.1 = (bf16[4,384,1664]{2,1,0:T(8,128)(2,1)}, bf16[1024,1536]{1,0:T(8,128)(2,1)}) custom-call(bf16[1024,1536]{1,0:T(8,128)(2,1)} %get-tuple-element.42.x_ref, bf16[1024,1536]{1,0:T(8,128)(2,1)} %bitcast.7, bf16[1024,128]{1,0:T(8,128)(2,1)S(1)} %copy-done.9, bf16[4,384,1664]{2,1,0:T(8,128)(2,1)} %get-tuple-element.45.w_ref, ...), custom_call_target="tpu_custom_call" | custom-call | flops 9663676416 | bytes 27000832 | tf_op jit(solution)/shard_map/mixer_backward/pallas_call | solution.py:351
  341.3 0.0 copy-start.2
  341.3 1.9 copy-done.2
  343.2 64.4 %sums.1 = (bf16[4,384,1664]{2,1,0:T(8,128)(2,1)S(1)}, bf16[4,3,288,1536]{3,2,1,0:T(8,128)(2,1)}, bf16[256,1536]{1,0:T(8,128)(2,1)S(1)}, f32[8,384]{1,0:T(8,128)S(1)}) custom-call(bf16[4,384,1664]{2,1,0:T(8,128)(2,1)} %get-tuple-element.49.mix_ref, bf16[1024,1536]{1,0:T(8,128)(2,1)S(1)} %copy-done.2, bf16[3,288,1536]{2,1,0:T(8,128)(2,1)S(1)} %copy-done.3, ...), custom_call_target="tpu_custom_call" | custom-call | flops 10223616 | bytes 20447232 | tf_op jit(solution)/shard_map/sums/pallas_call | solution.py:1829
  407.6 2.3 copy-done
  409.9 0.6 copy-done.6
  410.5 156.1 %tail.1 = (f32[1,975456]{1,0:T(1,128)}, f32[1,975456]{1,0:T(1,128)}, f32[1,975456]{1,0:T(1,128)}, f32[1,975456]{1,0:T(1,128)}, bf16[4,975456]{1,0:T(4,128)(2,1)}, /*index=5*/f32[2,512]{1,0:T(2,128)}) custom-call(bf16[4,384,1664]{2,1,0:T(8,128)(2,1)} %copy-done, bf16[4,3,288,1536]{3,2,1,0:T(8,128)(2,1)} %get-tuple-element.56.ffn_ref, f32[8,384]{1,0:T(8,128)} %copy-done.6, ...), custom_call_target="tpu_custom_call" | custom-call | flops 19509120 | bytes 39018240 | tf_op jit(solution)/shard_map/tail/pallas_call | solution.py:2192
  566.7 0.9 copy.32
  567.6 0.9 copy.33
  568.5 7.0 %copy.34 = f32[1,975456]{1,0:T(1,128)} copy(f32[1,975456]{1,0:T(1,128)} %get-tuple-element.76) | data formatting | bytes 7803648
  575.5 2.0 copy.35
  577.5 1.5 copy-done.11
  579.0 2.0 copy.36
  581.0 2.0 copy.37
  583.0 1.4 slice-done
  584.4 0.8 slice-done.1
  585.2 3.2 copy.38
  588.5 0.6 copy.39
  (27 shorter events, 0.1 us)
Async XLA Ops:
  163.0 133.8 %copy-start.9 = (bf16[1024,128]{1,0:T(8,128)(2,1)S(1)}, bf16[1024,128]{1,0:T(8,128)(2,1)}, u32[]{:S(2)}) copy-start(bf16[1024,128]{1,0:T(8,128)(2,1)} %get-tuple-element.44.pos_ref) | copy-start | bytes 786436
  296.8 1.6 copy-start.7
  298.4 1.2 copy-start.8
  299.6 41.6 %copy-start.1 = (bf16[256,1536]{1,0:T(8,128)(2,1)S(1)}, bf16[256,1536]{1,0:T(8,128)(2,1)}, u32[]{:S(2)}) copy-start(bf16[256,1536]{1,0:T(8,128)(2,1)} %tokens_ref.1) | copy-start | bytes 2359300
  299.6 41.6 %copy-start.3 = (bf16[3,288,1536]{2,1,0:T(8,128)(2,1)S(1)}, bf16[3,288,1536]{2,1,0:T(8,128)(2,1)}, u32[]{:S(2)}) copy-start(bf16[3,288,1536]{2,1,0:T(8,128)(2,1)} %get-tuple-element.51.ffn_ref) | copy-start | bytes 7962628
  299.6 41.7 %copy-start.4 = (f32[256,1536]{1,0:T(8,128)S(1)}, f32[256,1536]{1,0:T(8,128)}, u32[]{:S(2)}) copy-start(f32[256,1536]{1,0:T(8,128)} %get-tuple-element.52.res_ref) | copy-start | bytes 4718596
  299.6 41.7 %copy-start.5 = (f32[8,1536]{1,0:T(8,128)S(1)}, f32[8,1536]{1,0:T(8,128)}, u32[]{:S(2)}) copy-start(f32[8,1536]{1,0:T(8,128)} %get-tuple-element.53.gain_ref) | copy-start | bytes 147460
  341.3 1.9 copy-start.2
  407.6 2.3 copy-start
  409.9 0.6 copy-start.6
  410.5 156.2 %copy-start.13 = (bf16[256,1536]{1,0:T(8,128)(2,1)S(1)}, bf16[256,1536]{1,0:T(8,128)(2,1)}, u32[]{:S(2)}) copy-start(bf16[256,1536]{1,0:T(8,128)(2,1)} %get-tuple-element.74) | copy-start | bytes 2359300
  568.5 7.0 %copy-start.12 = (f32[1,975456]{1,0:T(1,128)S(1)}, f32[1,975456]{1,0:T(1,128)}, u32[]{:S(2)}) copy-start(f32[1,975456]{1,0:T(1,128)} %get-tuple-element.77) | copy-start | bytes 11705476
  575.5 3.5 copy-start.11
  575.5 5.5 copy-start.10
  579.0 5.4 slice-start
  581.0 4.3 slice-start.1
  585.2 3.2 copy-start.14

commit v7 on v6

--- a/solution.py
+++ b/solution.py
@@ -17,144 +17,12 @@
 corr_two = 1.0 - beta_two**10.0
 low_type = jnp.bfloat16
 wide = jnp.float32
-axes = ("dp", "shard")
 gelu_scale = 0.7978845608028654
 gelu_cube = 0.044715
 
 
-def device_pairs(target):
-    found = []
-    for chip in range(4):
-        for core in range(2):
-            for z in range(4):
-                to = target(chip, core, z)
-                if to is not None:
-                    source = (chip * 2 + core) * 4 + z
-                    found.append((source, (to[0] * 2 + to[1]) * 4 + to[2]))
-    return found
-
-
-def line_pairs(moves):
-    moves = dict(moves)
-
-    def target(chip, core, z):
-        end = z if core == 0 else 3 - z
-        if end not in moves:
-            return None
-        to = moves[end]
-        return (chip, core, to if core == 0 else 3 - to)
-
-    return device_pairs(target)
-
-
-def step_pairs(step):
-    return device_pairs(
-        lambda chip, core, z: (chip, core, z + step) if 0 <= z + step < 4 else None
-    )
-
-
-def plane_pairs(flip, owners_only=False):
-    return device_pairs(
-        lambda chip, core, z: None if owners_only and core != z // 2 else (chip ^ flip, core, z)
-    )
-
-
-core_pairs = device_pairs(lambda chip, core, z: (chip, 1 - core, z))
-owner_core_pairs = device_pairs(
-    lambda chip, core, z: (chip, 1 - core, z) if core == z // 2 else None
-)
-
-
-def move(value, pairs):
-    return lax.ppermute(value, axes, pairs)
-
-
-def plane_gather(value, dim=0, owners_only=False):
-    half = value.shape[dim] // 2
-    across_x = move(value, plane_pairs(1, owners_only))
-    across_y = move(value, plane_pairs(2, owners_only))
-    first = lax.slice_in_dim(across_x, 0, half, axis=dim)
-    second = lax.slice_in_dim(across_y, half, 2 * half, axis=dim)
-    first = move(first, plane_pairs(2, owners_only))
-    second = move(second, plane_pairs(1, owners_only))
-    return (value, across_x, across_y, jnp.concatenate([first, second], axis=dim))
-
-
-def plane_reduce(parts):
-    slots = parts.shape[0] // 4
-    half = slots // 2
-    mine, for_x, for_y, for_d = (
-        parts[number * slots : (number + 1) * slots] for number in range(4)
-    )
-    top = slice(0, half)
-    low = slice(half, slots)
-    from_x = move(jnp.concatenate([for_x[top], for_d[top]]), plane_pairs(1))
-    from_y = move(jnp.concatenate([for_y[low], for_d[low]]), plane_pairs(2))
-    send_y = (for_y[top].astype(wide) + from_x[half:].astype(wide)).astype(low_type)
-    send_x = (for_x[low].astype(wide) + from_y[half:].astype(wide)).astype(low_type)
-    last_top = move(send_y, plane_pairs(2))
-    last_low = move(send_x, plane_pairs(1))
-    return jnp.concatenate(
-        [
-            mine[top].astype(wide) + from_x[:half].astype(wide) + last_top.astype(wide),
-            mine[low].astype(wide) + from_y[:half].astype(wide) + last_low.astype(wide),
-        ]
-    )
-
-
-def pick(end, choices):
-    result = choices[3]
-    for number in (2, 1, 0):
-        result = jnp.where(end == number, choices[number], result)
-    return result
-
-
-def line_spread(own, end):
-    ahead = move(own, line_pairs({0: 1, 1: 2}))
-    back = move(own, line_pairs({1: 0}))
-    ahead_two = move(ahead, line_pairs({1: 2, 2: 3}))
-    ahead_three = move(ahead_two, line_pairs({2: 3}))
-    return (
-        pick(end, [own, ahead, ahead_two, ahead_three]),
-        pick(end, [back, own, ahead, ahead_two]),
-    )
-
-
 def add_low(left, right):
     return (left.astype(wide) + right.astype(wide)).astype(low_type)
-
-
-def line_sum(outer, inner, end):
-    first = add_low(outer, move(outer, line_pairs({3: 2})))
-    inner_one = add_low(inner, move(inner, line_pairs({3: 2, 0: 1})))
-    second = add_low(outer, move(first, line_pairs({2: 1})))
-    inner_two = add_low(inner_one, move(inner_one, line_pairs({2: 1})))
-    third = add_low(outer, move(second, line_pairs({1: 0})))
-    return jnp.where(end == 0, third, inner_two)
-
-
-def turn_pairs(turn):
-    return device_pairs(lambda chip, core, z: (chip, core, (z + turn) % 4))
-
-
-def all_slices(own, z):
-    found = [own] + [move(own, turn_pairs(turn)) for turn in (1, 2, 3)]
-    return jnp.concatenate(
-        [
-            sum(jnp.where((z - at) % 4 == turn, found[turn], 0) for turn in range(4))
-            for at in range(4)
-        ],
-        axis=-1,
-    )
-
-
-def shard_slices(value, z):
-    size = value.shape[-1] // 4
-
-    def part(turn):
-        return lax.dynamic_slice_in_dim(value, ((z + turn) % 4) * size, size, axis=1)
-
-    return part(0) + sum(move(part(turn), turn_pairs(turn)) for turn in (1, 2, 3))
 
 
 def dot_rows(left, right):
@@ -259,38 +127,20 @@
     return projected, states, mixed_low, dot_plain(mixed_low, out)
 
 
-def mixer_backward_kernel(
-    width,
-    x_ref,
-    res_ref,
-    pos_ref,
-    w_ref,
-    p_ref,
-    state_ref,
-    low_ref,
-    grad_ref,
-    gin_ref,
-    acc_w,
-    acc_in,
-):
-    head = pl.program_id(0)
-    block = pl.program_id(1)
-    slots, model = x_ref.shape
-    proj, out, gates, small = weight_views(w_ref, width)
-    position = slot_position(pos_ref[...])
-    first = p_ref[0, :, 0:width]
-    res_low = res_ref[...]
-    states = state_ref[0]
+def mixer_back_step(position, views, projected, states, res_low, width):
+    _, out, gates, small = views
+    first = projected[:, :width]
     conv_out, shifted, conv_low, recur_gate, input_gate, rate, decay, gone, root = mixer_parts(
         first, position, small, gates
     )
     grad_mixed = dot_rows(res_low, out)
-    active, slope = gelu_parts(p_ref[0, :, width:])
+    active, slope = gelu_parts(projected[:, width:])
     grad_second = grad_mixed * states * slope
     adjoint = scan_slots(shift_up(decay, 1), grad_mixed * active, shift_up)
     grad_decay = adjoint * shift_down(states, 1)
-    grad_root = adjoint * input_gate * conv_out
-    grad_input_gate = adjoint * root * conv_out
+    gated = adjoint * conv_out
+    grad_root = gated * input_gate
+    grad_input_gate = gated * root
     grad_conv = adjoint * root * input_gate
     grad_log = grad_decay * decay - grad_root * (1.0 - gone) / root
     grad_recur = -rate * grad_log
@@ -312,74 +162,8 @@
     sums.append(jnp.sum(grad_logit_a, axis=0, keepdims=True))
     sums.append(jnp.sum(grad_logit_b, axis=0, keepdims=True))
     sums.append(grad_param)
-    grad_small = jnp.concatenate(sums, axis=0)
     proj_low = jnp.concatenate([grad_first, grad_second], axis=1).astype(low_type)
-    part = dot_plain(proj_low, proj)
-    rows = pl.ds(pl.multiple_of(block * slots, slots), slots)
-
-    @pl.when(block == 0)
-    def _():
-        acc_w[...] = jnp.zeros_like(acc_w)
-
-    acc_w[0 : 2 * width, 0:model] += dot_slots(proj_low, x_ref[...])
-    acc_w[2 * width : 3 * width, 0:model] += dot_slots(low_ref[0], res_low)
-    acc_w[0:width, model:] += grad_gates[:, :width]
-    acc_w[width : 2 * width, model:] += grad_gates[:, width:]
-    acc_w[2 * width : 2 * width + 8, model:] += grad_small
-
-    @pl.when(head == 0)
-    def _():
-        acc_in[rows, :] = part
-
-    @pl.when(head > 0)
-    def _():
-        acc_in[rows, :] += part
-
-    @pl.when(block == pl.num_programs(1) - 1)
-    def _():
-        grad_ref[0] = acc_w[...].astype(low_type)
-
-    @pl.when(head == pl.num_programs(0) - 1)
-    def _():
-        gin_ref[rows, :] = acc_in[rows, :].astype(low_type)
-
-
-def mix_backward(mix_in, res_low, position, weights, saved, slots, width):
-    rows, model = mix_in.shape
-    heads = weights.shape[0]
-    blocks = rows // slots
-    return pl.pallas_call(
-        functools.partial(mixer_backward_kernel, width),
-        grid=(heads, blocks),
-        in_specs=[
-            pl.BlockSpec((slots, model), lambda h, b: (b, 0)),
-            pl.BlockSpec((slots, model), lambda h, b: (b, 0)),
-            pl.BlockSpec((slots, width), lambda h, b: (b, 0)),
-            pl.BlockSpec((1,) + weights.shape[1:], lambda h, b: (h, 0, 0)),
-            pl.BlockSpec((1, slots, 2 * width), lambda h, b: (h, b, 0)),
-            pl.BlockSpec((1, slots, width), lambda h, b: (h, b, 0)),
-            pl.BlockSpec((1, slots, width), lambda h, b: (h, b, 0)),
-        ],
-        out_specs=[
-            pl.BlockSpec((1,) + weights.shape[1:], lambda h, b: (h, 0, 0)),
-            pl.BlockSpec((rows, model), lambda h, b: (0, 0)),
-        ],
-        out_shape=[
-            jax.ShapeDtypeStruct(weights.shape, low_type),
-            jax.ShapeDtypeStruct((rows, model), low_type),
-        ],
-        scratch_shapes=[
-            pltpu.VMEM(weights.shape[1:], wide),
-            pltpu.VMEM((rows, model), wide),
-        ],
-        compiler_params=pltpu.CompilerParams(vmem_limit_bytes=48 * 1024 * 1024),
-        cost_estimate=pl.CostEstimate(
-            flops=2 * rows * model * heads * width * 6,
-            bytes_accessed=heads * rows * width * 14 + weights.size * 4 + rows * model * 6,
-            transcendentals=heads * rows * width * 6,
-        ),
-        name="mixer_backward",
-    )(mix_in, res_low, position, weights, *saved)
+    return proj_low, grad_gates, jnp.concatenate(sums, axis=0)
 
 
 def peer_x(chip):
@@ -1530,10 +1314,15 @@
         copy.wait_send()
 
 
-def sums_kernel(
+def back_kernel(
     sizes,
-    mix_ref,
-    part_ref,
+    x_hbm,
+    res_hbm,
+    starts_ref,
+    w_hbm,
+    p_hbm,
+    state_hbm,
+    low_hbm,
     ffn_ref,
     tokens_ref,
     res_ref,
@@ -1542,6 +1331,17 @@
     ffn_out,
     tokens_out,
     gain_out,
+    x_ref,
+    low_res,
+    w_ref,
+    p_ref,
+    state_ref,
+    low_ref,
+    proj_grads,
+    gate_acc,
+    small_acc,
+    grads,
+    part_ref,
     paired,
     arrived,
     total,
@@ -1553,6 +1353,7 @@
     gain_plane,
     gain_line,
     gain_seen,
+    load_sem,
     core_send,
     core_recv,
     line_send,
@@ -1571,18 +1372,41 @@
     end = z + core * (3 - 2 * z)
     slots = tokens_ref.shape[0]
     half = slots // 2
-    to_x = peer_x(chip) * 2 + core
-    to_y = peer_y(chip) * 2 + core
     other = chip * 2 + 1 - core
     scatter = Scatter(sizes, member, z, unit_send, unit_recv)
+
+    order = (2, 0, 3, 1)
+    common = [
+        pltpu.make_async_copy(x_hbm, x_ref, load_sem.at[4, 0]),
+        pltpu.make_async_copy(res_hbm, low_res, load_sem.at[4, 1]),
+    ]
+
+    def head_loads(head):
+        return [
+            pltpu.make_async_copy(source.at[head], target.at[head], load_sem.at[head, number])
+            for number, (source, target) in enumerate(
+                ((w_hbm, w_ref), (p_hbm, p_ref), (state_hbm, state_ref), (low_hbm, low_ref))
+            )
+        ]
+
+    for copy in head_loads(order[0]) + common:
+        copy.start()
+    for head in order[1:]:
+        for copy in head_loads(head):
+            copy.start()
     enter(member, z)
+
+    @pl.when(scatter.owner)
+    def _():
+        scatter.each(scatter.up_unit, 0, 2 * scatter.across, ffn_ref, ffn_out, begin)
+        scatter.each(scatter.down_unit, 0, 6, ffn_ref, ffn_out, begin)
 
     def rows(number):
         return pl.ds(number * width, width)
 
     def core_copy(slot, number):
         return remote(
-            mix_ref.at[2 + slot, rows(number)],
+            grads.at[2 + slot, rows(number)],
             paired.at[slot, rows(number)],
             core_send.at[slot, number],
             core_recv.at[slot, number],
@@ -1590,28 +1414,9 @@
             z,
         )
 
-    for slot in range(2):
-        for number in range(3):
-            core_copy(slot, number).start()
-
-    def plane_copy(number):
-        source, target, to = (
-            (part_ref.at[pl.ds(slots, half)], from_x.at[0], to_x),
-            (part_ref.at[pl.ds(3 * slots, half)], from_x.at[1], to_x),
-            (part_ref.at[pl.ds(2 * slots + half, half)], from_y.at[0], to_y),
-            (part_ref.at[pl.ds(3 * slots + half, half)], from_y.at[1], to_y),
-            (passing.at[0], last.at[0], to_y),
-            (passing.at[1], last.at[1], to_x),
-        )[number]
-        return remote(source, target, plane_send.at[number], plane_recv.at[number], to, z)
-
-    for number in (1, 3, 0, 2):
-        plane_copy(number).start()
-
-    @pl.when(scatter.owner)
-    def _():
-        scatter.each(scatter.up_unit, 0, 2 * scatter.across, ffn_ref, ffn_out, begin)
-        scatter.each(scatter.down_unit, 0, 6, ffn_ref, ffn_out, begin)
+    reduce = Reduce(
+        part_ref, from_x, from_y, passing, last, plane_send, plane_recv, member, z
+    )
 
     def line_copy(kind, number, source, to_end):
         return remote(
@@ -1623,10 +1428,10 @@
             line_place(to_end, core),
         )
 
-    for slot in range(2):
+    def pair_up(slot):
         for number in range(3):
             core_copy(slot, number).wait_recv()
-            both = mix_ref[slot, rows(number)].astype(wide) + paired[slot, rows(number)].astype(wide)
+            both = grads[slot, rows(number)].astype(wide) + paired[slot, rows(number)].astype(wide)
             paired[slot, rows(number)] = both.astype(low_type)
 
             @pl.when(end == 3)
@@ -1638,17 +1443,6 @@
                 @pl.when(end == 0)
                 def _():
                     line_copy(2, number, paired.at[slot, rows(number)], 1).start()
-
-    plane_copy(1).wait_recv()
-    passing[0] = (
-        part_ref[2 * slots : 2 * slots + half].astype(wide) + from_x[1].astype(wide)
-    ).astype(low_type)
-    plane_copy(4).start()
-    plane_copy(3).wait_recv()
-    passing[1] = (
-        part_ref[slots + half : 2 * slots].astype(wide) + from_y[1].astype(wide)
-    ).astype(low_type)
-    plane_copy(5).start()
 
     def summed(slot, kinds, number):
         result = paired[slot, rows(number)].astype(wide)
@@ -1658,6 +1452,13 @@
 
     def on_arrival(kind, number):
         line_copy(kind, number, paired.at[0, rows(number)], 0).wait_recv()
+
+    def outer_step(place, number):
+        @pl.when(end == place)
+        def _():
+            on_arrival(0, number)
+            paired[0, rows(number)] = summed(0, (0,), number)
+            line_copy(0, number, paired.at[0, rows(number)], place - 1).start()
 
     def share(number):
         if number < 2:
@@ -1670,20 +1471,71 @@
             scatter.each(scatter.out_unit, 0, 4, total, mix_out, begin)
             scatter.smalls(total, mix_out, begin)
 
-    for number in range(3):
-
-        @pl.when((end == 2) | (end == 1))
-        def _():
-            on_arrival(0, number)
-            paired[0, rows(number)] = summed(0, (0,), number)
-
-        @pl.when(end == 2)
-        def _():
-            line_copy(0, number, paired.at[0, rows(number)], 1).start()
-
-        @pl.when(end == 1)
-        def _():
-            line_copy(0, number, paired.at[0, rows(number)], 0).start()
+    for copy in common:
+        copy.wait()
+    for turn, head in enumerate(order):
+        for copy in head_loads(head):
+            copy.wait()
+        views = weight_views(w_ref.at[pl.ds(head, 1)], width)
+        gate_acc[...] = jnp.zeros_like(gate_acc)
+        small_acc[...] = jnp.zeros_like(small_acc)
+
+        def step_block(block, carry):
+            at = pl.ds(pl.multiple_of(block * slots, slots), slots)
+            proj_low, grad_gates, grad_small = mixer_back_step(
+                slot_position(starts_ref[at, :]),
+                views,
+                p_ref[head, at, :],
+                state_ref[head, at, :],
+                low_res[at, :],
+                width,
+            )
+            proj_grads[at, head * 2 * width : (head + 1) * 2 * width] = proj_low
+            gate_acc[...] += grad_gates
+            small_acc[...] += grad_small
+            return carry
+
+        lax.fori_loop(0, 4, step_block, 0)
+        grads[head, 0 : 2 * width, 0:model] = dot_slots(
+            proj_grads[:, head * 2 * width : (head + 1) * 2 * width], x_ref[...]
+        ).astype(low_type)
+        grads[head, 2 * width : 3 * width, 0:model] = dot_slots(
+            low_ref[head], low_res[...]
+        ).astype(low_type)
+        grads[head, 0:width, model:] = gate_acc[:, :width].astype(low_type)
+        grads[head, width : 2 * width, model:] = gate_acc[:, width:].astype(low_type)
+        grads[head, 2 * width : 3 * width, model:] = jnp.concatenate(
+            [small_acc[...], jnp.zeros((width - 8, width), wide)], axis=0
+        ).astype(low_type)
+        if head >= 2:
+            for number in range(3):
+                core_copy(head - 2, number).start()
+        if turn == 1:
+            pair_up(0)
+        elif turn == 2:
+            outer_step(2, 0)
+            outer_step(2, 1)
+        elif turn == 3:
+            outer_step(2, 2)
+            outer_step(1, 0)
+            outer_step(1, 1)
+
+    def in_block(block, carry):
+        at = pl.ds(pl.multiple_of(block * slots, slots), slots)
+        result = jnp.zeros((slots, model), wide)
+        for head in range(4):
+            result = result + dot_plain(
+                proj_grads[at, head * 2 * width : (head + 1) * 2 * width],
+                w_ref[head, 0 : 2 * width, 0:model],
+            )
+        part_ref[at, :] = result.astype(low_type)
+        return carry
+
+    pair_up(1)
+    lax.fori_loop(0, 4, in_block, 0)
+    reduce.begin()
+    outer_step(1, 2)
+    reduce.relay()
 
     for number in range(3):
 
@@ -1708,15 +1560,12 @@
         def _():
             share(number)
 
-    plane_copy(0).wait_recv()
-    plane_copy(2).wait_recv()
-    plane_copy(4).wait_recv()
-    plane_copy(5).wait_recv()
+    reduce.arrive()
     gain = gain_ref[0:1]
     gain_sum = jnp.zeros((1, model), wide)
-    for number, direct in ((0, from_x), (1, from_y)):
+    for number in range(2):
         at = slice(number * half, (number + 1) * half)
-        grad = part_ref[at].astype(wide) + direct[0].astype(wide) + last[number].astype(wide)
+        grad = reduce.result(number)
         value = tokens_ref[at].astype(wide)
         scale = lax.rsqrt(jnp.mean(value * value, axis=1, keepdims=True) + norm_eps)
         scaled = grad * gain
@@ -1796,8 +1645,7 @@
         scatter.each(scatter.out_unit, 0, 4, total, mix_out, finish_send)
         scatter.smalls(total, mix_out, finish_send)
 
-    for number in range(6):
-        plane_copy(number).wait_send()
+    reduce.finish()
     for slot in range(2):
         for number in range(3):
             core_copy(slot, number).wait_send()
@@ -1816,38 +1664,46 @@
             line_copy(2, number, paired.at[1, rows(number)], 1).wait_send()
 
 
-def sums(mix, part, ffn, tokens, residual_grad, gains, piece_length, width):
+def back(x, res, starts, weights, saved, ffn, tokens, residual_grad, gains, piece_length, width):
     model = tokens.shape[1]
     ffn_width = ffn.shape[1]
     sizes = (model, width, ffn_width, piece_length)
-    half = tokens.shape[0] // 2
-    block = mix.shape[1:]
+    slots = tokens.shape[0]
+    block = weights.shape[1:]
     count = Scatter(sizes, 0, 0, None, None).count
     dma = pltpu.SemaphoreType.DMA
     vmem = pl.BlockSpec(memory_space=pltpu.VMEM)
     anywhere = pl.BlockSpec(memory_space=pl.ANY)
+    held = lambda value: pltpu.VMEM(value.shape, value.dtype)
     return pl.pallas_call(
-        functools.partial(sums_kernel, sizes),
-        in_specs=[vmem, vmem, anywhere, vmem, vmem, vmem],
+        functools.partial(back_kernel, sizes),
+        in_specs=[anywhere, anywhere, vmem] + [anywhere] * 5 + [vmem] * 3,
         out_specs=[anywhere, anywhere, vmem, vmem],
         out_shape=[
-            jax.ShapeDtypeStruct(mix.shape, low_type),
+            jax.ShapeDtypeStruct(weights.shape, low_type),
             jax.ShapeDtypeStruct((4,) + ffn.shape, low_type),
             jax.ShapeDtypeStruct(tokens.shape, low_type),
             jax.ShapeDtypeStruct((8, model // 4), wide),
         ],
-        scratch_shapes=[
+        scratch_shapes=[held(x), held(res), held(weights)]
+        + [held(value) for value in saved]
+        + [
+            pltpu.VMEM((4 * slots, 8 * width), low_type),
+            pltpu.VMEM((width, 2 * width), wide),
+            pltpu.VMEM((8, width), wide),
+            pltpu.VMEM(weights.shape, low_type),
+            pltpu.VMEM((4 * slots, model), low_type),
             pltpu.VMEM((2,) + block, low_type),
             pltpu.VMEM((3,) + block, low_type),
             pltpu.VMEM(block, low_type),
-            pltpu.VMEM((2, half, model), low_type),
-            pltpu.VMEM((2, half, model), low_type),
-            pltpu.VMEM((2, half, model), low_type),
-            pltpu.VMEM((2, half, model), low_type),
+        ]
+        + Reduce.scratch(slots, model)
+        + [
             pltpu.VMEM((8, model), wide),
             pltpu.VMEM((8, 8, model), wide),
             pltpu.VMEM((4, 8, model // 4), wide),
             pltpu.VMEM((4, 8, model // 4), wide),
+            dma((5, 4)),
             dma((2, 3)),
             dma((2, 3)),
             dma((3, 3)),
@@ -1860,16 +1716,16 @@
             dma((4, count)),
         ],
         compiler_params=pltpu.CompilerParams(
-            collective_id=2, has_side_effects=True, vmem_limit_bytes=40 * 1024 * 1024
+            collective_id=2, has_side_effects=True, vmem_limit_bytes=60 * 1024 * 1024
         ),
         cost_estimate=pl.CostEstimate(
-            flops=mix.size * 4, bytes_accessed=mix.size * 8, transcendentals=0
+            flops=weights.size * 4 * slots * 4, bytes_accessed=weights.size * 8, transcendentals=0
         ),
-        name="sums",
-    )(mix, part, ffn, tokens, residual_grad, gains)
-
-
-def tail_kernel(
+        name="back",
+    )(x, res, starts, weights, *saved, ffn, tokens, residual_grad, gains)
+
+
+def adam_kernel(
     sizes,
     mix_ref,
     ffn_ref,
@@ -1881,17 +1737,12 @@
     new_master_ref,
     new_first_ref,
     new_second_ref,
-    weights_ref,
+    rows_ref,
     bias_ref,
     grad,
-    held,
-    spread,
-    send_sem,
-    recv_sem,
 ):
-    model, width, ffn_width, piece_length, chunks, lines, margin = sizes
+    model, width, ffn_width, piece_length, lines, margin = sizes
     member = lax.axis_index("dp")
-    z = lax.axis_index("shard")
     step = pl.program_id(0)
     lead = 128
     start_row = (member * piece_length) // lead
@@ -1900,40 +1751,8 @@
     tiles_ffn = 4 * ffn_width // lead
     tiles_model = model // lead
 
-    def copy_to(origin, chunk, side, to):
-        return pltpu.make_async_remote_copy(
-            src_ref=held.at[origin, chunk],
-            dst_ref=held.at[origin, chunk],
-            send_sem=send_sem.at[side, origin, chunk],
-            recv_sem=recv_sem.at[origin, chunk],
-            device_id=(member, to),
-            device_id_type=pl.DeviceIdType.MESH,
-        )
-
     @pl.when(step == 0)
     def _():
-        barrier = pltpu.get_barrier_semaphore()
-
-        @pl.when(z > 0)
-        def _():
-            pl.semaphore_signal(
-                barrier, inc=1, device_id=(member, z - 1), device_id_type=pl.DeviceIdType.MESH
-            )
-
-        @pl.when(z < 3)
-        def _():
-            pl.semaphore_signal(
-                barrier, inc=1, device_id=(member, z + 1), device_id_type=pl.DeviceIdType.MESH
-            )
-
-        @pl.when((z == 0) | (z == 3))
-        def _():
-            pl.semaphore_wait(barrier, 1)
-
-        @pl.when((z > 0) & (z < 3))
-        def _():
-            pl.semaphore_wait(barrier, 2)
-
         def clear(number, carry):
             grad[pl.ds(pl.multiple_of(number * 256, 256), 256), :] = jnp.zeros((256, lead), wide)
             return carry
@@ -2072,156 +1891,219 @@
         place(small_base, 8 * tiles_in + 6, small_body)
         bias_ref[...] = jnp.concatenate([small[5:7] for small in smalls], axis=1)
 
-    @pl.when(step < chunks)
-    def _():
-        row = margin + step * lines
-        shift = (lead - offset) % lead
-        here = pltpu.roll(grad[pl.ds(row, lines), :], shift, 1)
-        after = pltpu.roll(grad[pl.ds(row + 1, lines), :], shift, 1)
-        lane = lax.broadcasted_iota(jnp.int32, (lines, lead), 1)
-        piece = jnp.where(lane < lead - offset, here, after).reshape(1, lines * lead)
-        piece_ref[...] = piece
-        new_first = beta_one * first_ref[...] + (1.0 - beta_one) * piece
-        new_second = beta_two * second_ref[...] + (1.0 - beta_two) * piece * piece
-        master = master_ref[...]
-        new_master = master - learn_rate * (
-            new_first / corr_one / (jnp.sqrt(new_second / corr_two) + adam_eps)
-            + weight_decay * master
-        )
-        new_first_ref[...] = new_first
-        new_second_ref[...] = new_second
-        new_master_ref[...] = new_master
-        held[z, step] = new_master.reshape(lines, lead).astype(low_type)
-
-        @pl.when(z < 3)
-        def _():
-            copy_to(z, step, 0, z + 1).start()
-
-        @pl.when(z > 0)
-        def _():
-            copy_to(z, step, 1, z - 1).start()
-
-    def pass_on(origin, chunk, right):
-        copy_to(origin, chunk, 0, z).wait_recv()
-        if right:
-
-            @pl.when(z < 3)
-            def _():
-                copy_to(origin, chunk, 0, z + 1).start()
-        else:
-
-            @pl.when(z > 0)
-            def _():
-                copy_to(origin, chunk, 1, z - 1).start()
-
-    @pl.when((step >= chunks) & (step < 2 * chunks))
-    def _():
-        chunk = step - chunks
-
-        @pl.when(z > 0)
-        def _():
-            pass_on(z - 1, chunk, True)
-
-        @pl.when(z < 3)
-        def _():
-            pass_on(z + 1, chunk, False)
-
-    @pl.when(step >= 2 * chunks)
-    def _():
-        chunk = step - 2 * chunks
-
-        @pl.when(z >= 2)
-        def _():
-            pass_on(z - 2, chunk, True)
-
-        @pl.when(z <= 1)
-        def _():
-            pass_on(z + 2, chunk, False)
-
-        @pl.when(z == 3)
-        def _():
-            copy_to(0, chunk, 0, z).wait_recv()
-
-        @pl.when(z == 0)
-        def _():
-            copy_to(3, chunk, 0, z).wait_recv()
-
-        for origin in range(4):
-            spread[origin * lines : (origin + 1) * lines, :] = held[origin, chunk].astype(wide)
-
-        def line(number, carry):
-            weights_ref[:, pl.ds(pl.multiple_of(number * lead, lead), lead)] = spread[
-                pl.ds(number, 4, stride=lines), :
-            ].astype(low_type)
-            return carry
-
-        lax.fori_loop(0, lines, line, 0, unroll=8)
-
-    @pl.when(step == 3 * chunks - 1)
-    def _():
-        for origin in range(4):
-
-            def finish(chunk, carry):
-                @pl.when((origin <= z) & (z < 3))
-                def _():
-                    copy_to(origin, chunk, 0, z).wait_send()
-
-                @pl.when((origin >= z) & (z > 0))
-                def _():
-                    copy_to(origin, chunk, 1, z).wait_send()
-
-                return carry
-
-            lax.fori_loop(0, chunks, finish, 0)
-
-
-def tail(mix, ffn, gains, master, first, second, sizes):
+    row = margin + step * lines
+    shift = (lead - offset) % lead
+    here = pltpu.roll(grad[pl.ds(row, lines), :], shift, 1)
+    after = pltpu.roll(grad[pl.ds(row + 1, lines), :], shift, 1)
+    lane = lax.broadcasted_iota(jnp.int32, (lines, lead), 1)
+    piece = jnp.where(lane < lead - offset, here, after).reshape(1, lines * lead)
+    piece_ref[...] = piece
+    new_first = beta_one * first_ref[...] + (1.0 - beta_one) * piece
+    new_second = beta_two * second_ref[...] + (1.0 - beta_two) * piece * piece
+    master = master_ref[...]
+    new_master = master - learn_rate * (
+        new_first / corr_one / (jnp.sqrt(new_second / corr_two) + adam_eps)
+        + weight_decay * master
+    )
+    new_first_ref[...] = new_first
+    new_second_ref[...] = new_second
+    new_master_ref[...] = new_master
+    rows_ref[0] = new_master.reshape(lines, lead).astype(low_type)
+
+
+def adam(mix, ffn, gains, master, first, second, sizes, chunks):
     model, width, ffn_width = sizes
     piece_length = master.shape[1]
-    chunks = 8
     lines = -(-piece_length // (chunks * 128 * 16)) * 16
     block = lines * 128
     margin = 1536
     rows = -(-(2 * margin + chunks * lines + 8) // 256) * 256
     packed = jax.ShapeDtypeStruct(master.shape, wide)
-    whole = lambda shape: pl.BlockSpec(shape, lambda s: (0,) * len(shape))
-    chunk_spec = pl.BlockSpec((1, block), lambda s: (0, jnp.minimum(s, chunks - 1)))
+    chunk_spec = pl.BlockSpec((1, block), lambda s: (0, s))
     once = lambda shape: pl.BlockSpec(
         shape, lambda s: (0,) * len(shape), pipeline_mode=pl.Buffered(1)
     )
     return pl.pallas_call(
         functools.partial(
-            tail_kernel, (model, width, ffn_width, piece_length, chunks, lines, margin)
+            adam_kernel, (model, width, ffn_width, piece_length, lines, margin)
         ),
-        grid=(3 * chunks,),
+        grid=(chunks,),
         in_specs=[once(mix.shape), once(ffn.shape), once(gains.shape)] + [chunk_spec] * 3,
         out_specs=[chunk_spec] * 4
         + [
-            pl.BlockSpec((4, block), lambda s: (0, jnp.maximum(s - 2 * chunks, 0))),
-            whole((2, 4 * width)),
+            pl.BlockSpec((1, lines, 128), lambda s: (s, 0, 0)),
+            pl.BlockSpec((2, 4 * width), lambda s: (0, 0)),
         ],
         out_shape=[packed] * 4
         + [
-            jax.ShapeDtypeStruct((4, piece_length), low_type),
+            jax.ShapeDtypeStruct((chunks, lines, 128), low_type),
             jax.ShapeDtypeStruct((2, 4 * width), wide),
         ],
-        scratch_shapes=[
-            pltpu.VMEM((rows, 128), wide),
-            pltpu.VMEM((4, chunks, lines, 128), low_type),
-            pltpu.VMEM((4 * lines, 128), wide),
-            pltpu.SemaphoreType.DMA((2, 4, chunks)),
-            pltpu.SemaphoreType.DMA((4, chunks)),
-        ],
-        compiler_params=pltpu.CompilerParams(
-            collective_id=1, has_side_effects=True, vmem_limit_bytes=58 * 1024 * 1024
-        ),
+        scratch_shapes=[pltpu.VMEM((rows, 128), wide)],
+        compiler_params=pltpu.CompilerParams(vmem_limit_bytes=48 * 1024 * 1024),
         cost_estimate=pl.CostEstimate(
             flops=20 * piece_length,
             bytes_accessed=40 * piece_length,
             transcendentals=piece_length,
         ),
-        name="tail",
+        name="adam",
     )(mix, ffn, gains, master, first, second)
+
+
+def spread_kernel(own_ref, weights_ref, held, spread, load_sem, send_sem, recv_sem):
+    chunks, lines, lead = own_ref.shape
+    member = lax.axis_index("dp")
+    z = lax.axis_index("shard")
+    step = pl.program_id(0)
+
+    def copy_to(origin, chunk, side, to):
+        return remote(
+            held.at[origin, chunk],
+            held.at[origin, chunk],
+            send_sem.at[side, origin, chunk],
+            recv_sem.at[origin, chunk],
+            member,
+            to,
+        )
+
+    def own_load(chunk):
+        return pltpu.make_async_copy(own_ref.at[chunk], held.at[z, chunk], load_sem.at[chunk])
+
+    def pass_on(origin, chunk, right):
+        copy_to(origin, chunk, 0, z).wait_recv()
+        if right:
+
+            @pl.when(z < 3)
+            def _():
+                copy_to(origin, chunk, 0, z + 1).start()
+        else:
+
+            @pl.when(z > 0)
+            def _():
+                copy_to(origin, chunk, 1, z - 1).start()
+
+    @pl.when(step == 0)
+    def _():
+        for chunk in range(chunks):
+            own_load(chunk).start()
+        barrier = pltpu.get_barrier_semaphore()
+
+        @pl.when(z > 0)
+        def _():
+            pl.semaphore_signal(
+                barrier, inc=1, device_id=(member, z - 1), device_id_type=pl.DeviceIdType.MESH
+            )
+
+        @pl.when(z < 3)
+        def _():
+            pl.semaphore_signal(
+                barrier, inc=1, device_id=(member, z + 1), device_id_type=pl.DeviceIdType.MESH
+            )
+
+        @pl.when((z == 0) | (z == 3))
+        def _():
+            pl.semaphore_wait(barrier, 1)
+
+        @pl.when((z > 0) & (z < 3))
+        def _():
+            pl.semaphore_wait(barrier, 2)
+
+        def send_own(chunk, carry):
+            own_load(chunk).wait()
+
+            @pl.when(z < 3)
+            def _():
+                copy_to(z, chunk, 0, z + 1).start()
+
+            @pl.when(z > 0)
+            def _():
+                copy_to(z, chunk, 1, z - 1).start()
+
+            return carry
+
+        lax.fori_loop(0, chunks, send_own, 0)
+
+        def near(chunk, carry):
+            @pl.when(z > 0)
+            def _():
+                pass_on(z - 1, chunk, True)
+
+            @pl.when(z < 3)
+            def _():
+                pass_on(z + 1, chunk, False)
+
+            return carry
+
+        lax.fori_loop(0, chunks, near, 0)
+
+    @pl.when(z >= 2)
+    def _():
+        pass_on(z - 2, step, True)
+
+    @pl.when(z <= 1)
+    def _():
+        pass_on(z + 2, step, False)
+
+    @pl.when(z == 3)
+    def _():
+        copy_to(0, step, 0, z).wait_recv()
+
+    @pl.when(z == 0)
+    def _():
+        copy_to(3, step, 0, z).wait_recv()
+
+    for origin in range(4):
+        spread[origin * lines : (origin + 1) * lines, :] = held[origin, step].astype(wide)
+
+    def line(number, carry):
+        weights_ref[:, pl.ds(pl.multiple_of(number * lead, lead), lead)] = spread[
+            pl.ds(number, 4, stride=lines), :
+        ].astype(low_type)
+        return carry
+
+    lax.fori_loop(0, lines, line, 0, unroll=8)
+
+    @pl.when(step == chunks - 1)
+    def _():
+        for origin in range(4):
+
+            def finish(chunk, carry):
+                @pl.when((origin <= z) & (z < 3))
+                def _():
+                    copy_to(origin, chunk, 0, z).wait_send()
+
+                @pl.when((origin >= z) & (z > 0))
+                def _():
+                    copy_to(origin, chunk, 1, z).wait_send()
+
+                return carry
+
+            lax.fori_loop(0, chunks, finish, 0)
+
+
+def spread_weights(own, piece_length):
+    chunks, lines, lead = own.shape
+    return pl.pallas_call(
+        spread_kernel,
+        grid=(chunks,),
+        in_specs=[pl.BlockSpec(memory_space=pl.ANY)],
+        out_specs=pl.BlockSpec((4, lines * lead), lambda s: (0, s)),
+        out_shape=jax.ShapeDtypeStruct((4, piece_length), low_type),
+        scratch_shapes=[
+            pltpu.VMEM((4, chunks, lines, lead), low_type),
+            pltpu.VMEM((4 * lines, lead), wide),
+            pltpu.SemaphoreType.DMA((chunks,)),
+            pltpu.SemaphoreType.DMA((2, 4, chunks)),
+            pltpu.SemaphoreType.DMA((4, chunks)),
+        ],
+        compiler_params=pltpu.CompilerParams(
+            collective_id=1, has_side_effects=True, vmem_limit_bytes=32 * 1024 * 1024
+        ),
+        cost_estimate=pl.CostEstimate(
+            flops=4 * piece_length, bytes_accessed=16 * piece_length, transcendentals=0
+        ),
+        name="spread",
+    )(own)
 
 
 def group_body(
@@ -2248,14 +2130,7 @@
     width = slice_rec // 4
     ffn_width = slice_ffn // 4
     piece_length = master_shard.shape[1]
-    member = lax.axis_index("dp")
-    chip = member // 2
-    core = member % 2
-    z = lax.axis_index("shard")
-    end = jnp.where(core == 0, z, 3 - z)
-
     mask_rows = live_mask.astype(wide)[:, None]
-    stream = tokens.astype(wide)
     grad_stream = cotangent.astype(wide) * mask_rows
 
     starts = jnp.broadcast_to(seq_start.astype(low_type)[:, None], (slots, width))
@@ -2285,7 +2160,6 @@
         ffn_down,
         (model, width, ffn_width),
     )
-    saved = (saved_p, saved_state, saved_low)
     ffn_in = ffn_in.reshape(4 * slots, model)
     all_grad_out = all_grad_out.reshape(4 * slots, model)
     sum_ffn, res_low, grad_residual, gain_sums, block_out = middle(
@@ -2296,13 +2170,12 @@
         gains,
         jnp.broadcast_to(mask_rows.astype(low_type), (slots, width)),
     )
-    res_low = res_low.reshape(4 * slots, model)
-    grad_mix, mix_in_part = mix_backward(
-        mix_in, res_low, all_starts, mix_weights, saved, slots, width
-    )
-    four_mix, four_ffn, tokens_grad, gain_total = sums(
-        grad_mix,
-        mix_in_part,
+    four_mix, four_ffn, tokens_grad, gain_total = back(
+        mix_in,
+        res_low.reshape(4 * slots, model),
+        all_starts,
+        mix_weights,
+        (saved_p, saved_state, saved_low),
         sum_ffn,
         tokens,
         grad_residual,
@@ -2310,7 +2183,7 @@
         piece_length,
         width,
     )
-    piece, new_master, new_first, new_second, new_weights, bias_total = tail(
+    piece, new_master, new_first, new_second, rows, bias_total = adam(
         four_mix,
         four_ffn,
         gain_total,
@@ -2318,7 +2191,9 @@
         first_moment,
         second_moment,
         (model, width, ffn_width),
-    )
+        8,
+    )
+    new_weights = spread_weights(rows, piece_length)
     return (
         block_out,
         tokens_grad,

time: 598 us -> 559 us (0.935)
  local copies, waits for them, and re-layouts: 32.8 us -> 8.55 us
  Pallas kernels: 548 us -> 534 us
    unnamed x42 -> x11, local copies, waits for them, and re-layouts: 30 us -> 5.68 us
    pallas_call x3, Pallas kernels: 262 us -> 248 us  [the longest x1 141 us: spread_weights(): pl.pallas_call(spread_kernel, grid=(chunks,), in_specs=[pl.BlockSpec(memo...]
where the time goes in v7:
time: 559 us; the launch traced here: 551 us
  Pallas kernels  534 us (96%)
  local copies, waits for them, and re-layouts  8.55 us (2%)
  other arithmetic  7.06 us (1%)
    pallas_call x1, Pallas kernels, front(): pl.pallas_call(functools.partial(front_kernel, sizes), in_specs=[vmem] *...  152 us
    pallas_call x1, Pallas kernels, spread_weights(): pl.pallas_call(spread_kernel, grid=(chunks,), in_specs=[pl.BlockSpec(memo...  141 us
    pallas_call x1, Pallas kernels, middle(): pl.pallas_call(functools.partial(middle_kernel, (model, ffn_width)), in_s...  134 us
    pallas_call x1, Pallas kernels, back(): pl.pallas_call(functools.partial(back_kernel, sizes), in_specs=[anywhere,...  87 us
    pallas_call x1, Pallas kernels, adam(): pl.pallas_call(functools.partial(adam_kernel, (model, width, ffn_width, p...  20.5 us

profile of v7, /device:TPU:0, one launch (start us, length us, event | category | flops | bytes accessed | tf_op | source)
XLA Modules:
  0.0 551.2 jit_solution(8675469307718779169)
XLA Ops:
  0.6 0.7 convert_element_type.16
  1.3 0.1 pad.4.clone
  1.4 0.7 convert_convert_fusion
  2.1 0.7 broadcast_in_dim.9
  2.8 1.3 concatenate.10.gain_ref
  4.0 1.4 maximum_maximum_fusion.small_ref
  5.4 0.7 broadcast_in_dim.22.mask_ref
  6.2 0.1 broadcast_in_dim.8
  6.3 2.1 pad_maximum_fusion.tokens_ref
  8.4 2.2 multiply_convert_fusion.cot_ref
  10.6 152.3 %front.1 = (bf16[1024,1536]{1,0:T(8,128)(2,1)}, bf16[4,384,1664]{2,1,0:T(8,128)(2,1)}, bf16[3,1152,1536]{2,1,0:T(8,128)(2,1)}, f32[4,1024,256]{2,1,0:T(8,128)}, ...) custom-call(bf16[256,1664]{1,0:T(8,128)(2,1)} %pad_maximum_fusion.to, ...), custom_call_target="tpu_custom_call" | custom-call | flops 4831838208 | bytes 10616832 | tf_op jit(solution)/shard_map/front/pallas_call | solution.py:745
  162.9 133.7 %middle.1 = (bf16[3,288,1536]{2,1,0:T(8,128)(2,1)}, bf16[4,256,1536]{2,1,0:T(8,128)(2,1)}, f32[256,1536]{1,0:T(8,128)}, f32[8,1536]{1,0:T(8,128)}, bf16[256,1536]{1,0:T(8,128)(2,1)}) custom-call(bf16[1024,1536]{1,0:T(8,128)(2,1)} %bitcast.3, bf16[1024,1536]{1,0:T(8,128)(2,1)} %bitcast.4, bf16[3,1152,1536]{2,1,0:T(8,128)(2,1)} %get-tuple-element.36.weights_ref, ...), custom_call_target="tpu_custom_call" | custom-call | flops 32614907904 | bytes 46399488 | tf_op jit(solution)/shard_map/middle/pallas_call | solution.py:1081
  296.6 0.0 copy-start
  296.6 87.0 %back.1 = (bf16[4,384,1664]{2,1,0:T(8,128)(2,1)}, bf16[4,3,288,1536]{3,2,1,0:T(8,128)(2,1)}, bf16[256,1536]{1,0:T(8,128)(2,1)}, f32[8,384]{1,0:T(8,128)}) custom-call(bf16[1024,1536]{1,0:T(8,128)(2,1)} %get-tuple-element.40.x_hbm, bf16[1024,1536]{1,0:T(8,128)(2,1)} %bitcast.5, bf16[1024,128]{1,0:T(8,128)(2,1)} %get-tuple-element.42.starts_ref, ...), custom_call_target="tpu_custom_call" | custom-call | flops 10468982784 | bytes 20447232 | tf_op jit(solution)/shard_map/back/pallas_call | solution.py:1678
  383.7 0.0 copy-done
  383.7 0.0 copy-start.1
  383.7 0.7 copy-done.1
  384.4 20.5 %adam.1 = (f32[1,975456]{1,0:T(1,128)}, f32[1,975456]{1,0:T(1,128)}, f32[1,975456]{1,0:T(1,128)}, f32[1,975456]{1,0:T(1,128)}, bf16[8,960,128]{2,1,0:T(8,128)(2,1)S(1)}, /*index=5*/f32[2,512]{1,0:T(2,128)}) custom-call(bf16[4,384,1664]{2,1,0:T(8,128)(2,1)} %get-tuple-element.51.mix_ref, bf16[4,3,288,1536]{3,2,1,0:T(8,128)(2,1)} %get-tuple-element.52.ffn_ref, ...), custom_call_target="tpu_custom_call" | custom-call | flops 19509120 | bytes 39018240 | tf_op jit(solution)/shard_map/adam/pallas_call | solution.py:1926
  404.8 0.0 copy-start.2
  404.8 0.0 copy-start.3
  404.9 140.9 %spread.1 = bf16[4,975456]{1,0:T(4,128)(2,1)S(1)} custom-call(bf16[8,960,128]{2,1,0:T(8,128)(2,1)S(1)} %get-tuple-element.58.own_ref), custom_call_target="tpu_custom_call" | custom-call | flops 3901824 | bytes 15607296 | tf_op jit(solution)/shard_map/spread/pallas_call | solution.py:2086
  545.8 0.0 copy-done.2
  545.8 0.9 copy.27
  546.7 0.0 copy-done.3
  546.7 0.9 copy.28
  547.5 3.2 copy.29
  (1 shorter events, 0.0 us)
Async XLA Ops:
  296.6 87.0 %copy-start = (f32[1,975456]{1,0:T(1,128)S(1)}, f32[1,975456]{1,0:T(1,128)}, u32[]{:S(2)}) copy-start(f32[1,975456]{1,0:T(1,128)} %master_ref.1) | copy-start | bytes 11705476
  383.7 0.7 copy-start.1
  404.8 140.9 %copy-start.2 = (bf16[256,1536]{1,0:T(8,128)(2,1)S(1)}, bf16[256,1536]{1,0:T(8,128)(2,1)}, u32[]{:S(2)}) copy-start(bf16[256,1536]{1,0:T(8,128)(2,1)} %get-tuple-element.70) | copy-start | bytes 2359300
  404.8 141.8 %copy-start.3 = (bf16[256,1536]{1,0:T(8,128)(2,1)S(1)}, bf16[256,1536]{1,0:T(8,128)(2,1)}, u32[]{:S(2)}) copy-start(bf16[256,1536]{1,0:T(8,128)(2,1)} %get-tuple-element.71) | copy-start | bytes 2359300

commit v8 on v7

--- a/solution.py
+++ b/solution.py
@@ -274,7 +274,11 @@
         return remote(source, target, self.send.at[number], self.recv.at[number], to, self.z)
 
     def begin(self):
-        for number in (1, 3, 0, 2):
+        for block in (3, 1, 2):
+            self.begin_block(block)
+
+    def begin_block(self, block):
+        for number in {1: (0,), 2: (2,), 3: (1, 3)}.get(block, ()):
             self.copy(number).start()
 
     def relay(self):
@@ -806,18 +810,17 @@
     weights_ref,
     residual_ref,
     gain_ref,
-    mask_ref,
     total,
+    inner_down,
     res_low,
     res_out,
     gain_out,
-    block_out,
+    part_out,
     held,
     lows,
     paired,
     arrived,
     part_in,
-    part_out,
     in_x,
     in_y,
     in_pass,
@@ -829,8 +832,6 @@
     line_recv,
     i_send,
     i_recv,
-    o_send,
-    o_recv,
     g_send,
     g_recv,
 ):
@@ -881,17 +882,6 @@
         return carry
 
     reduce_in = Reduce(part_in, in_x, in_y, in_pass, in_last, i_send, i_recv, member, z)
-    reduce_out = Reduce(
-        part_out,
-        in_x.at[pl.ds(2, 2)],
-        in_y.at[pl.ds(2, 2)],
-        in_pass.at[pl.ds(2, 2)],
-        in_last.at[pl.ds(2, 2)],
-        o_send,
-        o_recv,
-        member,
-        z,
-    )
     gather = Gather(res_low.at[0], res_low, g_send, g_recv, member, z)
     middle = model // 2
 
@@ -934,11 +924,13 @@
             own = held[at, pl.ds(2 * slot * ffn_width + (number % 2) * half_ffn, half_ffn)]
             paired[slot, at, rows] = add_low(own, paired[slot, at, rows])
 
-            @pl.when(end == 3)
-            def _():
-                line_copy(slot, number, 2).start()
-
-            if slot == 1:
+            if slot == 0 or number < 4:
+
+                @pl.when(end == 3)
+                def _():
+                    line_copy(slot, number, 2).start()
+
+            if slot == 1 and number < 4:
 
                 @pl.when(end == 0)
                 def _():
@@ -986,12 +978,14 @@
     def last_step(number):
         at, rows = chunk(number)
 
-        @pl.when(end == 1)
-        def _():
-            line_copy(1, number, 0).wait_recv()
-            line_copy(2, number, 0).wait_recv()
-            paired[1, at, rows] = summed(1, (1, 2), number)
-            out_copy(1, number).start()
+        if number < 4:
+
+            @pl.when(end == 1)
+            def _():
+                line_copy(1, number, 0).wait_recv()
+                line_copy(2, number, 0).wait_recv()
+                paired[1, at, rows] = summed(1, (1, 2), number)
+                out_copy(1, number).start()
 
         @pl.when(end == 0)
         def _():
@@ -1004,6 +998,8 @@
     lax.fori_loop(0, 4, functools.partial(block_step, split, hidden), 0)
     reduce_in.begin()
     part_grads(1, split, hidden)
+    inner_copy = pltpu.make_async_copy(paired.at[1, 2], inner_down, load_sem.at[6])
+    inner_copy.start()
     for number in range(3):
         outer_step(number)
     reduce_in.relay()
@@ -1031,21 +1027,13 @@
     gather.relay()
     inner_step(1)
     inner_step(2)
+    inner_step(3)
     gather.arrive()
-    reduce_out.begin()
-    inner_step(3)
-    inner_step(4)
-    reduce_out.relay()
-    inner_step(5)
     for number in range(6):
         last_step(number)
-    reduce_out.arrive()
-    live = mask_ref[:, 0:1].astype(wide)
-    for number in range(2):
-        at = slice(number * half, (number + 1) * half)
-        block_out[at] = (live[at] * (residual_ref[at] + reduce_out.result(number))).astype(low_type)
-
-    for sent in (reduce_in, reduce_out, gather):
+    inner_copy.wait()
+
+    for sent in (reduce_in, gather):
         sent.finish()
     for slot in range(2):
         for kind in range(3):
@@ -1056,20 +1044,26 @@
         def _():
             line_copy(0, number, 0).wait_send()
 
+        @pl.when(end == 0)
+        def _():
+            out_copy(0, number).wait()
+
+    for number in range(4):
+
         @pl.when(end > 1)
         def _():
             line_copy(1, number, 0).wait_send()
 
+        @pl.when(end == 1)
+        def _():
+            out_copy(1, number).wait()
+
         @pl.when(end == 0)
         def _():
             line_copy(2, number, 1).wait_send()
 
-        @pl.when(end < 2)
-        def _():
-            out_copy(0, number).wait()
-
-
-def middle(x, grad_out, weights, residual, gains, mask):
+
+def middle(x, grad_out, weights, residual, gains):
     rows, model = x.shape
     hidden = weights.shape[1]
     ffn_width = hidden // 4
@@ -1080,14 +1074,15 @@
     quarter = (3, ffn_width, model)
     return pl.pallas_call(
         functools.partial(middle_kernel, (model, ffn_width)),
-        in_specs=[vmem, vmem, anywhere, vmem, vmem, vmem],
-        out_specs=[anywhere] + [vmem] * 4,
+        in_specs=[vmem, vmem, anywhere, vmem, vmem],
+        out_specs=[anywhere] * 2 + [vmem] * 4,
         out_shape=[
             jax.ShapeDtypeStruct(quarter, low_type),
+            jax.ShapeDtypeStruct(quarter[1:], low_type),
             jax.ShapeDtypeStruct((4, slots, model), low_type),
             jax.ShapeDtypeStruct((slots, model), wide),
             jax.ShapeDtypeStruct((8, model), wide),
-            jax.ShapeDtypeStruct((slots, model), low_type),
+            jax.ShapeDtypeStruct((rows, model), low_type),
         ],
         scratch_shapes=[
             pltpu.VMEM(weights.shape, low_type),
@@ -1095,17 +1090,14 @@
             pltpu.VMEM((2,) + quarter, low_type),
             pltpu.VMEM((3,) + quarter, low_type),
             pltpu.VMEM((rows, model), low_type),
-            pltpu.VMEM((rows, model), low_type),
         ]
-        + [pltpu.VMEM((4, slots // 2, model), low_type)] * 4
+        + Reduce.scratch(slots, model)
         + [
-            dma((6,)),
+            dma((7,)),
             dma((2, 3)),
             dma((2, 3)),
             dma((3, 6)),
             dma((3, 6)),
-            dma((6,)),
-            dma((6,)),
             dma((6,)),
             dma((6,)),
             dma((4,)),
@@ -1120,7 +1112,7 @@
             transcendentals=rows * hidden,
         ),
         name="middle",
-    )(x, grad_out, weights, residual, gains, mask)
+    )(x, grad_out, weights, residual, gains)
 
 
 class Scatter:
@@ -1186,8 +1178,9 @@
     def small_where(self):
         return (pl.ds(2 * self.width, 16), pl.ds(self.model, self.width))
 
-    def copies(self, unit, source, target, q, act):
+    def copies(self, unit, source, target, q, act, flat=False):
         number, where, low, high = unit
+        here = where[1:] if flat else where
         first = low // self.piece_length
         last = (high - 1) // self.piece_length
         for which, to in ((0, first), (1, last)):
@@ -1197,7 +1190,7 @@
             def _():
                 act(
                     remote(
-                        source.at[where],
+                        source.at[here],
                         target.at[(q,) + where],
                         self.send_sem.at[which, number],
                         self.recv_sem.at[q, number],
@@ -1211,14 +1204,14 @@
             def _():
                 act(
                     pltpu.make_async_copy(
-                        source.at[where], target.at[(q,) + where], self.recv_sem.at[q, number]
+                        source.at[here], target.at[(q,) + where], self.recv_sem.at[q, number]
                     ),
                     False,
                 )
 
-    def each(self, unit_of, low, high, source, target, act):
+    def each(self, unit_of, low, high, source, target, act, flat=False):
         def body(number, carry):
-            self.copies(unit_of(number, self.chip), source, target, self.chip, act)
+            self.copies(unit_of(number, self.chip), source, target, self.chip, act, flat)
             return carry
 
         lax.fori_loop(low, high, body, 0)
@@ -1324,6 +1317,7 @@
     state_hbm,
     low_hbm,
     ffn_ref,
+    inner_hbm,
     tokens_ref,
     res_ref,
     gain_ref,
@@ -1349,6 +1343,8 @@
     from_y,
     passing,
     last,
+    inner,
+    inner_seen,
     gain_part,
     gain_plane,
     gain_line,
@@ -1360,6 +1356,8 @@
     line_recv,
     plane_send,
     plane_recv,
+    inner_send,
+    inner_recv,
     gain_send,
     gain_recv,
     unit_send,
@@ -1380,6 +1378,7 @@
         pltpu.make_async_copy(x_hbm, x_ref, load_sem.at[4, 0]),
         pltpu.make_async_copy(res_hbm, low_res, load_sem.at[4, 1]),
     ]
+    early = [pltpu.make_async_copy(inner_hbm, inner, load_sem.at[4, 2])]
 
     def head_loads(head):
         return [
@@ -1389,16 +1388,65 @@
             )
         ]
 
-    for copy in head_loads(order[0]) + common:
+    for copy in early + head_loads(order[0]) + common:
         copy.start()
     for head in order[1:]:
         for copy in head_loads(head):
             copy.start()
     enter(member, z)
 
+    half_ffn = ffn_width // 2
+
+    def inner_copy(kind, number, to_end):
+        at = pl.ds(number * half_ffn, half_ffn)
+        return remote(
+            inner.at[at],
+            inner_seen.at[kind, at],
+            inner_send.at[kind, number],
+            inner_recv.at[kind, number],
+            member,
+            line_place(to_end, core),
+        )
+
+    def inner_add(kinds, number):
+        at = pl.ds(number * half_ffn, half_ffn)
+        result = inner[at].astype(wide)
+        for kind in kinds:
+            inner_copy(kind, number, 0).wait_recv()
+            result = result + inner_seen[kind, at].astype(wide)
+        inner[at] = result.astype(low_type)
+
+    def inner_far(number):
+        @pl.when(end == 2)
+        def _():
+            inner_add((0,), number)
+            inner_copy(0, number, 1).start()
+
+    def inner_last():
+        @pl.when(end == 1)
+        def _():
+            inner_add((0, 1), 0)
+            inner_add((0, 1), 1)
+            scatter.each(scatter.down_unit, 0, 6, inner, ffn_out, begin, True)
+
+    for copy in early:
+        copy.wait()
+    for number in range(2):
+
+        @pl.when(end == 3)
+        def _():
+            inner_copy(0, number, 2).start()
+
+        @pl.when(end == 0)
+        def _():
+            inner_copy(1, number, 1).start()
+
     @pl.when(scatter.owner)
     def _():
         scatter.each(scatter.up_unit, 0, 2 * scatter.across, ffn_ref, ffn_out, begin)
+
+    @pl.when(end == 0)
+    def _():
         scatter.each(scatter.down_unit, 0, 6, ffn_ref, ffn_out, begin)
 
     def rows(number):
@@ -1512,16 +1560,19 @@
                 core_copy(head - 2, number).start()
         if turn == 1:
             pair_up(0)
+            inner_far(0)
         elif turn == 2:
+            inner_far(1)
             outer_step(2, 0)
             outer_step(2, 1)
         elif turn == 3:
+            inner_last()
             outer_step(2, 2)
             outer_step(1, 0)
             outer_step(1, 1)
 
-    def in_block(block, carry):
-        at = pl.ds(pl.multiple_of(block * slots, slots), slots)
+    def in_block(block):
+        at = slice(block * slots, (block + 1) * slots)
         result = jnp.zeros((slots, model), wide)
         for head in range(4):
             result = result + dot_plain(
@@ -1529,12 +1580,20 @@
                 w_ref[head, 0 : 2 * width, 0:model],
             )
         part_ref[at, :] = result.astype(low_type)
-        return carry
-
-    pair_up(1)
-    lax.fori_loop(0, 4, in_block, 0)
-    reduce.begin()
+
+    for block in (3, 1, 2, 0):
+        in_block(block)
+        reduce.begin_block(block)
+        if block == 3:
+            pair_up(1)
     outer_step(1, 2)
+    across = scatter.across
+    scatter.arrivals(scatter.up_unit, 2 * across, ffn_ref, ffn_out)
+
+    @pl.when(scatter.owner)
+    def _():
+        scatter.each(scatter.up_unit, 0, 2 * across, ffn_ref, ffn_out, finish_send)
+
     reduce.relay()
 
     for number in range(3):
@@ -1570,8 +1629,8 @@
         scale = lax.rsqrt(jnp.mean(value * value, axis=1, keepdims=True) + norm_eps)
         scaled = grad * gain
         gain_sum = gain_sum + jnp.sum(grad * value * scale, axis=0, keepdims=True)
-        inner = jnp.mean(scaled * value, axis=1, keepdims=True)
-        back = scale * scaled - value * (scale * scale * scale * inner)
+        drift = jnp.mean(scaled * value, axis=1, keepdims=True)
+        back = scale * scaled - value * (scale * scale * scale * drift)
         tokens_out[at] = (res_ref[at] + back).astype(low_type)
     gain_part[...] = jnp.concatenate([gain_sum, gain_ref[1:2], jnp.zeros((6, model), wide)], axis=0)
 
@@ -1628,8 +1687,6 @@
                 gain_out[...] += gain_seen[place]
                 line_gain(place, z).wait_send()
 
-    across = scatter.across
-    scatter.arrivals(scatter.up_unit, 2 * across, ffn_ref, ffn_out)
     scatter.arrivals(scatter.down_unit, 6, ffn_ref, ffn_out)
     scatter.arrivals(scatter.in_unit, 2 * across, total, mix_out)
     scatter.arrivals(scatter.gate_unit, 2, total, mix_out)
@@ -1638,7 +1695,6 @@
 
     @pl.when(scatter.owner)
     def _():
-        scatter.each(scatter.up_unit, 0, 2 * across, ffn_ref, ffn_out, finish_send)
         scatter.each(scatter.down_unit, 0, 6, ffn_ref, ffn_out, finish_send)
         scatter.each(scatter.in_unit, 0, 2 * across, total, mix_out, finish_send)
         scatter.each(scatter.gate_unit, 0, 2, total, mix_out, finish_send)
@@ -1646,6 +1702,16 @@
         scatter.smalls(total, mix_out, finish_send)
 
     reduce.finish()
+    for number in range(2):
+
+        @pl.when(end >= 2)
+        def _():
+            inner_copy(0, number, 0).wait_send()
+
+        @pl.when(end == 0)
+        def _():
+            inner_copy(1, number, 0).wait_send()
+
     for slot in range(2):
         for number in range(3):
             core_copy(slot, number).wait_send()
@@ -1664,7 +1730,20 @@
             line_copy(2, number, paired.at[1, rows(number)], 1).wait_send()
 
 
-def back(x, res, starts, weights, saved, ffn, tokens, residual_grad, gains, piece_length, width):
+def back(
+    x,
+    res,
+    starts,
+    weights,
+    saved,
+    ffn,
+    inner,
+    tokens,
+    residual_grad,
+    gains,
+    piece_length,
+    width,
+):
     model = tokens.shape[1]
     ffn_width = ffn.shape[1]
     sizes = (model, width, ffn_width, piece_length)
@@ -1677,7 +1756,7 @@
     held = lambda value: pltpu.VMEM(value.shape, value.dtype)
     return pl.pallas_call(
         functools.partial(back_kernel, sizes),
-        in_specs=[anywhere, anywhere, vmem] + [anywhere] * 5 + [vmem] * 3,
+        in_specs=[anywhere, anywhere, vmem] + [anywhere] * 6 + [vmem] * 3,
         out_specs=[anywhere, anywhere, vmem, vmem],
         out_shape=[
             jax.ShapeDtypeStruct(weights.shape, low_type),
@@ -1699,6 +1778,8 @@
         ]
         + Reduce.scratch(slots, model)
         + [
+            held(inner),
+            pltpu.VMEM((2,) + inner.shape, low_type),
             pltpu.VMEM((8, model), wide),
             pltpu.VMEM((8, 8, model), wide),
             pltpu.VMEM((4, 8, model // 4), wide),
@@ -1710,6 +1791,8 @@
             dma((3, 3)),
             dma((6,)),
             dma((6,)),
+            dma((2, 2)),
+            dma((2, 2)),
             dma((5,)),
             dma((12,)),
             dma((3, count)),
@@ -1722,7 +1805,18 @@
             flops=weights.size * 4 * slots * 4, bytes_accessed=weights.size * 8, transcendentals=0
         ),
         name="back",
-    )(x, res, starts, weights, *saved, ffn, tokens, residual_grad, gains)
+    )(
+        x,
+        res,
+        starts,
+        weights,
+        *saved,
+        ffn,
+        inner,
+        tokens,
+        residual_grad,
+        gains,
+    )
 
 
 def adam_kernel(
@@ -1950,11 +2044,32 @@
     )(mix, ffn, gains, master, first, second)
 
 
-def spread_kernel(own_ref, weights_ref, held, spread, load_sem, send_sem, recv_sem):
+def spread_kernel(
+    own_ref,
+    part_hbm,
+    residual_ref,
+    mask_ref,
+    weights_ref,
+    block_out,
+    held,
+    spread,
+    part,
+    from_x,
+    from_y,
+    passing,
+    last,
+    load_sem,
+    send_sem,
+    recv_sem,
+    plane_send,
+    plane_recv,
+):
     chunks, lines, lead = own_ref.shape
     member = lax.axis_index("dp")
     z = lax.axis_index("shard")
     step = pl.program_id(0)
+    reduce = Reduce(part, from_x, from_y, passing, last, plane_send, plane_recv, member, z)
+    part_load = pltpu.make_async_copy(part_hbm, part, load_sem.at[chunks])
 
     def copy_to(origin, chunk, side, to):
         return remote(
@@ -1986,7 +2101,12 @@
     def _():
         for chunk in range(chunks):
             own_load(chunk).start()
+        part_load.start()
         barrier = pltpu.get_barrier_semaphore()
+        for to in (reduce.to_x, reduce.to_y):
+            pl.semaphore_signal(
+                barrier, inc=1, device_id=(to, z), device_id_type=pl.DeviceIdType.MESH
+            )
 
         @pl.when(z > 0)
         def _():
@@ -2002,11 +2122,11 @@
 
         @pl.when((z == 0) | (z == 3))
         def _():
-            pl.semaphore_wait(barrier, 1)
+            pl.semaphore_wait(barrier, 3)
 
         @pl.when((z > 0) & (z < 3))
         def _():
-            pl.semaphore_wait(barrier, 2)
+            pl.semaphore_wait(barrier, 4)
 
         def send_own(chunk, carry):
             own_load(chunk).wait()
@@ -2022,6 +2142,8 @@
             return carry
 
         lax.fori_loop(0, chunks, send_own, 0)
+        part_load.wait()
+        reduce.begin()
 
         def near(chunk, carry):
             @pl.when(z > 0)
@@ -2035,6 +2157,17 @@
             return carry
 
         lax.fori_loop(0, chunks, near, 0)
+        reduce.relay()
+
+    @pl.when(step == 1)
+    def _():
+        reduce.arrive()
+        live = mask_ref[:, 0:1].astype(wide)
+        half = reduce.half
+        for number in range(2):
+            at = slice(number * half, (number + 1) * half)
+            block_out[at] = (live[at] * (residual_ref[at] + reduce.result(number))).astype(low_type)
+        reduce.finish()
 
     @pl.when(z >= 2)
     def _():
@@ -2081,20 +2214,33 @@
             lax.fori_loop(0, chunks, finish, 0)
 
 
-def spread_weights(own, piece_length):
+def spread_weights(own, part, residual, mask, piece_length):
     chunks, lines, lead = own.shape
+    slots, model = residual.shape
+    once = lambda value: pl.BlockSpec(
+        value.shape, lambda s: (0, 0), pipeline_mode=pl.Buffered(1)
+    )
     return pl.pallas_call(
         spread_kernel,
         grid=(chunks,),
-        in_specs=[pl.BlockSpec(memory_space=pl.ANY)],
-        out_specs=pl.BlockSpec((4, lines * lead), lambda s: (0, s)),
-        out_shape=jax.ShapeDtypeStruct((4, piece_length), low_type),
+        in_specs=[pl.BlockSpec(memory_space=pl.ANY)] * 2 + [once(residual), once(mask)],
+        out_specs=[pl.BlockSpec((4, lines * lead), lambda s: (0, s)), once(residual)],
+        out_shape=[
+            jax.ShapeDtypeStruct((4, piece_length), low_type),
+            jax.ShapeDtypeStruct(residual.shape, low_type),
+        ],
         scratch_shapes=[
             pltpu.VMEM((4, chunks, lines, lead), low_type),
             pltpu.VMEM((4 * lines, lead), wide),
-            pltpu.SemaphoreType.DMA((chunks,)),
+            pltpu.VMEM(part.shape, low_type),
+        ]
+        + Reduce.scratch(slots, model)
+        + [
+            pltpu.SemaphoreType.DMA((chunks + 1,)),
             pltpu.SemaphoreType.DMA((2, 4, chunks)),
             pltpu.SemaphoreType.DMA((4, chunks)),
+            pltpu.SemaphoreType.DMA((6,)),
+            pltpu.SemaphoreType.DMA((6,)),
         ],
         compiler_params=pltpu.CompilerParams(
             collective_id=1, has_side_effects=True, vmem_limit_bytes=32 * 1024 * 1024
@@ -2103,7 +2249,7 @@
             flops=4 * piece_length, bytes_accessed=16 * piece_length, transcendentals=0
         ),
         name="spread",
-    )(own)
+    )(own, part, residual, mask)
 
 
 def group_body(
@@ -2162,13 +2308,8 @@
     )
     ffn_in = ffn_in.reshape(4 * slots, model)
     all_grad_out = all_grad_out.reshape(4 * slots, model)
-    sum_ffn, res_low, grad_residual, gain_sums, block_out = middle(
-        ffn_in,
-        all_grad_out,
-        ffn_weights,
-        residual,
-        gains,
-        jnp.broadcast_to(mask_rows.astype(low_type), (slots, width)),
+    sum_ffn, inner_down, res_low, grad_residual, gain_sums, ffn_part = middle(
+        ffn_in, all_grad_out, ffn_weights, residual, gains
     )
     four_mix, four_ffn, tokens_grad, gain_total = back(
         mix_in,
@@ -2177,6 +2318,7 @@
         mix_weights,
         (saved_p, saved_state, saved_low),
         sum_ffn,
+        inner_down,
         tokens,
         grad_residual,
         gain_sums,
@@ -2193,7 +2335,13 @@
         (model, width, ffn_width),
         8,
     )
-    new_weights = spread_weights(rows, piece_length)
+    new_weights, block_out = spread_weights(
+        rows,
+        ffn_part,
+        residual,
+        jnp.broadcast_to(mask_rows.astype(low_type), (slots, width)),
+        piece_length,
+    )
     return (
         block_out,
         tokens_grad,

time: 559 us -> 538 us (0.962)
  Pallas kernels: 534 us -> 516 us
    pallas_call x1, Pallas kernels: 134 us -> 109 us  [middle(): pl.pallas_call(functools.partial(middle_kernel, (model, ffn_width)), in_s...]
    pallas_call x1, Pallas kernels: 141 us -> 151 us  [spread_weights(): pl.pallas_call(spread_kernel, grid=(chunks,), in_specs=[pl.BlockSpec(memo...]
where the time goes in v8:
time: 538 us; the launch traced here: 530 us
  Pallas kernels  516 us (96%)
  local copies, waits for them, and re-layouts  6.58 us (1%)
  other arithmetic  6.37 us (1%)
    pallas_call x1, Pallas kernels, front(): pl.pallas_call(functools.partial(front_kernel, sizes), in_specs=[vmem] *...  152 us
    pallas_call x1, Pallas kernels, spread_weights(): pl.pallas_call(spread_kernel, grid=(chunks,), in_specs=[pl.BlockSpec(memo...  151 us
    pallas_call x1, Pallas kernels, middle(): pl.pallas_call(functools.partial(middle_kernel, (model, ffn_width)), in_s...  109 us
    pallas_call x1, Pallas kernels, back(): pl.pallas_call(functools.partial(back_kernel, sizes), in_specs=[anywhere,...  84 us
    pallas_call x1, Pallas kernels, adam(): pl.pallas_call(functools.partial(adam_kernel, (model, width, ffn_width, p...  20.6 us

profile of v8, /device:TPU:0, one launch (start us, length us, event | category | flops | bytes accessed | tf_op | source)
XLA Modules:
  0.0 530.5 jit_solution(15738101933138353246)
XLA Ops:
  0.6 0.0 copy-start.8
  0.6 0.0 copy-start.5
  0.7 0.0 copy-start.6
  0.7 0.0 copy-start.7
  0.7 0.7 convert_convert_fusion
  1.4 2.2 multiply_convert_fusion.cot_ref
  3.6 0.7 convert_element_type.16
  4.3 0.1 broadcast_in_dim.8
  4.4 2.1 pad_maximum_fusion.tokens_ref
  6.5 0.0 copy-done.8
  6.5 0.1 pad.4.clone
  6.6 0.0 copy-done.5
  6.6 0.0 copy-done.6
  6.6 0.7 maximum_maximum_fusion.small_ref
  7.2 0.0 copy-done.7
  7.3 0.6 concatenate.10.gain_ref
  7.9 152.5 %front.1 = (bf16[1024,1536]{1,0:T(8,128)(2,1)}, bf16[4,384,1664]{2,1,0:T(8,128)(2,1)}, bf16[3,1152,1536]{2,1,0:T(8,128)(2,1)}, f32[4,1024,256]{2,1,0:T(8,128)}, ...) custom-call(bf16[256,1664]{1,0:T(8,128)(2,1)} %pad_maximum_fusion.to, ...), custom_call_target="tpu_custom_call" | custom-call | flops 4831838208 | bytes 10616832 | tf_op jit(solution)/shard_map/front/pallas_call | solution.py:749
  160.3 108.6 %middle.1 = (bf16[3,288,1536]{2,1,0:T(8,128)(2,1)}, bf16[288,1536]{1,0:T(8,128)(2,1)}, bf16[4,256,1536]{2,1,0:T(8,128)(2,1)}, f32[256,1536]{1,0:T(8,128)}, f32[8...) custom-call(bf16[1024,1536]{1,0:T(8,128)(2,1)} %bitcast.3, bf16[1024,1536]{1,0:T(8,128)(2,1)} %bitcast.4, ...), custom_call_target="tpu_custom_call" | custom-call | flops 32614907904 | bytes 46399488 | tf_op jit(solution)/shard_map/middle/pallas_call | solution.py:1075
  269.0 0.0 copy-start
  269.0 84.0 %back.1 = (bf16[4,384,1664]{2,1,0:T(8,128)(2,1)}, bf16[4,3,288,1536]{3,2,1,0:T(8,128)(2,1)}, bf16[256,1536]{1,0:T(8,128)(2,1)}, f32[8,384]{1,0:T(8,128)}) custom-call(bf16[1024,1536]{1,0:T(8,128)(2,1)} %get-tuple-element.37.x_hbm, bf16[1024,1536]{1,0:T(8,128)(2,1)} %bitcast.5, bf16[1024,128]{1,0:T(8,128)(2,1)} %get-tuple-element.44.starts_ref, ...), custom_call_target="tpu_custom_call" | custom-call | flops 10468982784 | bytes 20447232 | tf_op jit(solution)/shard_map/back/pallas_call | solution.py:1757
  352.9 0.0 copy-done
  352.9 0.0 copy-start.3
  352.9 0.7 copy-done.3
  353.6 20.6 %adam.1 = (f32[1,975456]{1,0:T(1,128)}, f32[1,975456]{1,0:T(1,128)}, f32[1,975456]{1,0:T(1,128)}, f32[1,975456]{1,0:T(1,128)}, bf16[8,960,128]{2,1,0:T(8,128)(2,1)S(1)}, /*index=5*/f32[2,512]{1,0:T(2,128)}) custom-call(bf16[4,384,1664]{2,1,0:T(8,128)(2,1)} %get-tuple-element.53.mix_ref, bf16[4,3,288,1536]{3,2,1,0:T(8,128)(2,1)} %get-tuple-element.54.ffn_ref, ...), custom_call_target="tpu_custom_call" | custom-call | flops 19509120 | bytes 39018240 | tf_op jit(solution)/shard_map/adam/pallas_call | solution.py:2020
  374.2 0.1 broadcast_in_dim.22.mask_ref
  374.3 0.0 copy-done.1
  374.3 0.0 copy-done.2
  374.4 0.0 copy-start.4
  374.4 150.7 %spread.1 = (bf16[4,975456]{1,0:T(4,128)(2,1)S(1)}, bf16[256,1536]{1,0:T(8,128)(2,1)S(1)}) custom-call(bf16[8,960,128]{2,1,0:T(8,128)(2,1)S(1)} %get-tuple-element.56.own_ref, bf16[1024,1536]{1,0:T(8,128)(2,1)S(1)} %copy-done.1, f32[256,1536]{1,0:T(8,128)S(1)} %copy-done.2, bf16[256,128]{1,0:T(8,128)(2,1)S(1)} %broadcast_in_dim.22.mask_ref), custom_call_target="tpu_custom_call" | custom-call | flops 3901824 | bytes 15607296 | tf_op jit(solution)/shard_map/spread/pallas_call | solution.py:2223
  525.1 0.9 copy.27
  526.0 0.9 copy.28
  526.9 3.2 copy.29
  (5 shorter events, 0.0 us)
Async XLA Ops:
  0.6 5.8 %copy-start.8 = (bf16[512]{0:T(512)(128)(2,1)S(1)}, bf16[512]{0:T(512)(128)(2,1)}, u32[]{:S(2)}) copy-start(bf16[512]{0:T(512)(128)(2,1)} %param.27) | copy-start | bytes 3076
  0.6 5.9 %copy-start.5 = (bf16[5,512]{1,0:T(8,128)(2,1)S(1)}, bf16[5,512]{1,0:T(8,128)(2,1)}, u32[]{:S(2)}) copy-start(bf16[5,512]{1,0:T(8,128)(2,1)} %param.25) | copy-start | bytes 15364
  0.7 5.9 %copy-start.6 = (bf16[2,512]{1,0:T(2,128)(2,1)S(1)}, bf16[2,512]{1,0:T(2,128)(2,1)}, u32[]{:S(2)}) copy-start(bf16[2,512]{1,0:T(2,128)(2,1)} %param.26) | copy-start | bytes 6148
  0.7 6.6 %copy-start.7 = (bf16[2,384]{1,0:T(2,128)(2,1)S(1)}, bf16[2,384]{1,0:T(2,128)(2,1)}, u32[]{:S(2)}) copy-start(bf16[2,384]{1,0:T(2,128)(2,1)} %param.28) | copy-start | bytes 4612
  269.0 84.0 %copy-start = (f32[1,975456]{1,0:T(1,128)S(1)}, f32[1,975456]{1,0:T(1,128)}, u32[]{:S(2)}) copy-start(f32[1,975456]{1,0:T(1,128)} %master_ref.1) | copy-start | bytes 11705476
  352.9 0.7 copy-start.3
  353.6 20.7 %copy-start.1 = (bf16[1024,1536]{1,0:T(8,128)(2,1)S(1)}, bf16[1024,1536]{1,0:T(8,128)(2,1)}, u32[]{:S(2)}) copy-start(bf16[1024,1536]{1,0:T(8,128)(2,1)} %get-tuple-element.57.part_hbm) | copy-start | bytes 9437188
  353.6 20.7 %copy-start.2 = (f32[256,1536]{1,0:T(8,128)S(1)}, f32[256,1536]{1,0:T(8,128)}, u32[]{:S(2)}) copy-start(f32[256,1536]{1,0:T(8,128)} %get-tuple-element.41.residual_ref) | copy-start | bytes 4718596
  374.4 151.6 %copy-start.4 = (bf16[256,1536]{1,0:T(8,128)(2,1)S(1)}, bf16[256,1536]{1,0:T(8,128)(2,1)}, u32[]{:S(2)}) copy-start(bf16[256,1536]{1,0:T(8,128)(2,1)} %get-tuple-element.77) | copy-start | bytes 2359300

commit v9 on v8

--- a/solution.py
+++ b/solution.py
@@ -210,6 +210,17 @@
     pl.semaphore_wait(barrier, 10)
 
 
+def quarters(value_ref, shape):
+    slots = shape[0]
+    row = lax.broadcasted_iota(jnp.int32, shape, 0)
+    result = jnp.full(shape, value_ref[3 * slots // 4], jnp.int32)
+    for number in (2, 1, 0):
+        result = jnp.where(
+            row < (number + 1) * slots // 4, value_ref[number * slots // 4], result
+        )
+    return result
+
+
 class Gather:
     def __init__(self, own, target, send, recv, member, z):
         self.own, self.target = own, target
@@ -322,10 +333,14 @@
 
 def front_kernel(
     sizes,
-    tokens_ref,
-    cot_ref,
-    gain_ref,
-    small_ref,
+    tokens_in,
+    cot_in,
+    start_ref,
+    live_ref,
+    gain_in,
+    taps_ref,
+    bias_ref,
+    decay_ref,
     in_ref,
     gate_ref,
     out_ref,
@@ -342,6 +357,9 @@
     ffn_in,
     cot_out,
     gains_out,
+    tokens_ref,
+    cot_ref,
+    gain_ref,
     tokens_all,
     raw_in,
     raw_up,
@@ -376,7 +394,7 @@
     chip, core = member // 2, member % 2
     end = z + core * (3 - 2 * z)
     other = chip * 2 + 1 - core
-    slots = cot_ref.shape[0]
+    slots = cot_in.shape[0]
     half_ffn = ffn_width // 2
     owner = core == z // 2
 
@@ -388,10 +406,6 @@
     def loads():
         found = [
             (out_ref.at[quarter], weights.at[end, pl.ds(2 * width, width), pl.ds(0, model)]),
-            (
-                small_ref.at[:, quarter],
-                weights.at[end, pl.ds(2 * width, 16), pl.ds(model, width)],
-            ),
         ]
         for kind in range(2):
             found.append((in_ref.at[kind, :, quarter], raw_in.at[kind]))
@@ -425,6 +439,13 @@
         for copy in loads():
             copy.start()
 
+    tokens_ref[:, :model] = tokens_in[...]
+    tokens_ref[:, model:] = quarters(start_ref, (slots, width)).astype(wide).astype(low_type)
+    live = quarters(live_ref, (slots, 128))[:, 0:1].astype(wide)
+    cot_ref[...] = (cot_in[...].astype(wide) * live).astype(low_type)
+    gain_ref[...] = jnp.concatenate(
+        [gain_in[...].astype(wide), jnp.zeros((14, model // 4), wide)], axis=0
+    ).astype(low_type)
     enter(member, z)
 
     gather_tokens = Gather(tokens_ref, tokens_all, g_send.at[0], g_recv.at[0], member, z)
@@ -529,7 +550,7 @@
     def turn_in(kind):
         @pl.when(owner)
         def _():
-            for copy in loads()[2 + 2 * kind : 4 + 2 * kind]:
+            for copy in loads()[1 + 2 * kind : 3 + 2 * kind]:
                 copy.wait()
 
             def turn(at, carry):
@@ -547,7 +568,7 @@
     def turn_up(kind):
         @pl.when(owner)
         def _():
-            loads()[7 + kind].wait()
+            loads()[6 + kind].wait()
 
             def turn(at, carry):
                 columns = pl.ds(pl.multiple_of(at * 256, 256), 256)
@@ -559,10 +580,16 @@
 
     @pl.when(owner)
     def _():
-        for copy in loads()[:2]:
-            copy.wait()
-        for row in range(2 * width + 16, 3 * width, 16):
-            weights[end, row : row + 16, model:] = jnp.zeros((16, width), low_type)
+        weights[end, 2 * width : 3 * width, model:] = jnp.concatenate(
+            [
+                taps_ref[:, quarter].astype(wide),
+                bias_ref[:, quarter].astype(wide),
+                decay_ref[:, quarter].astype(wide),
+                jnp.zeros((width - 8, width), wide),
+            ],
+            axis=0,
+        ).astype(low_type)
+        loads()[0].wait()
 
     start_own(m_copy, m_core, (2,))
     pass_back(m_copy, (2,))
@@ -571,7 +598,7 @@
 
     @pl.when(owner)
     def _():
-        loads()[6].wait()
+        loads()[5].wait()
         turned_copy(2).start()
 
     turn_up(0)
@@ -738,17 +765,20 @@
                 copy(1, number, 1, 0).wait_send()
 
 
-def front(tokens, cot, gains, small, in_proj, gates, out_proj, gate_up, down, sizes):
+def front(
+    tokens, cot, starts, live, gains, taps, bias, decay, in_proj, gates, out_proj, gate_up, down, sizes
+):
     model, width, ffn_width = sizes
     slots = cot.shape[0]
     rows = 4 * slots
     dma = pltpu.SemaphoreType.DMA
     vmem = pl.BlockSpec(memory_space=pltpu.VMEM)
     anywhere = pl.BlockSpec(memory_space=pl.ANY)
+    scalars = pl.BlockSpec(memory_space=pltpu.SMEM)
     window = -(-ffn_width // 128) * 128
     return pl.pallas_call(
         functools.partial(front_kernel, sizes),
-        in_specs=[vmem] * 3 + [anywhere] * 6,
+        in_specs=[vmem] * 2 + [scalars] * 2 + [vmem] * 4 + [anywhere] * 5,
         out_specs=[vmem, vmem, anywhere, vmem, vmem, vmem, vmem, vmem, vmem, anywhere, vmem],
         out_shape=[
             jax.ShapeDtypeStruct((rows, model), low_type),
@@ -764,6 +794,9 @@
             jax.ShapeDtypeStruct((8, model), wide),
         ],
         scratch_shapes=[
+            pltpu.VMEM((slots, model + width), low_type),
+            pltpu.VMEM((slots, model), low_type),
+            pltpu.VMEM((16, model // 4), low_type),
             pltpu.VMEM((4, slots, model + width), low_type),
             pltpu.VMEM((2, model, width), low_type),
             pltpu.VMEM((2, model, window), low_type),
@@ -800,13 +833,13 @@
             transcendentals=rows * 4 * width * 6,
         ),
         name="front",
-    )(tokens, cot, gains, small, in_proj, gates, out_proj, gate_up, down)
+    )(tokens, cot, starts, live, gains, taps, bias, decay, in_proj, gates, out_proj, gate_up, down)
 
 
 def middle_kernel(
     sizes,
-    x_ref,
-    go_ref,
+    x_hbm,
+    go_hbm,
     weights_ref,
     residual_ref,
     gain_ref,
@@ -816,6 +849,8 @@
     res_out,
     gain_out,
     part_out,
+    x_ref,
+    go_ref,
     held,
     lows,
     paired,
@@ -846,17 +881,25 @@
     hidden = 4 * ffn_width
     half_ffn = ffn_width // 2
 
+    split = -(-2 * ffn_width // 128) * 128
+
+    def weight_load(low, high, number):
+        at = pl.ds(low, high - low)
+        return pltpu.make_async_copy(
+            weights_ref.at[:, at], held.at[:, at], load_sem.at[number]
+        )
+
     loads = [
-        pltpu.make_async_copy(weights_ref.at[kind], held.at[kind], load_sem.at[kind])
-        for kind in range(3)
+        weight_load(0, split, 0),
+        pltpu.make_async_copy(x_hbm, x_ref, load_sem.at[1]),
+        pltpu.make_async_copy(go_hbm, go_ref, load_sem.at[2]),
+        weight_load(split, hidden, 3),
     ]
     for load in loads:
         load.start()
     enter(member, z)
-    for load in loads:
+    for load in loads[:3]:
         load.wait()
-
-    split = -(-2 * ffn_width // 128) * 128
 
     def block_step(low, high, block, carry):
         rows = pl.ds(pl.multiple_of(block * slots, slots), slots)
@@ -995,6 +1038,7 @@
 
     lax.fori_loop(0, 4, functools.partial(block_step, 0, split), 0)
     part_grads(0, 0, split)
+    loads[3].wait()
     lax.fori_loop(0, 4, functools.partial(block_step, split, hidden), 0)
     reduce_in.begin()
     part_grads(1, split, hidden)
@@ -1074,7 +1118,7 @@
     quarter = (3, ffn_width, model)
     return pl.pallas_call(
         functools.partial(middle_kernel, (model, ffn_width)),
-        in_specs=[vmem, vmem, anywhere, vmem, vmem],
+        in_specs=[anywhere] * 3 + [vmem] * 2,
         out_specs=[anywhere] * 2 + [vmem] * 4,
         out_shape=[
             jax.ShapeDtypeStruct(quarter, low_type),
@@ -1085,6 +1129,8 @@
             jax.ShapeDtypeStruct((rows, model), low_type),
         ],
         scratch_shapes=[
+            pltpu.VMEM(x.shape, low_type),
+            pltpu.VMEM(x.shape, low_type),
             pltpu.VMEM(weights.shape, low_type),
             pltpu.VMEM((3, rows, hidden), low_type),
             pltpu.VMEM((2,) + quarter, low_type),
@@ -2162,7 +2208,7 @@
     @pl.when(step == 1)
     def _():
         reduce.arrive()
-        live = mask_ref[:, 0:1].astype(wide)
+        live = quarters(mask_ref, (2 * reduce.half, 128))[:, 0:1].astype(wide)
         half = reduce.half
         for number in range(2):
             at = slice(number * half, (number + 1) * half)
@@ -2223,7 +2269,10 @@
     return pl.pallas_call(
         spread_kernel,
         grid=(chunks,),
-        in_specs=[pl.BlockSpec(memory_space=pl.ANY)] * 2 + [once(residual), once(mask)],
+        in_specs=[pl.BlockSpec(memory_space=pl.ANY)] * 2 + [
+            once(residual),
+            pl.BlockSpec(memory_space=pltpu.SMEM),
+        ],
         out_specs=[pl.BlockSpec((4, lines * lead), lambda s: (0, s)), once(residual)],
         out_shape=[
             jax.ShapeDtypeStruct((4, piece_length), low_type),
@@ -2276,10 +2325,6 @@
     width = slice_rec // 4
     ffn_width = slice_ffn // 4
     piece_length = master_shard.shape[1]
-    mask_rows = live_mask.astype(wide)[:, None]
-    grad_stream = cotangent.astype(wide) * mask_rows
-
-    starts = jnp.broadcast_to(seq_start.astype(low_type)[:, None], (slots, width))
     (
         mix_in,
         mix_weights,
@@ -2293,12 +2338,14 @@
         all_grad_out,
         gains,
     ) = front(
-        jnp.concatenate([tokens, starts], axis=1),
-        grad_stream.astype(low_type),
-        jnp.concatenate([norm_gains, jnp.zeros((14, norm_gains.shape[1]), low_type)]),
-        jnp.concatenate(
-            [conv_taps, gate_bias, decay_param[None], jnp.zeros((8, slice_rec), low_type)]
-        ),
+        tokens,
+        cotangent,
+        seq_start,
+        live_mask,
+        norm_gains,
+        conv_taps,
+        gate_bias,
+        decay_param[None],
         input_proj,
         gate_blocks,
         output_proj,
@@ -2339,7 +2386,7 @@
         rows,
         ffn_part,
         residual,
-        jnp.broadcast_to(mask_rows.astype(low_type), (slots, width)),
+        live_mask,
         piece_length,
     )
     return (

time: 538 us -> 531 us (0.987)
  other arithmetic: 6.37 us -> 0 us
where the time goes in v9:
time: 531 us; the launch traced here: 523 us
  Pallas kernels  515 us (97%)
  local copies, waits for them, and re-layouts  6.94 us (1%)
    pallas_call x1, Pallas kernels, front(): pl.pallas_call(functools.partial(front_kernel, sizes), in_specs=[vmem] *...  153 us
    pallas_call x1, Pallas kernels, spread_weights(): pl.pallas_call(spread_kernel, grid=(chunks,), in_specs=[pl.BlockSpec(memo...  151 us
    pallas_call x1, Pallas kernels, middle(): pl.pallas_call(functools.partial(middle_kernel, (model, ffn_width)), in_s...  107 us
    pallas_call x1, Pallas kernels, back(): pl.pallas_call(functools.partial(back_kernel, sizes), in_specs=[anywhere,...  83.9 us
    pallas_call x1, Pallas kernels, adam(): pl.pallas_call(functools.partial(adam_kernel, (model, width, ffn_width, p...  20.6 us

profile of v9, /device:TPU:0, one launch (start us, length us, event | category | flops | bytes accessed | tf_op | source)
XLA Modules:
  0.0 523.1 jit_solution(6867222083801980664)
XLA Ops:
  0.6 1.3 broadcast_in_dim.3.decay_ref
  1.9 152.6 %front.1 = (bf16[1024,1536]{1,0:T(8,128)(2,1)}, bf16[4,384,1664]{2,1,0:T(8,128)(2,1)}, bf16[3,1152,1536]{2,1,0:T(8,128)(2,1)}, f32[4,1024,256]{2,1,0:T(8,128)}, ...) custom-call(bf16[256,1536]{1,0:T(8,128)(2,1)} %tokens_ref.1, ...), custom_call_target="tpu_custom_call" | custom-call | flops 4831838208 | bytes 10616832 | tf_op jit(solution)/shard_map/front/pallas_call | solution.py:779
  154.5 107.1 %middle.1 = (bf16[3,288,1536]{2,1,0:T(8,128)(2,1)}, bf16[288,1536]{1,0:T(8,128)(2,1)}, bf16[4,256,1536]{2,1,0:T(8,128)(2,1)}, f32[256,1536]{1,0:T(8,128)}, f32[8...) custom-call(bf16[1024,1536]{1,0:T(8,128)(2,1)} %bitcast.4, bf16[1024,1536]{1,0:T(8,128)(2,1)} %bitcast.5, ...), custom_call_target="tpu_custom_call" | custom-call | flops 32614907904 | bytes 46399488 | tf_op jit(solution)/shard_map/middle/pallas_call | solution.py:1119
  261.6 0.0 copy-start
  261.6 83.9 %back.1 = (bf16[4,384,1664]{2,1,0:T(8,128)(2,1)}, bf16[4,3,288,1536]{3,2,1,0:T(8,128)(2,1)}, bf16[256,1536]{1,0:T(8,128)(2,1)}, f32[8,384]{1,0:T(8,128)}) custom-call(bf16[1024,1536]{1,0:T(8,128)(2,1)} %get-tuple-element.37.x_hbm, bf16[1024,1536]{1,0:T(8,128)(2,1)} %bitcast.3, bf16[1024,128]{1,0:T(8,128)(2,1)} %get-tuple-element.44.starts_ref, ...), custom_call_target="tpu_custom_call" | custom-call | flops 10468982784 | bytes 20447232 | tf_op jit(solution)/shard_map/back/pallas_call | solution.py:1803
  345.5 0.0 copy-done
  345.5 0.0 copy-start.3
  345.6 0.7 copy-done.3
  346.3 0.0 copy-start.1
  346.3 0.0 copy-start.2
  346.3 0.0 copy-start.4
  346.3 20.6 %adam.1 = (f32[1,975456]{1,0:T(1,128)}, f32[1,975456]{1,0:T(1,128)}, f32[1,975456]{1,0:T(1,128)}, f32[1,975456]{1,0:T(1,128)}, bf16[8,960,128]{2,1,0:T(8,128)(2,1)S(1)}, /*index=5*/f32[2,512]{1,0:T(2,128)}) custom-call(bf16[4,384,1664]{2,1,0:T(8,128)(2,1)} %get-tuple-element.53.mix_ref, bf16[4,3,288,1536]{3,2,1,0:T(8,128)(2,1)} %get-tuple-element.54.ffn_ref, ...), custom_call_target="tpu_custom_call" | custom-call | flops 19509120 | bytes 39018240 | tf_op jit(solution)/shard_map/adam/pallas_call | solution.py:2066
  366.8 0.0 copy-done.1
  366.9 0.0 copy-done.2
  366.9 0.0 copy-done.4
  366.9 0.0 copy-start.5
  366.9 150.8 %spread.1 = (bf16[4,975456]{1,0:T(4,128)(2,1)S(1)}, bf16[256,1536]{1,0:T(8,128)(2,1)S(1)}) custom-call(bf16[8,960,128]{2,1,0:T(8,128)(2,1)S(1)} %get-tuple-element.56.own_ref, bf16[1024,1536]{1,0:T(8,128)(2,1)S(1)} %copy-done.1, f32[256,1536]{1,0:T(8,128)S(1)} %copy-done.2, s32[256]{0:T(256)S(1)} %copy-done.4), custom_call_target="tpu_custom_call" | custom-call | flops 3901824 | bytes 15607296 | tf_op jit(solution)/shard_map/spread/pallas_call | solution.py:2269
  517.7 0.9 copy.27
  518.6 0.0 copy-done.5
  518.6 0.9 copy.28
  519.5 3.2 copy.29
Async XLA Ops:
  261.6 84.0 %copy-start = (f32[1,975456]{1,0:T(1,128)S(1)}, f32[1,975456]{1,0:T(1,128)}, u32[]{:S(2)}) copy-start(f32[1,975456]{1,0:T(1,128)} %master_ref.1) | copy-start | bytes 11705476
  345.5 0.7 copy-start.3
  346.3 20.6 %copy-start.1 = (bf16[1024,1536]{1,0:T(8,128)(2,1)S(1)}, bf16[1024,1536]{1,0:T(8,128)(2,1)}, u32[]{:S(2)}) copy-start(bf16[1024,1536]{1,0:T(8,128)(2,1)} %get-tuple-element.57.part_hbm) | copy-start | bytes 9437188
  346.3 20.6 %copy-start.2 = (f32[256,1536]{1,0:T(8,128)S(1)}, f32[256,1536]{1,0:T(8,128)}, u32[]{:S(2)}) copy-start(f32[256,1536]{1,0:T(8,128)} %get-tuple-element.41.residual_ref) | copy-start | bytes 4718596
  346.3 20.6 %copy-start.4 = (s32[256]{0:T(256)S(1)}, s32[256]{0:T(256)}, u32[]{:S(2)}) copy-start(s32[256]{0:T(256)} %mask_ref.1) | copy-start | bytes 3076
  366.9 151.7 %copy-start.5 = (bf16[256,1536]{1,0:T(8,128)(2,1)S(1)}, bf16[256,1536]{1,0:T(8,128)(2,1)}, u32[]{:S(2)}) copy-start(bf16[256,1536]{1,0:T(8,128)(2,1)} %get-tuple-element.75) | copy-start | bytes 2359300

commit v10 on v9

--- a/solution.py
+++ b/solution.py
@@ -544,7 +544,7 @@
 
             @pl.when(end == slot)
             def _():
-                for number in numbers:
+                for number in numbers[slot]:
                     pass_on(copy, core_copy, slot, number)
 
     def turn_in(kind):
@@ -562,7 +562,7 @@
 
             lax.fori_loop(0, model // 256, turn, 0)
 
-        start_own(m_copy, m_core, (kind,))
+        start_own(m_copy, m_core, ((kind,), (kind,)))
         pass_back(m_copy, (kind,))
 
     def turn_up(kind):
@@ -591,7 +591,7 @@
         ).astype(low_type)
         loads()[0].wait()
 
-    start_own(m_copy, m_core, (2,))
+    start_own(m_copy, m_core, ((2,), (2,)))
     pass_back(m_copy, (2,))
     turn_in(0)
     turn_in(1)
@@ -621,7 +621,7 @@
         for kind in range(3):
             turned_copy(kind).wait()
 
-    f_order = (4, 5, 0, 1, 2, 3)
+    f_order = ((4, 5, 0, 1, 2, 3), (4, 5, 0, 2))
     start_own(f_copy, f_core, f_order)
 
     def f_pass(slot, numbers):
@@ -636,15 +636,23 @@
 
         @pl.when(end == 2)
         def _():
-            f_pass(1, ((4,), (5, 0), (1, 2), (3,), (), ())[step])
-            f_pass(0, ((), (), (), (4,), (5, 0), (1, 2, 3))[step])
-
-        if step == 0:
-            pass_back(f_copy, f_order)
-
+            f_pass(1, ((4,), (5, 0), (2,), (), (), ())[step])
+            f_pass(0, ((), (), (4,), (5, 0), (1, 2), (3,))[step])
+
+        if step == 2:
+            pass_back(f_copy, f_order[1])
+
+    def far_step(items):
+        @pl.when(end == 3)
+        def _():
+            for slot, number in items:
+                f_copy(slot, number, 0, 0).wait_recv()
+                f_core(slot, number).start()
+
+    def near_step(step):
         @pl.when(end == 0)
         def _():
-            f_pass(1, ((), (), (), (), (), f_order)[step])
+            f_pass(1, ((), (), (), (), (), f_order[1])[step])
 
     for to in range(4):
 
@@ -710,11 +718,15 @@
         if turn == 3:
             reduce.begin()
         f_step(turn + 1)
+        near_step(turn + 1)
         if turn == 0:
             gather_cot.relay()
 
+    far_step(((1, 4), (1, 5)))
     reduce.relay()
     f_step(5)
+    near_step(5)
+    far_step(((1, 0), (1, 2)))
     reduce.arrive()
     half = slots // 2
     for number in range(2):
@@ -723,20 +735,16 @@
         residual_out[at, :] = residual
         ffn_in[0, at, :] = norm_rows(residual, gains_out[1:2]).astype(low_type)
     gather_ffn.begin()
+    far_step(((0, 4), (0, 5), (0, 0)))
     gather_ffn.relay()
 
-    @pl.when(end == 3)
-    def _():
-        for slot in (1, 0):
-            for number in f_order:
-                f_copy(slot, number, 0, 0).wait_recv()
-                f_core(slot, number).start()
+    far_step(((0, 1), (0, 2), (0, 3)))
 
     gather_ffn.arrive()
     gather_cot.arrive()
     own_cot.wait()
     for slot in range(2):
-        for number in range(6):
+        for number in f_order[slot]:
             f_core(slot, number).wait_recv()
 
     for gather in (gather_tokens, gather_cot, gather_ffn, reduce):
@@ -747,14 +755,19 @@
         def _():
             gain_copy(to, z).wait_send()
 
-    for copy, core_copy, count in ((m_copy, m_core, 3), (f_copy, f_core, 6)):
-        for number in range(count):
-            for slot in range(2):
-                core_copy(slot, number).wait_send()
+    for copy, core_copy, numbers in (
+        (m_copy, m_core, (m_order, m_order)),
+        (f_copy, f_core, f_order),
+    ):
+        for number in numbers[0]:
+            core_copy(0, number).wait_send()
 
             @pl.when(end < 3)
             def _():
                 copy(0, number, 0, 0).wait_send()
+
+        for number in numbers[1]:
+            core_copy(1, number).wait_send()
 
             @pl.when((end == 1) | (end == 2))
             def _():
@@ -861,6 +874,10 @@
     in_pass,
     in_last,
     load_sem,
+    late_send,
+    late_recv,
+    late_core_send,
+    late_core_recv,
     core_send,
     core_recv,
     line_send,
@@ -883,23 +900,96 @@
 
     split = -(-2 * ffn_width // 128) * 128
 
-    def weight_load(low, high, number):
+    late_low = 2 * ffn_width + half_ffn
+    peer_low = 3 * ffn_width + half_ffn
+
+    def weight_load(kinds, low, high, number):
         at = pl.ds(low, high - low)
         return pltpu.make_async_copy(
-            weights_ref.at[:, at], held.at[:, at], load_sem.at[number]
+            weights_ref.at[kinds, at], held.at[kinds, at], load_sem.at[number]
         )
 
     loads = [
-        weight_load(0, split, 0),
+        weight_load(pl.ds(0, 3), 0, split, 0),
         pltpu.make_async_copy(x_hbm, x_ref, load_sem.at[1]),
         pltpu.make_async_copy(go_hbm, go_ref, load_sem.at[2]),
-        weight_load(split, hidden, 3),
+        weight_load(pl.ds(0, 2), split, late_low, 3),
+        weight_load(pl.ds(0, 2), 3 * ffn_width, peer_low, 4),
+        weight_load(pl.ds(2, 1), split, hidden, 5),
     ]
+    own_late = weight_load(pl.ds(0, 2), late_low, 3 * ffn_width, 7)
+
+    def late_copy(kind, way, to_end):
+        place = held.at[kind, pl.ds(late_low, half_ffn)]
+        return remote(
+            place,
+            place,
+            late_send.at[way, kind],
+            late_recv.at[kind],
+            member,
+            line_place(to_end, core),
+        )
+
+    def late_core(kind):
+        return remote(
+            held.at[kind, pl.ds(late_low, half_ffn)],
+            held.at[kind, pl.ds(peer_low, half_ffn)],
+            late_core_send.at[kind],
+            late_core_recv.at[kind],
+            other,
+            z,
+        )
+
+    @pl.when(end == 1)
+    def _():
+        own_late.start()
+
     for load in loads:
         load.start()
     enter(member, z)
+
+    @pl.when(end == 1)
+    def _():
+        own_late.wait()
+        for kind in range(2):
+            late_copy(kind, 0, 2).start()
+            late_copy(kind, 1, 0).start()
+            late_core(kind).start()
+
     for load in loads[:3]:
         load.wait()
+
+    def late_step(block):
+        for kind in range(2):
+
+            @pl.when((end == 2) & (block == kind + 1))
+            def _():
+                late_copy(kind, 0, 0).wait_recv()
+                late_copy(kind, 0, 3).start()
+                late_core(kind).start()
+
+    def late_end():
+        for kind in range(2):
+
+            @pl.when((end == 0) | (end == 3))
+            def _():
+                late_copy(kind, 0, 0).wait_recv()
+                late_core(kind).start()
+
+        for kind in range(2):
+            late_core(kind).wait_recv()
+
+    def late_sent():
+        for kind in range(2):
+            late_core(kind).wait_send()
+
+            @pl.when((end == 1) | (end == 2))
+            def _():
+                late_copy(kind, 0, 0).wait_send()
+
+            @pl.when(end == 1)
+            def _():
+                late_copy(kind, 1, 0).wait_send()
 
     def block_step(low, high, block, carry):
         rows = pl.ds(pl.multiple_of(block * slots, slots), slots)
@@ -917,7 +1007,9 @@
         lows[0, rows, low:high] = gate_low
         lows[1, rows, low:high] = up_low
         lows[2, rows, low:high] = ffn_low
-        if low > 0:
+        if low == 0:
+            late_step(block)
+        else:
             sum_in = sum_in + part_in[rows, :].astype(wide)
             sum_out = sum_out + part_out[rows, :].astype(wide)
         part_in[rows, :] = sum_in.astype(low_type)
@@ -1038,9 +1130,12 @@
 
     lax.fori_loop(0, 4, functools.partial(block_step, 0, split), 0)
     part_grads(0, 0, split)
-    loads[3].wait()
+    for load in loads[3:]:
+        load.wait()
+    late_end()
     lax.fori_loop(0, 4, functools.partial(block_step, split, hidden), 0)
     reduce_in.begin()
+    late_sent()
     part_grads(1, split, hidden)
     inner_copy = pltpu.make_async_copy(paired.at[1, 2], inner_down, load_sem.at[6])
     inner_copy.start()
@@ -1139,7 +1234,11 @@
         ]
         + Reduce.scratch(slots, model)
         + [
-            dma((7,)),
+            dma((8,)),
+            dma((2, 2)),
+            dma((2,)),
+            dma((2,)),
+            dma((2,)),
             dma((2, 3)),
             dma((2, 3)),
             dma((3, 6)),

time: 531 us -> 513 us (0.966)
  Pallas kernels: 515 us -> 498 us
    pallas_call x1, Pallas kernels: 153 us -> 136 us  [front(): pl.pallas_call(functools.partial(front_kernel, sizes), in_specs=[vmem] *...]
where the time goes in v10:
time: 513 us; the launch traced here: 506 us
  Pallas kernels  498 us (97%)
  local copies, waits for them, and re-layouts  6.94 us (1%)
    pallas_call x1, Pallas kernels, spread_weights(): pl.pallas_call(spread_kernel, grid=(chunks,), in_specs=[pl.BlockSpec(memo...  151 us
    pallas_call x1, Pallas kernels, front(): pl.pallas_call(functools.partial(front_kernel, sizes), in_specs=[vmem] *...  136 us
    pallas_call x1, Pallas kernels, middle(): pl.pallas_call(functools.partial(middle_kernel, (model, ffn_width)), in_s...  109 us
    pallas_call x1, Pallas kernels, back(): pl.pallas_call(functools.partial(back_kernel, sizes), in_specs=[anywhere,...  82 us
    pallas_call x1, Pallas kernels, adam(): pl.pallas_call(functools.partial(adam_kernel, (model, width, ffn_width, p...  20.6 us

profile of v10, /device:TPU:0, one launch (start us, length us, event | category | flops | bytes accessed | tf_op | source)
XLA Modules:
  0.0 506.0 jit_solution(5278902907300062988)
XLA Ops:
  0.6 1.3 broadcast_in_dim.3.decay_ref
  1.9 135.7 %front.1 = (bf16[1024,1536]{1,0:T(8,128)(2,1)}, bf16[4,384,1664]{2,1,0:T(8,128)(2,1)}, bf16[3,1152,1536]{2,1,0:T(8,128)(2,1)}, f32[4,1024,256]{2,1,0:T(8,128)}, ...) custom-call(bf16[256,1536]{1,0:T(8,128)(2,1)} %tokens_ref.1, ...), custom_call_target="tpu_custom_call" | custom-call | flops 4831838208 | bytes 10616832 | tf_op jit(solution)/shard_map/front/pallas_call | solution.py:792
  137.6 108.9 %middle.1 = (bf16[3,288,1536]{2,1,0:T(8,128)(2,1)}, bf16[288,1536]{1,0:T(8,128)(2,1)}, bf16[4,256,1536]{2,1,0:T(8,128)(2,1)}, f32[256,1536]{1,0:T(8,128)}, f32[8...) custom-call(bf16[1024,1536]{1,0:T(8,128)(2,1)} %bitcast.4, bf16[1024,1536]{1,0:T(8,128)(2,1)} %bitcast.5, ...), custom_call_target="tpu_custom_call" | custom-call | flops 32614907904 | bytes 46399488 | tf_op jit(solution)/shard_map/middle/pallas_call | solution.py:1214
  246.4 0.0 copy-start
  246.4 82.0 %back.1 = (bf16[4,384,1664]{2,1,0:T(8,128)(2,1)}, bf16[4,3,288,1536]{3,2,1,0:T(8,128)(2,1)}, bf16[256,1536]{1,0:T(8,128)(2,1)}, f32[8,384]{1,0:T(8,128)}) custom-call(bf16[1024,1536]{1,0:T(8,128)(2,1)} %get-tuple-element.37.x_hbm, bf16[1024,1536]{1,0:T(8,128)(2,1)} %bitcast.3, bf16[1024,128]{1,0:T(8,128)(2,1)} %get-tuple-element.44.starts_ref, ...), custom_call_target="tpu_custom_call" | custom-call | flops 10468982784 | bytes 20447232 | tf_op jit(solution)/shard_map/back/pallas_call | solution.py:1902
  328.4 0.0 copy-done
  328.4 0.0 copy-start.3
  328.4 0.7 copy-done.3
  329.1 0.0 copy-start.1
  329.1 0.0 copy-start.2
  329.1 0.0 copy-start.4
  329.1 20.6 %adam.1 = (f32[1,975456]{1,0:T(1,128)}, f32[1,975456]{1,0:T(1,128)}, f32[1,975456]{1,0:T(1,128)}, f32[1,975456]{1,0:T(1,128)}, bf16[8,960,128]{2,1,0:T(8,128)(2,1)S(1)}, /*index=5*/f32[2,512]{1,0:T(2,128)}) custom-call(bf16[4,384,1664]{2,1,0:T(8,128)(2,1)} %get-tuple-element.53.mix_ref, bf16[4,3,288,1536]{3,2,1,0:T(8,128)(2,1)} %get-tuple-element.54.ffn_ref, ...), custom_call_target="tpu_custom_call" | custom-call | flops 19509120 | bytes 39018240 | tf_op jit(solution)/shard_map/adam/pallas_call | solution.py:2165
  349.7 0.0 copy-done.1
  349.7 0.0 copy-done.2
  349.7 0.0 copy-done.4
  349.8 0.0 copy-start.5
  349.8 150.8 %spread.1 = (bf16[4,975456]{1,0:T(4,128)(2,1)S(1)}, bf16[256,1536]{1,0:T(8,128)(2,1)S(1)}) custom-call(bf16[8,960,128]{2,1,0:T(8,128)(2,1)S(1)} %get-tuple-element.56.own_ref, bf16[1024,1536]{1,0:T(8,128)(2,1)S(1)} %copy-done.1, f32[256,1536]{1,0:T(8,128)S(1)} %copy-done.2, s32[256]{0:T(256)S(1)} %copy-done.4), custom_call_target="tpu_custom_call" | custom-call | flops 3901824 | bytes 15607296 | tf_op jit(solution)/shard_map/spread/pallas_call | solution.py:2368
  500.6 0.9 copy.27
  501.5 0.0 copy-done.5
  501.5 0.9 copy.28
  502.4 3.2 copy.29
Async XLA Ops:
  246.4 82.0 %copy-start = (f32[1,975456]{1,0:T(1,128)S(1)}, f32[1,975456]{1,0:T(1,128)}, u32[]{:S(2)}) copy-start(f32[1,975456]{1,0:T(1,128)} %master_ref.1) | copy-start | bytes 11705476
  328.4 0.7 copy-start.3
  329.1 20.6 %copy-start.1 = (bf16[1024,1536]{1,0:T(8,128)(2,1)S(1)}, bf16[1024,1536]{1,0:T(8,128)(2,1)}, u32[]{:S(2)}) copy-start(bf16[1024,1536]{1,0:T(8,128)(2,1)} %get-tuple-element.57.part_hbm) | copy-start | bytes 9437188
  329.1 20.6 %copy-start.2 = (f32[256,1536]{1,0:T(8,128)S(1)}, f32[256,1536]{1,0:T(8,128)}, u32[]{:S(2)}) copy-start(f32[256,1536]{1,0:T(8,128)} %get-tuple-element.41.residual_ref) | copy-start | bytes 4718596
  329.1 20.6 %copy-start.4 = (s32[256]{0:T(256)S(1)}, s32[256]{0:T(256)}, u32[]{:S(2)}) copy-start(s32[256]{0:T(256)} %mask_ref.1) | copy-start | bytes 3076
  349.8 151.7 %copy-start.5 = (bf16[256,1536]{1,0:T(8,128)(2,1)S(1)}, bf16[256,1536]{1,0:T(8,128)(2,1)}, u32[]{:S(2)}) copy-start(bf16[256,1536]{1,0:T(8,128)(2,1)} %get-tuple-element.75) | copy-start | bytes 2359300

commit v11 on v10

--- a/solution.py
+++ b/solution.py
@@ -697,7 +697,8 @@
 
         views = weight_views(weights.at[pl.ds(head, 1)], width)
 
-        def step_block(block, carry):
+        def step_block(count, carry):
+            block = 3 - count
             rows = pl.ds(pl.multiple_of(block * slots, slots), slots)
             position = slot_position(starts_out[rows, :])
             projected, states, mixed_low, product = mixer_step(
@@ -712,11 +713,15 @@
                 acc[rows, :] += product
             else:
                 part[rows, :] = (acc[rows, :] + product).astype(low_type)
+                for number in (3, 2, 1):
+
+                    @pl.when(block == number)
+                    def _():
+                        reduce.begin_block(number)
+
             return carry
 
         lax.fori_loop(0, 4, step_block, 0)
-        if turn == 3:
-            reduce.begin()
         f_step(turn + 1)
         near_step(turn + 1)
         if turn == 0:
@@ -1533,7 +1538,7 @@
             )
         ]
 
-    for copy in early + head_loads(order[0]) + common:
+    for copy in head_loads(order[0]) + common[1:] + early + common[:1]:
         copy.start()
     for head in order[1:]:
         for copy in head_loads(head):
@@ -1653,6 +1658,13 @@
             paired[0, rows(number)] = summed(0, (0,), number)
             line_copy(0, number, paired.at[0, rows(number)], place - 1).start()
 
+    def far_inner(number):
+        @pl.when(end == 2)
+        def _():
+            on_arrival(1, number)
+            paired[1, rows(number)] = summed(1, (1,), number)
+            line_copy(1, number, paired.at[1, rows(number)], 1).start()
+
     def share(number):
         if number < 2:
             across = scatter.across
@@ -1664,8 +1676,7 @@
             scatter.each(scatter.out_unit, 0, 4, total, mix_out, begin)
             scatter.smalls(total, mix_out, begin)
 
-    for copy in common:
-        copy.wait()
+    common[1].wait()
     for turn, head in enumerate(order):
         for copy in head_loads(head):
             copy.wait()
@@ -1689,6 +1700,8 @@
             return carry
 
         lax.fori_loop(0, 4, step_block, 0)
+        if turn == 0:
+            common[0].wait()
         grads[head, 0 : 2 * width, 0:model] = dot_slots(
             proj_grads[:, head * 2 * width : (head + 1) * 2 * width], x_ref[...]
         ).astype(low_type)
@@ -1739,15 +1752,12 @@
     def _():
         scatter.each(scatter.up_unit, 0, 2 * across, ffn_ref, ffn_out, finish_send)
 
+    far_inner(0)
+    far_inner(1)
     reduce.relay()
 
+    far_inner(2)
     for number in range(3):
-
-        @pl.when(end == 2)
-        def _():
-            on_arrival(1, number)
-            paired[1, rows(number)] = summed(1, (1,), number)
-            line_copy(1, number, paired.at[1, rows(number)], 1).start()
 
         @pl.when(end == 1)
         def _():
@@ -1966,8 +1976,8 @@
 
 def adam_kernel(
     sizes,
-    mix_ref,
-    ffn_ref,
+    mix_hbm,
+    ffn_hbm,
     gain_ref,
     master_ref,
     first_ref,
@@ -1979,6 +1989,9 @@
     rows_ref,
     bias_ref,
     grad,
+    mix_ref,
+    ffn_ref,
+    load_sem,
 ):
     model, width, ffn_width, piece_length, lines, margin = sizes
     member = lax.axis_index("dp")
@@ -1990,6 +2003,42 @@
     tiles_ffn = 4 * ffn_width // lead
     tiles_model = model // lead
 
+    def needed(first, last):
+        low = member * piece_length
+        return (first < low + piece_length) & (last > low)
+
+    up_first = 2 * model * 4 * width + 8 * width * width + 4 * width * model
+    whole_mix = pltpu.make_async_copy(mix_hbm, mix_ref, load_sem.at[0])
+    small = (pl.ds(0, 4), pl.ds(2 * width, 16), pl.ds(model, width))
+    small_mix = pltpu.make_async_copy(mix_hbm.at[small], mix_ref.at[small], load_sem.at[1])
+    need_mix = needed(0, up_first)
+    kinds = [
+        (
+            needed(
+                up_first + kind * 4 * ffn_width * model,
+                up_first + (kind + 1) * 4 * ffn_width * model,
+            ),
+            pltpu.make_async_copy(
+                ffn_hbm.at[:, kind], ffn_ref.at[:, kind], load_sem.at[2 + kind]
+            ),
+        )
+        for kind in range(3)
+    ]
+
+    @pl.when((step == 0) & need_mix)
+    def _():
+        whole_mix.start()
+
+    @pl.when((step == 0) & jnp.logical_not(need_mix))
+    def _():
+        small_mix.start()
+
+    for wanted, copy in kinds:
+
+        @pl.when((step == 0) & wanted)
+        def _():
+            copy.start()
+
     @pl.when(step == 0)
     def _():
         def clear(number, carry):
@@ -1997,6 +2046,20 @@
             return carry
 
         lax.fori_loop(0, grad.shape[0] // 256, clear, 0)
+
+        @pl.when(need_mix)
+        def _():
+            whole_mix.wait()
+
+        @pl.when(jnp.logical_not(need_mix))
+        def _():
+            small_mix.wait()
+
+        for wanted, copy in kinds:
+
+            @pl.when(wanted)
+            def _():
+                copy.wait()
 
         def place(row, count, body):
             low = member * piece_length
@@ -2167,7 +2230,7 @@
             adam_kernel, (model, width, ffn_width, piece_length, lines, margin)
         ),
         grid=(chunks,),
-        in_specs=[once(mix.shape), once(ffn.shape), once(gains.shape)] + [chunk_spec] * 3,
+        in_specs=[pl.BlockSpec(memory_space=pl.ANY)] * 2 + [once(gains.shape)] + [chunk_spec] * 3,
         out_specs=[chunk_spec] * 4
         + [
             pl.BlockSpec((1, lines, 128), lambda s: (s, 0, 0)),
@@ -2178,7 +2241,12 @@
             jax.ShapeDtypeStruct((chunks, lines, 128), low_type),
             jax.ShapeDtypeStruct((2, 4 * width), wide),
         ],
-        scratch_shapes=[pltpu.VMEM((rows, 128), wide)],
+        scratch_shapes=[
+            pltpu.VMEM((rows, 128), wide),
+            pltpu.VMEM(mix.shape, low_type),
+            pltpu.VMEM(ffn.shape, low_type),
+            pltpu.SemaphoreType.DMA((5,)),
+        ],
         compiler_params=pltpu.CompilerParams(vmem_limit_bytes=48 * 1024 * 1024),
         cost_estimate=pl.CostEstimate(
             flops=20 * piece_length,

time: 513 us -> 508 us (level)
  Pallas kernels: 498 us -> 492 us
where the time goes in v11:
time: 508 us; the launch traced here: 500 us
  Pallas kernels  492 us (97%)
  local copies, waits for them, and re-layouts  6.94 us (1%)
    pallas_call x1, Pallas kernels, spread_weights(): pl.pallas_call(spread_kernel, grid=(chunks,), in_specs=[pl.BlockSpec(memo...  150 us
    pallas_call x1, Pallas kernels, front(): pl.pallas_call(functools.partial(front_kernel, sizes), in_specs=[vmem] *...  134 us
    pallas_call x1, Pallas kernels, middle(): pl.pallas_call(functools.partial(middle_kernel, (model, ffn_width)), in_s...  108 us
    pallas_call x1, Pallas kernels, back(): pl.pallas_call(functools.partial(back_kernel, sizes), in_specs=[anywhere,...  81.4 us
    pallas_call x1, Pallas kernels, adam(): pl.pallas_call(functools.partial(adam_kernel, (model, width, ffn_width, p...  18.7 us

profile of v11, /device:TPU:0, one launch (start us, length us, event | category | flops | bytes accessed | tf_op | source)
XLA Modules:
  0.0 500.3 jit_solution(18403822981604258595)
XLA Ops:
  0.6 1.3 broadcast_in_dim.3.decay_ref
  1.9 133.6 %front.1 = (bf16[1024,1536]{1,0:T(8,128)(2,1)}, bf16[4,384,1664]{2,1,0:T(8,128)(2,1)}, bf16[3,1152,1536]{2,1,0:T(8,128)(2,1)}, f32[4,1024,256]{2,1,0:T(8,128)}, ...) custom-call(bf16[256,1536]{1,0:T(8,128)(2,1)} %tokens_ref.1, ...), custom_call_target="tpu_custom_call" | custom-call | flops 4831838208 | bytes 10616832 | tf_op jit(solution)/shard_map/front/pallas_call | solution.py:797
  135.5 107.9 %middle.1 = (bf16[3,288,1536]{2,1,0:T(8,128)(2,1)}, bf16[288,1536]{1,0:T(8,128)(2,1)}, bf16[4,256,1536]{2,1,0:T(8,128)(2,1)}, f32[256,1536]{1,0:T(8,128)}, f32[8...) custom-call(bf16[1024,1536]{1,0:T(8,128)(2,1)} %bitcast.4, bf16[1024,1536]{1,0:T(8,128)(2,1)} %bitcast.5, ...), custom_call_target="tpu_custom_call" | custom-call | flops 32614907904 | bytes 46399488 | tf_op jit(solution)/shard_map/middle/pallas_call | solution.py:1219
  243.4 0.0 copy-start
  243.4 81.4 %back.1 = (bf16[4,384,1664]{2,1,0:T(8,128)(2,1)}, bf16[4,3,288,1536]{3,2,1,0:T(8,128)(2,1)}, bf16[256,1536]{1,0:T(8,128)(2,1)}, f32[8,384]{1,0:T(8,128)}) custom-call(bf16[1024,1536]{1,0:T(8,128)(2,1)} %get-tuple-element.37.x_hbm, bf16[1024,1536]{1,0:T(8,128)(2,1)} %bitcast.3, bf16[1024,128]{1,0:T(8,128)(2,1)} %get-tuple-element.44.starts_ref, ...), custom_call_target="tpu_custom_call" | custom-call | flops 10468982784 | bytes 20447232 | tf_op jit(solution)/shard_map/back/pallas_call | solution.py:1912
  324.9 0.0 copy-done
  324.9 0.0 copy-start.3
  324.9 0.7 copy-done.3
  325.6 0.0 copy-start.1
  325.6 0.0 copy-start.2
  325.6 0.0 copy-start.4
  325.6 18.7 %adam.1 = (f32[1,975456]{1,0:T(1,128)}, f32[1,975456]{1,0:T(1,128)}, f32[1,975456]{1,0:T(1,128)}, f32[1,975456]{1,0:T(1,128)}, bf16[8,960,128]{2,1,0:T(8,128)(2,1)S(1)}, /*index=5*/f32[2,512]{1,0:T(2,128)}) custom-call(bf16[4,384,1664]{2,1,0:T(8,128)(2,1)} %get-tuple-element.53.mix_hbm, bf16[4,3,288,1536]{3,2,1,0:T(8,128)(2,1)} %get-tuple-element.54.ffn_hbm, ...), custom_call_target="tpu_custom_call" | custom-call | flops 19509120 | bytes 39018240 | tf_op jit(solution)/shard_map/adam/pallas_call | solution.py:2228
  344.3 0.0 copy-done.1
  344.4 0.0 copy-done.2
  344.4 0.0 copy-done.4
  344.4 0.0 copy-start.5
  344.4 150.5 %spread.1 = (bf16[4,975456]{1,0:T(4,128)(2,1)S(1)}, bf16[256,1536]{1,0:T(8,128)(2,1)S(1)}) custom-call(bf16[8,960,128]{2,1,0:T(8,128)(2,1)S(1)} %get-tuple-element.56.own_ref, bf16[1024,1536]{1,0:T(8,128)(2,1)S(1)} %copy-done.1, f32[256,1536]{1,0:T(8,128)S(1)} %copy-done.2, s32[256]{0:T(256)S(1)} %copy-done.4), custom_call_target="tpu_custom_call" | custom-call | flops 3901824 | bytes 15607296 | tf_op jit(solution)/shard_map/spread/pallas_call | solution.py:2436
  494.9 0.9 copy.27
  495.7 0.0 copy-done.5
  495.7 0.9 copy.28
  496.6 3.2 copy.29
Async XLA Ops:
  243.4 81.4 %copy-start = (f32[1,975456]{1,0:T(1,128)S(1)}, f32[1,975456]{1,0:T(1,128)}, u32[]{:S(2)}) copy-start(f32[1,975456]{1,0:T(1,128)} %master_ref.1) | copy-start | bytes 11705476
  324.9 0.7 copy-start.3
  325.6 18.8 %copy-start.1 = (bf16[1024,1536]{1,0:T(8,128)(2,1)S(1)}, bf16[1024,1536]{1,0:T(8,128)(2,1)}, u32[]{:S(2)}) copy-start(bf16[1024,1536]{1,0:T(8,128)(2,1)} %get-tuple-element.57.part_hbm) | copy-start | bytes 9437188
  325.6 18.8 %copy-start.2 = (f32[256,1536]{1,0:T(8,128)S(1)}, f32[256,1536]{1,0:T(8,128)}, u32[]{:S(2)}) copy-start(f32[256,1536]{1,0:T(8,128)} %get-tuple-element.41.residual_ref) | copy-start | bytes 4718596
  325.6 18.8 %copy-start.4 = (s32[256]{0:T(256)S(1)}, s32[256]{0:T(256)}, u32[]{:S(2)}) copy-start(s32[256]{0:T(256)} %mask_ref.1) | copy-start | bytes 3076
  344.4 151.4 %copy-start.5 = (bf16[256,1536]{1,0:T(8,128)(2,1)S(1)}, bf16[256,1536]{1,0:T(8,128)(2,1)}, u32[]{:S(2)}) copy-start(bf16[256,1536]{1,0:T(8,128)(2,1)} %get-tuple-element.75) | copy-start | bytes 2359300

commit v12 on v11

--- a/solution.py
+++ b/solution.py
@@ -996,7 +996,8 @@
             def _():
                 late_copy(kind, 1, 0).wait_send()
 
-    def block_step(low, high, block, carry):
+    def block_step(low, high, count, carry):
+        block = 3 - count
         rows = pl.ds(pl.multiple_of(block * slots, slots), slots)
         x = x_ref[rows, :]
         grad_out = go_ref[rows, :]
@@ -1013,11 +1014,18 @@
         lows[1, rows, low:high] = up_low
         lows[2, rows, low:high] = ffn_low
         if low == 0:
-            late_step(block)
+            late_step(count)
         else:
             sum_in = sum_in + part_in[rows, :].astype(wide)
             sum_out = sum_out + part_out[rows, :].astype(wide)
         part_in[rows, :] = sum_in.astype(low_type)
+        if low > 0:
+            for number in (3, 2, 1):
+
+                @pl.when(block == number)
+                def _():
+                    reduce_in.begin_block(number)
+
         part_out[rows, :] = sum_out.astype(low_type)
         return carry
 
@@ -1080,7 +1088,9 @@
         for kind in range(3):
             weight_grads(kind, low, high)
             core_copy(slot, kind).start()
-            if kind > 0:
+            if kind == 0 and slot == 0:
+                pair_up(0, 0)
+            elif kind > 1 - slot:
                 pair_up(slot, kind - 1)
         pair_up(slot, 2)
 
@@ -1139,7 +1149,6 @@
         load.wait()
     late_end()
     lax.fori_loop(0, 4, functools.partial(block_step, split, hidden), 0)
-    reduce_in.begin()
     late_sent()
     part_grads(1, split, hidden)
     inner_copy = pltpu.make_async_copy(paired.at[1, 2], inner_down, load_sem.at[6])
@@ -1287,14 +1296,85 @@
         self.first_down = self.first_up + 2 * self.across
         self.count = self.first_down + 6
 
-    def in_unit(self, number, q):
-        kind, at = number // self.across, number % self.across
-        low = (kind * self.model + at * 128) * self.rec
-        where = (
-            pl.ds(pl.multiple_of(kind * self.width, self.width), self.width),
-            pl.ds(pl.multiple_of(at * 128, 128), 128),
-        )
-        return self.first_in + number, where, low, low + 128 * self.rec
+    def spans(self, base, row):
+        found = []
+        for piece in range(8):
+            low = piece * self.piece_length
+            for kind in range(2):
+                start = base + kind * self.model * row
+                first = max(low - start, 0)
+                last = min(low + self.piece_length - start, self.model * row)
+                if first < last:
+                    left = first // row // 128 * 128
+                    right = -(-last // (row * 128)) * 128
+                    found.append((len(found), piece, kind, pl.ds(left, right - left)))
+        return found
+
+    def in_spans(self, kinds=(0, 1)):
+        return [
+            (self.first_in + at, piece, (pl.ds(kind * self.width, self.width), columns))
+            for at, piece, kind, columns in self.spans(0, self.rec)
+            if kind in kinds
+        ]
+
+    def up_spans(self):
+        return [
+            (self.first_up + at, piece, (kind, pl.ds(0, self.ffn_width), columns))
+            for at, piece, kind, columns in self.spans(self.up_base, self.ffn)
+        ]
+
+    def span_copies(self, spans, source, target, act):
+        for index, piece, where in spans:
+            into = target.at[(self.chip,) + where]
+
+            @pl.when(self.member != piece)
+            def _():
+                act(
+                    remote(
+                        source.at[where],
+                        into,
+                        self.send_sem.at[0, index],
+                        self.recv_sem.at[self.chip, index],
+                        piece,
+                        self.z,
+                    ),
+                    True,
+                )
+
+            @pl.when(self.member == piece)
+            def _():
+                act(
+                    pltpu.make_async_copy(
+                        source.at[where], into, self.recv_sem.at[self.chip, index]
+                    ),
+                    False,
+                )
+
+    def span_arrivals(self, spans, source, target):
+        for index, piece, where in spans:
+
+            @pl.when(self.member == piece)
+            def _():
+                for q in range(4):
+                    here = (self.chip == q) & self.owner
+                    into = target.at[(q,) + where]
+
+                    @pl.when(here)
+                    def _():
+                        pltpu.make_async_copy(
+                            source.at[where], into, self.recv_sem.at[q, index]
+                        ).wait()
+
+                    @pl.when(jnp.logical_not(here))
+                    def _():
+                        remote(
+                            source.at[where],
+                            into,
+                            self.send_sem.at[0, index],
+                            self.recv_sem.at[q, index],
+                            self.member,
+                            self.z,
+                        ).wait_recv()
 
     def gate_unit(self, kind, q):
         low = self.gate_base + (kind * 4 + q) * self.width * self.width
@@ -1312,12 +1392,6 @@
             pl.ds(0, self.model),
         )
         return self.first_out + number, where, low, low + rows * self.model
-
-    def up_unit(self, number, q):
-        kind, at = number // self.across, number % self.across
-        low = self.up_base + (kind * self.model + at * 128) * self.ffn
-        where = (kind, pl.ds(0, self.ffn_width), pl.ds(pl.multiple_of(at * 128, 128), 128))
-        return self.first_up + number, where, low, low + 128 * self.ffn
 
     def down_unit(self, number, q):
         rows = self.ffn_width // 6
@@ -1593,7 +1667,7 @@
 
     @pl.when(scatter.owner)
     def _():
-        scatter.each(scatter.up_unit, 0, 2 * scatter.across, ffn_ref, ffn_out, begin)
+        scatter.span_copies(scatter.up_spans(), ffn_ref, ffn_out, begin)
 
     @pl.when(end == 0)
     def _():
@@ -1667,10 +1741,7 @@
 
     def share(number):
         if number < 2:
-            across = scatter.across
-            scatter.each(
-                scatter.in_unit, number * across, (number + 1) * across, total, mix_out, begin
-            )
+            scatter.span_copies(scatter.in_spans((number,)), total, mix_out, begin)
             scatter.each(scatter.gate_unit, number, number + 1, total, mix_out, begin)
         else:
             scatter.each(scatter.out_unit, 0, 4, total, mix_out, begin)
@@ -1745,12 +1816,11 @@
         if block == 3:
             pair_up(1)
     outer_step(1, 2)
-    across = scatter.across
-    scatter.arrivals(scatter.up_unit, 2 * across, ffn_ref, ffn_out)
+    scatter.span_arrivals(scatter.up_spans(), ffn_ref, ffn_out)
 
     @pl.when(scatter.owner)
     def _():
-        scatter.each(scatter.up_unit, 0, 2 * across, ffn_ref, ffn_out, finish_send)
+        scatter.span_copies(scatter.up_spans(), ffn_ref, ffn_out, finish_send)
 
     far_inner(0)
     far_inner(1)
@@ -1843,7 +1913,7 @@
                 line_gain(place, z).wait_send()
 
     scatter.arrivals(scatter.down_unit, 6, ffn_ref, ffn_out)
-    scatter.arrivals(scatter.in_unit, 2 * across, total, mix_out)
+    scatter.span_arrivals(scatter.in_spans(), total, mix_out)
     scatter.arrivals(scatter.gate_unit, 2, total, mix_out)
     scatter.arrivals(scatter.out_unit, 4, total, mix_out)
     scatter.small_arrivals(total, mix_out)
@@ -1851,7 +1921,7 @@
     @pl.when(scatter.owner)
     def _():
         scatter.each(scatter.down_unit, 0, 6, ffn_ref, ffn_out, finish_send)
-        scatter.each(scatter.in_unit, 0, 2 * across, total, mix_out, finish_send)
+        scatter.span_copies(scatter.in_spans(), total, mix_out, finish_send)
         scatter.each(scatter.gate_unit, 0, 2, total, mix_out, finish_send)
         scatter.each(scatter.out_unit, 0, 4, total, mix_out, finish_send)
         scatter.smalls(total, mix_out, finish_send)

time: 508 us -> 506 us (level)
    pallas_call x1, Pallas kernels: 108 us -> 103 us  [middle(): pl.pallas_call(functools.partial(middle_kernel, (model, ffn_width)), in_s...]
where the time goes in v12:
time: 506 us; the launch traced here: 498 us
  Pallas kernels  490 us (97%)
  local copies, waits for them, and re-layouts  6.94 us (1%)
    pallas_call x1, Pallas kernels, spread_weights(): pl.pallas_call(spread_kernel, grid=(chunks,), in_specs=[pl.BlockSpec(memo...  150 us
    pallas_call x1, Pallas kernels, front(): pl.pallas_call(functools.partial(front_kernel, sizes), in_specs=[vmem] *...  134 us
    pallas_call x1, Pallas kernels, middle(): pl.pallas_call(functools.partial(middle_kernel, (model, ffn_width)), in_s...  103 us
    pallas_call x1, Pallas kernels, back(): pl.pallas_call(functools.partial(back_kernel, sizes), in_specs=[anywhere,...  85 us
    pallas_call x1, Pallas kernels, adam(): pl.pallas_call(functools.partial(adam_kernel, (model, width, ffn_width, p...  18.7 us

profile of v12, /device:TPU:0, one launch (start us, length us, event | category | flops | bytes accessed | tf_op | source)
XLA Modules:
  0.0 498.4 jit_solution(11429561783414462008)
XLA Ops:
  0.6 1.3 broadcast_in_dim.3.decay_ref
  1.9 133.6 %front.1 = (bf16[1024,1536]{1,0:T(8,128)(2,1)}, bf16[4,384,1664]{2,1,0:T(8,128)(2,1)}, bf16[3,1152,1536]{2,1,0:T(8,128)(2,1)}, f32[4,1024,256]{2,1,0:T(8,128)}, ...) custom-call(bf16[256,1536]{1,0:T(8,128)(2,1)} %tokens_ref.1, ...), custom_call_target="tpu_custom_call" | custom-call | flops 4831838208 | bytes 10616832 | tf_op jit(solution)/shard_map/front/pallas_call | solution.py:797
  135.5 102.7 %middle.1 = (bf16[3,288,1536]{2,1,0:T(8,128)(2,1)}, bf16[288,1536]{1,0:T(8,128)(2,1)}, bf16[4,256,1536]{2,1,0:T(8,128)(2,1)}, f32[256,1536]{1,0:T(8,128)}, f32[8...) custom-call(bf16[1024,1536]{1,0:T(8,128)(2,1)} %bitcast.4, bf16[1024,1536]{1,0:T(8,128)(2,1)} %bitcast.5, ...), custom_call_target="tpu_custom_call" | custom-call | flops 32614907904 | bytes 46399488 | tf_op jit(solution)/shard_map/middle/pallas_call | solution.py:1228
  238.2 0.0 copy-start
  238.2 85.0 %back.1 = (bf16[4,384,1664]{2,1,0:T(8,128)(2,1)}, bf16[4,3,288,1536]{3,2,1,0:T(8,128)(2,1)}, bf16[256,1536]{1,0:T(8,128)(2,1)}, f32[8,384]{1,0:T(8,128)}) custom-call(bf16[1024,1536]{1,0:T(8,128)(2,1)} %get-tuple-element.37.x_hbm, bf16[1024,1536]{1,0:T(8,128)(2,1)} %bitcast.3, bf16[1024,128]{1,0:T(8,128)(2,1)} %get-tuple-element.44.starts_ref, ...), custom_call_target="tpu_custom_call" | custom-call | flops 10468982784 | bytes 20447232 | tf_op jit(solution)/shard_map/back/pallas_call | solution.py:1982
  323.3 0.0 copy-done
  323.3 0.0 copy-start.3
  323.3 0.7 copy-done.3
  324.0 0.0 copy-start.1
  324.0 0.0 copy-start.2
  324.0 0.0 copy-start.4
  324.0 18.7 %adam.1 = (f32[1,975456]{1,0:T(1,128)}, f32[1,975456]{1,0:T(1,128)}, f32[1,975456]{1,0:T(1,128)}, f32[1,975456]{1,0:T(1,128)}, bf16[8,960,128]{2,1,0:T(8,128)(2,1)S(1)}, /*index=5*/f32[2,512]{1,0:T(2,128)}) custom-call(bf16[4,384,1664]{2,1,0:T(8,128)(2,1)} %get-tuple-element.53.mix_hbm, bf16[4,3,288,1536]{3,2,1,0:T(8,128)(2,1)} %get-tuple-element.54.ffn_hbm, ...), custom_call_target="tpu_custom_call" | custom-call | flops 19509120 | bytes 39018240 | tf_op jit(solution)/shard_map/adam/pallas_call | solution.py:2298
  342.7 0.0 copy-done.1
  342.8 0.0 copy-done.2
  342.8 0.0 copy-done.4
  342.8 0.0 copy-start.5
  342.8 150.2 %spread.1 = (bf16[4,975456]{1,0:T(4,128)(2,1)S(1)}, bf16[256,1536]{1,0:T(8,128)(2,1)S(1)}) custom-call(bf16[8,960,128]{2,1,0:T(8,128)(2,1)S(1)} %get-tuple-element.56.own_ref, bf16[1024,1536]{1,0:T(8,128)(2,1)S(1)} %copy-done.1, f32[256,1536]{1,0:T(8,128)S(1)} %copy-done.2, s32[256]{0:T(256)S(1)} %copy-done.4), custom_call_target="tpu_custom_call" | custom-call | flops 3901824 | bytes 15607296 | tf_op jit(solution)/shard_map/spread/pallas_call | solution.py:2506
  493.0 0.9 copy.27
  493.9 0.0 copy-done.5
  493.9 0.9 copy.28
  494.8 3.2 copy.29
Async XLA Ops:
  238.2 85.1 %copy-start = (f32[1,975456]{1,0:T(1,128)S(1)}, f32[1,975456]{1,0:T(1,128)}, u32[]{:S(2)}) copy-start(f32[1,975456]{1,0:T(1,128)} %master_ref.1) | copy-start | bytes 11705476
  323.3 0.7 copy-start.3
  324.0 18.8 %copy-start.1 = (bf16[1024,1536]{1,0:T(8,128)(2,1)S(1)}, bf16[1024,1536]{1,0:T(8,128)(2,1)}, u32[]{:S(2)}) copy-start(bf16[1024,1536]{1,0:T(8,128)(2,1)} %get-tuple-element.57.part_hbm) | copy-start | bytes 9437188
  324.0 18.8 %copy-start.2 = (f32[256,1536]{1,0:T(8,128)S(1)}, f32[256,1536]{1,0:T(8,128)}, u32[]{:S(2)}) copy-start(f32[256,1536]{1,0:T(8,128)} %get-tuple-element.41.residual_ref) | copy-start | bytes 4718596
  324.0 18.8 %copy-start.4 = (s32[256]{0:T(256)S(1)}, s32[256]{0:T(256)}, u32[]{:S(2)}) copy-start(s32[256]{0:T(256)} %mask_ref.1) | copy-start | bytes 3076
  342.8 151.1 %copy-start.5 = (bf16[256,1536]{1,0:T(8,128)(2,1)S(1)}, bf16[256,1536]{1,0:T(8,128)(2,1)}, u32[]{:S(2)}) copy-start(bf16[256,1536]{1,0:T(8,128)(2,1)} %get-tuple-element.75) | copy-start | bytes 2359300
